TPU v7x, 32 devices: a whole 2x2x4 slice. The times are simulated.
32 devices in a mesh: pipe: 2 (over core), grp: 4 (over z), dp: 4 (over y, x).
Axes of the slice: x: 2, y: 2, z: 4, core: 2. Of those that a mesh axis runs over, the one named last changes fastest.
Arguments:
- block_input: bfloat16 [2, 16, 512, 512], P(None, ('grp', 'dp')), may hold values from -6 to 6
- cotangent: bfloat16 [2, 16, 512, 512], P(None, ('grp', 'dp')), may hold values from -6 to 6
- segments: int32 [2, 16, 512], P(None, ('grp', 'dp')), may hold values from 0 to 7, never falling along the last dimension, each value on 1 to 256 neighbouring positions
- ln1_gain: float32 [2, 512], P('pipe'), may hold values from 0.5 to 1.5
- ln1_shift: float32 [2, 512], P('pipe'), may hold values from -1.25 to 1.25
- qkv_weight: bfloat16 [2, 512, 1536], P('pipe'), may hold values from -0.25 to 0.25
- qkv_bias: float32 [2, 1536], P('pipe'), may hold values from -1.25 to 1.25
- attn_weight: bfloat16 [2, 512, 512], P('pipe'), may hold values from -1.5 to 1.5
- attn_bias: float32 [2, 512], P('pipe'), may hold values from -1.25 to 1.25
- ln2_gain: float32 [2, 512], P('pipe'), may hold values from 0.5 to 1.5
- ln2_shift: float32 [2, 512], P('pipe'), may hold values from -1.25 to 1.25
- ff_in_weight: bfloat16 [2, 512, 2048], P('pipe'), may hold values from -0.25 to 0.25
- ff_in_bias: float32 [2, 2048], P('pipe'), may hold values from -1.25 to 1.25
- ff_out_weight: bfloat16 [2, 2048, 512], P('pipe'), may hold values from -0.125 to 0.125
- ff_out_bias: float32 [2, 512], P('pipe'), may hold values from -1.25 to 1.25
- prefix_embed: float32 [10, 512], replicated, may hold values from -6 to 6
- up_weight: float32 [512, 512], replicated, may hold values from -0.25 to 0.25
- up_bias: float32 [512], replicated, may hold values from -3 to 3
- out_weight: float32 [512, 2048], replicated, may hold values from -0.375 to 0.375
- out_bias: float32 [2048], replicated, may hold values from -1.75 to 1.75
Outputs:
- activations: bfloat16 [2, 2, 16, 512, 512], P('pipe', None, ('grp', 'dp'))
- input_grads: float32 [2, 2, 16, 512, 512], P('pipe', None, ('grp', 'dp'))
- grad_embed: float32 [10, 512], replicated
- grad_up_weight: float32 [512, 512], replicated
- grad_up_bias: float32 [512], replicated
- grad_out_weight: float32 [512, 2048], P(None, ('pipe', 'dp'))
- grad_out_bias: float32 [2048], P(('pipe', 'dp'))
Inputs may be any that keep to these rules, and one draw needn't show every extreme that they name: `segments`: within a packed row segment numbers never fall, and every segment holds 1 to 256 tokens.
All inputs are finite; a program needn't handle non-finite values.
Results may differ from a plain program's by a relative error of at most 0.019.
Values may be sent and summed in bfloat16 or wider, within the bound.
No kernel may reach another device: no remote copies, remote signals or barrier semaphores. Data moves between devices by JAX's collectives and lax.ppermute only.
A program may use at most 192 MiB of HBM per device.

v0:
```python
from functools import partial
import math

import jax
import jax.numpy as jnp
from jax import lax
from jax.sharding import PartitionSpec as P

D = 512
HEADS = 8
HD = 64
FF = 2048
ROT = 16
PREFIX = 10


def passed_along(shard, axis, by):
    peers = lax.axis_size(axis)
    pairs = [(i, i + by) for i in range(peers) if 0 <= i + by < peers]
    return lax.ppermute(shard, axis, pairs)


def matmul_hi(left_mat, right_mat):
    return jnp.dot(
        left_mat, right_mat, precision=lax.Precision.HIGHEST, preferred_element_type=jnp.float32
    )


def layer_norm(values, gain_vec, shift_vec):
    row_mean = jnp.mean(values, axis=-1, keepdims=True)
    centered = values - row_mean
    variance = jnp.mean(centered * centered, axis=-1, keepdims=True)
    return centered * lax.rsqrt(variance + 1e-05) * gain_vec + shift_vec


def rotate_heads(head_rows):
    half_rot = ROT // 2
    positions = jnp.arange(head_rows.shape[0]).astype(head_rows.dtype)
    inv_freq = jnp.exp(
        jnp.arange(half_rot).astype(head_rows.dtype) * (-2.0 * math.log(10000.0) / ROT)
    )
    angles = positions[:, None] * inv_freq[None, :]
    cosine = jnp.cos(angles)[:, None, :]
    sine_val = jnp.sin(angles)[:, None, :]
    lead_part = head_rows[..., :half_rot]
    tail_part = head_rows[..., half_rot:ROT]
    return jnp.concatenate(
        [
            lead_part * cosine - tail_part * sine_val,
            tail_part * cosine + lead_part * sine_val,
            head_rows[..., ROT:],
        ],
        axis=-1,
    )


def block_mask(seg_row, row_start, block_rows):
    query_pos = row_start + jnp.arange(block_rows)
    key_pos = jnp.arange(seg_row.shape[0])
    seg_query = seg_row[row_start : row_start + block_rows]
    inner_mask = (key_pos[None, :] <= query_pos[:, None]) & (seg_row[None, :] == seg_query[:, None])
    return jnp.concatenate([jnp.ones((block_rows, PREFIX), dtype=jnp.bool_), inner_mask], axis=1)


def attention_forward(queries, key_list, value_list, seg_row):
    seq_len = queries.shape[0]
    block_rows = min(512, seq_len)
    scores = jnp.einsum(
        "qhd,khd->hqk", queries, key_list, preferred_element_type=jnp.float32
    ) * HD ** (-0.5)
    scores = jnp.where(block_mask(seg_row, 0, block_rows)[None], scores, -1e30)
    row_peak = jnp.max(scores, axis=-1, keepdims=True)
    exponent = jnp.exp(scores - row_peak)
    row_total = jnp.sum(exponent, axis=-1, keepdims=True)
    probs_low = (exponent / row_total).astype(jnp.bfloat16)
    outputs = [
        jnp.einsum(
            "hqk,khd->qhd", probs_low, value_list, preferred_element_type=jnp.float32
        ).astype(jnp.bfloat16)
    ]
    totals = [(row_peak + jnp.log(row_total))[..., 0]]
    return (jnp.concatenate(outputs, axis=0), jnp.concatenate(totals, axis=1))


def attention_backward(queries, key_list, value_list, log_totals, grad_mixed, seg_row):
    seq_len = queries.shape[0]
    block_rows = min(512, seq_len)
    grad_keys = jnp.zeros(key_list.shape, jnp.float32)
    grad_values = jnp.zeros(value_list.shape, jnp.float32)
    grad_query_parts = []
    for row_start in range(0, seq_len, block_rows):
        query_block = queries[row_start : row_start + block_rows]
        grad_block = grad_mixed[row_start : row_start + block_rows]
        allowed = block_mask(seg_row, row_start, block_rows)[None]
        scores = jnp.einsum(
            "qhd,khd->hqk", query_block, key_list, preferred_element_type=jnp.float32
        ) * HD ** (-0.5)
        block_lse = log_totals[:, row_start : row_start + block_rows][:, :, None]
        probs_full = jnp.where(allowed, jnp.exp(scores - block_lse), 0.0)
        probs_low = probs_full.astype(jnp.bfloat16)
        grad_values = grad_values + jnp.einsum(
            "hqk,qhd->khd", probs_low, grad_block, preferred_element_type=jnp.float32
        )
        grad_probs = jnp.einsum(
            "qhd,khd->hqk", grad_block, value_list, preferred_element_type=jnp.float32
        )
        inner_sum = jnp.sum(probs_full * grad_probs, axis=-1, keepdims=True)
        grad_scores = (probs_full * (grad_probs - inner_sum)).astype(jnp.bfloat16)
        grad_query_parts.append(
            jnp.einsum("hqk,khd->qhd", grad_scores, key_list, preferred_element_type=jnp.float32)
            * HD ** (-0.5)
        )
        grad_keys = grad_keys + jnp.einsum(
            "hqk,qhd->khd", grad_scores, query_block, preferred_element_type=jnp.float32
        ) * HD ** (-0.5)
    return (jnp.concatenate(grad_query_parts, axis=0), grad_keys, grad_values)


def forward_layer(row_in, seg_row, prefix_keys, prefix_values, params):
    (
        gain_one,
        shift_one,
        w_qkv,
        b_qkv,
        w_attn,
        b_attn,
        gain_two,
        shift_two,
        w_in,
        bias_in,
        w_back,
        bias_back,
    ) = params
    seq_len = row_in.shape[0]
    hidden = row_in.astype(jnp.float32)
    normed_one = layer_norm(hidden, gain_one, shift_one).astype(jnp.bfloat16)
    packed = jnp.dot(normed_one, w_qkv, preferred_element_type=jnp.float32) + b_qkv
    queries = rotate_heads(packed[:, :D].reshape(seq_len, HEADS, HD)).astype(jnp.bfloat16)
    key_rows = rotate_heads(packed[:, D : 2 * D].reshape(seq_len, HEADS, HD)).astype(jnp.bfloat16)
    value_rows = packed[:, 2 * D :].reshape(seq_len, HEADS, HD).astype(jnp.bfloat16)
    key_list = jnp.concatenate([prefix_keys, key_rows], axis=0)
    value_list = jnp.concatenate([prefix_values, value_rows], axis=0)
    mixed_heads, log_totals = attention_forward(queries, key_list, value_list, seg_row)
    attn_out = (
        jnp.dot(mixed_heads.reshape(seq_len, D), w_attn, preferred_element_type=jnp.float32)
        + b_attn
    )
    normed_two = layer_norm(hidden, gain_two, shift_two).astype(jnp.bfloat16)
    before = jnp.dot(normed_two, w_in, preferred_element_type=jnp.float32) + bias_in
    activated = jax.nn.gelu(before, approximate=False).astype(jnp.bfloat16)
    result = (
        hidden
        + attn_out
        + jnp.dot(activated, w_back, preferred_element_type=jnp.float32)
        + bias_back
    )
    return (result.astype(jnp.bfloat16), (queries, key_rows, value_rows, log_totals, before))


def backward_layer(grad_out, row_in, seg_row, prefix_keys, prefix_values, kept_state, params):
    (
        gain_one,
        shift_one,
        w_qkv,
        b_qkv,
        w_attn,
        b_attn,
        gain_two,
        shift_two,
        w_in,
        bias_in,
        w_back,
        bias_back,
    ) = params
    queries, key_rows, value_rows, log_totals, before = kept_state
    seq_len = row_in.shape[0]
    hidden = row_in.astype(jnp.float32)
    grad_activated = jnp.dot(grad_out, w_back.T, preferred_element_type=jnp.float32)
    gelu_back = jax.vjp(partial(jax.nn.gelu, approximate=False), before)[1]
    grad_before = gelu_back(grad_activated)[0].astype(jnp.bfloat16)
    grad_normed_two = jnp.dot(grad_before, w_in.T, preferred_element_type=jnp.float32)
    norm_two_back = jax.vjp(partial(layer_norm, gain_vec=gain_two, shift_vec=shift_two), hidden)[1]
    grad_mixed = (
        jnp.dot(grad_out, w_attn.T, preferred_element_type=jnp.float32)
        .astype(jnp.bfloat16)
        .reshape(seq_len, HEADS, HD)
    )
    key_list = jnp.concatenate([prefix_keys, key_rows], axis=0)
    value_list = jnp.concatenate([prefix_values, value_rows], axis=0)
    grad_queries, grad_keys, grad_values = attention_backward(
        queries, key_list, value_list, log_totals, grad_mixed, seg_row
    )
    grad_q_raw = jax.vjp(rotate_heads, grad_queries)[1](grad_queries)[0]
    grad_key_part = grad_keys[PREFIX:]
    grad_k_raw = jax.vjp(rotate_heads, grad_key_part)[1](grad_key_part)[0]
    grad_packed = jnp.concatenate(
        [
            grad_q_raw.reshape(seq_len, D),
            grad_k_raw.reshape(seq_len, D),
            grad_values[PREFIX:].reshape(seq_len, D),
        ],
        axis=1,
    ).astype(jnp.bfloat16)
    grad_normed_one = jnp.dot(grad_packed, w_qkv.T, preferred_element_type=jnp.float32)
    norm_one_back = jax.vjp(partial(layer_norm, gain_vec=gain_one, shift_vec=shift_one), hidden)[1]
    grad_in = (
        grad_out.astype(jnp.float32)
        + norm_two_back(grad_normed_two)[0]
        + norm_one_back(grad_normed_one)[0]
    )
    prefix_grad = jnp.concatenate(
        [grad_keys[:PREFIX].reshape(PREFIX, D), grad_values[:PREFIX].reshape(PREFIX, D)], axis=1
    )
    return (grad_in, prefix_grad)


def local(
    block_input,
    cotangent,
    segments,
    ln1_gain,
    ln1_shift,
    qkv_weight,
    qkv_bias,
    attn_weight,
    attn_bias,
    ln2_gain,
    ln2_shift,
    ff_in_weight,
    ff_in_bias,
    ff_out_weight,
    ff_out_bias,
    prefix_embed,
    up_weight,
    up_bias,
    out_weight,
    out_bias,
):
    section_id = lax.axis_index("pipe")
    micro_count = block_input.shape[0]
    seq_len = block_input.shape[2]
    hidden_units = jnp.tanh(matmul_hi(prefix_embed, up_weight) + up_bias)
    prefix_states = matmul_hi(hidden_units, out_weight) + out_bias
    seg_rows = segments[:, 0]
    params = tuple(
        (
            array_in[0]
            for array_in in (
                ln1_gain,
                ln1_shift,
                qkv_weight,
                qkv_bias,
                attn_weight,
                attn_bias,
                ln2_gain,
                ln2_shift,
                ff_in_weight,
                ff_in_bias,
                ff_out_weight,
                ff_out_bias,
            )
        )
    )
    section_states = lax.dynamic_slice_in_dim(prefix_states, section_id * (2 * D), 2 * D, 1).astype(
        jnp.bfloat16
    )
    prefix_keys = section_states[:, :D].reshape(PREFIX, HEADS, HD)
    prefix_values = section_states[:, D:].reshape(PREFIX, HEADS, HD)

    def run_full(row_in, seg_row):
        return forward_layer(row_in, seg_row, prefix_keys, prefix_values, params)

    def skip_full(row_in, seg_row):
        return (
            jnp.zeros((seq_len, D), jnp.bfloat16),
            (
                jnp.zeros((seq_len, HEADS, HD), jnp.bfloat16),
                jnp.zeros((seq_len, HEADS, HD), jnp.bfloat16),
                jnp.zeros((seq_len, HEADS, HD), jnp.bfloat16),
                jnp.zeros((HEADS, seq_len), jnp.float32),
                jnp.zeros((seq_len, FF), jnp.float32),
            ),
        )

    received = jnp.zeros((seq_len, D), jnp.bfloat16)
    tick_inputs = []
    tick_outputs = []
    tick_kept = []
    for tick_num in range(micro_count + 1):
        micro_idx = tick_num - section_id
        active = (micro_idx >= 0) & (micro_idx < micro_count)
        clamped = jnp.clip(micro_idx, 0, micro_count - 1)
        own_row = block_input[min(tick_num, micro_count - 1), 0]
        row_in = jnp.where(section_id == 0, own_row, received)
        seg_row = lax.dynamic_index_in_dim(seg_rows, clamped, 0, keepdims=False)
        result, kept_state = lax.cond(active, run_full, skip_full, row_in, seg_row)
        tick_kept.append(kept_state)
        tick_inputs.append(row_in)
        tick_outputs.append(result)
        if tick_num < micro_count:
            received = passed_along(result, "pipe", 1)

    def by_section(early_val, later_val):
        return jnp.where(section_id == 0, early_val, later_val)

    inputs_by_micro = jnp.stack(
        [
            by_section(tick_inputs[micro_num], tick_inputs[micro_num + 1])
            for micro_num in range(micro_count)
        ]
    )
    outputs_by_micro = jnp.stack(
        [
            by_section(tick_outputs[micro_num], tick_outputs[micro_num + 1])
            for micro_num in range(micro_count)
        ]
    )
    kept_by_micro = jax.tree.map(
        lambda *leaf_list: jnp.stack(leaf_list),
        *[
            jax.tree.map(by_section, tick_kept[micro_num], tick_kept[micro_num + 1])
            for micro_num in range(micro_count)
        ]
    )

    def back_kept(grad_out, row_in, seg_row, kept_state):
        return backward_layer(
            grad_out, row_in, seg_row, prefix_keys, prefix_values, kept_state, params
        )

    def skip_kept(grad_out, row_in, seg_row, kept_state):
        return (jnp.zeros((seq_len, D), jnp.float32), jnp.zeros((PREFIX, 2 * D), jnp.float32))

    received_grad = jnp.zeros((seq_len, D), jnp.bfloat16)
    prefix_total = jnp.zeros((PREFIX, 2 * D), jnp.float32)
    tick_grads = []
    for tick_num in range(micro_count + 1):
        micro_idx = tick_num - 1 + section_id
        active = (micro_idx >= 0) & (micro_idx < micro_count)
        clamped = jnp.clip(micro_idx, 0, micro_count - 1)
        own_cot = cotangent[min(tick_num, micro_count - 1), 0]
        grad_out = jnp.where(section_id == 1, own_cot, received_grad)
        row_in = lax.dynamic_index_in_dim(inputs_by_micro, clamped, 0, keepdims=False)
        seg_row = lax.dynamic_index_in_dim(seg_rows, clamped, 0, keepdims=False)
        kept_state = jax.tree.map(
            partial(lax.dynamic_index_in_dim, index=clamped, axis=0, keepdims=False), kept_by_micro
        )
        grad_in, prefix_grad = lax.cond(
            active, back_kept, skip_kept, grad_out, row_in, seg_row, kept_state
        )
        prefix_total = prefix_total + prefix_grad
        tick_grads.append(grad_in)
        if tick_num < micro_count:
            received_grad = passed_along(grad_in.astype(jnp.bfloat16), "pipe", -1)
    grads_by_micro = jnp.stack(
        [
            jnp.where(section_id == 1, tick_grads[micro_num], tick_grads[micro_num + 1])
            for micro_num in range(micro_count)
        ]
    )
    dp_index = lax.axis_index("dp")
    col_width = 2 * D // lax.axis_size("dp")
    local_cols = lax.psum_scatter(prefix_total, "dp", scatter_dimension=1, tiled=True)
    local_cols = lax.psum(local_cols, "grp")
    grad_out_weight = matmul_hi(hidden_units.T, local_cols)
    grad_out_bias = jnp.sum(local_cols, axis=0)
    out_cols = lax.dynamic_slice_in_dim(
        out_weight, section_id * (2 * D) + dp_index * col_width, col_width, 1
    )
    hidden_part = matmul_hi(local_cols, out_cols.T)
    hidden_grad = lax.psum(hidden_part, ("pipe", "dp"))
    grad_pre = hidden_grad * (1.0 - hidden_units * hidden_units)
    grad_up_weight = matmul_hi(prefix_embed.T, grad_pre)
    grad_up_bias = jnp.sum(grad_pre, axis=0)
    grad_embed = matmul_hi(grad_pre, up_weight.T)
    activations = outputs_by_micro[None, :, None]
    input_grads = grads_by_micro[None, :, None]
    return (
        activations,
        input_grads,
        grad_embed,
        grad_up_weight,
        grad_up_bias,
        grad_out_weight,
        grad_out_bias,
    )


def solution(mesh):
    return jax.shard_map(
        local,
        mesh=mesh,
        in_specs=(
            P(None, ("grp", "dp"), None, None),
            P(None, ("grp", "dp"), None, None),
            P(None, ("grp", "dp"), None),
            P("pipe", None),
            P("pipe", None),
            P("pipe", None, None),
            P("pipe", None),
            P("pipe", None, None),
            P("pipe", None),
            P("pipe", None),
            P("pipe", None),
            P("pipe", None, None),
            P("pipe", None),
            P("pipe", None, None),
            P("pipe", None),
            P(),
            P(),
            P(),
            P(),
            P(),
        ),
        out_specs=(
            P("pipe", None, ("grp", "dp"), None, None),
            P("pipe", None, ("grp", "dp"), None, None),
            P(),
            P(),
            P(),
            P(None, ("pipe", "dp")),
            P(("pipe", "dp")),
        ),
        check_vma=False,
    )
```

profile of v0, /device:TPU:0, one launch (start us, length us, event | category | flops | bytes accessed | tf_op | source)
XLA Modules:
  0.0 516.0 jit_solution(15525232900893411581)
XLA Ops:
  10.4 4.3 fusion.604
  16.2 54.0 %conditional.6 = (bf16[512,512]{1,0:T(8,128)(2,1)}, bf16[512,8,64]{0,2,1:T(8,128)(2,1)}, bf16[512,8,64]{0,2,1:T(8,128)(2,1)}, bf16[512,8,64]{0,2,1:T(8,128)(2,1)...) conditional(s32[]{:T(128)} %convert_element_type.537, () %tuple.74, (bf16[512,512]{1,0:T(8,128)(2,1)S(1)}, ...), branch_computations={%region_0.1_spmd, %region_1.6_spmd} | conditional | flops 3878450176 | bytes 134584976 | solution.py:296
  47.8 6.5 %fusion.353 = bf16[8,64,512]{2,1,0:T(8,128)(2,1)S(1)} fusion(f32[8,512,522]{1,2,0:T(8,128)} %copy-done.3, f32[8,512]{1,0:T(8,128)S(1)} %fusion.336, f32[8,512]{1,0:T(8,128)S(1)} %get-tuple-element.1324, pred[512,522]{0,1:T(8,128)(4,1)S(1)} %copy-done.30, bf16[512,8,64]{0,2,1:T(8,128)(2,1)} %bitcast.2, bf16[10,8,64]{0,2,1:T(8,128)(2,1)} %copy.129), kind=kOutput, calls=%fused_computation.470 | convolution fusion | flops 285700096 | bytes 9911296 | tf_op jit(solution)/shard_map/cond/branch_1_fun/hqk,khd->qhd/dot_general | solution.py:77
  57.7 10.9 %fusion.348 = f32[512,512]{1,0:T(8,128)S(1)} fusion(bf16[2048,512]{1,0:T(8,128)(2,1)S(1)} %copy-done.70, f32[512,2048]{1,0:T(8,128)} %convolution_add_fusion.1), kind=kOutput, calls=%fused_computation.462 | convolution fusion | flops 1141899264 | bytes 7340032 | tf_op jit(solution)/shard_map/cond/branch_1_fun/dot_general | solution.py:154
  74.2 54.7 %conditional.7 = (bf16[512,512]{1,0:T(8,128)(2,1)}, bf16[512,8,64]{0,2,1:T(8,128)(2,1)}, bf16[512,8,64]{0,2,1:T(8,128)(2,1)}, bf16[512,8,64]{0,2,1:T(8,128)(2,1)...) conditional(s32[]{:T(128)} %convert_element_type.539, () %tuple.76, (bf16[512,512]{1,0:T(8,128)(2,1)S(1)}, ...), branch_computations={%region_6.7_spmd, %region_7.12_spmd} | conditional | flops 3878450176 | bytes 134601392 | solution.py:296
  106.3 6.5 %fusion.437 = bf16[8,64,512]{2,1,0:T(8,128)(2,1)S(1)} fusion(f32[8,512,522]{1,2,0:T(8,128)} %copy-done.4, f32[8,512]{1,0:T(8,128)S(1)} %fusion.420, f32[8,512]{1,0:T(8,128)S(1)} %get-tuple-element.1338, pred[512,522]{0,1:T(8,128)(4,1)S(1)} %copy-done.32, bf16[512,8,64]{0,2,1:T(8,128)(2,1)} %bitcast.15, bf16[10,8,64]{0,2,1:T(8,128)(2,1)} %copy.131), kind=kOutput, calls=%fused_computation.587 | convolution fusion | flops 285700096 | bytes 9911296 | tf_op jit(solution)/shard_map/cond/branch_1_fun/hqk,khd->qhd/dot_general | solution.py:77
  116.4 11.1 %fusion.432 = f32[512,512]{1,0:T(8,128)S(1)} fusion(bf16[2048,512]{1,0:T(8,128)(2,1)S(1)} %copy-done.71, f32[512,2048]{1,0:T(8,128)} %convolution_add_fusion.4), kind=kOutput, calls=%fused_computation.579 | convolution fusion | flops 1141899264 | bytes 7340032 | tf_op jit(solution)/shard_map/cond/branch_1_fun/dot_general | solution.py:154
  134.6 10.2 %conditional.8 = (bf16[512,512]{1,0:T(8,128)(2,1)}, bf16[512,8,64]{0,2,1:T(8,128)(2,1)}, bf16[512,8,64]{0,2,1:T(8,128)(2,1)}, bf16[512,8,64]{0,2,1:T(8,128)(2,1)...) conditional(s32[]{:T(128)} %convert_element_type.540, () %tuple.78, (bf16[512,512]{1,0:T(8,128)(2,1)S(1)}, ...), branch_computations={%region_12.13_spmd, %region_13.18_spmd} | conditional | flops 3878450176 | bytes 134044168 | solution.py:296
  150.8 4.8 select_bitcast_fusion.1
  155.7 3.9 pad_maximum_fusion.18
  160.4 7.0 %conditional.9 = (f32[512,512]{0,1:T(8,128)}, f32[10,1024]{1,0:T(8,128)}) conditional(s32[]{:T(128)} %convert_element_type.541, () %tuple.80, (bf16[2,1,512,512]{3,2,1,0:T(8,128)(2,1)}, pred[512,512]{1,0:T(32,128)(4,1)}, bf16[]{:T(256)}, s32[]{:T(128)}, f32[2,512,2048]{2,1,0:T(8,128)}, /*index=5*/bf16[2048,512]{1,0:T(8,128)(2,1)}, ...), branch_computations={%region_18.19_spmd, %region_19.27_spmd} | conditional | flops 4719746048 | bytes 179329520 | solution.py:348
  174.9 105.2 %collective-permute-done.2 = bf16[512,512]{0,1:T(8,128)(2,1)} collective-permute-done((bf16[512,512]{0,1:T(8,128)(2,1)}, bf16[512,512]{0,1:T(8,128)(2,1)}, u32[]{:S(2)}, u32[]{:S(2)}) %collective-permute-start.2) | collective-permute-done | bytes 524320 | tf_op jit(solution)/shard_map/ppermute | solution.py:20
  280.1 74.9 %conditional.10 = (f32[512,512]{0,1:T(8,128)}, f32[10,1024]{1,0:T(8,128)}) conditional(s32[]{:T(128)} %convert_element_type.542, () %tuple.82, (pred[512,512]{1,0:T(32,128)(4,1)}, bf16[512,512]{0,1:T(8,128)(2,1)}, bf16[512,512]{0,1:T(8,128)(2,1)}, s32[]{:T(128)}, f32[2,512,2048]{2,1,0:T(8,128)}, /*index=5*/bf16[2048,512]{1,0:T(8,128)(2,1)}, ...), branch_computations={%region_27.28_spmd, %region_28.36_spmd} | conditional | flops 4719221760 | bytes 178427408 | solution.py:348
  283.2 6.8 %fusion.179 = f32[8,512,522]{1,2,0:T(8,128)} fusion(bf16[2,512,8,64]{1,3,2,0:T(8,128)(2,1)S(1)} %get-tuple-element.801, s32[]{:T(128)S(6)} %min.26, bf16[512,8,64]{0,2,1:T(8,128)(2,1)} %get-tuple-element.1297, bf16[10,8,64]{0,2,1:T(8,128)(2,1)S(1)} %copy.143), kind=kOutput, calls=%fused_computation.224 | convolution fusion | flops 274747392 | bytes 9732100 | tf_op jit(solution)/shard_map/cond/branch_1_fun/qhd,khd->hqk/dot_general | solution.py:95
  297.9 7.1 %multiply_reduce_fusion.1 = (f32[8,512]{1,0:T(8,128)S(1)}, f32[8,512,522]{1,2,0:T(8,128)S(1)}) fusion(f32[8,512,522]{1,2,0:T(8,128)} %fusion.179, f32[8,512]{1,0:T(8,128)S(1)} %dynamic-slice_bitcast_fusion.5, pred[512,522]{0,1:T(8,128)(4,1)} %concatenate.126, bf16[512,8,64]{0,2,1:T(8,128)(2,1)} %bitcast.615, bf16[512,8,64]{0,2,1:T(8,128)(2,1)} %get-tuple-element.1296, ...), kind=kOutput, calls=%fused_computation.148 | convolution fusion | flops 285433856 | bytes 18463744 | tf_op jit(solution)/shard_map/cond/branch_1_fun/qhd,khd->hqk/dot_general | solution.py:104
  313.4 5.5 %fusion.154 = f32[522,8,64]{0,2,1:T(8,128)S(1)} fusion(bf16[512,8,64]{0,2,1:T(8,128)(2,1)} %bitcast.616, f32[8,512,522]{1,2,0:T(8,128)} %fusion.179, f32[8,512]{1,0:T(8,128)S(1)} %dynamic-slice_bitcast_fusion.5, pred[512,522]{0,1:T(8,128)(4,1)} %concatenate.126), kind=kOutput, calls=%fused_computation.195 | convolution fusion | flops 282230784 | bytes 10429440 | tf_op jit(solution)/shard_map/cond/branch_1_fun/hqk,qhd->khd/dot_general | solution.py:101
  332.8 16.5 %fusion.171 = (f32[512]{0:T(512)S(1)}, f32[512]{0:T(512)S(1)}, f32[512]{0:T(512)S(1)}, f32[512,512]{0,1:T(8,128)}) fusion(f32[512]{0:T(512)S(1)} %broadcast_multiply_fusion.1, bf16[2,512,512]{1,2,0:T(8,128)(2,1)} %copy.142, s32[]{:T(128)S(6)} %min.26, f32[512,512]{0,1:T(8,128)} %fusion.158, f32[512]{0:T(512)S(1)} %bitcast.682, ...), kind=kOutput, calls=%fused_computation.210 | convolution fusion | flops 2225338880 | bytes 11545600 | tf_op jit(solution)/shard_map/cond/branch_1_fun/dot_general | solution.py:181
  365.9 61.1 %conditional.11 = (f32[10,1024]{1,0:T(8,128)S(1)}, f32[512,512]{1,0:T(8,128)}) conditional(s32[]{:T(128)} %convert_element_type.544, () %tuple.84, (pred[512,512]{1,0:T(32,128)(4,1)}, bf16[512,512]{0,1:T(8,128)(2,1)}, bf16[512,512]{0,1:T(8,128)(2,1)}, s32[]{:T(128)}, f32[2,512,2048]{2,1,0:T(8,128)}, /*index=5*/bf16[2048,512]{1,0:T(8,128)(2,1)}, ...), branch_computations={%region_36.37_spmd, %region_37.45_spmd} | conditional | flops 4719221760 | bytes 166295056 | solution.py:348
  368.3 6.8 %fusion.288 = f32[8,512,522]{1,2,0:T(8,128)} fusion(bf16[2,512,8,64]{1,3,2,0:T(8,128)(2,1)S(1)} %get-tuple-element.820, s32[]{:T(128)S(6)} %min.27, bf16[512,8,64]{0,2,1:T(8,128)(2,1)} %get-tuple-element.1313, bf16[10,8,64]{0,2,1:T(8,128)(2,1)S(1)} %copy.149), kind=kOutput, calls=%fused_computation.368 | convolution fusion | flops 274747392 | bytes 9732100 | tf_op jit(solution)/shard_map/cond/branch_1_fun/qhd,khd->hqk/dot_general | solution.py:95
  383.0 7.1 %multiply_reduce_fusion.2 = (f32[8,512]{1,0:T(8,128)S(1)}, f32[8,512,522]{1,2,0:T(8,128)S(1)}) fusion(f32[8,512,522]{1,2,0:T(8,128)} %fusion.288, f32[8,512]{1,0:T(8,128)S(1)} %dynamic-slice_bitcast_fusion.8, pred[512,522]{0,1:T(8,128)(4,1)} %concatenate.131, bf16[512,8,64]{0,2,1:T(8,128)(2,1)} %bitcast.613, bf16[512,8,64]{0,2,1:T(8,128)(2,1)} %get-tuple-element.1312, ...), kind=kOutput, calls=%fused_computation.292 | convolution fusion | flops 285433856 | bytes 18463744 | tf_op jit(solution)/shard_map/cond/branch_1_fun/qhd,khd->hqk/dot_general | solution.py:104
  402.3 16.4 %fusion.280 = (f32[512]{0:T(512)S(1)}, f32[512]{0:T(512)S(1)}, f32[512]{0:T(512)S(1)}, f32[512,512]{0,1:T(8,128)}) fusion(f32[512]{0:T(512)S(1)} %broadcast_multiply_fusion.2, bf16[2,512,512]{1,2,0:T(8,128)(2,1)S(1)} %copy.148, s32[]{:T(128)S(6)} %min.27, f32[512,512]{0,1:T(8,128)} %fusion.267, f32[512]{0:T(512)S(1)} %bitcast.683, ...), kind=kOutput, calls=%fused_computation.354 | convolution fusion | flops 2225338880 | bytes 11545600 | tf_op jit(solution)/shard_map/cond/branch_1_fun/dot_general | solution.py:181
  431.9 23.1 %reduce-scatter.2.cloned.1.call-done = f32[10,256]{1,0:T(8,128)} async-done(((f32[10,1024]{1,0:T(8,128)}), f32[10,256]{1,0:T(8,128)}) %reduce-scatter.2.cloned.1.call-update) | async-done | bytes 10256 | tf_op jit(solution)/shard_map/reduce_scatter | solution.py:363
  455.0 19.4 %psum.14 = f32[10,256]{1,0:T(8,128)S(1)} all-reduce(f32[10,256]{1,0:T(8,128)} %reduce-scatter.2.cloned.1.call-done), channel_id=1, replica_groups=mesh['pipe'=2,'grp'=4,'dp'=4] {'grp'}, use_global_device_ids=true, to_apply=%region_46.47 | all-reduce | flops 2560 | bytes 20480 | tf_op jit(solution)/shard_map/psum | solution.py:364
  477.4 26.5 %psum.15 = f32[10,512]{1,0:T(8,128)S(1)} all-reduce(f32[10,512]{1,0:T(8,128)S(1)} %fusion.588), channel_id=1, replica_groups=mesh['pipe'=2,'grp'=4,'dp'=4] {'pipe','dp'}, use_global_device_ids=true, to_apply=%region_47.48 | all-reduce | flops 5120 | bytes 40960 | tf_op jit(solution)/shard_map/psum | solution.py:371
  (352 shorter events, 201.8 us)
Async XLA Ops:
  7.2 8.9 %copy-start.15 = (bf16[2,1,512,512]{3,2,1,0:T(8,128)(2,1)S(1)}, bf16[2,1,512,512]{3,2,1,0:T(8,128)(2,1)}, u32[]{:S(2)}) copy-start(bf16[2,1,512,512]{3,2,1,0:T(8,128)(2,1)} %param.32) | copy-start | bytes 3145732
  7.2 8.9 %copy-start.22 = (bf16[1,512,512]{2,1,0:T(8,128)(2,1)S(1)}, bf16[1,512,512]{2,1,0:T(8,128)(2,1)}, u32[]{:S(2)}) copy-start(bf16[1,512,512]{2,1,0:T(8,128)(2,1)} %param.39) | copy-start | bytes 1572868
  7.2 8.9 %copy-start.53 = (s32[2,1,512]{2,1,0:T(1,128)S(1)}, s32[2,1,512]{2,1,0:T(1,128)}, u32[]{:S(2)}) copy-start(s32[2,1,512]{2,1,0:T(1,128)} %param.34) | copy-start | bytes 12292
  7.2 8.9 %copy-start.89 = (f32[1,512]{1,0:T(1,128)S(1)}, f32[1,512]{1,0:T(1,128)}, u32[]{:S(2)}) copy-start(f32[1,512]{1,0:T(1,128)} %param.35) | copy-start | bytes 6148
  7.2 8.9 %copy-start.79 = (f32[1,512]{1,0:T(1,128)S(1)}, f32[1,512]{1,0:T(1,128)}, u32[]{:S(2)}) copy-start(f32[1,512]{1,0:T(1,128)} %param.36) | copy-start | bytes 6148
  7.2 8.9 %copy-start.52 = (f32[1,1536]{1,0:T(1,128)S(1)}, f32[1,1536]{1,0:T(1,128)}, u32[]{:S(2)}) copy-start(f32[1,1536]{1,0:T(1,128)} %param.38) | copy-start | bytes 18436
  7.3 447.8 %reduce-scatter.2.cloned.1.call-start = ((), (), s32[]{:S(2)}) async-start(), calls=%async_computation.1 | async-start | bytes 81920 | tf_op jit(solution)/shard_map/reduce_scatter | solution.py:363
  38.8 8.9 %copy-start.30 = (pred[512,522]{0,1:T(8,128)(4,1)S(1)}, pred[512,522]{0,1:T(8,128)(4,1)}, u32[]{:S(2)}) copy-start(pred[512,522]{0,1:T(8,128)(4,1)} %concatenate.106) | copy-start | bytes 801796 | tf_op jit(solution)/shard_map/cond
  57.7 10.9 %copy-start.80 = (f32[1,512]{1,0:T(1,128)S(1)}, f32[1,512]{1,0:T(1,128)}, u32[]{:S(2)}) copy-start(f32[1,512]{1,0:T(1,128)} %get-tuple-element.729) | copy-start | bytes 6148 | tf_op jit(solution)/shard_map/cond
  57.7 10.9 %copy-start.86 = (f32[1,512]{1,0:T(1,128)S(1)}, f32[1,512]{1,0:T(1,128)}, u32[]{:S(2)}) copy-start(f32[1,512]{1,0:T(1,128)} %get-tuple-element.735) | copy-start | bytes 6148 | tf_op jit(solution)/shard_map/cond
  70.1 3.2 collective-permute-start
  81.1 10.0 %copy-start.56 = (s32[2,1,512]{2,1,0:T(1,128)S(1)}, s32[2,1,512]{2,1,0:T(1,128)}, u32[]{:S(2)}) copy-start(s32[2,1,512]{2,1,0:T(1,128)} %get-tuple-element.742) | copy-start | bytes 12292 | tf_op jit(solution)/shard_map/cond
  97.3 8.9 %copy-start.32 = (pred[512,522]{0,1:T(8,128)(4,1)S(1)}, pred[512,522]{0,1:T(8,128)(4,1)}, u32[]{:S(2)}) copy-start(pred[512,522]{0,1:T(8,128)(4,1)} %concatenate.111) | copy-start | bytes 801796 | tf_op jit(solution)/shard_map/cond
  116.4 11.1 %copy-start.81 = (f32[1,512]{1,0:T(1,128)S(1)}, f32[1,512]{1,0:T(1,128)}, u32[]{:S(2)}) copy-start(f32[1,512]{1,0:T(1,128)} %get-tuple-element.746) | copy-start | bytes 6148 | tf_op jit(solution)/shard_map/cond
  116.4 11.1 %copy-start.87 = (f32[1,512]{1,0:T(1,128)S(1)}, f32[1,512]{1,0:T(1,128)}, u32[]{:S(2)}) copy-start(f32[1,512]{1,0:T(1,128)} %get-tuple-element.752) | copy-start | bytes 6148 | tf_op jit(solution)/shard_map/cond
  128.8 4.9 collective-permute-start.1
  148.3 12.1 %copy-start.48 = (f32[2,8,512]{2,1,0:T(8,128)}, f32[2,8,512]{2,1,0:T(8,128)S(1)}, u32[]{:S(2)}) copy-start(f32[2,8,512]{2,1,0:T(8,128)S(1)} %pad_maximum_fusion.23) | copy-start | bytes 98308
  169.6 110.5 %collective-permute-start.2 = (bf16[512,512]{0,1:T(8,128)(2,1)}, bf16[512,512]{0,1:T(8,128)(2,1)}, u32[]{:S(2)}, u32[]{:S(2)}) collective-permute-start(bf16[512,512]{0,1:T(8,128)(2,1)} %convert_element_type.543), channel_id=1, source_target_pairs={{16,0},{17,1},{18,2},{19,3},{20,4},{21,5},{22,6},{23,7},{24,8},{25... | collective-permute-start | bytes 1572872 | tf_op jit(solution)/shard_map/ppermute | solution.py:20
  296.4 8.7 %slice-start.3 = ((s8[8650752]{0:T(1024)(128)(4,1)}), s8[262144]{0:T(1024)(128)(4,1)S(1)}, s32[]{:S(2)}) async-start(s8[8650752]{0:T(1024)(128)(4,1)} %bitcast.588), calls=%async_computation.5 | async-start | bytes 524288 | tf_op jit(solution)/shard_map/cond
  357.1 8.8 %collective-permute-start.3 = (bf16[512,512]{0,1:T(8,128)(2,1)}, bf16[512,512]{0,1:T(8,128)(2,1)}, u32[]{:S(2)}, u32[]{:S(2)}) collective-permute-start(bf16[512,512]{0,1:T(8,128)(2,1)} %convert_element_type.545), channel_id=1, source_target_pairs={{16,0},{17,1},{18,2},{19,3},{20,4},{21,5},{22,6},{23,7},{24,8},{25... | collective-permute-start | bytes 1572872 | tf_op jit(solution)/shard_map/ppermute | solution.py:20
  381.4 8.7 %slice-start = ((s8[8650752]{0:T(1024)(128)(4,1)}), s8[262144]{0:T(1024)(128)(4,1)S(1)}, s32[]{:S(2)}) async-start(s8[8650752]{0:T(1024)(128)(4,1)} %bitcast.586), calls=%async_computation.2 | async-start | bytes 524288 | tf_op jit(solution)/shard_map/cond
  402.3 18.5 %copy-start.13 = (bf16[512,512]{0,1:T(8,128)(2,1)S(1)}, bf16[512,512]{0,1:T(8,128)(2,1)}, u32[]{:S(2)}) copy-start(bf16[512,512]{0,1:T(8,128)(2,1)} %copy-done.12) | copy-start | bytes 1572868 | tf_op jit(solution)/shard_map/cond
  428.5 45.9 %copy-start.28 = (f32[10,512]{1,0:T(8,128)S(1)}, f32[10,512]{1,0:T(8,128)}, u32[]{:S(2)}) copy-start(f32[10,512]{1,0:T(8,128)} %copy-done.27) | copy-start | bytes 61444
  428.5 75.3 %copy-start.51 = (f32[10,512]{1,0:T(8,128)S(1)}, f32[10,512]{1,0:T(8,128)}, u32[]{:S(2)}) copy-start(f32[10,512]{1,0:T(8,128)} %param.47) | copy-start | bytes 61444
  (66 other events, 304.3 us)
Sparse Core Ops, SparseCore 0:
  428.6 26.3 reduce-scatter.1
where the time goes:
time: 522 us; the launch traced here: 516 us
  matrix products  152 us (29%)
  waiting for transfers between devices  130 us (25%)
  local copies, waits for them, and re-layouts  88.3 us (17%)
  other arithmetic  64.8 us (12%)
  blocking collectives  45.8 us (9%)
  between operations  14.6 us (3%)
  loops' own time  11.4 us (2%)
  starting transfers between devices  8.55 us (2%)
    ppermute x4, waiting for transfers between devices, passed_along(): return lax.ppermute(shard, axis, pairs)  107 us
    dot_general x2, matrix products, backward_layer(): jnp.dot(grad_before, w_in.T, preferred_element_type=jnp.float32)  32.9 us
    psum x1, blocking collectives, local(): hidden_grad = lax.psum(hidden_part, ('pipe', 'dp'))  26.5 us
    reduce_scatter x1, waiting for transfers between devices, local(): lax.psum_scatter(prefix_total, 'dp', scatter_dimension=1, tiled=True)  23.1 us
    dot_general x2, matrix products, forward_layer(): jnp.dot(activated, w_back, preferred_element_type=jnp.float32)  22 us
    another operation x20, local copies, waits for them, and re-layouts  21.3 us
    psum x1, blocking collectives, local(): local_cols = lax.psum(local_cols, 'grp')  19.4 us
    another operation x9, other arithmetic, local(): jnp.stack(leaf_list)  14.7 us
  transfers between devices with their start and end apart: 5, of which 4 were waited for; matrix products, arithmetic and copies ran while one was open for 3% of the time, Pallas kernels for 0%

commit v1 on v0

v1 whole, which is shorter than its diff:
```python
import math

import jax
import jax.numpy as jnp
import numpy as np
from jax import lax
from jax.experimental import pallas as pl
from jax.experimental.pallas import tpu as pltpu
from jax.sharding import PartitionSpec as P

D = 512
SEQ = 512
HEADS = 8
HD = 64
FF = 2048
ROT = 16
PREFIX = 10
PAD = 16
BLK = 128
BLOCKS = SEQ // BLK
PAIRS = HEADS // 2
LIVE = (1, 2, 3, 3)
P_ROWS = BLK * sum(LIVE)
P_START = (0, 128, 384, 768)

f32 = jnp.float32
bf16 = jnp.bfloat16
LOG2E = math.log2(math.e)
Q_SCALE = LOG2E * HD**-0.5
K_BACK = 1.0 / LOG2E
Q_BACK = HD**-0.5
NEG = -1e30

NN = (((1,), (0,)), ((), ()))
NT = (((1,), (1,)), ((), ()))
TN = (((0,), (0,)), ((), ()))

VMEM = pl.BlockSpec(memory_space=pltpu.VMEM)
ANY = pl.BlockSpec(memory_space=pl.ANY)
MIB = 1024 * 1024

G1, B1, G2, B2, B_ATTN, B_OUT, B_QKV, B_IN = 0, 1, 2, 3, 4, 5, 6, 9
SMALL_ROWS = 16


def dot(left, right, dims):
    return lax.dot_general(left, right, dims, preferred_element_type=f32)


def shape_of(shape, dtype):
    return jax.ShapeDtypeStruct(shape, dtype)


def params_of(mib):
    return pltpu.CompilerParams(vmem_limit_bytes=mib * MIB)


def rope_tables():
    inv_freq = 10000.0 ** (-2.0 * np.arange(ROT // 2) / ROT)
    angles = inv_freq[:, None] * np.arange(SEQ)[None, :]
    return np.concatenate([np.cos(angles), np.sin(angles)], axis=0).astype(np.float32)


def start_of_layer(section, layer, own, other, dst, sem):
    @pl.when(section == layer)
    def _():
        pltpu.make_async_copy(own, dst, sem).start()

    @pl.when(section != layer)
    def _():
        pltpu.make_async_copy(other, dst, sem).start()


def wait_for(src, dst, sem):
    pltpu.make_async_copy(src, dst, sem).wait()


def normalized(hidden):
    mean = jnp.mean(hidden, axis=-1, keepdims=True)
    centered = hidden - mean
    variance = jnp.mean(centered * centered, axis=-1, keepdims=True)
    scale = lax.rsqrt(variance + 1e-05)
    return centered * scale, scale


def rope_heads(rows, cos, sin):
    parts = []
    for head in range(rows.shape[0] // HD):
        base = head * HD
        lead = rows[base : base + 8]
        tail = rows[base + 8 : base + 16]
        parts += [lead * cos - tail * sin, tail * cos + lead * sin, rows[base + 16 : base + HD]]
    return jnp.concatenate(parts, axis=0)


def fill_mask(seg_ref, section, mask_ref):
    seg_row = seg_ref[pl.ds(section, 1), :].astype(f32)
    seg_col = jnp.transpose(jnp.broadcast_to(seg_row, (8, SEQ)))[:, 0:1]
    for block in range(BLOCKS):
        for key_block in range(block + 1 - LIVE[block], block + 1):
            seen = seg_col[key_block * BLK : (key_block + 1) * BLK] == (
                seg_row[:, block * BLK : (block + 1) * BLK]
            )
            if key_block == block:
                key_pos = lax.broadcasted_iota(jnp.int32, (BLK, BLK), 0)
                query_pos = lax.broadcasted_iota(jnp.int32, (BLK, BLK), 1)
                seen = seen & (key_pos <= query_pos)
            start = P_START[block] + (key_block - (block + 1 - LIVE[block])) * BLK
            mask_ref[start : start + BLK, :] = jnp.where(seen, 0.0, NEG)


def project_heads(normed, w_ref, small_ref, cos, sin, q_t, k_t, k_m, v_m, v_t):
    bias = small_ref[B_QKV : B_QKV + 1, :]
    rows = dot(normed, w_ref[:, :D], NN) + bias
    q_t[...] = (rope_heads(jnp.transpose(rows), cos, sin) * Q_SCALE).astype(bf16)
    bias = small_ref[B_QKV + 1 : B_QKV + 2, :]
    rows = dot(normed, w_ref[:, D : 2 * D], NN) + bias
    keys = rope_heads(jnp.transpose(rows), cos, sin).astype(bf16)
    k_t[...] = keys
    k_m[...] = jnp.transpose(keys)
    bias = small_ref[B_QKV + 2 : B_QKV + 3, :]
    values = (dot(normed, w_ref[:, 2 * D :], NN) + bias).astype(bf16)
    v_m[...] = values
    v_t[...] = jnp.transpose(values)


def block_diagonal(pair_rows):
    zeros = jnp.zeros((HD, BLK), pair_rows.dtype)
    return jnp.concatenate(
        [
            jnp.concatenate([pair_rows[:HD], zeros], axis=1),
            jnp.concatenate([zeros, pair_rows[HD:]], axis=1),
        ],
        axis=0,
    )


def from_diagonal(both):
    return jnp.concatenate([both[:HD, :BLK], both[HD:, BLK:]], axis=0)


def per_head(row, rows=HD):
    return jnp.concatenate(
        [
            jnp.broadcast_to(row[:, :BLK], (rows, BLK)),
            jnp.broadcast_to(row[:, BLK:], (rows, BLK)),
        ],
        axis=0,
    )


def attend(q_t, k_m, v_t, pre_k, pre_v_t, mask_ref, p_ref, pp_ref, inv_ref, mixed_ref):
    pad_mask = jnp.where(lax.broadcasted_iota(jnp.int32, (PAD, 1), 0) < PREFIX, 0.0, NEG)

    def one_pair(pair, carry):
        feats = pl.ds(pl.multiple_of(pair * BLK, BLK), BLK)
        prefix_keys = pre_k[:, feats]
        prefix_values = pre_v_t[feats, :]
        for block in range(BLOCKS):
            live = LIVE[block] * BLK
            key_start = (block + 1) * BLK - live
            tokens = slice(block * BLK, (block + 1) * BLK)
            queries = block_diagonal(q_t[feats, tokens])
            mask = mask_ref[P_START[block] : P_START[block] + live, :]
            scores = dot(k_m[key_start : key_start + live, feats], queries, NN)
            scores = scores + jnp.concatenate([mask, mask], axis=1)
            pre_scores = dot(prefix_keys, queries, NN) + pad_mask
            peak = jnp.maximum(
                jnp.max(scores, axis=0, keepdims=True), jnp.max(pre_scores, axis=0, keepdims=True)
            )
            expo = jnp.exp2(scores - peak)
            pre_expo = jnp.exp2(pre_scores - peak)
            total = jnp.sum(expo, axis=0, keepdims=True) + jnp.sum(pre_expo, axis=0, keepdims=True)
            inverse = 1.0 / total
            expo = expo.astype(bf16)
            pre_expo = pre_expo.astype(bf16)
            mixed = dot(v_t[feats, key_start : key_start + live], expo, NN) + dot(
                prefix_values, pre_expo, NN
            )
            mixed_ref[feats, tokens] = (from_diagonal(mixed) * per_head(inverse)).astype(bf16)
            p_ref[pair, P_START[block] : P_START[block] + live, :] = expo
            pp_ref[pair, block] = pre_expo
            inv_ref[pair, block] = jnp.broadcast_to(inverse, (8, 2 * BLK))
        return carry

    lax.fori_loop(0, PAIRS, one_pair, 0)


def attend_back(grad_t, q_t, k_t, v_m, pre_k_t, pre_v, p_ref, pp_ref, inv_ref, mixed_ref,
                dq_ref, dk_ref, dv_ref, pre_grad, pre_row):
    def one_pair(pair, carry):
        feats = pl.ds(pl.multiple_of(pair * BLK, BLK), BLK)
        prefix_values = pre_v[:, feats]
        prefix_keys_t = pre_k_t[feats, :]
        pre_dk = jnp.zeros((PAD, BLK), f32)
        pre_dv = jnp.zeros((PAD, BLK), f32)
        for block in range(BLOCKS):
            live = LIVE[block] * BLK
            key_start = (block + 1) * BLK - live
            keys = slice(key_start, key_start + live)
            tokens = slice(block * BLK, (block + 1) * BLK)
            scaled = (grad_t[feats, tokens] * per_head(inv_ref[pair, block][0:1, :])).astype(bf16)
            products = scaled.astype(f32) * mixed_ref[feats, tokens].astype(f32)
            inner = jnp.concatenate(
                [
                    jnp.sum(products[:HD], axis=0, keepdims=True),
                    jnp.sum(products[HD:], axis=0, keepdims=True),
                ],
                axis=1,
            )
            grads = block_diagonal(scaled)
            queries = block_diagonal(q_t[feats, tokens])
            probs = p_ref[pair, P_START[block] : P_START[block] + live, :]
            pre_probs = pp_ref[pair, block]
            grad_probs = dot(v_m[keys, feats], grads, NN)
            pre_grad_probs = dot(prefix_values, grads, NN)
            grad_scores = (probs.astype(f32) * (grad_probs - inner)).astype(bf16)
            pre_scores = (pre_probs.astype(f32) * (pre_grad_probs - inner)).astype(bf16)
            dq = dot(k_t[feats, keys], grad_scores, NN) + dot(prefix_keys_t, pre_scores, NN)
            dq_ref[feats, tokens] = from_diagonal(dq)
            dv = dot(grads, probs, NT)
            dk = dot(queries, grad_scores, NT)
            if live > BLK:
                old = slice(key_start, block * BLK)
                dv_ref[feats, old] += dv[:, : live - BLK]
                dk_ref[feats, old] += dk[:, : live - BLK]
            dv_ref[feats, tokens] = dv[:, live - BLK :]
            dk_ref[feats, tokens] = dk[:, live - BLK :]
            pre_dk = pre_dk + dot(pre_scores, queries, NT)
            pre_dv = pre_dv + dot(pre_probs, grads, NT)
        pre_grad[pre_row : pre_row + PAD, feats] = pre_dk * K_BACK
        pre_grad[pre_row + PAD : pre_row + 2 * PAD, feats] = pre_dv
        return carry

    lax.fori_loop(0, PAIRS, one_pair, 0)


def pack_grads(dq_ref, dk_ref, dv_ref, cos, sin, packed_t):
    packed_t[:D, :] = (rope_heads(dq_ref[...], cos, -sin) * Q_BACK).astype(bf16)
    packed_t[D : 2 * D, :] = (rope_heads(dk_ref[...], cos, -sin) * K_BACK).astype(bf16)
    packed_t[2 * D :, :] = dv_ref[...].astype(bf16)


def gelu_both(before):
    cdf = 0.5 + 0.5 * lax.erf(before * (0.5**0.5))
    density = jnp.exp2(before * before * (-0.5 * LOG2E)) * (1.0 / math.sqrt(2.0 * math.pi))
    return before * cdf, cdf + before * density


FF_CHUNK = 512


def feed_in(normed, w_ref, small_ref, act_ref, slope_ref):
    for chunk in range(FF // FF_CHUNK):
        cols = slice(chunk * FF_CHUNK, (chunk + 1) * FF_CHUNK)
        before = dot(normed, w_ref[:, cols], NN) + small_ref[B_IN + chunk : B_IN + chunk + 1, :]
        act, slope = gelu_both(before)
        act_ref[:, cols] = act.astype(bf16)
        slope_ref[:, cols] = slope.astype(bf16)


def layer_result(hidden, mixed_t, w_attn, act_ref, w_out, small_ref):
    attn_out = dot(jnp.transpose(mixed_t), w_attn, NN) + small_ref[B_ATTN : B_ATTN + 1, :]
    ff_out = dot(act_ref[...], w_out, NN) + small_ref[B_OUT : B_OUT + 1, :]
    return hidden + attn_out + ff_out


def feed_back(grad, w_out, w_in, slope_ref):
    total = jnp.zeros((SEQ, D), f32)
    for chunk in range(FF // FF_CHUNK):
        cols = slice(chunk * FF_CHUNK, (chunk + 1) * FF_CHUNK)
        grad_act = dot(grad, w_out[cols, :], NT)
        grad_before = (grad_act * slope_ref[:, cols].astype(f32)).astype(bf16)
        total = total + dot(grad_before, w_in[:, cols], NT)
    return total


def norms_back(grad, hidden, grad_two, packed_t, w_qkv, small_ref):
    grad_one = jnp.transpose(dot(w_qkv, packed_t, NN))
    grad_hat = (
        grad_one * small_ref[G1 : G1 + 1, :] + grad_two * small_ref[G2 : G2 + 1, :]
    )
    hat, scale = normalized(hidden)
    mean_one = jnp.mean(grad_hat, axis=-1, keepdims=True)
    mean_two = jnp.mean(grad_hat * hat, axis=-1, keepdims=True)
    return grad.astype(f32) + scale * (grad_hat - mean_one - hat * mean_two)


def prefix_kernel(embed, up_w, up_b, out_w, out_b, hidden_ref, low_ref, low_t_ref):
    high = lax.Precision.HIGHEST
    units = jnp.tanh(
        jnp.dot(embed[...], up_w[...], precision=high, preferred_element_type=f32) + up_b[...]
    )
    hidden_ref[...] = units
    for part in range(4):
        cols = slice(part * D, (part + 1) * D)
        states = (
            jnp.dot(units, out_w[:, cols], precision=high, preferred_element_type=f32)
            + out_b[:, cols]
        )
        padded = jnp.concatenate([states, jnp.zeros((BLK - PREFIX, D), f32)], axis=0)
        low_ref[part] = padded[:PAD].astype(bf16)
        low_t_ref[part] = jnp.transpose(padded)[:, :PAD].astype(bf16)


def prefix_call(embed, up_w, up_b, out_w, out_b):
    return pl.pallas_call(
        prefix_kernel,
        name="prefix",
        out_shape=[
            shape_of((PREFIX, D), f32),
            shape_of((4, PAD, D), bf16),
            shape_of((4, D, PAD), bf16),
        ],
        compiler_params=params_of(32),
    )(embed, up_w, up_b.reshape(1, D), out_w, out_b.reshape(1, 4 * D))


def head_outputs():
    return [
        shape_of((D, SEQ), bf16),
        shape_of((D, SEQ), bf16),
        shape_of((SEQ, D), bf16),
        shape_of((PAIRS, P_ROWS, 2 * BLK), bf16),
        shape_of((PAIRS, BLOCKS, PAD, 2 * BLK), bf16),
        shape_of((PAIRS, BLOCKS, 8, 2 * BLK), f32),
        shape_of((D, SEQ), bf16),
    ]


def first_kernel(x_hbm, seg, own_small, other_small, own_qkv, other_qkv, low, low_t, tables,
                 q_t, k_t, v_m, p_ref, pp_ref, inv_ref, mixed_ref, two_ref, mask_ref,
                 x_ref, w_ref, small_ref, k_m, v_t, sems):
    section = lax.axis_index("pipe")
    x_copy = pltpu.make_async_copy(x_hbm.at[section, 0], x_ref, sems.at[0])
    x_copy.start()
    start_of_layer(section, 0, own_small, other_small, small_ref, sems.at[1])
    start_of_layer(section, 0, own_qkv.at[0], other_qkv.at[0], w_ref, sems.at[2])
    fill_mask(seg, section, mask_ref)
    x_copy.wait()
    wait_for(own_small, small_ref, sems.at[1])
    hat, _ = normalized(x_ref[...].astype(f32))
    normed = (hat * small_ref[G1 : G1 + 1, :] + small_ref[B1 : B1 + 1, :]).astype(bf16)
    two_ref[...] = (hat * small_ref[G2 : G2 + 1, :] + small_ref[B2 : B2 + 1, :]).astype(bf16)
    wait_for(own_qkv.at[0], w_ref, sems.at[2])
    cos, sin = tables[:8, :], tables[8:, :]
    project_heads(normed, w_ref, small_ref, cos, sin, q_t, k_t, k_m, v_m, v_t)
    attend(q_t, k_m, v_t, low.at[0], low_t.at[1], mask_ref, p_ref, pp_ref, inv_ref, mixed_ref)


def first_call(block_input, seg, own_small, other_small, own_qkv, other_qkv, low, low_t, tables):
    return pl.pallas_call(
        first_kernel,
        name="first_attention",
        out_shape=head_outputs() + [shape_of((SEQ, D), bf16), shape_of((P_ROWS, BLK), f32)],
        in_specs=[ANY, VMEM, ANY, ANY, ANY, ANY, VMEM, VMEM, VMEM],
        out_specs=[VMEM] * 9,
        scratch_shapes=[
            pltpu.VMEM((SEQ, D), bf16),
            pltpu.VMEM((D, 3 * D), bf16),
            pltpu.VMEM((SMALL_ROWS, D), f32),
            pltpu.VMEM((SEQ, D), bf16),
            pltpu.VMEM((D, SEQ), bf16),
            pltpu.SemaphoreType.DMA((3,)),
        ],
        compiler_params=params_of(48),
    )(block_input, seg, own_small, other_small, own_qkv, other_qkv, low, low_t, tables)


def feed_kernel(two_ref, own_small, other_small, own_in, other_in, act_ref, slope_ref,
                w_ref, small_ref, sems):
    section = lax.axis_index("pipe")
    start_of_layer(section, 0, own_small, other_small, small_ref, sems.at[0])
    start_of_layer(section, 0, own_in.at[0], other_in.at[0], w_ref, sems.at[1])
    wait_for(own_small, small_ref, sems.at[0])
    wait_for(own_in.at[0], w_ref, sems.at[1])
    feed_in(two_ref[...], w_ref, small_ref, act_ref, slope_ref)


def feed_call(normed_two, own_small, other_small, own_in, other_in):
    return pl.pallas_call(
        feed_kernel,
        name="first_feed",
        out_shape=[shape_of((SEQ, FF), bf16)] * 2,
        in_specs=[VMEM, ANY, ANY, ANY, ANY],
        out_specs=[VMEM] * 2,
        scratch_shapes=[
            pltpu.VMEM((D, FF), bf16),
            pltpu.VMEM((SMALL_ROWS, D), f32),
            pltpu.SemaphoreType.DMA((2,)),
        ],
        compiler_params=params_of(32),
    )(normed_two, own_small, other_small, own_in, other_in)


def middle_kernel(x_hbm, cot_hbm, mask_ref, own_small, other_small, own_qkv, other_qkv,
                  own_attn, other_attn, own_in, other_in, own_out, other_out, low, low_t, tables,
                  q0_hbm, k0_hbm, v0_hbm, p0_hbm, pp0_ref, inv0_ref, mixed0_ref, act0_hbm,
                  h_one, act_one, mixed_one, grad_one, grad_low, packed_zero, prefix_grad,
                  x_ref, cot_ref, small_zero, small_one, w_qkv, w_attn_zero, w_attn, w_in, w_out_zero, w_out,
                  act_ref, q_t, k_t, k_m, v_m, v_t, p_ref, pp_ref, inv_ref, slope_ref,
                  q0, k0, v0, p0, dq, dk, dv, packed, pre_grad, sems):
    section = lax.axis_index("pipe")
    copies = []

    def fetch(src, dst, sem):
        copy = pltpu.make_async_copy(src, dst, sems.at[sem])
        copy.start()
        return copy

    start_of_layer(section, 0, own_small, other_small, small_zero, sems.at[0])
    start_of_layer(section, 0, own_attn.at[0], other_attn.at[0], w_attn_zero, sems.at[1])
    x_copy = fetch(x_hbm.at[section, 0], x_ref, 2)
    start_of_layer(section, 0, own_out.at[0], other_out.at[0], w_out_zero, sems.at[3])
    act_copy = fetch(act0_hbm, act_ref, 4)
    start_of_layer(section, 1, own_small, other_small, small_one, sems.at[5])
    start_of_layer(section, 1, own_qkv.at[0], other_qkv.at[0], w_qkv, sems.at[6])
    start_of_layer(section, 1, own_in.at[0], other_in.at[0], w_in, sems.at[7])
    cot_copy = fetch(cot_hbm.at[section, 0], cot_ref, 8)
    start_of_layer(section, 1, own_out.at[0], other_out.at[0], w_out, sems.at[9])
    start_of_layer(section, 1, own_attn.at[0], other_attn.at[0], w_attn, sems.at[10])
    late = [
        fetch(src, dst, 11 + i)
        for i, (src, dst) in enumerate(((q0_hbm, q0), (k0_hbm, k0), (v0_hbm, v0), (p0_hbm, p0)))
    ]
    cos, sin = tables[:8, :], tables[8:, :]

    wait_for(own_small, small_zero, sems.at[0])
    wait_for(own_attn.at[0], w_attn_zero, sems.at[1])
    x_copy.wait()
    wait_for(own_out.at[0], w_out_zero, sems.at[3])
    act_copy.wait()
    h_one[...] = layer_result(
        x_ref[...].astype(f32), mixed0_ref[...], w_attn_zero[...], act_ref, w_out_zero[...], small_zero
    ).astype(bf16)

    hidden = h_one[...].astype(f32)
    hat, _ = normalized(hidden)
    wait_for(own_small, small_one, sems.at[5])
    normed = (hat * small_one[G1 : G1 + 1, :] + small_one[B1 : B1 + 1, :]).astype(bf16)
    two = (hat * small_one[G2 : G2 + 1, :] + small_one[B2 : B2 + 1, :]).astype(bf16)
    wait_for(own_qkv.at[0], w_qkv, sems.at[6])
    project_heads(normed, w_qkv, small_one, cos, sin, q_t, k_t, k_m, v_m, v_t)
    attend(q_t, k_m, v_t, low.at[2], low_t.at[3], mask_ref, p_ref, pp_ref, inv_ref, mixed_one)
    wait_for(own_in.at[0], w_in, sems.at[7])
    feed_in(two, w_in, small_one, act_one, slope_ref)

    cot_copy.wait()
    wait_for(own_out.at[0], w_out, sems.at[9])
    grad = cot_ref[...]
    grad_two = feed_back(grad, w_out, w_in, slope_ref)
    wait_for(own_attn.at[0], w_attn, sems.at[10])
    dq[...] = dot(w_attn[...], grad, NT)
    attend_back(dq, q_t, k_t, v_m, low_t.at[2], low.at[3], p_ref, pp_ref, inv_ref, mixed_one,
                dq, dk, dv, pre_grad, 2 * PAD)
    pack_grads(dq, dk, dv, cos, sin, packed)
    result = norms_back(grad, hidden, grad_two, packed[...], w_qkv[...], small_one)
    grad_one[...] = result
    grad_low[...] = result.astype(bf16)

    dq[...] = dot(w_attn_zero[...], grad_low[...], NT)
    for copy in late:
        copy.wait()
    attend_back(dq, q0, k0, v0, low_t.at[0], low.at[1], p0, pp0_ref, inv0_ref, mixed0_ref,
                dq, dk, dv, pre_grad, 0)
    pack_grads(dq, dk, dv, cos, sin, packed_zero)
    for part in range(4):
        prefix_grad[part * PREFIX : (part + 1) * PREFIX, :] = pre_grad[
            part * PAD : part * PAD + PREFIX, :
        ]


def middle_call(block_input, cotangent, mask, own_small, other_small, own, other, low, low_t, tables,
                heads_zero, act_zero):
    q0, k0, v0, p0, pp0, inv0, mixed0 = heads_zero
    own_qkv, own_attn, own_in, own_out = own
    other_qkv, other_attn, other_in, other_out = other
    return pl.pallas_call(
        middle_kernel,
        name="middle",
        out_shape=[
            shape_of((SEQ, D), bf16),
            shape_of((SEQ, FF), bf16),
            shape_of((D, SEQ), bf16),
            shape_of((SEQ, D), f32),
            shape_of((SEQ, D), bf16),
            shape_of((3 * D, SEQ), bf16),
            shape_of((4 * PREFIX, D), f32),
        ],
        in_specs=[ANY, ANY, VMEM] + [ANY] * 10 + [VMEM] * 3 + [ANY] * 4 + [VMEM] * 3 + [ANY],
        out_specs=[VMEM] * 7,
        scratch_shapes=[
            pltpu.VMEM((SEQ, D), bf16),
            pltpu.VMEM((SEQ, D), bf16),
            pltpu.VMEM((SMALL_ROWS, D), f32),
            pltpu.VMEM((SMALL_ROWS, D), f32),
            pltpu.VMEM((D, 3 * D), bf16),
            pltpu.VMEM((D, D), bf16),
            pltpu.VMEM((D, D), bf16),
            pltpu.VMEM((D, FF), bf16),
            pltpu.VMEM((FF, D), bf16),
            pltpu.VMEM((FF, D), bf16),
            pltpu.VMEM((SEQ, FF), bf16),
            pltpu.VMEM((D, SEQ), bf16),
            pltpu.VMEM((D, SEQ), bf16),
            pltpu.VMEM((SEQ, D), bf16),
            pltpu.VMEM((SEQ, D), bf16),
            pltpu.VMEM((D, SEQ), bf16),
            pltpu.VMEM((PAIRS, P_ROWS, 2 * BLK), bf16),
            pltpu.VMEM((PAIRS, BLOCKS, PAD, 2 * BLK), bf16),
            pltpu.VMEM((PAIRS, BLOCKS, 8, 2 * BLK), f32),
            pltpu.VMEM((SEQ, FF), bf16),
            pltpu.VMEM((D, SEQ), bf16),
            pltpu.VMEM((D, SEQ), bf16),
            pltpu.VMEM((SEQ, D), bf16),
            pltpu.VMEM((PAIRS, P_ROWS, 2 * BLK), bf16),
            pltpu.VMEM((D, SEQ), f32),
            pltpu.VMEM((D, SEQ), f32),
            pltpu.VMEM((D, SEQ), f32),
            pltpu.VMEM((3 * D, SEQ), bf16),
            pltpu.VMEM((4 * PAD, D), f32),
            pltpu.SemaphoreType.DMA((15,)),
        ],
        compiler_params=params_of(60),
    )(
        block_input, cotangent, mask, own_small, other_small, own_qkv, other_qkv, own_attn,
        other_attn, own_in, other_in, own_out, other_out, low, low_t, tables, q0, k0, v0, p0, pp0,
        inv0, mixed0, act_zero,
    )


def late_kernel(x_hbm, own_small, other_small, own_qkv, other_qkv, own_attn, other_attn, own_in,
                other_in, own_out, other_out, h_one, act_one, mixed_one, grad_one, grad_low,
                packed_zero, slope_zero, act_keep, act_send, grad_keep, grad_send,
                x_ref, small_zero, small_one, w_qkv, w_attn, w_in, w_out_zero, w_out, sems):
    section = lax.axis_index("pipe")
    start_of_layer(section, 0, own_small, other_small, small_zero, sems.at[0])
    start_of_layer(section, 0, own_out.at[0], other_out.at[0], w_out_zero, sems.at[1])
    start_of_layer(section, 0, own_in.at[0], other_in.at[0], w_in, sems.at[2])
    start_of_layer(section, 0, own_qkv.at[0], other_qkv.at[0], w_qkv, sems.at[3])
    x_copy = pltpu.make_async_copy(x_hbm.at[section, 0], x_ref, sems.at[4])
    x_copy.start()
    start_of_layer(section, 1, own_small, other_small, small_one, sems.at[5])
    start_of_layer(section, 1, own_attn.at[0], other_attn.at[0], w_attn, sems.at[6])
    start_of_layer(section, 1, own_out.at[0], other_out.at[0], w_out, sems.at[7])

    wait_for(own_small, small_zero, sems.at[0])
    wait_for(own_out.at[0], w_out_zero, sems.at[1])
    wait_for(own_in.at[0], w_in, sems.at[2])
    grad_two = feed_back(grad_low[...], w_out_zero, w_in, slope_zero)
    wait_for(own_qkv.at[0], w_qkv, sems.at[3])
    x_copy.wait()
    grad_zero = norms_back(
        grad_low[...], x_ref[...].astype(f32), grad_two, packed_zero[...], w_qkv[...], small_zero
    )

    wait_for(own_small, small_one, sems.at[5])
    wait_for(own_attn.at[0], w_attn, sems.at[6])
    wait_for(own_out.at[0], w_out, sems.at[7])
    h_two = layer_result(
        h_one[...].astype(f32), mixed_one[...], w_attn[...], act_one, w_out[...], small_one
    ).astype(bf16)

    @pl.when(section == 0)
    def _():
        act_keep[...] = h_one[...]
        act_send[...] = h_two
        grad_keep[...] = grad_zero
        grad_send[...] = grad_one[...].astype(grad_send.dtype)

    @pl.when(section != 0)
    def _():
        act_keep[...] = h_two
        act_send[...] = h_one[...]
        grad_keep[...] = grad_one[...]
        grad_send[...] = grad_zero.astype(grad_send.dtype)


def late_call(block_input, own_small, other_small, own, other, middle, slope_zero):
    h_one, act_one, mixed_one, grad_one, grad_low, packed_zero = middle
    own_qkv, own_attn, own_in, own_out = own
    other_qkv, other_attn, other_in, other_out = other
    return pl.pallas_call(
        late_kernel,
        name="late",
        out_shape=[
            shape_of((SEQ, D), bf16),
            shape_of((SEQ, D), bf16),
            shape_of((SEQ, D), f32),
            shape_of((SEQ, D), f32),
        ],
        in_specs=[ANY] * 11 + [VMEM] * 7,
        out_specs=[VMEM] * 4,
        scratch_shapes=[
            pltpu.VMEM((SEQ, D), bf16),
            pltpu.VMEM((SMALL_ROWS, D), f32),
            pltpu.VMEM((SMALL_ROWS, D), f32),
            pltpu.VMEM((D, 3 * D), bf16),
            pltpu.VMEM((D, D), bf16),
            pltpu.VMEM((D, FF), bf16),
            pltpu.VMEM((FF, D), bf16),
            pltpu.VMEM((FF, D), bf16),
            pltpu.SemaphoreType.DMA((8,)),
        ],
        compiler_params=params_of(48),
    )(
        block_input, own_small, other_small, own_qkv, other_qkv, own_attn, other_attn, own_in,
        other_in, own_out, other_out, h_one, act_one, mixed_one, grad_one, grad_low, packed_zero,
        slope_zero,
    )


def final_kernel(col_width, grads_ref, hidden_ref, embed, up_w, out_w, act_keep, act_other, grad_keep,
                 grad_other, d_embed, d_up, d_up_b, d_out, d_out_b, act_out, grad_out, sems):
    section = lax.axis_index("pipe")
    shard = lax.axis_index("dp")
    copies = [
        pltpu.make_async_copy(act_keep, act_out.at[0, section, 0], sems.at[0]),
        pltpu.make_async_copy(act_other, act_out.at[0, 1 - section, 0], sems.at[1]),
        pltpu.make_async_copy(grad_keep, grad_out.at[0, section, 0], sems.at[2]),
        pltpu.make_async_copy(grad_other, grad_out.at[0, 1 - section, 0], sems.at[3]),
    ]
    for copy in copies:
        copy.start()
    high = lax.Precision.HIGHEST
    units = hidden_ref[...]
    grad_units = jnp.zeros((PREFIX, D), f32)
    for part in range(4):
        grad_units = grad_units + lax.dot_general(
            grads_ref[part * PREFIX : (part + 1) * PREFIX, :], out_w[:, part * D : (part + 1) * D],
            NT, precision=high, preferred_element_type=f32,
        )
    grad_pre = grad_units * (1.0 - units * units)
    d_up_b[...] = jnp.sum(grad_pre, axis=0, keepdims=True)
    d_up[...] = lax.dot_general(embed[...], grad_pre, TN, precision=high, preferred_element_type=f32)
    d_embed[...] = lax.dot_general(grad_pre, up_w[...], NT, precision=high, preferred_element_type=f32)
    column = section * (2 * D) + shard * col_width
    own_part = column // D
    own_cols = jnp.zeros((PREFIX, col_width), f32)
    for part in range(4):
        for piece in range(D // col_width):
            here = (column == part * D + piece * col_width).astype(f32)
            own_cols = own_cols + here * grads_ref[
                part * PREFIX : (part + 1) * PREFIX, piece * col_width : (piece + 1) * col_width
            ]
    d_out[...] = lax.dot_general(units, own_cols, TN, precision=high, preferred_element_type=f32)
    d_out_b[...] = jnp.sum(own_cols, axis=0, keepdims=True)
    for copy in copies:
        copy.wait()


def final_call(col_width, prefix_grad, hidden_units, embed, up_w, out_w, act_keep, act_other, grad_keep, grad_other):
    def body(*refs):
        final_kernel(col_width, *refs)

    return pl.pallas_call(
        body,
        name="reparam",
        out_shape=[
            shape_of((PREFIX, D), f32),
            shape_of((D, D), f32),
            shape_of((1, D), f32),
            shape_of((D, col_width), f32),
            shape_of((1, col_width), f32),
            shape_of((1, 2, 1, SEQ, D), bf16),
            shape_of((1, 2, 1, SEQ, D), f32),
        ],
        in_specs=[VMEM] * 5 + [ANY] * 4,
        out_specs=[VMEM] * 5 + [ANY] * 2,
        scratch_shapes=[pltpu.SemaphoreType.DMA((4,))],
        compiler_params=params_of(48),
    )(prefix_grad, hidden_units, embed, up_w, out_w, act_keep, act_other, grad_keep, grad_other)


def swapped(array_in):
    return lax.ppermute(array_in, "pipe", [(0, 1), (1, 0)])


def summed(array_in, axis):
    size = lax.axis_size(axis)
    if size & (size - 1):
        return lax.psum(array_in, axis)
    step = 1
    while step < size:
        array_in = array_in + lax.ppermute(array_in, axis, [(i, i ^ step) for i in range(size)])
        step *= 2
    return array_in


def local(
    block_input,
    cotangent,
    segments,
    ln1_gain,
    ln1_shift,
    qkv_weight,
    qkv_bias,
    attn_weight,
    attn_bias,
    ln2_gain,
    ln2_shift,
    ff_in_weight,
    ff_in_bias,
    ff_out_weight,
    ff_out_bias,
    prefix_embed,
    up_weight,
    up_bias,
    out_weight,
    out_bias,
):
    small = jnp.concatenate(
        [ln1_gain, ln1_shift, ln2_gain, ln2_shift, attn_bias, ff_out_bias]
        + [qkv_bias.reshape(3, D), ff_in_bias.reshape(4, D), jnp.zeros((3, D), f32)],
        axis=0,
    )
    own = (qkv_weight, attn_weight, ff_in_weight, ff_out_weight)
    other_small = swapped(small)
    other_qkv = swapped(qkv_weight)
    other_in = swapped(ff_in_weight)
    other_out = swapped(ff_out_weight)
    other_attn = swapped(attn_weight)
    other = (other_qkv, other_attn, other_in, other_out)
    tables = jnp.asarray(rope_tables())
    hidden_units, low, low_t = prefix_call(prefix_embed, up_weight, up_bias, out_weight, out_bias)
    *heads_zero, normed_two, mask = first_call(
        block_input, segments[:, 0], small, other_small, qkv_weight, other_qkv, low, low_t, tables
    )
    act_zero, slope_zero = feed_call(normed_two, small, other_small, ff_in_weight, other_in)
    *middle, prefix_grad = middle_call(
        block_input, cotangent, mask, small, other_small, own, other, low, low_t, tables,
        heads_zero, act_zero,
    )
    act_keep, act_send, grad_keep, grad_send = late_call(
        block_input, small, other_small, own, other, middle, slope_zero
    )
    act_other = swapped(act_send)
    grad_other = swapped(grad_send)
    for axis in ("pipe", "dp", "grp"):
        prefix_grad = summed(prefix_grad, axis)
    col_width = 2 * D // lax.axis_size("dp")
    grad_embed, grad_up, grad_up_b, grad_out, grad_out_b, activations, input_grads = final_call(
        col_width, prefix_grad, hidden_units, prefix_embed, up_weight, out_weight,
        act_keep, act_other, grad_keep, grad_other,
    )
    return (
        activations,
        input_grads,
        grad_embed,
        grad_up,
        grad_up_b[0],
        grad_out,
        grad_out_b[0],
    )


def solution(mesh):
    return jax.shard_map(
        local,
        mesh=mesh,
        in_specs=(
            P(None, ("grp", "dp"), None, None),
            P(None, ("grp", "dp"), None, None),
            P(None, ("grp", "dp"), None),
            P("pipe", None),
            P("pipe", None),
            P("pipe", None, None),
            P("pipe", None),
            P("pipe", None, None),
            P("pipe", None),
            P("pipe", None),
            P("pipe", None),
            P("pipe", None, None),
            P("pipe", None),
            P("pipe", None, None),
            P("pipe", None),
            P(),
            P(),
            P(),
            P(),
            P(),
        ),
        out_specs=(
            P("pipe", None, ("grp", "dp"), None, None),
            P("pipe", None, ("grp", "dp"), None, None),
            P(),
            P(),
            P(),
            P(None, ("pipe", "dp")),
            P(("pipe", "dp")),
        ),
        check_vma=False,
    )
```

time: 522 us -> 115 us (0.22); the launches traced: 516 us -> 114 us
  matrix products: 152 us -> 0 us
  waiting for transfers between devices: 130 us -> 13.3 us
  local copies, waits for them, and re-layouts: 88.3 us -> 15.4 us
  Pallas kernels: 0 us -> 67.9 us
  other arithmetic: 64.8 us -> 2.14 us
  blocking collectives: 45.8 us -> 0 us
  between operations: 14.6 us -> 1.22 us
  loops' own time: 11.4 us -> 0 us
  starting transfers between devices: 8.55 us -> 14.5 us
    dot_general x34 -> x0, matrix products: 152 us -> none  [the longest x2 32.9 us: backward_layer(): jnp.dot(grad_before, w_in.T, preferred_element_type=jnp.float32)]
    ppermute x4 -> x12, waiting for transfers between devices: 107 us -> 13.3 us  [the longest x5 13.3 us: summed(): lax.ppermute(array_in, axis, [(i, i ^ step) for i in range(size)])]
    pallas_call x0 -> x6, Pallas kernels: none -> 67.9 us  [the longest x1 32.1 us: middle_call(): pl.pallas_call(middle_kernel, name='middle', out_shape=[shape_of((SEQ, D)...]
    psum x2 -> x0, blocking collectives: 45.8 us -> none  [the longest x1 26.5 us: local(): hidden_grad = lax.psum(hidden_part, ('pipe', 'dp'))]
    slice x24 -> x0, local copies, waits for them, and re-layouts: 30 us -> none  [the longest x4 8.28 us: forward_layer(): packed[:, 2 * D:].reshape(seq_len, HEADS, HD).astype(jnp.bfloat16)]
    reduce_scatter x1 -> x0, waiting for transfers between devices: 23.1 us -> none  [local(): lax.psum_scatter(prefix_total, 'dp', scatter_dimension=1, tiled=True)]
    another operation x22 -> x0, other arithmetic: 23.1 us -> none  [the longest x9 14.7 us: local(): jnp.stack(leaf_list)]
    another operation x20 -> x0, local copies, waits for them, and re-layouts: 21.3 us -> none
  transfers between devices with their start and end apart: 5 -> 12, of which waited for: 4 -> 5; matrix products, arithmetic and copies ran while one was open for 3% -> 4% of each run, Pallas kernels for 0% -> 13%
where the time goes in v1:
time: 115 us; the launch traced here: 114 us
  Pallas kernels  67.9 us (59%)
  local copies, waits for them, and re-layouts  15.4 us (13%)
  starting transfers between devices  14.5 us (13%)
  waiting for transfers between devices  13.3 us (12%)
  other arithmetic  2.14 us (2%)
  between operations  1.22 us (1%)
    pallas_call x1, Pallas kernels, middle_call(): pl.pallas_call(middle_kernel, name='middle', out_shape=[shape_of((SEQ, D)...  32.1 us
    unnamed x66, local copies, waits for them, and re-layouts  14.5 us
    ppermute x5, waiting for transfers between devices, summed(): lax.ppermute(array_in, axis, [(i, i ^ step) for i in range(size)])  13.3 us
    pallas_call x1, Pallas kernels, late_call(): pl.pallas_call(late_kernel, name='late', out_shape=[shape_of((SEQ, D), bf...  11.2 us
    ppermute x5, starting transfers between devices, summed(): lax.ppermute(array_in, axis, [(i, i ^ step) for i in range(size)])  10.3 us
    pallas_call x1, Pallas kernels, final_call(): pl.pallas_call(body, name='reparam', out_shape=[shape_of((PREFIX, D), f32...  9.98 us
    pallas_call x1, Pallas kernels, first_call(): pl.pallas_call(first_kernel, name='first_attention', out_shape=head_outpu...  9.23 us
    ppermute x7, starting transfers between devices, swapped(): return lax.ppermute(array_in, 'pipe', [(0, 1), (1, 0)])  4.18 us
  transfers between devices with their start and end apart: 12, of which 5 were waited for; matrix products, arithmetic and copies ran while one was open for 4% of the time, Pallas kernels for 13%

profile of v1, /device:TPU:0, one launch (start us, length us, event | category | flops | bytes accessed | tf_op | source)
XLA Modules:
  0.0 114.4 jit_solution(12733601300254127515)
XLA Ops:
  2.3 1.4 %reduce.4 = f32[2048]{0:T(1024)S(1)} reduce(f32[1,2048]{1,0:T(1,128)} %param.33, f32[]{:T(128)} %broadcast.4), dimensions={0}, to_apply=%param.33.reduce_sub_computation.3 | reduce | bytes 16388 | tf_op args[12]
  6.5 2.2 %copy-done.1 = f32[512,2048]{1,0:T(8,128)S(1)} copy-done((f32[512,2048]{1,0:T(8,128)S(1)}, f32[512,2048]{1,0:T(8,128)}, u32[]{:S(2)}) %copy-start.1) | copy-done | bytes 4194328
  8.7 1.2 %copy-done.3 = f32[512,512]{1,0:T(8,128)S(1)} copy-done((f32[512,512]{1,0:T(8,128)S(1)}, f32[512,512]{1,0:T(8,128)}, u32[]{:S(2)}) %copy-start.3) | copy-done | bytes 1048600
  12.0 2.6 %prefix.1 = (f32[10,512]{1,0:T(8,128)S(1)}, bf16[4,16,512]{2,1,0:T(8,128)(2,1)S(1)}, bf16[4,512,16]{2,1,0:T(8,128)(2,1)S(1)}) custom-call(f32[10,512]{1,0:T(8,128)S(1)} %copy-done.26, f32[512,512]{1,0:T(8,128)S(1)} %copy-done.3, f32[1,512]{1,0:T(1,128)S(1)} %bitcast.9, f32[512,2048]{1,0:T(8,128)S(1)} %copy-done.1, f32[1,2048]{1,0:T(1,128)S(1)} %bitcast.8), custom_call_target="tpu_custom_call" | custom-call | tf_op jit(solution)/shard_map/prefix/pallas_call | solution.py:307
  14.7 9.2 %first_attention.1 = (bf16[512,512]{1,0:T(8,128)(2,1)S(1)}, bf16[512,512]{1,0:T(8,128)(2,1)S(1)}, bf16[512,512]{1,0:T(8,128)(2,1)S(1)}, bf16[4,1152,256]{2,1,0:T...) custom-call(bf16[2,1,512,512]{3,2,1,0:T(8,128)(2,1)S(1)} %copy-done., ...), custom_call_target="tpu_custom_call" | custom-call | tf_op jit(solution)/shard_map/first_attention/pallas_call | solution.py:352
  24.1 2.7 %first_feed.1 = (bf16[512,2048]{1,0:T(8,128)(2,1)S(1)}, bf16[512,2048]{1,0:T(8,128)(2,1)S(1)}) custom-call(bf16[512,512]{1,0:T(8,128)(2,1)S(1)} %get-tuple-element.49.two_ref, f32[16,512]{1,0:T(8,128)S(1)} %concatenate.3.own_small, f32[16,512]{1,0:T(8,128)S(1)} %collective-permute-done.other_small, bf16[1,512,2048]{2,1,0:T(8,128)(2,1)S(1)} %copy-done, ...), custom_call_target="tpu_custom_call" | custom-call | tf_op jit(solution)/shard_map/first_feed/pallas_call | solution.py:381
  26.9 1.4 %copy-done.9 = bf16[512,2048]{1,0:T(8,128)(2,1)} copy-done((bf16[512,2048]{1,0:T(8,128)(2,1)}, bf16[512,2048]{1,0:T(8,128)(2,1)S(1)}, u32[]{:S(2)}) %copy-start.9) | copy-done | bytes 2097176
  28.3 1.3 %copy-done.10 = bf16[512,2048]{1,0:T(8,128)(2,1)} copy-done((bf16[512,2048]{1,0:T(8,128)(2,1)}, bf16[512,2048]{1,0:T(8,128)(2,1)S(1)}, u32[]{:S(2)}) %copy-start.10) | copy-done | bytes 2097176
  30.4 32.1 %middle.1 = (bf16[512,512]{1,0:T(8,128)(2,1)}, bf16[512,2048]{1,0:T(8,128)(2,1)}, bf16[512,512]{1,0:T(8,128)(2,1)}, f32[512,512]{1,0:T(8,128)}, bf16[512,512]{1,...) custom-call(bf16[2,1,512,512]{3,2,1,0:T(8,128)(2,1)} %x_hbm.5, bf16[2,1,512,512]{3,2,1,0:T(8,128)(2,1)} %cot_hbm.1, ...), custom_call_target="tpu_custom_call" | custom-call | tf_op jit(solution)/shard_map/middle/pallas_call | solution.py:478
  63.6 1.0 copy-done.20
  64.6 1.0 copy-done.21
  65.7 1.0 copy-done.22
  66.7 11.2 %late.1 = (bf16[512,512]{1,0:T(8,128)(2,1)S(1)}, bf16[512,512]{1,0:T(8,128)(2,1)S(1)}, f32[512,512]{1,0:T(8,128)S(1)}, f32[512,512]{1,0:T(8,128)S(1)}) custom-call(bf16[2,1,512,512]{3,2,1,0:T(8,128)(2,1)} %x_hbm.5, f32[16,512]{1,0:T(8,128)S(1)} %copy-done.12, f32[16,512]{1,0:T(8,128)S(1)} %copy-done.15, bf16[1,512,1536]{2,1,0:T(8,128)(2,1)} %own_qkv.5, ...), custom_call_target="tpu_custom_call" | custom-call | tf_op jit(solution)/shard_map/late/pallas_call | solution.py:583
  77.9 2.5 %collective-permute-start.11 = (f32[512,512]{1,0:T(8,128)S(1)}, f32[512,512]{1,0:T(8,128)S(1)}, u32[]{:S(2)}, u32[]{:S(2)}) collective-permute-start(f32[512,512]{1,0:T(8,128)S(1)} %get-tuple-element.63), channel_id=1, source_target_pairs={{0,16},{16,0},{1,17},{17,1},{2,18},{18,2},{3,19},{19,3},{4,20},{20... | collective-permute-start | bytes 3145736 | tf_op jit(solution)/shard_map/ppermute | solution.py:676
  81.0 2.6 %collective-permute-done.5 = f32[40,512]{1,0:T(8,128)S(1)} collective-permute-done((f32[40,512]{1,0:T(8,128)S(1)}, f32[40,512]{1,0:T(8,128)S(1)}, u32[]{:S(2)}, u32[]{:S(2)}) %collective-permute-start.5) | collective-permute-done | bytes 81952 | tf_op jit(solution)/shard_map/ppermute | solution.py:685
  83.6 3.0 %collective-permute-start.6 = (f32[40,512]{1,0:T(8,128)S(1)}, f32[40,512]{1,0:T(8,128)S(1)}, u32[]{:S(2)}, u32[]{:S(2)}) collective-permute-start(f32[40,512]{1,0:T(8,128)S(1)} %add.15), channel_id=1, source_target_pairs={{0,1},{1,0},{2,3},{3,2},{4,5},{5,4},{6,7},{7,6},{8,9},{9,8},{10,11... | collective-permute-start | bytes 245768 | tf_op jit(solution)/shard_map/ppermute | solution.py:685
  86.6 3.0 %collective-permute-done.6 = f32[40,512]{1,0:T(8,128)S(1)} collective-permute-done((f32[40,512]{1,0:T(8,128)S(1)}, f32[40,512]{1,0:T(8,128)S(1)}, u32[]{:S(2)}, u32[]{:S(2)}) %collective-permute-start.6) | collective-permute-done | bytes 81952 | tf_op jit(solution)/shard_map/ppermute | solution.py:685
  89.6 1.8 %collective-permute-start.7 = (f32[40,512]{1,0:T(8,128)S(1)}, f32[40,512]{1,0:T(8,128)S(1)}, u32[]{:S(2)}, u32[]{:S(2)}) collective-permute-start(f32[40,512]{1,0:T(8,128)S(1)} %add.16), channel_id=1, source_target_pairs={{0,2},{1,3},{2,0},{3,1},{4,6},{5,7},{6,4},{7,5},{8,10},{9,11},{10,... | collective-permute-start | bytes 245768 | tf_op jit(solution)/shard_map/ppermute | solution.py:685
  91.4 2.7 %collective-permute-done.7 = f32[40,512]{1,0:T(8,128)S(1)} collective-permute-done((f32[40,512]{1,0:T(8,128)S(1)}, f32[40,512]{1,0:T(8,128)S(1)}, u32[]{:S(2)}, u32[]{:S(2)}) %collective-permute-start.7) | collective-permute-done | bytes 81952 | tf_op jit(solution)/shard_map/ppermute | solution.py:685
  94.1 1.9 %collective-permute-start.8 = (f32[40,512]{1,0:T(8,128)S(1)}, f32[40,512]{1,0:T(8,128)S(1)}, u32[]{:S(2)}, u32[]{:S(2)}) collective-permute-start(f32[40,512]{1,0:T(8,128)S(1)} %add.17), channel_id=1, source_target_pairs={{0,4},{4,0},{8,12},{12,8},{1,5},{5,1},{9,13},{13,9},{2,6},{6,2},{1... | collective-permute-start | bytes 245768 | tf_op jit(solution)/shard_map/ppermute | solution.py:685
  96.0 2.6 %collective-permute-done.8 = f32[40,512]{1,0:T(8,128)S(1)} collective-permute-done((f32[40,512]{1,0:T(8,128)S(1)}, f32[40,512]{1,0:T(8,128)S(1)}, u32[]{:S(2)}, u32[]{:S(2)}) %collective-permute-start.8) | collective-permute-done | bytes 81952 | tf_op jit(solution)/shard_map/ppermute | solution.py:685
  98.6 3.1 %collective-permute-start.9 = (f32[40,512]{1,0:T(8,128)S(1)}, f32[40,512]{1,0:T(8,128)S(1)}, u32[]{:S(2)}, u32[]{:S(2)}) collective-permute-start(f32[40,512]{1,0:T(8,128)S(1)} %add.18), channel_id=1, source_target_pairs={{0,8},{4,12},{8,0},{12,4},{1,9},{5,13},{9,1},{13,5},{2,10},{6,14},... | collective-permute-start | bytes 245768 | tf_op jit(solution)/shard_map/ppermute | solution.py:685
  101.8 2.4 %collective-permute-done.9 = f32[40,512]{1,0:T(8,128)S(1)} collective-permute-done((f32[40,512]{1,0:T(8,128)S(1)}, f32[40,512]{1,0:T(8,128)S(1)}, u32[]{:S(2)}, u32[]{:S(2)}) %collective-permute-start.9) | collective-permute-done | bytes 81952 | tf_op jit(solution)/shard_map/ppermute | solution.py:685
  104.2 10.0 %reparam.1 = (f32[10,512]{1,0:T(8,128)}, f32[512,512]{1,0:T(8,128)}, f32[1,512]{1,0:T(1,128)}, f32[512,256]{1,0:T(8,128)}, f32[1,256]{1,0:T(1,128)}, /*index=5*/...) custom-call(f32[40,512]{1,0:T(8,128)S(1)} %add.19.refs_0_, f32[10,512]{1,0:T(8,128)S(1)} %get-tuple-element.52.refs_1_, ...), custom_call_target="tpu_custom_call" | custom-call | tf_op jit(solution)/shard_map/reparam/pallas_call | solution.py:656
  (83 shorter events, 9.1 us)
Async XLA Ops:
  0.6 23.4 %collective-permute-start.3 = (bf16[1,512,2048]{2,1,0:T(8,128)(2,1)}, bf16[1,512,2048]{2,1,0:T(8,128)(2,1)}, u32[]{:S(2)}, u32[]{:S(2)}) collective-permute-start(bf16[1,512,2048]{2,1,0:T(8,128)(2,1)} %own_in.5), channel_id=1, source_target_pairs={{0,16},{16,0},{1,17},{17,1},{2,18},{18,2},{3,19},{19,3},{4,20},{20... | collective-permute-start | bytes 6291464 | tf_op jit(solution)/shard_map/ppermute | solution.py:676
  1.1 28.4 %collective-permute-start.4 = (bf16[1,2048,512]{2,1,0:T(8,128)(2,1)}, bf16[1,2048,512]{2,1,0:T(8,128)(2,1)}, u32[]{:S(2)}, u32[]{:S(2)}) collective-permute-start(bf16[1,2048,512]{2,1,0:T(8,128)(2,1)} %own_out.3), channel_id=1, source_target_pairs={{0,16},{16,0},{1,17},{17,1},{2,18},{18,2},{3,19},{19,3},{4,20},{20... | collective-permute-start | bytes 6291464 | tf_op jit(solution)/shard_map/ppermute | solution.py:676
  1.2 13.4 %collective-permute-start.1 = (bf16[1,512,1536]{2,1,0:T(8,128)(2,1)}, bf16[1,512,1536]{2,1,0:T(8,128)(2,1)}, u32[]{:S(2)}, u32[]{:S(2)}) collective-permute-start(bf16[1,512,1536]{2,1,0:T(8,128)(2,1)} %own_qkv.5), channel_id=1, source_target_pairs={{0,16},{16,0},{1,17},{17,1},{2,18},{18,2},{3,19},{19,3},{4,20},{20... | collective-permute-start | bytes 4718600 | tf_op jit(solution)/shard_map/ppermute | solution.py:676
  1.7 27.9 %collective-permute-start.2 = (bf16[1,512,512]{2,1,0:T(8,128)(2,1)}, bf16[1,512,512]{2,1,0:T(8,128)(2,1)S(1)}, u32[]{:S(2)}, u32[]{:S(2)}) collective-permute-start(bf16[1,512,512]{2,1,0:T(8,128)(2,1)} %own_attn.3), channel_id=1, source_target_pairs={{0,16},{16,0},{1,17},{17,1},{2,18},{18,2},{3,19},{19,3},{4,20},{20... | collective-permute-start | bytes 1572872 | tf_op jit(solution)/shard_map/ppermute | solution.py:676
  5.3 18.8 %copy-start.11 = (f32[16,512]{1,0:T(8,128)}, f32[16,512]{1,0:T(8,128)S(1)}, u32[]{:S(2)}) copy-start(f32[16,512]{1,0:T(8,128)S(1)} %concatenate.3.own_small) | copy-start | bytes 98308
  5.3 9.4 %collective-permute-start = (f32[16,512]{1,0:T(8,128)S(1)}, f32[16,512]{1,0:T(8,128)S(1)}, u32[]{:S(2)}, u32[]{:S(2)}) collective-permute-start(f32[16,512]{1,0:T(8,128)S(1)} %concatenate.3.own_small), channel_id=1, source_target_pairs={{0,16},{16,0},{1,17},{17,1},{2,18},{18,2},{3,19},{19,3},{4,20},{20... | collective-permute-start | bytes 98312 | tf_op jit(solution)/shard_map/ppermute | solution.py:676
  14.6 9.3 %copy-start.8 = (bf16[4,512,16]{2,1,0:T(8,128)(2,1)}, bf16[4,512,16]{2,1,0:T(8,128)(2,1)S(1)}, u32[]{:S(2)}) copy-start(bf16[4,512,16]{2,1,0:T(8,128)(2,1)S(1)} %get-tuple-element.40.low_t) | copy-start | bytes 196612
  14.6 9.3 %copy-start.23 = (bf16[4,16,512]{2,1,0:T(8,128)(2,1)}, bf16[4,16,512]{2,1,0:T(8,128)(2,1)S(1)}, u32[]{:S(2)}) copy-start(bf16[4,16,512]{2,1,0:T(8,128)(2,1)S(1)} %get-tuple-element.39.low) | copy-start | bytes 196612
  14.7 9.4 %copy-start.14 = (f32[16,512]{1,0:T(8,128)}, f32[16,512]{1,0:T(8,128)S(1)}, u32[]{:S(2)}) copy-start(f32[16,512]{1,0:T(8,128)S(1)} %collective-permute-done.other_small) | copy-start | bytes 98308
  14.7 9.4 %copy-start = (bf16[1,512,2048]{2,1,0:T(8,128)(2,1)S(1)}, bf16[1,512,2048]{2,1,0:T(8,128)(2,1)}, u32[]{:S(2)}) copy-start(bf16[1,512,2048]{2,1,0:T(8,128)(2,1)} %own_in.5) | copy-start | bytes 6291460
  24.0 2.9 %copy-start.13 = (f32[1152,128]{1,0:T(8,128)}, f32[1152,128]{1,0:T(8,128)S(1)}, u32[]{:S(2)}) copy-start(f32[1152,128]{1,0:T(8,128)S(1)} %get-tuple-element.41.mask_ref) | copy-start | bytes 1769476
  30.4 32.1 %copy-start.5 = (bf16[1,512,512]{2,1,0:T(8,128)(2,1)S(1)}, bf16[1,512,512]{2,1,0:T(8,128)(2,1)}, u32[]{:S(2)}) copy-start(bf16[1,512,512]{2,1,0:T(8,128)(2,1)} %own_attn.3) | copy-start | bytes 1572868
  30.4 32.1 %copy-start.12 = (f32[16,512]{1,0:T(8,128)S(1)}, f32[16,512]{1,0:T(8,128)}, u32[]{:S(2)}) copy-start(f32[16,512]{1,0:T(8,128)} %copy-done.11) | copy-start | bytes 98308
  30.4 32.1 %copy-start.15 = (f32[16,512]{1,0:T(8,128)S(1)}, f32[16,512]{1,0:T(8,128)}, u32[]{:S(2)}) copy-start(f32[16,512]{1,0:T(8,128)} %copy-done.14) | copy-start | bytes 98308
  66.7 13.8 %copy-start.31 = (f32[40,512]{1,0:T(8,128)S(1)}, f32[40,512]{1,0:T(8,128)}, u32[]{:S(2)}) copy-start(f32[40,512]{1,0:T(8,128)} %get-tuple-element.51) | copy-start | bytes 245764
  66.7 37.5 %copy-start.4 = (f32[512,512]{1,0:T(8,128)S(1)}, f32[512,512]{1,0:T(8,128)}, u32[]{:S(2)}) copy-start(f32[512,512]{1,0:T(8,128)} %refs_3_.1) | copy-start | bytes 3145732
  66.7 37.5 %copy-start.27 = (f32[10,512]{1,0:T(8,128)S(1)}, f32[10,512]{1,0:T(8,128)}, u32[]{:S(2)}) copy-start(f32[10,512]{1,0:T(8,128)} %refs_2_.1) | copy-start | bytes 61444
  77.9 26.3 %collective-permute-start.11 = (f32[512,512]{1,0:T(8,128)S(1)}, f32[512,512]{1,0:T(8,128)S(1)}, u32[]{:S(2)}, u32[]{:S(2)}) collective-permute-start(f32[512,512]{1,0:T(8,128)S(1)} %get-tuple-element.63), channel_id=1, source_target_pairs={{0,16},{16,0},{1,17},{17,1},{2,18},{18,2},{3,19},{19,3},{4,20},{20... | collective-permute-start | bytes 3145736 | tf_op jit(solution)/shard_map/ppermute | solution.py:676
  80.4 23.8 %collective-permute-start.10 = (bf16[512,512]{1,0:T(8,128)(2,1)S(1)}, bf16[512,512]{1,0:T(8,128)(2,1)S(1)}, u32[]{:S(2)}, u32[]{:S(2)}) collective-permute-start(bf16[512,512]{1,0:T(8,128)(2,1)S(1)} %get-tuple-element.61), channel_id=1, source_target_pairs={{0,16},{16,0},{1,17},{17,1},{2,18},{18,2},{3,19},{19,3},{4,20},{20... | collective-permute-start | bytes 1572872 | tf_op jit(solution)/shard_map/ppermute | solution.py:676
  80.5 3.1 %collective-permute-start.5 = (f32[40,512]{1,0:T(8,128)S(1)}, f32[40,512]{1,0:T(8,128)S(1)}, u32[]{:S(2)}, u32[]{:S(2)}) collective-permute-start(f32[40,512]{1,0:T(8,128)S(1)} %copy-done.31), channel_id=1, source_target_pairs={{0,16},{16,0},{1,17},{17,1},{2,18},{18,2},{3,19},{19,3},{4,20},{20... | collective-permute-start | bytes 245768 | tf_op jit(solution)/shard_map/ppermute | solution.py:685
  83.6 6.0 %collective-permute-start.6 = (f32[40,512]{1,0:T(8,128)S(1)}, f32[40,512]{1,0:T(8,128)S(1)}, u32[]{:S(2)}, u32[]{:S(2)}) collective-permute-start(f32[40,512]{1,0:T(8,128)S(1)} %add.15), channel_id=1, source_target_pairs={{0,1},{1,0},{2,3},{3,2},{4,5},{5,4},{6,7},{7,6},{8,9},{9,8},{10,11... | collective-permute-start | bytes 245768 | tf_op jit(solution)/shard_map/ppermute | solution.py:685
  89.6 4.5 %collective-permute-start.7 = (f32[40,512]{1,0:T(8,128)S(1)}, f32[40,512]{1,0:T(8,128)S(1)}, u32[]{:S(2)}, u32[]{:S(2)}) collective-permute-start(f32[40,512]{1,0:T(8,128)S(1)} %add.16), channel_id=1, source_target_pairs={{0,2},{1,3},{2,0},{3,1},{4,6},{5,7},{6,4},{7,5},{8,10},{9,11},{10,... | collective-permute-start | bytes 245768 | tf_op jit(solution)/shard_map/ppermute | solution.py:685
  94.1 4.5 %collective-permute-start.8 = (f32[40,512]{1,0:T(8,128)S(1)}, f32[40,512]{1,0:T(8,128)S(1)}, u32[]{:S(2)}, u32[]{:S(2)}) collective-permute-start(f32[40,512]{1,0:T(8,128)S(1)} %add.17), channel_id=1, source_target_pairs={{0,4},{4,0},{8,12},{12,8},{1,5},{5,1},{9,13},{13,9},{2,6},{6,2},{1... | collective-permute-start | bytes 245768 | tf_op jit(solution)/shard_map/ppermute | solution.py:685
  98.6 5.6 %collective-permute-start.9 = (f32[40,512]{1,0:T(8,128)S(1)}, f32[40,512]{1,0:T(8,128)S(1)}, u32[]{:S(2)}, u32[]{:S(2)}) collective-permute-start(f32[40,512]{1,0:T(8,128)S(1)} %add.18), channel_id=1, source_target_pairs={{0,8},{4,12},{8,0},{12,4},{1,9},{5,13},{9,1},{13,5},{2,10},{6,14},... | collective-permute-start | bytes 245768 | tf_op jit(solution)/shard_map/ppermute | solution.py:685
  (20 other events, 35.6 us)

commit v2 on v1

v2 whole, which is shorter than its diff:
```python
import math

import jax
import jax.numpy as jnp
import numpy as np
from jax import lax
from jax.experimental import pallas as pl
from jax.experimental.pallas import tpu as pltpu
from jax.sharding import PartitionSpec as P

D = 512
SEQ = 512
HEADS = 8
HD = 64
FF = 2048
ROT = 16
PREFIX = 10
PAD = 16
BLK = 128
BLOCKS = SEQ // BLK
PAIRS = HEADS // 2
LIVE = (1, 2, 3, 3)
P_ROWS = BLK * sum(LIVE)
P_START = (0, 128, 384, 768)

f32 = jnp.float32
bf16 = jnp.bfloat16
LOG2E = math.log2(math.e)
Q_SCALE = LOG2E * HD**-0.5
K_BACK = 1.0 / LOG2E
Q_BACK = HD**-0.5
NEG = -1e30

NN = (((1,), (0,)), ((), ()))
NT = (((1,), (1,)), ((), ()))
TN = (((0,), (0,)), ((), ()))

VMEM = pl.BlockSpec(memory_space=pltpu.VMEM)
NO_COPIES = ((),) * 4
ANY = pl.BlockSpec(memory_space=pltpu.HBM)
MIB = 1024 * 1024
LATE_MIB = 16

G1, B1, G2, B2, B_ATTN, B_OUT, B_QKV, B_IN = 0, 1, 2, 3, 4, 5, 6, 9
SMALL = 13 * D


def dot(left, right, dims):
    return lax.dot_general(left, right, dims, preferred_element_type=f32)


def shape_of(shape, dtype):
    return jax.ShapeDtypeStruct(shape, dtype)


def params_of(mib):
    return pltpu.CompilerParams(vmem_limit_bytes=mib * MIB)


def all_vmem():
    return pltpu.CompilerParams(vmem_limit_bytes=64 * MIB - 64 * 1024)


def small_row(small_ref, place):
    return small_ref[:, place * D : (place + 1) * D]


def estimate(flops, bytes_accessed):
    return pl.CostEstimate(flops=flops, bytes_accessed=bytes_accessed, transcendentals=0)


def rope_tables():
    inv_freq = 10000.0 ** (-2.0 * np.arange(ROT // 2) / ROT)
    angles = inv_freq[:, None] * np.arange(SEQ)[None, :]
    return np.concatenate([np.cos(angles), np.sin(angles)], axis=0).astype(np.float32)


class Copies:
    def __init__(self, sems):
        self.sems = sems
        self.count = 0

    def start(self, src, dst):
        copy = pltpu.make_async_copy(src, dst, self.sems.at[self.count])
        self.count += 1
        copy.start()
        return copy

    def of_layer(self, here, own, other, dst):
        sem = self.sems.at[self.count]
        self.count += 1
        copy = pltpu.make_async_copy(own, dst, sem)

        @pl.when(here)
        def _():
            copy.start()

        @pl.when(jnp.logical_not(here))
        def _():
            pltpu.make_async_copy(other, dst, sem).start()

        return copy


def wait_all(*copies):
    for copy in copies:
        copy.wait()


def normalized(hidden):
    mean = jnp.mean(hidden, axis=-1, keepdims=True)
    centered = hidden - mean
    variance = jnp.mean(centered * centered, axis=-1, keepdims=True)
    scale = lax.rsqrt(variance + 1e-05)
    return centered * scale, scale


def rope_heads(rows, cos, sin):
    parts = []
    for head in range(rows.shape[0] // HD):
        base = head * HD
        lead = rows[base : base + 8]
        tail = rows[base + 8 : base + 16]
        parts += [lead * cos - tail * sin, tail * cos + lead * sin, rows[base + 16 : base + HD]]
    return jnp.concatenate(parts, axis=0)


def fill_mask(seg_ref, mask_ref):
    seg_row = seg_ref[...].astype(f32)
    seg_col = jnp.transpose(jnp.broadcast_to(seg_row, (8, SEQ)))[:, 0:1]
    for block in range(BLOCKS):
        for key_block in range(block + 1 - LIVE[block], block + 1):
            seen = seg_col[key_block * BLK : (key_block + 1) * BLK] == (
                seg_row[:, block * BLK : (block + 1) * BLK]
            )
            if key_block == block:
                key_pos = lax.broadcasted_iota(jnp.int32, (BLK, BLK), 0)
                query_pos = lax.broadcasted_iota(jnp.int32, (BLK, BLK), 1)
                seen = seen & (key_pos <= query_pos)
            start = P_START[block] + (key_block - (block + 1 - LIVE[block])) * BLK
            mask_ref[start : start + BLK, :] = jnp.where(seen, 0.0, NEG)


def project_heads(normed, w_ref, small_ref, cos, sin, q_t, k_t, k_m, v_m, v_t):
    bias = small_row(small_ref, B_QKV)
    rows = dot(normed, w_ref[:, :D], NN) + bias
    q_t[...] = (rope_heads(jnp.transpose(rows), cos, sin) * Q_SCALE).astype(bf16)
    bias = small_row(small_ref, B_QKV + 1)
    rows = dot(normed, w_ref[:, D : 2 * D], NN) + bias
    keys = rope_heads(jnp.transpose(rows), cos, sin).astype(bf16)
    k_t[...] = keys
    k_m[...] = jnp.transpose(keys)
    bias = small_row(small_ref, B_QKV + 2)
    values = (dot(normed, w_ref[:, 2 * D :], NN) + bias).astype(bf16)
    v_m[...] = values
    v_t[...] = jnp.transpose(values)


def block_diagonal(pair_rows):
    zeros = jnp.zeros((HD, BLK), pair_rows.dtype)
    return jnp.concatenate(
        [
            jnp.concatenate([pair_rows[:HD], zeros], axis=1),
            jnp.concatenate([zeros, pair_rows[HD:]], axis=1),
        ],
        axis=0,
    )


def from_diagonal(both):
    return jnp.concatenate([both[:HD, :BLK], both[HD:, BLK:]], axis=0)


def per_head(row, rows=HD):
    return jnp.concatenate(
        [
            jnp.broadcast_to(row[:, :BLK], (rows, BLK)),
            jnp.broadcast_to(row[:, BLK:], (rows, BLK)),
        ],
        axis=0,
    )


def geometry(block):
    live = LIVE[block] * BLK
    end = (block + 1) * BLK
    start = P_START[block]
    return slice(end - live, end), slice(block * BLK, end), slice(start, start + live)


def attend(q_t, k_m, v_t, pre_k, pre_v_t, mask_ref, p_ref, pp_ref, inv_ref, mixed_ref, then=None):
    pad_mask = jnp.where(lax.broadcasted_iota(jnp.int32, (PAD, 1), 0) < PREFIX, 0.0, NEG)

    def score(feats, block):
        keys, tokens, rows = geometry(block)
        queries = block_diagonal(q_t[feats, tokens])
        mask = mask_ref[rows, :]
        scores = dot(k_m[keys, feats], queries, NN) + jnp.concatenate([mask, mask], axis=1)
        return scores, dot(pre_k[:, feats], queries, NN) + pad_mask

    def soften(pair, block, scores, pre_scores):
        _, _, rows = geometry(block)
        peak = jnp.maximum(
            jnp.max(scores, axis=0, keepdims=True), jnp.max(pre_scores, axis=0, keepdims=True)
        )
        expo = jnp.exp2(scores - peak)
        pre_expo = jnp.exp2(pre_scores - peak)
        total = jnp.sum(expo, axis=0, keepdims=True) + jnp.sum(pre_expo, axis=0, keepdims=True)
        inverse = 1.0 / total
        expo = expo.astype(bf16)
        pre_expo = pre_expo.astype(bf16)
        p_ref[pair, rows, :] = expo
        pp_ref[pair, block] = pre_expo
        inv_ref[pair, block] = jnp.broadcast_to(inverse, (8, 2 * BLK))
        return expo, pre_expo, inverse

    def mix(feats, block, expo, pre_expo, inverse):
        keys, tokens, _ = geometry(block)
        mixed = dot(v_t[feats, keys], expo, NN) + dot(pre_v_t[feats, :], pre_expo, NN)
        mixed_ref[feats, tokens] = (from_diagonal(mixed) * per_head(inverse)).astype(bf16)

    for pair in range(PAIRS):
        feats = slice(pair * BLK, (pair + 1) * BLK)
        scores = [score(feats, block) for block in range(BLOCKS)]
        soft = [soften(pair, block, *scores[block]) for block in range(BLOCKS)]
        for block in range(BLOCKS):
            mix(feats, block, *soft[block])
        if then is not None:
            then(pair)


def attend_back(grad_t, q_t, k_t, v_m, pre_k_t, pre_v, p_ref, pp_ref, inv_ref, mixed_ref,
                dq_ref, dk_ref, dv_ref, pre_grad, pre_row):
    def value_grads(pair, feats, block):
        keys, tokens, _ = geometry(block)
        scaled = (grad_t[feats, tokens] * per_head(inv_ref[pair, block][0:1, :])).astype(bf16)
        products = scaled.astype(f32) * mixed_ref[feats, tokens].astype(f32)
        inner = jnp.concatenate(
            [
                jnp.sum(products[:HD], axis=0, keepdims=True),
                jnp.sum(products[HD:], axis=0, keepdims=True),
            ],
            axis=1,
        )
        grads = block_diagonal(scaled)
        return grads, inner, dot(v_m[keys, feats], grads, NN), dot(pre_v[:, feats], grads, NN)

    def score_grads(pair, block, inner, grad_probs, pre_grad_probs):
        _, _, rows = geometry(block)
        probs = p_ref[pair, rows, :].astype(f32)
        pre_probs = pp_ref[pair, block].astype(f32)
        return (
            (probs * (grad_probs - inner)).astype(bf16),
            (pre_probs * (pre_grad_probs - inner)).astype(bf16),
        )

    def out_grads(pair, feats, block, grads, grad_scores, pre_scores):
        keys, tokens, rows = geometry(block)
        queries = block_diagonal(q_t[feats, tokens])
        dq = dot(k_t[feats, keys], grad_scores, NN) + dot(pre_k_t[feats, :], pre_scores, NN)
        dq_ref[feats, tokens] = from_diagonal(dq)
        return (
            dot(queries, grad_scores, NT),
            dot(grads, p_ref[pair, rows, :], NT),
            dot(pre_scores, queries, NT),
            dot(pp_ref[pair, block], grads, NT),
        )

    def by_keys(outs, which, key_block):
        total = None
        for block in range(BLOCKS):
            place = key_block - (block + 1 - LIVE[block])
            if 0 <= place < LIVE[block]:
                part = outs[block][which][:, place * BLK : (place + 1) * BLK]
                total = part if total is None else total + part
        return total

    for pair in range(PAIRS):
        feats = slice(pair * BLK, (pair + 1) * BLK)
        first = [value_grads(pair, feats, block) for block in range(BLOCKS)]
        second = [score_grads(pair, block, *first[block][1:]) for block in range(BLOCKS)]
        outs = [
            out_grads(pair, feats, block, first[block][0], *second[block])
            for block in range(BLOCKS)
        ]
        for key_block in range(BLOCKS):
            keys = slice(key_block * BLK, (key_block + 1) * BLK)
            dk_ref[feats, keys] = by_keys(outs, 0, key_block)
            dv_ref[feats, keys] = by_keys(outs, 1, key_block)
        pre_dk = outs[0][2] + outs[1][2] + outs[2][2] + outs[3][2]
        pre_dv = outs[0][3] + outs[1][3] + outs[2][3] + outs[3][3]
        pre_grad[pre_row : pre_row + PAD, feats] = pre_dk * K_BACK
        pre_grad[pre_row + PAD : pre_row + 2 * PAD, feats] = pre_dv


def pack_grads(dq_ref, dk_ref, dv_ref, cos, sin, packed_t):
    packed_t[:D, :] = (rope_heads(dq_ref[...], cos, -sin) * Q_BACK).astype(bf16)
    packed_t[D : 2 * D, :] = (rope_heads(dk_ref[...], cos, -sin) * K_BACK).astype(bf16)
    packed_t[2 * D :, :] = dv_ref[...].astype(bf16)


def gelu_both(before):
    cdf = 0.5 + 0.5 * lax.erf(before * (0.5**0.5))
    density = jnp.exp2(before * before * (-0.5 * LOG2E)) * (1.0 / math.sqrt(2.0 * math.pi))
    return before * cdf, cdf + before * density


FF_CHUNK = 512


def chunk_of(index):
    return slice(index * FF_CHUNK, (index + 1) * FF_CHUNK)


def feed_in(normed, w_ref, small_ref, act_ref, slope_ref, arrivals):
    for chunk in range(FF // FF_CHUNK):
        cols = chunk_of(chunk)
        wait_all(*arrivals[chunk])
        before = dot(normed, w_ref[:, cols], NN) + small_row(small_ref, B_IN + chunk)
        act, slope = gelu_both(before)
        act_ref[:, cols] = act.astype(bf16)
        slope_ref[:, cols] = slope.astype(bf16)


def layer_result(hidden, mixed_t, w_attn, act_ref, w_out, small_ref):
    attn_out = dot(jnp.transpose(mixed_t), w_attn, NN) + small_row(small_ref, B_ATTN)
    ff_out = dot(act_ref[...], w_out, NN) + small_row(small_ref, B_OUT)
    return hidden + attn_out + ff_out


def feed_back(grad, w_out, w_in, slope_ref, arrivals):
    total = jnp.zeros((SEQ, D), f32)
    for chunk in range(FF // FF_CHUNK):
        cols = chunk_of(chunk)
        wait_all(*arrivals[chunk])
        grad_act = dot(grad, w_out[cols, :], NT)
        grad_before = (grad_act * slope_ref[:, cols].astype(f32)).astype(bf16)
        total = total + dot(grad_before, w_in[:, cols], NT)
    return total


def norms_back(grad, hidden, grad_two, packed_t, w_qkv, small_ref):
    grad_one = jnp.transpose(dot(w_qkv, packed_t, NN))
    grad_hat = (
        grad_one * small_row(small_ref, G1) + grad_two * small_row(small_ref, G2)
    )
    hat, scale = normalized(hidden)
    mean_one = jnp.mean(grad_hat, axis=-1, keepdims=True)
    mean_two = jnp.mean(grad_hat * hat, axis=-1, keepdims=True)
    return grad.astype(f32) + scale * (grad_hat - mean_one - hat * mean_two)


def halves(values):
    high = values.astype(bf16)
    return high, (values - high.astype(f32)).astype(bf16)


def padded(values):
    return jnp.concatenate([values, jnp.zeros((PAD - PREFIX, values.shape[1]), f32)], axis=0)


def few_rows_dot(left, right):
    left_high, left_rest = halves(padded(left))
    right_high, right_rest = halves(right)
    both = dot(jnp.concatenate([left_high, left_rest], axis=0), right_high, NN)
    return both[:PAD] + both[PAD:] + dot(left_high, right_rest, NN)


def stacked_dot(left, right):
    left_high, left_rest = halves(padded(left))
    right_high, right_rest = halves(padded(right))
    return dot(
        jnp.concatenate([left_high, left_high, left_rest], axis=0),
        jnp.concatenate([right_high, right_rest, right_high], axis=0),
        TN,
    )


def small_kernel(gain_one, shift_one, gain_two, shift_two, attn_b, out_b, qkv_b, in_b, packed_out, packed, sems):
    copies = Copies(sems)
    places = [(gain_one, 0), (shift_one, 1), (gain_two, 2), (shift_two, 3), (attn_b, 4), (out_b, 5)]
    places += [(qkv_b, 6), (in_b, 9)]
    wait_all(
        *[
            copies.start(row, packed.at[:, place * D : place * D + row.shape[1]])
            for row, place in places
        ]
    )
    wait_all(copies.start(packed, packed_out))


def small_call(*arrays):
    return pl.pallas_call(
        small_kernel,
        name="small_parameters",
        cost_estimate=estimate(SMALL, 8 * SMALL),
        out_shape=shape_of((1, SMALL), f32),
        in_specs=[ANY] * 8,
        out_specs=ANY,
        scratch_shapes=[pltpu.VMEM((1, SMALL), f32), pltpu.SemaphoreType.DMA((9,))],
        compiler_params=all_vmem(),
    )(*arrays)


def prefix_kernel(embed_hbm, up_hbm, up_b_hbm, out_hbm, out_b_hbm, hidden_out, low_out, low_t_out,
                  hidden, low, low_t, embed, up_w, up_b, out_w, out_b, sems):
    copies = Copies(sems)
    early = [
        copies.start(src, dst)
        for src, dst in ((embed_hbm, embed), (up_hbm, up_w), (up_b_hbm, up_b.at[0]))
    ]
    parts = [
        copies.start(out_hbm.at[:, i * D : (i + 1) * D], out_w.at[:, i * D : (i + 1) * D])
        for i in range(4)
    ]
    late = [copies.start(out_b_hbm, out_b.at[0])]
    wait_all(*early)
    units = jnp.tanh(few_rows_dot(embed[...], up_w[...])[:PREFIX] + up_b[...])
    hidden[...] = units
    wait_all(*late)
    real = lax.broadcasted_iota(jnp.int32, (PAD, 1), 0) < PREFIX
    for part in range(4):
        cols = slice(part * D, (part + 1) * D)
        parts[part].wait()
        states = jnp.where(real, few_rows_dot(units, out_w[:, cols]) + out_b[:, cols], 0.0)
        low[part] = states.astype(bf16)
        tall = jnp.concatenate([states, jnp.zeros((BLK - PAD, D), f32)], axis=0)
        low_t[part] = jnp.transpose(tall)[:, :PAD].astype(bf16)
    wait_all(
        copies.start(low, low_out), copies.start(low_t, low_t_out), copies.start(hidden, hidden_out)
    )


def prefix_call(*arrays):
    shapes = (((PREFIX, D), f32), ((4, PAD, D), bf16), ((4, D, PAD), bf16))
    return pl.pallas_call(
        prefix_kernel,
        name="prefix",
        cost_estimate=estimate(2 * 6 * PAD * D * 5 * D, 6 * MIB),
        out_shape=[shape_of(*pair) for pair in shapes],
        in_specs=[ANY] * 5,
        out_specs=[ANY] * 3,
        scratch_shapes=[pltpu.VMEM(*pair) for pair in shapes]
        + [
            pltpu.VMEM((PREFIX, D), f32),
            pltpu.VMEM((D, D), f32),
            pltpu.VMEM((1, D), f32),
            pltpu.VMEM((D, 4 * D), f32),
            pltpu.VMEM((1, 4 * D), f32),
            pltpu.SemaphoreType.DMA((11,)),
        ],
        compiler_params=all_vmem(),
    )(*arrays)


HEAD_SHAPES = (
    ((D, SEQ), bf16),
    ((D, SEQ), bf16),
    ((SEQ, D), bf16),
    ((PAIRS, P_ROWS, 2 * BLK), bf16),
    ((PAIRS, BLOCKS, PAD, 2 * BLK), bf16),
    ((PAIRS, BLOCKS, 8, 2 * BLK), f32),
    ((D, SEQ), bf16),
)
FIRST_SHAPES = HEAD_SHAPES + (((SEQ, D), bf16),)


def first_kernel(x_hbm, seg_hbm, own_small, other_small, own_qkv, other_qkv, low_hbm, low_t_hbm, tables_hbm,
                 *refs):
    outs, (q_t, k_t, v_m, p_ref, pp_ref, inv_ref, mixed_ref, two_ref), rest = refs[:8], refs[8:16], refs[16:]
    mask_ref, x_ref, small_ref, w_ref, low, low_t, tables, seg, k_m, v_t, sems = rest
    section = lax.axis_index("pipe")
    here = section == 0
    copies = Copies(sems)
    x_copy = copies.start(x_hbm.at[section, 0], x_ref)
    seg_copy = copies.start(seg_hbm.at[section], seg)
    small_copy = copies.of_layer(here, own_small, other_small, small_ref)
    late = [
        copies.of_layer(here, own_qkv.at[0, rows], other_qkv.at[0, rows], w_ref.at[rows])
        for rows in (slice(i * BLK, (i + 1) * BLK) for i in range(4))
    ]
    late += [
        copies.start(src, dst)
        for src, dst in ((tables_hbm, tables), (low_hbm, low), (low_t_hbm, low_t))
    ]
    seg_copy.wait()
    fill_mask(seg, mask_ref)
    wait_all(x_copy, small_copy)
    hat, _ = normalized(x_ref[...].astype(f32))
    normed = (hat * small_row(small_ref, G1) + small_row(small_ref, B1)).astype(bf16)
    two_ref[...] = (hat * small_row(small_ref, G2) + small_row(small_ref, B2)).astype(bf16)
    done = [copies.start(two_ref, outs[7])]
    wait_all(*late)
    project_heads(normed, w_ref, small_ref, tables[:8, :], tables[8:, :], q_t, k_t, k_m, v_m, v_t)
    done += [copies.start(*pair) for pair in zip((q_t, k_t, v_m), outs[:3])]

    def then(pair):
        done.append(copies.start(p_ref.at[pair], outs[3].at[pair]))

    attend(q_t, k_m, v_t, low.at[0], low_t.at[1], mask_ref, p_ref, pp_ref, inv_ref, mixed_ref, then)
    done += [copies.start(*pair) for pair in zip((pp_ref, inv_ref, mixed_ref), outs[4:7])]
    wait_all(*done)


def first_call(*arrays):
    return pl.pallas_call(
        first_kernel,
        name="first_attention",
        cost_estimate=estimate(200 * SEQ * D * 3 * D, 40 * MIB),
        out_shape=[shape_of(*pair) for pair in FIRST_SHAPES],
        in_specs=[ANY] * 9,
        out_specs=[ANY] * 8,
        scratch_shapes=[pltpu.VMEM(*pair) for pair in FIRST_SHAPES]
        + [
            pltpu.VMEM((P_ROWS, BLK), f32),
            pltpu.VMEM((SEQ, D), bf16),
            pltpu.VMEM((1, SMALL), f32),
            pltpu.VMEM((D, 3 * D), bf16),
            pltpu.VMEM((4, PAD, D), bf16),
            pltpu.VMEM((4, D, PAD), bf16),
            pltpu.VMEM((2 * 8, SEQ), f32),
            pltpu.VMEM((1, SEQ), jnp.int32),
            pltpu.VMEM((SEQ, D), bf16),
            pltpu.VMEM((D, SEQ), bf16),
            pltpu.SemaphoreType.DMA((21,)),
        ],
        compiler_params=all_vmem(),
    )(*arrays)


WEIGHT_SHAPES = (((D, 3 * D), bf16), ((D, D), bf16), ((D, FF), bf16), ((FF, D), bf16))


def middle_kernel(*refs):
    def take(count):
        nonlocal refs
        taken, refs = refs[:count], refs[count:]
        return taken

    x_hbm, cot_hbm, seg_hbm, own_small, other_small = take(5)
    own, other = take(4), take(4)
    low_hbm, low_t_hbm, tables_hbm = take(3)
    saved_hbm = take(8)
    act_out, act_send, grad_out, grad_send, prefix_out = take(5)
    q0, k0, v0, p0, pp0, inv0, mixed0, two0 = take(8)
    w_qkv_zero, w_attn_zero, w_in_zero, w_out_zero = take(4)
    w_qkv, w_attn, w_in, w_out = take(4)
    q_t, k_t, v_m, p_ref, pp_ref, inv_ref, mixed_one = take(7)
    (x_ref, cot_ref, seg, mask, small_zero, small_one, low, low_t, tables, h_one, h_two, act_zero, slope_zero,
     act_one, slope_one, k_m, v_t, dq, dk, dv, packed, pre_grad, prefix_grad, grad_one, grad_low, grad_zero,
     sems) = refs
    section = lax.axis_index("pipe")
    zero, one = section == 0, section == 1
    copies = Copies(sems)

    def fetch_saved(which, dst):
        return copies.start(saved_hbm[which], dst)

    def weights(here, which, dst, index=()):
        index = (0,) + index
        view = dst.at[index[1:]] if len(index) > 1 else dst
        return copies.of_layer(here, own[which].at[index], other[which].at[index], view)

    def hand_over(layer, value, whole, send):
        sem = copies.sems.at[copies.count]
        copies.count += 1

        @pl.when(section == layer)
        def _():
            pltpu.make_async_copy(value, whole.at[0, section, 0], sem).start()

        @pl.when(section != layer)
        def _():
            pltpu.make_async_copy(value, send, sem).start()

        done.append(pltpu.make_async_copy(value, send, sem))

    everything = slice(None)
    done = []
    small_copy = copies.of_layer(zero, own_small, other_small, small_zero)
    two_copy = fetch_saved(7, two0)
    in_zero = [[weights(zero, 2, w_in_zero, (everything, chunk_of(i)))] for i in range(4)]
    out_copies = [
        fetch_saved(6, mixed0),
        weights(zero, 1, w_attn_zero),
        copies.start(x_hbm.at[section, 0], x_ref),
    ]
    out_copies += [weights(zero, 3, w_out_zero, (chunk_of(i),)) for i in range(4)]
    seg_copy = copies.start(seg_hbm.at[section], seg)
    wait_all(small_copy, two_copy)
    feed_in(two0[...], w_in_zero, small_zero, act_zero, slope_zero, in_zero)
    head_copies = [
        copies.of_layer(one, own_small, other_small, small_one),
        weights(one, 0, w_qkv),
        copies.start(tables_hbm, tables),
        copies.start(low_hbm, low),
        copies.start(low_t_hbm, low_t),
    ]
    in_one = [[weights(one, 2, w_in, (everything, chunk_of(i)))] for i in range(4)]
    seg_copy.wait()
    fill_mask(seg, mask)
    wait_all(*out_copies)
    h_one[...] = layer_result(
        x_ref[...].astype(f32), mixed0[...], w_attn_zero[...], act_zero, w_out_zero[...], small_zero
    ).astype(bf16)
    hand_over(0, h_one, act_out, act_send)

    back_copies = [copies.start(cot_hbm.at[section, 0], cot_ref)]
    back_copies += [weights(one, 3, w_out, (chunk_of(i),)) for i in range(4)]
    attn_copy = weights(one, 1, w_attn)
    late = [
        fetch_saved(which, dst)
        for which, dst in ((0, q0), (1, k0), (2, v0), (3, p0), (4, pp0), (5, inv0))
    ]
    qkv_copy = weights(zero, 0, w_qkv_zero)
    wait_all(*head_copies)
    cos, sin = tables[:8, :], tables[8:, :]
    hat, _ = normalized(h_one[...].astype(f32))
    normed = (hat * small_row(small_one, G1) + small_row(small_one, B1)).astype(bf16)
    two = (hat * small_row(small_one, G2) + small_row(small_one, B2)).astype(bf16)
    project_heads(normed, w_qkv, small_one, cos, sin, q_t, k_t, k_m, v_m, v_t)
    attend(q_t, k_m, v_t, low.at[2], low_t.at[3], mask, p_ref, pp_ref, inv_ref, mixed_one)
    feed_in(two, w_in, small_one, act_one, slope_one, in_one)
    wait_all(*back_copies)
    attn_copy.wait()
    h_two[...] = layer_result(
        h_one[...].astype(f32), mixed_one[...], w_attn[...], act_one, w_out[...], small_one
    ).astype(bf16)
    hand_over(1, h_two, act_out, act_send)

    grad = cot_ref[...]
    grad_two = feed_back(grad, w_out, w_in, slope_one, NO_COPIES)
    dq[...] = dot(w_attn[...], grad, NT)
    attend_back(dq, q_t, k_t, v_m, low_t.at[2], low.at[3], p_ref, pp_ref, inv_ref, mixed_one,
                dq, dk, dv, pre_grad, 2 * PAD)
    pack_grads(dq, dk, dv, cos, sin, packed)
    result = norms_back(grad, h_one[...].astype(f32), grad_two, packed[...], w_qkv[...], small_one)
    grad_one[...] = result
    grad_low[...] = result.astype(bf16)
    hand_over(1, grad_one, grad_out, grad_send)

    grad = grad_low[...]
    dq[...] = dot(w_attn_zero[...], grad, NT)
    wait_all(*late)
    attend_back(dq, q0, k0, v0, low_t.at[0], low.at[1], p0, pp0, inv0, mixed0,
                dq, dk, dv, pre_grad, 0)
    for part in range(4):
        prefix_grad[part * PREFIX : (part + 1) * PREFIX, :] = pre_grad[
            part * PAD : part * PAD + PREFIX, :
        ]
    done.append(copies.start(prefix_grad, prefix_out))
    pack_grads(dq, dk, dv, cos, sin, packed)
    grad_two = feed_back(grad, w_out_zero, w_in_zero, slope_zero, NO_COPIES)
    qkv_copy.wait()
    grad_zero[...] = norms_back(
        grad, x_ref[...].astype(f32), grad_two, packed[...], w_qkv_zero[...], small_zero
    )
    hand_over(0, grad_zero, grad_out, grad_send)
    wait_all(*done)


def middle_call(*arrays):
    scratch = FIRST_SHAPES + WEIGHT_SHAPES + WEIGHT_SHAPES + HEAD_SHAPES
    scratch += (
        ((SEQ, D), bf16),
        ((SEQ, D), bf16),
        ((1, SEQ), jnp.int32),
        ((P_ROWS, BLK), f32),
        ((1, SMALL), f32),
        ((1, SMALL), f32),
        ((4, PAD, D), bf16),
        ((4, D, PAD), bf16),
        ((2 * 8, SEQ), f32),
        ((SEQ, D), bf16),
        ((SEQ, D), bf16),
        ((SEQ, FF), bf16),
        ((SEQ, FF), bf16),
        ((SEQ, FF), bf16),
        ((SEQ, FF), bf16),
        ((SEQ, D), bf16),
        ((D, SEQ), bf16),
        ((D, SEQ), f32),
        ((D, SEQ), f32),
        ((D, SEQ), f32),
        ((3 * D, SEQ), bf16),
        ((4 * PAD, D), f32),
        ((4 * PREFIX, D), f32),
        ((SEQ, D), f32),
        ((SEQ, D), bf16),
        ((SEQ, D), f32),
    )
    return pl.pallas_call(
        middle_kernel,
        name="middle",
        cost_estimate=estimate(20 * SEQ * D * 6 * D, 20 * MIB),
        out_shape=[
            shape_of((1, 2, 1, SEQ, D), bf16),
            shape_of((SEQ, D), bf16),
            shape_of((1, 2, 1, SEQ, D), f32),
            shape_of((SEQ, D), f32),
            shape_of((4 * PREFIX, D), f32),
        ],
        in_specs=[ANY] * 24,
        out_specs=[ANY] * 5,
        scratch_shapes=[pltpu.VMEM(*pair) for pair in scratch] + [pltpu.SemaphoreType.DMA((44,))],
        compiler_params=all_vmem(),
    )(*arrays)


def turn_kernel(out_hbm, up_hbm, wide, up_high, up_rest, out_w, up_w, sems):
    copies = Copies(sems)
    up = copies.start(up_hbm, up_w)
    parts = [
        copies.start(out_hbm.at[:, i * D : (i + 1) * D], out_w.at[:, i * D : (i + 1) * D])
        for i in range(4)
    ]
    up.wait()
    up_high[...], up_rest[...] = halves(jnp.transpose(up_w[...]))
    for part in range(4):
        cols = slice(part * D, (part + 1) * D)
        parts[part].wait()
        wide[cols, :] = jnp.transpose(out_w[:, cols].astype(bf16))


def turn_call(*arrays):
    return pl.pallas_call(
        turn_kernel,
        name="turned_matrices",
        out_shape=[shape_of((4 * D, D), bf16), shape_of((D, D), bf16), shape_of((D, D), bf16)],
        in_specs=[ANY] * 2,
        out_specs=[VMEM] * 3,
        scratch_shapes=[
            pltpu.VMEM((D, 4 * D), f32),
            pltpu.VMEM((D, D), f32),
            pltpu.SemaphoreType.DMA((5,)),
        ],
        compiler_params=params_of(LATE_MIB),
        cost_estimate=estimate(SEQ * D * D, 8 * MIB),
    )(*arrays)


def final_kernel(col_width, grads_ref, hidden, embed, wide, up_high, up_rest, act_other, grad_other,
                 act_in, grad_in, d_embed, d_up, d_up_b, d_out, d_out_b, act_out, grad_out, sems):
    section = lax.axis_index("pipe")
    shard = lax.axis_index("dp")
    copies = Copies(sems)
    placed = [
        copies.start(act_other, act_out.at[0, 1 - section, 0]),
        copies.start(grad_other, grad_out.at[0, 1 - section, 0]),
    ]
    units = hidden[...]
    both = jnp.zeros((2 * PAD, D), f32)
    for part in range(4):
        high, rest = halves(padded(grads_ref[part * PREFIX : (part + 1) * PREFIX, :]))
        both = both + dot(
            jnp.concatenate([high, rest], axis=0), wide[part * D : (part + 1) * D, :], NN
        )
    grad_units = (both[:PAD] + both[PAD:])[:PREFIX]
    grad_pre = grad_units * (1.0 - units * units)
    d_up_b[...] = jnp.sum(grad_pre, axis=0, keepdims=True)
    d_up[...] = stacked_dot(embed[...], grad_pre)
    high, rest = halves(padded(grad_pre))
    both = dot(jnp.concatenate([high, rest], axis=0), up_high[...], NN)
    both = both[:PAD] + both[PAD:] + dot(high, up_rest[...], NN)
    d_embed[...] = both[:PREFIX]
    column = section * (2 * D) + shard * col_width
    own_cols = jnp.zeros((PREFIX, col_width), f32)
    for part in range(4):
        for piece in range(D // col_width):
            here = column == part * D + piece * col_width
            cols = slice(piece * col_width, (piece + 1) * col_width)
            rows = slice(part * PREFIX, (part + 1) * PREFIX)
            own_cols = jnp.where(here, grads_ref[rows, cols], own_cols)
    d_out[...] = stacked_dot(units, own_cols)
    d_out_b[...] = jnp.sum(own_cols, axis=0, keepdims=True)
    wait_all(*placed)


def final_call(col_width, *arrays):
    def body(*refs):
        final_kernel(col_width, *refs)

    return pl.pallas_call(
        body,
        name="reparam",
        out_shape=[
            shape_of((PREFIX, D), f32),
            shape_of((D, D), f32),
            shape_of((1, D), f32),
            shape_of((D, col_width), f32),
            shape_of((1, col_width), f32),
            shape_of((1, 2, 1, SEQ, D), bf16),
            shape_of((1, 2, 1, SEQ, D), f32),
        ],
        in_specs=[VMEM] * 8 + [ANY] * 2,
        out_specs=[VMEM] * 5 + [ANY] * 2,
        scratch_shapes=[pltpu.SemaphoreType.DMA((2,))],
        input_output_aliases={8: 5, 9: 6},
        compiler_params=params_of(LATE_MIB),
    )(*arrays)


def swapped(array_in):
    return lax.ppermute(array_in, "pipe", [(0, 1), (1, 0)])


def hops(axis):
    size = lax.axis_size(axis)
    steps = []
    step = 1
    while step < size:
        steps.append((axis, [(i, i ^ step) for i in range(size)]))
        step *= 2
    assert step == size
    return steps


def local(
    block_input,
    cotangent,
    segments,
    ln1_gain,
    ln1_shift,
    qkv_weight,
    qkv_bias,
    attn_weight,
    attn_bias,
    ln2_gain,
    ln2_shift,
    ff_in_weight,
    ff_in_bias,
    ff_out_weight,
    ff_out_bias,
    prefix_embed,
    up_weight,
    up_bias,
    out_weight,
    out_bias,
):
    other_qkv = swapped(qkv_weight)
    small = small_call(
        ln1_gain, ln1_shift, ln2_gain, ln2_shift, attn_bias, ff_out_bias, qkv_bias, ff_in_bias
    )
    other_small = swapped(small)
    small, prefix_embed = lax.optimization_barrier((small, prefix_embed))
    tables = jnp.asarray(rope_tables())
    hidden_units, low, low_t = prefix_call(prefix_embed, up_weight, up_bias, out_weight, out_bias)
    _, *later = lax.optimization_barrier((small, attn_weight, ff_in_weight, ff_out_weight))
    own = (qkv_weight, attn_weight, ff_in_weight, ff_out_weight)
    other = (other_qkv,) + tuple(swapped(weight) for weight in later)
    saved = first_call(
        block_input, segments, small, other_small, qkv_weight, other_qkv, low, low_t, tables
    )
    act, act_send, grad, grad_send, prefix_grad = middle_call(
        block_input, cotangent, segments, small, other_small, *own, *other, low, low_t, tables, *saved
    )

    def swap_acts(state):
        return dict(state, act=swapped(state["act"]))

    def swap_grads(state):
        return dict(state, grad=swapped(state["grad"]))

    def turn(state):
        return dict(state, turned=turn_call(state["out_weight"], up_weight))

    works = [None, swap_acts, swap_grads, turn]
    state = {"act": act_send, "grad": grad_send, "out_weight": out_weight}
    for axis, pairs in hops("pipe") + hops("dp") + hops("grp"):
        moved = lax.ppermute(prefix_grad, axis, pairs)
        work = works.pop(0) if works else None
        if work:
            state = work(state)
        prefix_grad, moved, state = lax.optimization_barrier((prefix_grad, moved, state))
        prefix_grad = prefix_grad + moved
    for work in works:
        state = work(state)
    col_width = 2 * D // lax.axis_size("dp")
    grad_embed, grad_up, grad_up_b, grad_out, grad_out_b, activations, input_grads = final_call(
        col_width, prefix_grad, hidden_units, prefix_embed, *state["turned"], state["act"], state["grad"],
        act, grad,
    )
    return (
        activations,
        input_grads,
        grad_embed,
        grad_up,
        grad_up_b[0],
        grad_out,
        grad_out_b[0],
    )


def solution(mesh):
    return jax.shard_map(
        local,
        mesh=mesh,
        in_specs=(
            P(None, ("grp", "dp"), None, None),
            P(None, ("grp", "dp"), None, None),
            P(None, ("grp", "dp"), None),
            P("pipe", None),
            P("pipe", None),
            P("pipe", None, None),
            P("pipe", None),
            P("pipe", None, None),
            P("pipe", None),
            P("pipe", None),
            P("pipe", None),
            P("pipe", None, None),
            P("pipe", None),
            P("pipe", None, None),
            P("pipe", None),
            P(),
            P(),
            P(),
            P(),
            P(),
        ),
        out_specs=(
            P("pipe", None, ("grp", "dp"), None, None),
            P("pipe", None, ("grp", "dp"), None, None),
            P(),
            P(),
            P(),
            P(None, ("pipe", "dp")),
            P(("pipe", "dp")),
        ),
        check_vma=False,
    )
```

time: 115 us -> 76.3 us (0.66)
  Pallas kernels: 67.9 us -> 48.5 us
  local copies, waits for them, and re-layouts: 15.4 us -> 3.42 us
  starting transfers between devices: 14.5 us -> 11.2 us
  waiting for transfers between devices: 13.3 us -> 11 us
  other arithmetic: 2.14 us -> 0.95 us
    pallas_call x5, Pallas kernels: 57.9 us -> 45.5 us  [the longest x1 30.7 us: middle_call(): pl.pallas_call(middle_kernel, name='middle', cost_estimate=estimate(20 *...]
    unnamed x66 -> x8, local copies, waits for them, and re-layouts: 14.5 us -> 3.42 us
    pallas_call x1, Pallas kernels: 9.98 us -> 3.07 us  [final_call(): pl.pallas_call(body, name='reparam', out_shape=[shape_of((PREFIX, D), f32...]
    ppermute x7, starting transfers between devices: 4.18 us -> 1.76 us  [swapped(): return lax.ppermute(array_in, 'pipe', [(0, 1), (1, 0)])]
    ppermute x5, waiting for transfers between devices: 13.3 us -> 11 us  [local(): moved = lax.ppermute(prefix_grad, axis, pairs)]
    unnamed x2 -> x0, other arithmetic: 2.08 us -> none
  transfers between devices with their start and end apart: 12 -> 12, of which waited for: 5 -> 4; matrix products, arithmetic and copies ran while one was open for 4% -> 1% of each run, Pallas kernels for 13% -> 19%
where the time goes in v2:
time: 76.3 us; the launch traced here: 76 us
  Pallas kernels  48.5 us (64%)
  starting transfers between devices  11.2 us (15%)
  waiting for transfers between devices  11 us (14%)
  local copies, waits for them, and re-layouts  3.42 us (4%)
  other arithmetic  0.95 us (1%)
  between operations  0.95 us (1%)
    pallas_call x1, Pallas kernels, middle_call(): pl.pallas_call(middle_kernel, name='middle', cost_estimate=estimate(20 *...  30.7 us
    ppermute x5, waiting for transfers between devices, local(): moved = lax.ppermute(prefix_grad, axis, pairs)  11 us
    ppermute x5, starting transfers between devices, local(): moved = lax.ppermute(prefix_grad, axis, pairs)  9.4 us
    pallas_call x1, Pallas kernels, first_call(): pl.pallas_call(first_kernel, name='first_attention', cost_estimate=estima...  6.3 us
    pallas_call x1, Pallas kernels, prefix_call(): pl.pallas_call(prefix_kernel, name='prefix', cost_estimate=estimate(2 * 6...  4.71 us
    unnamed x8, local copies, waits for them, and re-layouts  3.42 us
    pallas_call x1, Pallas kernels, final_call(): pl.pallas_call(body, name='reparam', out_shape=[shape_of((PREFIX, D), f32...  3.07 us
    pallas_call x1, Pallas kernels, turn_call(): pl.pallas_call(turn_kernel, name='turned_matrices', out_shape=[shape_of((...  2.23 us
  transfers between devices with their start and end apart: 12, of which 4 were waited for; matrix products, arithmetic and copies ran while one was open for 1% of the time, Pallas kernels for 19%

profile of v2, /device:TPU:0, one launch (start us, length us, event | category | flops | bytes accessed | tf_op | source)
XLA Modules:
  0.0 76.0 jit_solution(9431848343695602074)
XLA Ops:
  0.6 0.5 collective-permute-start.1
  1.2 1.5 %small_parameters.1.own_small.refs_3_ = f32[1,6656]{1,0:T(1,128)} custom-call(f32[1,512]{1,0:T(1,128)} %gain_one.1, f32[1,512]{1,0:T(1,128)} %shift_one.1, f32[1,512]{1,0:T(1,128)} %gain_two.1, f32[1,512]{1,0:T(1,128)} %shift_two.1, f32[1,512]{1,0:T(1,128)} %attn_b.1, f32[1,512]{1,0:T(1,128)} %out_b.1, f32[1,1536]{1,0:T(1,128)} %qkv_b.1, f32[1,2048]{1,0:T(1,128)} %in_b.1), custom_call_target="tpu_custom_call" | custom-call | flops 6656 | bytes 53248 | tf_op jit(solution)/shard_map/small_parameters/pallas_call | solution.py:393
  2.6 0.1 collective-permute-start
  2.8 0.5 collective-permute-start.2
  3.2 0.1 collective-permute-start.3
  3.3 0.4 collective-permute-start.4
  3.7 4.7 %prefix.1 = (f32[10,512]{1,0:T(8,128)}, bf16[4,16,512]{2,1,0:T(8,128)(2,1)}, bf16[4,512,16]{2,1,0:T(8,128)(2,1)}) custom-call(f32[10,512]{1,0:T(8,128)} %refs_2_.2, f32[512,512]{1,0:T(8,128)} %up_hbm.3, f32[512]{0:T(512)} %up_b_hbm.1, f32[512,2048]{1,0:T(8,128)} %out_hbm.2, f32[2048]{0:T(1024)} %out_b_hbm.1), custom_call_target="tpu_custom_call" | custom-call | flops 251658240 | bytes 6291456 | tf_op jit(solution)/shard_map/prefix/pallas_call | solution.py:436
  8.5 6.3 %first_attention.1 = (bf16[512,512]{1,0:T(8,128)(2,1)}, bf16[512,512]{1,0:T(8,128)(2,1)}, bf16[512,512]{1,0:T(8,128)(2,1)}, bf16[4,1152,256]{2,1,0:T(8,128)(2,1)...) custom-call(bf16[2,1,512,512]{3,2,1,0:T(8,128)(2,1)} %refs_0_.1, ...), custom_call_target="tpu_custom_call" | custom-call | flops 80530636800 | bytes 41943040 | tf_op jit(solution)/shard_map/first_attention/pallas_call | solution.py:506
  14.8 30.7 %middle.1 = (bf16[1,2,1,512,512]{4,3,2,1,0:T(8,128)(2,1)}, bf16[512,512]{1,0:T(8,128)(2,1)}, f32[1,2,1,512,512]{4,3,2,1,0:T(8,128)}, f32[512,512]{1,0:T(8,128)}, f32[40,512]{1,0:T(8,128)}) custom-call(bf16[2,1,512,512]{3,2,1,0:T(8,128)(2,1)} %refs_0_.1, bf16[2,1,512,512]{3,2,1,0:T(8,128)(2,1)} %refs_1_.1, s32[2,1,512]{2,1,0:T(1,128)} %refs_2_.1, ...), custom_call_target="tpu_custom_call" | custom-call | flops 16106127360 | bytes 20971520 | tf_op jit(solution)/shard_map/middle/pallas_call | solution.py:692
  45.6 0.1 collective-permute-start.5
  45.7 1.4 %collective-permute-done.5 = f32[40,512]{1,0:T(8,128)S(1)} collective-permute-done((f32[40,512]{1,0:T(8,128)}, f32[40,512]{1,0:T(8,128)S(1)}, u32[]{:S(2)}, u32[]{:S(2)}) %collective-permute-start.5) | collective-permute-done | bytes 81952 | tf_op jit(solution)/shard_map/ppermute | solution.py:870
  47.1 0.2 collective-permute-start.7
  47.3 0.9 %add.15 = f32[40,512]{1,0:T(8,128)S(1)} add(f32[40,512]{1,0:T(8,128)} %get-tuple-element.85, f32[40,512]{1,0:T(8,128)S(1)} %collective-permute-done.5) | non-fusion elementwise | flops 20480 | bytes 245760 | tf_op jit(solution)/shard_map/add | solution.py:875
  48.2 2.9 %collective-permute-start.6 = (f32[40,512]{1,0:T(8,128)S(1)}, f32[40,512]{1,0:T(8,128)S(1)}, u32[]{:S(2)}, u32[]{:S(2)}) collective-permute-start(f32[40,512]{1,0:T(8,128)S(1)} %add.15), channel_id=1, source_target_pairs={{0,1},{1,0},{2,3},{3,2},{4,5},{5,4},{6,7},{7,6},{8,9},{9,8},{10,11... | collective-permute-start | bytes 245768 | tf_op jit(solution)/shard_map/ppermute | solution.py:870
  51.1 2.8 %collective-permute-done.6 = f32[40,512]{1,0:T(8,128)S(1)} collective-permute-done((f32[40,512]{1,0:T(8,128)S(1)}, f32[40,512]{1,0:T(8,128)S(1)}, u32[]{:S(2)}, u32[]{:S(2)}) %collective-permute-start.6) | collective-permute-done | bytes 81952 | tf_op jit(solution)/shard_map/ppermute | solution.py:870
  53.9 1.8 %collective-permute-start.8 = (f32[40,512]{1,0:T(8,128)S(1)}, f32[40,512]{1,0:T(8,128)S(1)}, u32[]{:S(2)}, u32[]{:S(2)}) collective-permute-start(f32[40,512]{1,0:T(8,128)S(1)} %add.16), channel_id=1, source_target_pairs={{0,2},{1,3},{2,0},{3,1},{4,6},{5,7},{6,4},{7,5},{8,10},{9,11},{10,... | collective-permute-start | bytes 245768 | tf_op jit(solution)/shard_map/ppermute | solution.py:870
  55.7 3.1 %collective-permute-done.8 = f32[40,512]{1,0:T(8,128)S(1)} collective-permute-done((f32[40,512]{1,0:T(8,128)S(1)}, f32[40,512]{1,0:T(8,128)S(1)}, u32[]{:S(2)}, u32[]{:S(2)}) %collective-permute-start.8) | collective-permute-done | bytes 81952 | tf_op jit(solution)/shard_map/ppermute | solution.py:870
  58.8 1.9 %collective-permute-start.10 = (f32[40,512]{1,0:T(8,128)S(1)}, f32[40,512]{1,0:T(8,128)S(1)}, u32[]{:S(2)}, u32[]{:S(2)}) collective-permute-start(f32[40,512]{1,0:T(8,128)S(1)} %add.17), channel_id=1, source_target_pairs={{0,4},{4,0},{8,12},{12,8},{1,5},{5,1},{9,13},{13,9},{2,6},{6,2},{1... | collective-permute-start | bytes 245768 | tf_op jit(solution)/shard_map/ppermute | solution.py:870
  60.7 2.2 %copy-done = f32[512,2048]{1,0:T(8,128)S(1)} copy-done((f32[512,2048]{1,0:T(8,128)S(1)}, f32[512,2048]{1,0:T(8,128)}, u32[]{:S(2)}) %copy-start) | copy-done | bytes 4194328
  62.9 1.2 %copy-done.1 = f32[512,512]{1,0:T(8,128)S(1)} copy-done((f32[512,512]{1,0:T(8,128)S(1)}, f32[512,512]{1,0:T(8,128)}, u32[]{:S(2)}) %copy-start.1) | copy-done | bytes 1048600
  64.1 2.2 %turned_matrices.1 = (bf16[2048,512]{1,0:T(8,128)(2,1)S(1)}, bf16[512,512]{1,0:T(8,128)(2,1)S(1)}, bf16[512,512]{1,0:T(8,128)(2,1)S(1)}) custom-call(f32[512,2048]{1,0:T(8,128)S(1)} %copy-done, f32[512,512]{1,0:T(8,128)S(1)} %copy-done.1), custom_call_target="tpu_custom_call" | custom-call | flops 134217728 | bytes 8388608 | tf_op jit(solution)/shard_map/turned_matrices/pallas_call | solution.py:726
  66.4 2.7 %collective-permute-start.11 = (f32[40,512]{1,0:T(8,128)S(1)}, f32[40,512]{1,0:T(8,128)S(1)}, u32[]{:S(2)}, u32[]{:S(2)}) collective-permute-start(f32[40,512]{1,0:T(8,128)S(1)} %add.18), channel_id=1, source_target_pairs={{0,8},{4,12},{8,0},{12,4},{1,9},{5,13},{9,1},{13,5},{2,10},{6,14},... | collective-permute-start | bytes 245768 | tf_op jit(solution)/shard_map/ppermute | solution.py:870
  69.0 3.7 %collective-permute-done.11 = f32[40,512]{1,0:T(8,128)S(1)} collective-permute-done((f32[40,512]{1,0:T(8,128)S(1)}, f32[40,512]{1,0:T(8,128)S(1)}, u32[]{:S(2)}, u32[]{:S(2)}) %collective-permute-start.11) | collective-permute-done | bytes 81952 | tf_op jit(solution)/shard_map/ppermute | solution.py:870
  72.8 3.1 %reparam.1 = (f32[10,512]{1,0:T(8,128)}, f32[512,512]{1,0:T(8,128)}, f32[1,512]{1,0:T(1,128)}, f32[512,256]{1,0:T(8,128)}, f32[1,256]{1,0:T(1,128)}, /*index=5*/...) custom-call(f32[40,512]{1,0:T(8,128)S(1)} %add.19.refs_0_, ...), custom_call_target="tpu_custom_call", output_to_operand_aliasing={{5}: (8, {}), {6}: (9, {})} | custom-call | tf_op jit(solution)/shard_map/reparam/pallas_call | solution.py:783
  (19 shorter events, 0.1 us)
Async XLA Ops:
  0.6 7.8 %collective-permute-start.1 = (bf16[1,512,1536]{2,1,0:T(8,128)(2,1)}, bf16[1,512,1536]{2,1,0:T(8,128)(2,1)}, u32[]{:S(2)}, u32[]{:S(2)}) collective-permute-start(bf16[1,512,1536]{2,1,0:T(8,128)(2,1)} %refs_5_.1), channel_id=1, source_target_pairs={{0,16},{16,0},{1,17},{17,1},{2,18},{18,2},{3,19},{19,3},{4,20},{20... | collective-permute-start | bytes 4718600 | tf_op jit(solution)/shard_map/ppermute | solution.py:804
  2.6 5.8 %collective-permute-start = (f32[1,6656]{1,0:T(1,128)}, f32[1,6656]{1,0:T(1,128)}, u32[]{:S(2)}, u32[]{:S(2)}) collective-permute-start(f32[1,6656]{1,0:T(1,128)} %small_parameters.1.own_small.refs_3_), channel_id=1, source_target_pairs={{0,16},{16,0},{1,17},{17,1},{2,18},{18,2},{3,19},{19,3},{4,20},{20... | collective-permute-start | bytes 79880 | tf_op jit(solution)/shard_map/ppermute | solution.py:804
  2.8 12.0 %collective-permute-start.2 = (bf16[1,512,512]{2,1,0:T(8,128)(2,1)}, bf16[1,512,512]{2,1,0:T(8,128)(2,1)}, u32[]{:S(2)}, u32[]{:S(2)}) collective-permute-start(bf16[1,512,512]{2,1,0:T(8,128)(2,1)} %refs_6_.1), channel_id=1, source_target_pairs={{0,16},{16,0},{1,17},{17,1},{2,18},{18,2},{3,19},{19,3},{4,20},{20... | collective-permute-start | bytes 1572872 | tf_op jit(solution)/shard_map/ppermute | solution.py:804
  3.2 11.6 %collective-permute-start.3 = (bf16[1,512,2048]{2,1,0:T(8,128)(2,1)}, bf16[1,512,2048]{2,1,0:T(8,128)(2,1)}, u32[]{:S(2)}, u32[]{:S(2)}) collective-permute-start(bf16[1,512,2048]{2,1,0:T(8,128)(2,1)} %refs_7_.1), channel_id=1, source_target_pairs={{0,16},{16,0},{1,17},{17,1},{2,18},{18,2},{3,19},{19,3},{4,20},{20... | collective-permute-start | bytes 6291464 | tf_op jit(solution)/shard_map/ppermute | solution.py:804
  3.3 11.5 %collective-permute-start.4 = (bf16[1,2048,512]{2,1,0:T(8,128)(2,1)}, bf16[1,2048,512]{2,1,0:T(8,128)(2,1)}, u32[]{:S(2)}, u32[]{:S(2)}) collective-permute-start(bf16[1,2048,512]{2,1,0:T(8,128)(2,1)} %refs_8_.1), channel_id=1, source_target_pairs={{0,16},{16,0},{1,17},{17,1},{2,18},{18,2},{3,19},{19,3},{4,20},{20... | collective-permute-start | bytes 6291464 | tf_op jit(solution)/shard_map/ppermute | solution.py:804
  45.6 1.6 %collective-permute-start.5 = (f32[40,512]{1,0:T(8,128)}, f32[40,512]{1,0:T(8,128)S(1)}, u32[]{:S(2)}, u32[]{:S(2)}) collective-permute-start(f32[40,512]{1,0:T(8,128)} %get-tuple-element.85), channel_id=1, source_target_pairs={{0,16},{16,0},{1,17},{17,1},{2,18},{18,2},{3,19},{19,3},{4,20},{20... | collective-permute-start | bytes 245768 | tf_op jit(solution)/shard_map/ppermute | solution.py:870
  47.1 6.7 %collective-permute-start.7 = (bf16[512,512]{1,0:T(8,128)(2,1)}, bf16[512,512]{1,0:T(8,128)(2,1)S(1)}, u32[]{:S(2)}, u32[]{:S(2)}) collective-permute-start(bf16[512,512]{1,0:T(8,128)(2,1)} %get-tuple-element.87), channel_id=1, source_target_pairs={{0,16},{16,0},{1,17},{17,1},{2,18},{18,2},{3,19},{19,3},{4,20},{20... | collective-permute-start | bytes 1572872 | tf_op jit(solution)/shard_map/ppermute | solution.py:804
  48.2 5.7 %collective-permute-start.6 = (f32[40,512]{1,0:T(8,128)S(1)}, f32[40,512]{1,0:T(8,128)S(1)}, u32[]{:S(2)}, u32[]{:S(2)}) collective-permute-start(f32[40,512]{1,0:T(8,128)S(1)} %add.15), channel_id=1, source_target_pairs={{0,1},{1,0},{2,3},{3,2},{4,5},{5,4},{6,7},{7,6},{8,9},{9,8},{10,11... | collective-permute-start | bytes 245768 | tf_op jit(solution)/shard_map/ppermute | solution.py:870
  53.8 5.0 %collective-permute-start.9 = (f32[512,512]{1,0:T(8,128)}, f32[512,512]{1,0:T(8,128)S(1)}, u32[]{:S(2)}, u32[]{:S(2)}) collective-permute-start(f32[512,512]{1,0:T(8,128)} %get-tuple-element.93), channel_id=1, source_target_pairs={{0,16},{16,0},{1,17},{17,1},{2,18},{18,2},{3,19},{19,3},{4,20},{20... | collective-permute-start | bytes 3145736 | tf_op jit(solution)/shard_map/ppermute | solution.py:804
  53.9 5.0 %collective-permute-start.8 = (f32[40,512]{1,0:T(8,128)S(1)}, f32[40,512]{1,0:T(8,128)S(1)}, u32[]{:S(2)}, u32[]{:S(2)}) collective-permute-start(f32[40,512]{1,0:T(8,128)S(1)} %add.16), channel_id=1, source_target_pairs={{0,2},{1,3},{2,0},{3,1},{4,6},{5,7},{6,4},{7,5},{8,10},{9,11},{10,... | collective-permute-start | bytes 245768 | tf_op jit(solution)/shard_map/ppermute | solution.py:870
  58.8 7.5 %collective-permute-start.10 = (f32[40,512]{1,0:T(8,128)S(1)}, f32[40,512]{1,0:T(8,128)S(1)}, u32[]{:S(2)}, u32[]{:S(2)}) collective-permute-start(f32[40,512]{1,0:T(8,128)S(1)} %add.17), channel_id=1, source_target_pairs={{0,4},{4,0},{8,12},{12,8},{1,5},{5,1},{9,13},{13,9},{2,6},{6,2},{1... | collective-permute-start | bytes 245768 | tf_op jit(solution)/shard_map/ppermute | solution.py:870
  60.7 2.2 %copy-start = (f32[512,2048]{1,0:T(8,128)S(1)}, f32[512,2048]{1,0:T(8,128)}, u32[]{:S(2)}) copy-start(f32[512,2048]{1,0:T(8,128)} %out_hbm.2) | copy-start | bytes 12582916
  62.9 1.2 %copy-start.1 = (f32[512,512]{1,0:T(8,128)S(1)}, f32[512,512]{1,0:T(8,128)}, u32[]{:S(2)}) copy-start(f32[512,512]{1,0:T(8,128)} %up_hbm.3) | copy-start | bytes 3145732
  64.1 8.6 %copy-start.2 = (f32[10,512]{1,0:T(8,128)S(1)}, f32[10,512]{1,0:T(8,128)}, u32[]{:S(2)}) copy-start(f32[10,512]{1,0:T(8,128)} %refs_2_.2) | copy-start | bytes 61444
  64.1 8.7 %copy-start.3 = (f32[10,512]{1,0:T(8,128)S(1)}, f32[10,512]{1,0:T(8,128)}, u32[]{:S(2)}) copy-start(f32[10,512]{1,0:T(8,128)} %get-tuple-element.112.refs_1_) | copy-start | bytes 61444
  66.4 6.4 %collective-permute-start.11 = (f32[40,512]{1,0:T(8,128)S(1)}, f32[40,512]{1,0:T(8,128)S(1)}, u32[]{:S(2)}, u32[]{:S(2)}) collective-permute-start(f32[40,512]{1,0:T(8,128)S(1)} %add.18), channel_id=1, source_target_pairs={{0,8},{4,12},{8,0},{12,4},{1,9},{5,13},{9,1},{13,5},{2,10},{6,14},... | collective-permute-start | bytes 245768 | tf_op jit(solution)/shard_map/ppermute | solution.py:870

commit v3 on v2

--- a/solution.py
+++ b/solution.py
@@ -35,10 +35,10 @@
 NT = (((1,), (1,)), ((), ()))
 TN = (((0,), (0,)), ((), ()))
 
-VMEM = pl.BlockSpec(memory_space=pltpu.VMEM)
 NO_COPIES = ((),) * 4
-ANY = pl.BlockSpec(memory_space=pltpu.HBM)
 MIB = 1024 * 1024
+FIRST_MIB = 40
+MIDDLE_MIB = 34
 LATE_MIB = 16
 
 G1, B1, G2, B2, B_ATTN, B_OUT, B_QKV, B_IN = 0, 1, 2, 3, 4, 5, 6, 9
@@ -49,24 +49,40 @@
     return lax.dot_general(left, right, dims, preferred_element_type=f32)
 
 
-def shape_of(shape, dtype):
-    return jax.ShapeDtypeStruct(shape, dtype)
-
-
-def params_of(mib):
-    return pltpu.CompilerParams(vmem_limit_bytes=mib * MIB)
-
-
-def all_vmem():
-    return pltpu.CompilerParams(vmem_limit_bytes=64 * MIB - 64 * 1024)
+def call_kernel(kernel, name, ins, outs, scratch, sems, mib, cost, aliases=None):
+    operands = [pltpu.with_memory_space_constraint(array, space) for array, space in ins]
+    return pl.pallas_call(
+        kernel,
+        name=name,
+        out_shape=[space(shape, dtype) for space, shape, dtype in outs],
+        in_specs=[pl.BlockSpec(memory_space=space) for _, space in ins],
+        out_specs=[pl.BlockSpec(memory_space=space) for space, _, _ in outs],
+        scratch_shapes=[pltpu.VMEM(*pair) for pair in scratch]
+        + ([pltpu.SemaphoreType.DMA((sems,))] if sems else []),
+        input_output_aliases=aliases or {},
+        compiler_params=pltpu.CompilerParams(vmem_limit_bytes=mib * MIB),
+        cost_estimate=pl.CostEstimate(flops=cost, bytes_accessed=8 * MIB, transcendentals=0),
+    )(*operands)
+
+
+def in_hbm(*arrays):
+    return [(array, pltpu.HBM) for array in arrays]
+
+
+def anywhere(*arrays):
+    return [(array, pl.ANY) for array in arrays]
+
+
+def in_vmem(*arrays):
+    return [(array, pltpu.VMEM) for array in arrays]
+
+
+def vmem(shapes):
+    return [(pltpu.VMEM, *pair) for pair in shapes]
 
 
 def small_row(small_ref, place):
     return small_ref[:, place * D : (place + 1) * D]
-
-
-def estimate(flops, bytes_accessed):
-    return pl.CostEstimate(flops=flops, bytes_accessed=bytes_accessed, transcendentals=0)
 
 
 def rope_tables():
@@ -188,7 +204,7 @@
     return slice(end - live, end), slice(block * BLK, end), slice(start, start + live)
 
 
-def attend(q_t, k_m, v_t, pre_k, pre_v_t, mask_ref, p_ref, pp_ref, inv_ref, mixed_ref, then=None):
+def attend(q_t, k_m, v_t, pre_k, pre_v, mask_ref, p_ref, pp_ref, inv_ref, mixed_ref):
     pad_mask = jnp.where(lax.broadcasted_iota(jnp.int32, (PAD, 1), 0) < PREFIX, 0.0, NEG)
 
     def score(feats, block):
@@ -216,7 +232,7 @@
 
     def mix(feats, block, expo, pre_expo, inverse):
         keys, tokens, _ = geometry(block)
-        mixed = dot(v_t[feats, keys], expo, NN) + dot(pre_v_t[feats, :], pre_expo, NN)
+        mixed = dot(v_t[feats, keys], expo, NN) + dot(pre_v[:, feats], pre_expo, TN)
         mixed_ref[feats, tokens] = (from_diagonal(mixed) * per_head(inverse)).astype(bf16)
 
     for pair in range(PAIRS):
@@ -225,11 +241,9 @@
         soft = [soften(pair, block, *scores[block]) for block in range(BLOCKS)]
         for block in range(BLOCKS):
             mix(feats, block, *soft[block])
-        if then is not None:
-            then(pair)
-
-
-def attend_back(grad_t, q_t, k_t, v_m, pre_k_t, pre_v, p_ref, pp_ref, inv_ref, mixed_ref,
+
+
+def attend_back(grad_t, q_t, k_t, v_m, pre_k, pre_v, p_ref, pp_ref, inv_ref, mixed_ref,
                 dq_ref, dk_ref, dv_ref, pre_grad, pre_row):
     def value_grads(pair, feats, block):
         keys, tokens, _ = geometry(block)
@@ -257,7 +271,7 @@
     def out_grads(pair, feats, block, grads, grad_scores, pre_scores):
         keys, tokens, rows = geometry(block)
         queries = block_diagonal(q_t[feats, tokens])
-        dq = dot(k_t[feats, keys], grad_scores, NN) + dot(pre_k_t[feats, :], pre_scores, NN)
+        dq = dot(k_t[feats, keys], grad_scores, NN) + dot(pre_k[:, feats], pre_scores, TN)
         dq_ref[feats, tokens] = from_diagonal(dq)
         return (
             dot(queries, grad_scores, NT),
@@ -376,7 +390,7 @@
     )
 
 
-def small_kernel(gain_one, shift_one, gain_two, shift_two, attn_b, out_b, qkv_b, in_b, packed_out, packed, sems):
+def small_kernel(gain_one, shift_one, gain_two, shift_two, attn_b, out_b, qkv_b, in_b, packed, sems):
     copies = Copies(sems)
     places = [(gain_one, 0), (shift_one, 1), (gain_two, 2), (shift_two, 3), (attn_b, 4), (out_b, 5)]
     places += [(qkv_b, 6), (in_b, 9)]
@@ -386,71 +400,24 @@
             for row, place in places
         ]
     )
-    wait_all(copies.start(packed, packed_out))
 
 
 def small_call(*arrays):
-    return pl.pallas_call(
-        small_kernel,
-        name="small_parameters",
-        cost_estimate=estimate(SMALL, 8 * SMALL),
-        out_shape=shape_of((1, SMALL), f32),
-        in_specs=[ANY] * 8,
-        out_specs=ANY,
-        scratch_shapes=[pltpu.VMEM((1, SMALL), f32), pltpu.SemaphoreType.DMA((9,))],
-        compiler_params=all_vmem(),
-    )(*arrays)
-
-
-def prefix_kernel(embed_hbm, up_hbm, up_b_hbm, out_hbm, out_b_hbm, hidden_out, low_out, low_t_out,
-                  hidden, low, low_t, embed, up_w, up_b, out_w, out_b, sems):
-    copies = Copies(sems)
-    early = [
-        copies.start(src, dst)
-        for src, dst in ((embed_hbm, embed), (up_hbm, up_w), (up_b_hbm, up_b.at[0]))
-    ]
-    parts = [
-        copies.start(out_hbm.at[:, i * D : (i + 1) * D], out_w.at[:, i * D : (i + 1) * D])
-        for i in range(4)
-    ]
-    late = [copies.start(out_b_hbm, out_b.at[0])]
-    wait_all(*early)
+    (packed,) = call_kernel(
+        small_kernel, "small_parameters", in_hbm(*arrays), vmem([((1, SMALL), f32)]), [], 8, 8, SMALL
+    )
+    return packed
+
+
+def prefix_states(embed, up_w, up_b, out_w, out_b, arrivals, hidden, low):
     units = jnp.tanh(few_rows_dot(embed[...], up_w[...])[:PREFIX] + up_b[...])
     hidden[...] = units
-    wait_all(*late)
     real = lax.broadcasted_iota(jnp.int32, (PAD, 1), 0) < PREFIX
     for part in range(4):
         cols = slice(part * D, (part + 1) * D)
-        parts[part].wait()
-        states = jnp.where(real, few_rows_dot(units, out_w[:, cols]) + out_b[:, cols], 0.0)
-        low[part] = states.astype(bf16)
-        tall = jnp.concatenate([states, jnp.zeros((BLK - PAD, D), f32)], axis=0)
-        low_t[part] = jnp.transpose(tall)[:, :PAD].astype(bf16)
-    wait_all(
-        copies.start(low, low_out), copies.start(low_t, low_t_out), copies.start(hidden, hidden_out)
-    )
-
-
-def prefix_call(*arrays):
-    shapes = (((PREFIX, D), f32), ((4, PAD, D), bf16), ((4, D, PAD), bf16))
-    return pl.pallas_call(
-        prefix_kernel,
-        name="prefix",
-        cost_estimate=estimate(2 * 6 * PAD * D * 5 * D, 6 * MIB),
-        out_shape=[shape_of(*pair) for pair in shapes],
-        in_specs=[ANY] * 5,
-        out_specs=[ANY] * 3,
-        scratch_shapes=[pltpu.VMEM(*pair) for pair in shapes]
-        + [
-            pltpu.VMEM((PREFIX, D), f32),
-            pltpu.VMEM((D, D), f32),
-            pltpu.VMEM((1, D), f32),
-            pltpu.VMEM((D, 4 * D), f32),
-            pltpu.VMEM((1, 4 * D), f32),
-            pltpu.SemaphoreType.DMA((11,)),
-        ],
-        compiler_params=all_vmem(),
-    )(*arrays)
+        arrivals[part].wait()
+        states = few_rows_dot(units, out_w[:, cols]) + out_b[:, cols]
+        low[part] = jnp.where(real, states, 0.0).astype(bf16)
 
 
 HEAD_SHAPES = (
@@ -462,13 +429,21 @@
     ((PAIRS, BLOCKS, 8, 2 * BLK), f32),
     ((D, SEQ), bf16),
 )
-FIRST_SHAPES = HEAD_SHAPES + (((SEQ, D), bf16),)
-
-
-def first_kernel(x_hbm, seg_hbm, own_small, other_small, own_qkv, other_qkv, low_hbm, low_t_hbm, tables_hbm,
-                 *refs):
-    outs, (q_t, k_t, v_m, p_ref, pp_ref, inv_ref, mixed_ref, two_ref), rest = refs[:8], refs[8:16], refs[16:]
-    mask_ref, x_ref, small_ref, w_ref, low, low_t, tables, seg, k_m, v_t, sems = rest
+FIRST_SHAPES = HEAD_SHAPES + (
+    ((SEQ, D), bf16),
+    ((4, PAD, D), bf16),
+    ((P_ROWS, BLK), f32),
+    ((SEQ, D), bf16),
+    ((1, SMALL), f32),
+    ((D, 3 * D), bf16),
+    ((PREFIX, D), f32),
+)
+
+
+def first_kernel(own_small, other_small, other_qkv, x_hbm, seg_hbm, own_qkv, embed_hbm, up_hbm, up_b_hbm,
+                 out_hbm, out_b_hbm, tables_hbm, *refs):
+    q_t, k_t, v_m, p_ref, pp_ref, inv_ref, mixed_ref, two_ref, low, mask_ref, x_ref, small_ref = refs[:12]
+    w_ref, hidden, embed, up_w, up_b, out_w, out_b, tables, seg, k_m, v_t, sems = refs[12:]
     section = lax.axis_index("pipe")
     here = section == 0
     copies = Copies(sems)
@@ -479,9 +454,14 @@
         copies.of_layer(here, own_qkv.at[0, rows], other_qkv.at[0, rows], w_ref.at[rows])
         for rows in (slice(i * BLK, (i + 1) * BLK) for i in range(4))
     ]
-    late += [
+    late.append(copies.start(tables_hbm, tables))
+    prefix_copies = [
         copies.start(src, dst)
-        for src, dst in ((tables_hbm, tables), (low_hbm, low), (low_t_hbm, low_t))
+        for src, dst in ((embed_hbm, embed), (up_hbm, up_w), (up_b_hbm, up_b.at[0]), (out_b_hbm, out_b.at[0]))
+    ]
+    parts = [
+        copies.start(out_hbm.at[:, i * D : (i + 1) * D], out_w.at[:, i * D : (i + 1) * D])
+        for i in range(4)
     ]
     seg_copy.wait()
     fill_mask(seg, mask_ref)
@@ -489,46 +469,49 @@
     hat, _ = normalized(x_ref[...].astype(f32))
     normed = (hat * small_row(small_ref, G1) + small_row(small_ref, B1)).astype(bf16)
     two_ref[...] = (hat * small_row(small_ref, G2) + small_row(small_ref, B2)).astype(bf16)
-    done = [copies.start(two_ref, outs[7])]
     wait_all(*late)
     project_heads(normed, w_ref, small_ref, tables[:8, :], tables[8:, :], q_t, k_t, k_m, v_m, v_t)
-    done += [copies.start(*pair) for pair in zip((q_t, k_t, v_m), outs[:3])]
-
-    def then(pair):
-        done.append(copies.start(p_ref.at[pair], outs[3].at[pair]))
-
-    attend(q_t, k_m, v_t, low.at[0], low_t.at[1], mask_ref, p_ref, pp_ref, inv_ref, mixed_ref, then)
-    done += [copies.start(*pair) for pair in zip((pp_ref, inv_ref, mixed_ref), outs[4:7])]
-    wait_all(*done)
-
-
-def first_call(*arrays):
-    return pl.pallas_call(
-        first_kernel,
-        name="first_attention",
-        cost_estimate=estimate(200 * SEQ * D * 3 * D, 40 * MIB),
-        out_shape=[shape_of(*pair) for pair in FIRST_SHAPES],
-        in_specs=[ANY] * 9,
-        out_specs=[ANY] * 8,
-        scratch_shapes=[pltpu.VMEM(*pair) for pair in FIRST_SHAPES]
-        + [
-            pltpu.VMEM((P_ROWS, BLK), f32),
-            pltpu.VMEM((SEQ, D), bf16),
-            pltpu.VMEM((1, SMALL), f32),
-            pltpu.VMEM((D, 3 * D), bf16),
-            pltpu.VMEM((4, PAD, D), bf16),
-            pltpu.VMEM((4, D, PAD), bf16),
-            pltpu.VMEM((2 * 8, SEQ), f32),
-            pltpu.VMEM((1, SEQ), jnp.int32),
-            pltpu.VMEM((SEQ, D), bf16),
-            pltpu.VMEM((D, SEQ), bf16),
-            pltpu.SemaphoreType.DMA((21,)),
-        ],
-        compiler_params=all_vmem(),
-    )(*arrays)
+    wait_all(*prefix_copies)
+    prefix_states(embed, up_w, up_b, out_w, out_b, parts, hidden, low)
+    attend(q_t, k_m, v_t, low.at[0], low.at[1], mask_ref, p_ref, pp_ref, inv_ref, mixed_ref)
+
+
+def first_call(smalls, other_qkv, *arrays):
+    scratch = [
+        ((PREFIX, D), f32),
+        ((D, D), f32),
+        ((1, D), f32),
+        ((D, 4 * D), f32),
+        ((1, 4 * D), f32),
+        ((2 * 8, SEQ), f32),
+        ((1, SEQ), jnp.int32),
+        ((SEQ, D), bf16),
+        ((D, SEQ), bf16),
+    ]
+    return call_kernel(
+        first_kernel, "first_attention", in_vmem(*smalls) + anywhere(other_qkv) + in_hbm(*arrays),
+        vmem(FIRST_SHAPES), scratch, 16, FIRST_MIB, 200 * SEQ * D * 3 * D,
+    )
 
 
 WEIGHT_SHAPES = (((D, 3 * D), bf16), ((D, D), bf16), ((D, FF), bf16), ((FF, D), bf16))
+
+
+MIDDLE_OUTS = (
+    ((SEQ, D), bf16),
+    ((SEQ, FF), bf16),
+    ((D, SEQ), bf16),
+    ((SEQ, D), f32),
+    ((SEQ, D), bf16),
+    ((SEQ, FF), bf16),
+    ((3 * D, SEQ), bf16),
+    ((4 * PREFIX, D), f32),
+    ((1, SMALL), f32),
+    ((D, FF), bf16),
+    ((FF, D), bf16),
+    ((D, D), bf16),
+    ((FF, D), bf16),
+)
 
 
 def middle_kernel(*refs):
@@ -537,144 +520,80 @@
         taken, refs = refs[:count], refs[count:]
         return taken
 
-    x_hbm, cot_hbm, seg_hbm, own_small, other_small = take(5)
-    own, other = take(4), take(4)
-    low_hbm, low_t_hbm, tables_hbm = take(3)
-    saved_hbm = take(8)
-    act_out, act_send, grad_out, grad_send, prefix_out = take(5)
-    q0, k0, v0, p0, pp0, inv0, mixed0, two0 = take(8)
-    w_qkv_zero, w_attn_zero, w_in_zero, w_out_zero = take(4)
-    w_qkv, w_attn, w_in, w_out = take(4)
-    q_t, k_t, v_m, p_ref, pp_ref, inv_ref, mixed_one = take(7)
-    (x_ref, cot_ref, seg, mask, small_zero, small_one, low, low_t, tables, h_one, h_two, act_zero, slope_zero,
-     act_one, slope_one, k_m, v_t, dq, dk, dv, packed, pre_grad, prefix_grad, grad_one, grad_low, grad_zero,
-     sems) = refs
+    own_small, other_small, q0, k0, v0, p0, pp0, inv0, mixed0, two0, low, mask, x_ref, small_zero = take(14)
+    other = take(4)
+    (cot_hbm,) = take(1)
+    own = take(4)
+    (tables_hbm,) = take(1)
+    (h_one, act_one, mixed_one, grad_one, grad_low, slope_zero, packed_zero, prefix_grad,
+     small_one, w_in_zero, w_out_zero, w_attn, w_out) = take(13)
+    w_attn_zero, w_qkv, w_in = take(3)
+    q_t, k_t, v_m, p_ref, pp_ref, inv_ref = take(6)
+    cot_ref, tables, act_zero, slope_one, k_m, v_t, dq, dk, dv, packed, pre_grad, sems = refs
     section = lax.axis_index("pipe")
     zero, one = section == 0, section == 1
     copies = Copies(sems)
-
-    def fetch_saved(which, dst):
-        return copies.start(saved_hbm[which], dst)
 
     def weights(here, which, dst, index=()):
         index = (0,) + index
         view = dst.at[index[1:]] if len(index) > 1 else dst
         return copies.of_layer(here, own[which].at[index], other[which].at[index], view)
 
-    def hand_over(layer, value, whole, send):
-        sem = copies.sems.at[copies.count]
-        copies.count += 1
-
-        @pl.when(section == layer)
-        def _():
-            pltpu.make_async_copy(value, whole.at[0, section, 0], sem).start()
-
-        @pl.when(section != layer)
-        def _():
-            pltpu.make_async_copy(value, send, sem).start()
-
-        done.append(pltpu.make_async_copy(value, send, sem))
-
     everything = slice(None)
-    done = []
-    small_copy = copies.of_layer(zero, own_small, other_small, small_zero)
-    two_copy = fetch_saved(7, two0)
     in_zero = [[weights(zero, 2, w_in_zero, (everything, chunk_of(i)))] for i in range(4)]
-    out_copies = [
-        fetch_saved(6, mixed0),
-        weights(zero, 1, w_attn_zero),
-        copies.start(x_hbm.at[section, 0], x_ref),
-    ]
+    out_copies = [weights(zero, 1, w_attn_zero)]
     out_copies += [weights(zero, 3, w_out_zero, (chunk_of(i),)) for i in range(4)]
-    seg_copy = copies.start(seg_hbm.at[section], seg)
-    wait_all(small_copy, two_copy)
     feed_in(two0[...], w_in_zero, small_zero, act_zero, slope_zero, in_zero)
     head_copies = [
         copies.of_layer(one, own_small, other_small, small_one),
         weights(one, 0, w_qkv),
         copies.start(tables_hbm, tables),
-        copies.start(low_hbm, low),
-        copies.start(low_t_hbm, low_t),
     ]
     in_one = [[weights(one, 2, w_in, (everything, chunk_of(i)))] for i in range(4)]
-    seg_copy.wait()
-    fill_mask(seg, mask)
     wait_all(*out_copies)
     h_one[...] = layer_result(
         x_ref[...].astype(f32), mixed0[...], w_attn_zero[...], act_zero, w_out_zero[...], small_zero
     ).astype(bf16)
-    hand_over(0, h_one, act_out, act_send)
 
     back_copies = [copies.start(cot_hbm.at[section, 0], cot_ref)]
     back_copies += [weights(one, 3, w_out, (chunk_of(i),)) for i in range(4)]
     attn_copy = weights(one, 1, w_attn)
-    late = [
-        fetch_saved(which, dst)
-        for which, dst in ((0, q0), (1, k0), (2, v0), (3, p0), (4, pp0), (5, inv0))
-    ]
-    qkv_copy = weights(zero, 0, w_qkv_zero)
     wait_all(*head_copies)
     cos, sin = tables[:8, :], tables[8:, :]
     hat, _ = normalized(h_one[...].astype(f32))
     normed = (hat * small_row(small_one, G1) + small_row(small_one, B1)).astype(bf16)
     two = (hat * small_row(small_one, G2) + small_row(small_one, B2)).astype(bf16)
     project_heads(normed, w_qkv, small_one, cos, sin, q_t, k_t, k_m, v_m, v_t)
-    attend(q_t, k_m, v_t, low.at[2], low_t.at[3], mask, p_ref, pp_ref, inv_ref, mixed_one)
+    attend(q_t, k_m, v_t, low.at[2], low.at[3], mask, p_ref, pp_ref, inv_ref, mixed_one)
     feed_in(two, w_in, small_one, act_one, slope_one, in_one)
+
     wait_all(*back_copies)
-    attn_copy.wait()
-    h_two[...] = layer_result(
-        h_one[...].astype(f32), mixed_one[...], w_attn[...], act_one, w_out[...], small_one
-    ).astype(bf16)
-    hand_over(1, h_two, act_out, act_send)
-
     grad = cot_ref[...]
     grad_two = feed_back(grad, w_out, w_in, slope_one, NO_COPIES)
+    attn_copy.wait()
     dq[...] = dot(w_attn[...], grad, NT)
-    attend_back(dq, q_t, k_t, v_m, low_t.at[2], low.at[3], p_ref, pp_ref, inv_ref, mixed_one,
+    attend_back(dq, q_t, k_t, v_m, low.at[2], low.at[3], p_ref, pp_ref, inv_ref, mixed_one,
                 dq, dk, dv, pre_grad, 2 * PAD)
     pack_grads(dq, dk, dv, cos, sin, packed)
     result = norms_back(grad, h_one[...].astype(f32), grad_two, packed[...], w_qkv[...], small_one)
     grad_one[...] = result
     grad_low[...] = result.astype(bf16)
-    hand_over(1, grad_one, grad_out, grad_send)
-
-    grad = grad_low[...]
-    dq[...] = dot(w_attn_zero[...], grad, NT)
-    wait_all(*late)
-    attend_back(dq, q0, k0, v0, low_t.at[0], low.at[1], p0, pp0, inv0, mixed0,
+
+    dq[...] = dot(w_attn_zero[...], grad_low[...], NT)
+    attend_back(dq, q0, k0, v0, low.at[0], low.at[1], p0, pp0, inv0, mixed0,
                 dq, dk, dv, pre_grad, 0)
     for part in range(4):
         prefix_grad[part * PREFIX : (part + 1) * PREFIX, :] = pre_grad[
             part * PAD : part * PAD + PREFIX, :
         ]
-    done.append(copies.start(prefix_grad, prefix_out))
-    pack_grads(dq, dk, dv, cos, sin, packed)
-    grad_two = feed_back(grad, w_out_zero, w_in_zero, slope_zero, NO_COPIES)
-    qkv_copy.wait()
-    grad_zero[...] = norms_back(
-        grad, x_ref[...].astype(f32), grad_two, packed[...], w_qkv_zero[...], small_zero
-    )
-    hand_over(0, grad_zero, grad_out, grad_send)
-    wait_all(*done)
-
-
-def middle_call(*arrays):
-    scratch = FIRST_SHAPES + WEIGHT_SHAPES + WEIGHT_SHAPES + HEAD_SHAPES
+    pack_grads(dq, dk, dv, cos, sin, packed_zero)
+
+
+def middle_call(saved, other, *arrays):
+    scratch = (((D, D), bf16), ((D, 3 * D), bf16), ((D, FF), bf16)) + HEAD_SHAPES[:6]
     scratch += (
         ((SEQ, D), bf16),
-        ((SEQ, D), bf16),
-        ((1, SEQ), jnp.int32),
-        ((P_ROWS, BLK), f32),
-        ((1, SMALL), f32),
-        ((1, SMALL), f32),
-        ((4, PAD, D), bf16),
-        ((4, D, PAD), bf16),
         ((2 * 8, SEQ), f32),
-        ((SEQ, D), bf16),
-        ((SEQ, D), bf16),
-        ((SEQ, FF), bf16),
-        ((SEQ, FF), bf16),
         ((SEQ, FF), bf16),
         ((SEQ, FF), bf16),
         ((SEQ, D), bf16),
@@ -684,27 +603,67 @@
         ((D, SEQ), f32),
         ((3 * D, SEQ), bf16),
         ((4 * PAD, D), f32),
-        ((4 * PREFIX, D), f32),
-        ((SEQ, D), f32),
-        ((SEQ, D), bf16),
-        ((SEQ, D), f32),
-    )
-    return pl.pallas_call(
-        middle_kernel,
-        name="middle",
-        cost_estimate=estimate(20 * SEQ * D * 6 * D, 20 * MIB),
-        out_shape=[
-            shape_of((1, 2, 1, SEQ, D), bf16),
-            shape_of((SEQ, D), bf16),
-            shape_of((1, 2, 1, SEQ, D), f32),
-            shape_of((SEQ, D), f32),
-            shape_of((4 * PREFIX, D), f32),
-        ],
-        in_specs=[ANY] * 24,
-        out_specs=[ANY] * 5,
-        scratch_shapes=[pltpu.VMEM(*pair) for pair in scratch] + [pltpu.SemaphoreType.DMA((44,))],
-        compiler_params=all_vmem(),
-    )(*arrays)
+    )
+    return call_kernel(
+        middle_kernel, "middle", in_vmem(*saved) + anywhere(*other) + in_hbm(*arrays),
+        vmem(MIDDLE_OUTS), scratch, 24, MIDDLE_MIB, 20 * SEQ * D * 6 * D,
+    )
+
+
+def hand_over(section, values, keep, send_ref, whole, sem):
+    @pl.when(section == 0)
+    def _():
+        keep[...] = values[0]
+        send_ref[...] = values[1]
+
+    @pl.when(section != 0)
+    def _():
+        keep[...] = values[1]
+        send_ref[...] = values[0]
+
+    wait_all(Copies(sem).start(keep, whole.at[0, section, 0]))
+
+
+def result_kernel(h_one, act, mixed, small, w_attn, w_out, whole, send_ref, keep, sem):
+    result = layer_result(
+        h_one[...].astype(f32), mixed[...], w_attn[...], act, w_out[...], small
+    ).astype(bf16)
+    hand_over(lax.axis_index("pipe"), (h_one[...], result), keep, send_ref, whole, sem)
+
+
+def result_call(*arrays):
+    return call_kernel(
+        result_kernel, "layer_one_out", in_vmem(*arrays),
+        [(pltpu.HBM, (1, 2, 1, SEQ, D), bf16), (pltpu.VMEM, (SEQ, D), bf16)],
+        [((SEQ, D), bf16)], 1, LATE_MIB, 2 * SEQ * D * (D + FF),
+    )
+
+
+def feed_back_kernel(grad, slope, w_in, w_out, total):
+    total[...] = feed_back(grad[...], w_out, w_in, slope, NO_COPIES)
+
+
+def feed_back_call(*arrays):
+    (total,) = call_kernel(
+        feed_back_kernel, "layer_zero_feed_back", in_vmem(*arrays), vmem([((SEQ, D), f32)]), [], 0,
+        LATE_MIB, 4 * SEQ * D * FF,
+    )
+    return total
+
+
+def norms_kernel(x_ref, grad, two, packed, grad_one, small, w_qkv, whole, send_ref, keep, sem):
+    result = norms_back(
+        grad[...], x_ref[...].astype(f32), two[...], packed[...], w_qkv[...], small
+    )
+    hand_over(lax.axis_index("pipe"), (result, grad_one[...]), keep, send_ref, whole, sem)
+
+
+def norms_call(*arrays):
+    return call_kernel(
+        norms_kernel, "layer_zero_norms", in_vmem(*arrays),
+        [(pltpu.HBM, (1, 2, 1, SEQ, D), f32), (pltpu.VMEM, (SEQ, D), f32)],
+        [((SEQ, D), f32)], 1, LATE_MIB, 6 * SEQ * D * D,
+    )
 
 
 def turn_kernel(out_hbm, up_hbm, wide, up_high, up_rest, out_w, up_w, sems):
@@ -723,24 +682,16 @@
 
 
 def turn_call(*arrays):
-    return pl.pallas_call(
-        turn_kernel,
-        name="turned_matrices",
-        out_shape=[shape_of((4 * D, D), bf16), shape_of((D, D), bf16), shape_of((D, D), bf16)],
-        in_specs=[ANY] * 2,
-        out_specs=[VMEM] * 3,
-        scratch_shapes=[
-            pltpu.VMEM((D, 4 * D), f32),
-            pltpu.VMEM((D, D), f32),
-            pltpu.SemaphoreType.DMA((5,)),
-        ],
-        compiler_params=params_of(LATE_MIB),
-        cost_estimate=estimate(SEQ * D * D, 8 * MIB),
-    )(*arrays)
+    return call_kernel(
+        turn_kernel, "turned_matrices", in_hbm(*arrays),
+        vmem([((4 * D, D), bf16), ((D, D), bf16), ((D, D), bf16)]),
+        [((D, 4 * D), f32), ((D, D), f32)], 5, LATE_MIB, SEQ * D * D,
+    )
 
 
 def final_kernel(col_width, grads_ref, hidden, embed, wide, up_high, up_rest, act_other, grad_other,
-                 act_in, grad_in, d_embed, d_up, d_up_b, d_out, d_out_b, act_out, grad_out, sems):
+                 act_in, grad_in, *refs):
+    results, (act_out, grad_out, d_embed, d_up, d_up_b, d_out, d_out_b, sems) = refs[:5], refs[5:]
     section = lax.axis_index("pipe")
     shard = lax.axis_index("dp")
     copies = Copies(sems)
@@ -759,10 +710,12 @@
     grad_pre = grad_units * (1.0 - units * units)
     d_up_b[...] = jnp.sum(grad_pre, axis=0, keepdims=True)
     d_up[...] = stacked_dot(embed[...], grad_pre)
+    placed += [copies.start(d_up_b, results[2]), copies.start(d_up, results[1])]
     high, rest = halves(padded(grad_pre))
     both = dot(jnp.concatenate([high, rest], axis=0), up_high[...], NN)
     both = both[:PAD] + both[PAD:] + dot(high, up_rest[...], NN)
     d_embed[...] = both[:PREFIX]
+    placed.append(copies.start(d_embed, results[0]))
     column = section * (2 * D) + shard * col_width
     own_cols = jnp.zeros((PREFIX, col_width), f32)
     for part in range(4):
@@ -773,31 +726,21 @@
             own_cols = jnp.where(here, grads_ref[rows, cols], own_cols)
     d_out[...] = stacked_dot(units, own_cols)
     d_out_b[...] = jnp.sum(own_cols, axis=0, keepdims=True)
+    placed += [copies.start(d_out, results[3]), copies.start(d_out_b, results[4])]
     wait_all(*placed)
 
 
-def final_call(col_width, *arrays):
+def final_call(col_width, wholes, *arrays):
     def body(*refs):
         final_kernel(col_width, *refs)
 
-    return pl.pallas_call(
-        body,
-        name="reparam",
-        out_shape=[
-            shape_of((PREFIX, D), f32),
-            shape_of((D, D), f32),
-            shape_of((1, D), f32),
-            shape_of((D, col_width), f32),
-            shape_of((1, col_width), f32),
-            shape_of((1, 2, 1, SEQ, D), bf16),
-            shape_of((1, 2, 1, SEQ, D), f32),
-        ],
-        in_specs=[VMEM] * 8 + [ANY] * 2,
-        out_specs=[VMEM] * 5 + [ANY] * 2,
-        scratch_shapes=[pltpu.SemaphoreType.DMA((2,))],
-        input_output_aliases={8: 5, 9: 6},
-        compiler_params=params_of(LATE_MIB),
-    )(*arrays)
+    shapes = [((PREFIX, D), f32), ((D, D), f32), ((1, D), f32), ((D, col_width), f32), ((1, col_width), f32)]
+    whole_shapes = [((1, 2, 1, SEQ, D), bf16), ((1, 2, 1, SEQ, D), f32)]
+    return call_kernel(
+        body, "reparam", in_vmem(*arrays) + in_hbm(*wholes),
+        [(pltpu.HBM, *pair) for pair in shapes + whole_shapes], shapes, 7, LATE_MIB, SEQ * D * D,
+        {8: 5, 9: 6},
+    )
 
 
 def swapped(array_in):
@@ -844,41 +787,51 @@
     other_small = swapped(small)
     small, prefix_embed = lax.optimization_barrier((small, prefix_embed))
     tables = jnp.asarray(rope_tables())
-    hidden_units, low, low_t = prefix_call(prefix_embed, up_weight, up_bias, out_weight, out_bias)
     _, *later = lax.optimization_barrier((small, attn_weight, ff_in_weight, ff_out_weight))
     own = (qkv_weight, attn_weight, ff_in_weight, ff_out_weight)
     other = (other_qkv,) + tuple(swapped(weight) for weight in later)
-    saved = first_call(
-        block_input, segments, small, other_small, qkv_weight, other_qkv, low, low_t, tables
-    )
-    act, act_send, grad, grad_send, prefix_grad = middle_call(
-        block_input, cotangent, segments, small, other_small, *own, *other, low, low_t, tables, *saved
-    )
-
-    def swap_acts(state):
-        return dict(state, act=swapped(state["act"]))
+    *saved, qkv_zero, hidden_units = first_call(
+        (small, other_small), other_qkv, block_input, segments, qkv_weight, prefix_embed, up_weight,
+        up_bias, out_weight, out_bias, tables,
+    )
+    x_zero, small_zero = saved[10:]
+    (h_one, act_one, mixed_one, grad_one, grad_low, slope_zero, packed_zero, prefix_grad, small_one,
+     in_zero, out_zero, attn_one, out_one) = middle_call(
+        (small, other_small, *saved), other, cotangent, *own, tables
+    )
+
+    def layer_one_out(state):
+        keep, send = result_call(state["h_one"], act_one, mixed_one, small_one, attn_one, out_one)
+        return dict(state, act=keep, act_send=send)
+
+    def layer_zero_feed(state):
+        two = feed_back_call(state["grad_low"], slope_zero, in_zero, out_zero)
+        return dict(state, grad_two=two, act_other=swapped(state["act_send"]))
+
+    def layer_zero_norms(state):
+        keep, send = norms_call(
+            x_zero, grad_low, state["grad_two"], packed_zero, grad_one, small_zero, qkv_zero
+        )
+        return dict(state, grad=keep, grad_send=send)
 
     def swap_grads(state):
-        return dict(state, grad=swapped(state["grad"]))
-
-    def turn(state):
-        return dict(state, turned=turn_call(state["out_weight"], up_weight))
-
-    works = [None, swap_acts, swap_grads, turn]
-    state = {"act": act_send, "grad": grad_send, "out_weight": out_weight}
+        turned = turn_call(state["out_weight"], up_weight)
+        return dict(state, grad_other=swapped(state["grad_send"]), turned=turned)
+
+    works = [layer_one_out, layer_zero_feed, layer_zero_norms, swap_grads]
+    state = {"h_one": h_one, "grad_low": grad_low, "out_weight": out_weight}
     for axis, pairs in hops("pipe") + hops("dp") + hops("grp"):
         moved = lax.ppermute(prefix_grad, axis, pairs)
-        work = works.pop(0) if works else None
-        if work:
-            state = work(state)
+        if works:
+            state = works.pop(0)(state)
         prefix_grad, moved, state = lax.optimization_barrier((prefix_grad, moved, state))
         prefix_grad = prefix_grad + moved
     for work in works:
         state = work(state)
     col_width = 2 * D // lax.axis_size("dp")
     grad_embed, grad_up, grad_up_b, grad_out, grad_out_b, activations, input_grads = final_call(
-        col_width, prefix_grad, hidden_units, prefix_embed, *state["turned"], state["act"], state["grad"],
-        act, grad,
+        col_width, (state["act"], state["grad"]), prefix_grad, hidden_units, prefix_embed,
+        *state["turned"], state["act_other"], state["grad_other"],
     )
     return (
         activations,

time: 76.3 us -> 66.5 us (0.87)
  waiting for transfers between devices: 11 us -> 6.31 us
  Pallas kernels: 48.5 us -> 45.3 us
  local copies, waits for them, and re-layouts: 3.42 us -> 2.14 us
  other arithmetic: 0.95 us -> 0.07 us
    ppermute x5, waiting for transfers between devices: 11 us -> 5.03 us  [local(): moved = lax.ppermute(prefix_grad, axis, pairs)]
    pallas_call x6 -> x8, Pallas kernels: 48.5 us -> 45.3 us  [call_kernel(): pl.pallas_call(kernel, name=name, out_shape=[space(shape, dtype) for spac...]
    unnamed x8 -> x10, local copies, waits for them, and re-layouts: 3.42 us -> 2.14 us
    ppermute x7, waiting for transfers between devices: 0.02 us -> 1.29 us  [swapped(): return lax.ppermute(array_in, 'pipe', [(0, 1), (1, 0)])]
    add x5, other arithmetic: 0.95 us -> 0.07 us  [local(): prefix_grad = prefix_grad + moved]
  transfers between devices with their start and end apart: 12 -> 12, of which waited for: 4 -> 5; matrix products, arithmetic and copies ran while one was open for 1% -> 0% of each run, Pallas kernels for 19% -> 28%
where the time goes in v3:
time: 66.5 us; the launch traced here: 66.2 us
  Pallas kernels  45.3 us (68%)
  starting transfers between devices  11.5 us (17%)
  waiting for transfers between devices  6.31 us (9%)
  local copies, waits for them, and re-layouts  2.14 us (3%)
  between operations  0.99 us (1%)
    pallas_call x8, Pallas kernels, call_kernel(): pl.pallas_call(kernel, name=name, out_shape=[space(shape, dtype) for spac...  45.3 us
    ppermute x5, starting transfers between devices, local(): moved = lax.ppermute(prefix_grad, axis, pairs)  9.47 us
    ppermute x5, waiting for transfers between devices, local(): moved = lax.ppermute(prefix_grad, axis, pairs)  5.03 us
    unnamed x10, local copies, waits for them, and re-layouts  2.14 us
    ppermute x7, starting transfers between devices, swapped(): return lax.ppermute(array_in, 'pipe', [(0, 1), (1, 0)])  1.99 us
  transfers between devices with their start and end apart: 12, of which 5 were waited for; matrix products, arithmetic and copies ran while one was open for 0% of the time, Pallas kernels for 28%

profile of v3, /device:TPU:0, one launch (start us, length us, event | category | flops | bytes accessed | tf_op | source)
XLA Modules:
  0.0 66.2 jit_solution(11802731618181034891)
XLA Ops:
  0.6 0.5 collective-permute-start.1
  1.2 0.9 %small_parameters.1.own_small.refs_0_ = f32[1,6656]{1,0:T(1,128)S(1)} custom-call(f32[1,512]{1,0:T(1,128)} %gain_one.1, f32[1,512]{1,0:T(1,128)} %shift_one.1, f32[1,512]{1,0:T(1,128)} %gain_two.1, f32[1,512]{1,0:T(1,128)} %shift_two.1, f32[1,512]{1,0:T(1,128)} %attn_b.1, f32[1,512]{1,0:T(1,128)} %out_b.1, f32[1,1536]{1,0:T(1,128)} %qkv_b.1, f32[1,2048]{1,0:T(1,128)} %in_b.1), custom_call_target="tpu_custom_call" | custom-call | flops 6656 | bytes 8388608 | tf_op jit(solution)/shard_map/small_parameters/pallas_call | solution.py:54
  2.2 0.5 collective-permute-start.2
  2.7 0.4 collective-permute-start.4
  3.1 1.1 %collective-permute-done.other_small.refs_1_ = f32[1,6656]{1,0:T(1,128)S(1)} collective-permute-done((f32[1,6656]{1,0:T(1,128)S(1)}, f32[1,6656]{1,0:T(1,128)S(1)}, u32[]{:S(2)}, u32[]{:S(2)}) %collective-permute-start) | collective-permute-done | bytes 26656 | tf_op jit(solution)/shard_map/ppermute | solution.py:747
  4.3 0.1 collective-permute-done.1.other_qkv.refs_14_
  4.4 7.2 %first_attention.1 = (bf16[512,512]{1,0:T(8,128)(2,1)S(1)}, bf16[512,512]{1,0:T(8,128)(2,1)S(1)}, bf16[512,512]{1,0:T(8,128)(2,1)S(1)}, bf16[4,1152,256]{2,1,0:T...) custom-call(f32[1,6656]{1,0:T(1,128)S(1)} %small_parameters.1.own_sm, ...), custom_call_target="tpu_custom_call" | custom-call | flops 80530636800 | bytes 8388608 | tf_op jit(solution)/shard_map/first_attention/pallas_call | solution.py:54
  11.7 1.3 %copy-done.2 = bf16[1,512,2048]{2,1,0:T(8,128)(2,1)} copy-done((bf16[1,512,2048]{2,1,0:T(8,128)(2,1)}, bf16[1,512,2048]{2,1,0:T(8,128)(2,1)S(1)}, u32[]{:S(2)}) %copy-start.2) | copy-done | bytes 2097176
  13.0 0.7 %copy-done.3 = bf16[1,2048,512]{2,1,0:T(8,128)(2,1)} copy-done((bf16[1,2048,512]{2,1,0:T(8,128)(2,1)}, bf16[1,2048,512]{2,1,0:T(8,128)(2,1)S(1)}, u32[]{:S(2)}) %copy-start.3) | copy-done | bytes 2097176
  13.8 24.2 %middle.1 = (bf16[512,512]{1,0:T(8,128)(2,1)S(1)}, bf16[512,2048]{1,0:T(8,128)(2,1)S(1)}, bf16[512,512]{1,0:T(8,128)(2,1)S(1)}, f32[512,512]{1,0:T(8,128)S(1)}, ...) custom-call(f32[1,6656]{1,0:T(1,128)S(1)} %small_parameters.1.own_sm, ...), custom_call_target="tpu_custom_call" | custom-call | flops 16106127360 | bytes 8388608 | tf_op jit(solution)/shard_map/middle/pallas_call | solution.py:54
  38.1 0.3 collective-permute-start.5
  38.4 2.4 %layer_one_out.1 = (bf16[1,2,1,512,512]{4,3,2,1,0:T(8,128)(2,1)}, bf16[512,512]{1,0:T(8,128)(2,1)S(1)}) custom-call(bf16[512,512]{1,0:T(8,128)(2,1)S(1)} %get-tuple-element.108.h_one, bf16[512,2048]{1,0:T(8,128)(2,1)S(1)} %get-tuple-element.109.act, bf16[512,512]{1,0:T(8,128)(2,1)S(1)} %get-tuple-element.110.mixed, f32[1,6656]{1,0:T(1,128)S(1)} %get-tuple-element.111.small, ...), custom_call_target="tpu_custom_call" | custom-call | flops 1342177280 | bytes 8388608 | tf_op jit(solution)/shard_map/layer_one_out/pallas_call | solution.py:54
  40.8 0.3 collective-permute-start.7
  41.2 2.9 %collective-permute-start.6 = (f32[40,512]{1,0:T(8,128)S(1)}, f32[40,512]{1,0:T(8,128)S(1)}, u32[]{:S(2)}, u32[]{:S(2)}) collective-permute-start(f32[40,512]{1,0:T(8,128)S(1)} %add.15), channel_id=1, source_target_pairs={{0,1},{1,0},{2,3},{3,2},{4,5},{5,4},{6,7},{7,6},{8,9},{9,8},{10,11... | collective-permute-start | bytes 245768 | tf_op jit(solution)/shard_map/ppermute | solution.py:824
  44.1 2.4 %layer_zero_feed_back.1.two = f32[512,512]{1,0:T(8,128)S(1)} custom-call(bf16[512,512]{1,0:T(8,128)(2,1)S(1)} %get-tuple-element.121.grad, bf16[512,2048]{1,0:T(8,128)(2,1)S(1)} %get-tuple-element.122.slope, bf16[512,2048]{1,0:T(8,128)(2,1)S(1)} %get-tuple-element.123.w_in, bf16[2048,512]{1,0:T(8,128)(2,1)S(1)} %get-tuple-element.124.w_out), custom_call_target="tpu_custom_call" | custom-call | flops 2147483648 | bytes 8388608 | tf_op jit(solution)/shard_map/layer_zero_feed_back/pallas_call | solution.py:54
  46.5 0.3 collective-permute-done.6
  46.8 1.9 %collective-permute-start.8 = (f32[40,512]{1,0:T(8,128)S(1)}, f32[40,512]{1,0:T(8,128)S(1)}, u32[]{:S(2)}, u32[]{:S(2)}) collective-permute-start(f32[40,512]{1,0:T(8,128)S(1)} %add.16), channel_id=1, source_target_pairs={{0,2},{1,3},{2,0},{3,1},{4,6},{5,7},{6,4},{7,5},{8,10},{9,11},{10,... | collective-permute-start | bytes 245768 | tf_op jit(solution)/shard_map/ppermute | solution.py:824
  48.6 2.9 %layer_zero_norms.1 = (f32[1,2,1,512,512]{4,3,2,1,0:T(8,128)}, f32[512,512]{1,0:T(8,128)S(1)}) custom-call(bf16[512,512]{1,0:T(8,128)(2,1)S(1)} %get-tuple-element.102.refs_12_.x_ref, bf16[512,512]{1,0:T(8,128)(2,1)S(1)} %get-tuple-element.121.grad, f32[512,512]{1,0:T(8,128)S(1)} %layer_zero_feed_back.1.two, ...), custom_call_target="tpu_custom_call" | custom-call | flops 805306368 | bytes 8388608 | tf_op jit(solution)/shard_map/layer_zero_norms/pallas_call | solution.py:54
  51.7 1.6 %collective-permute-start.9 = (f32[40,512]{1,0:T(8,128)S(1)}, f32[40,512]{1,0:T(8,128)S(1)}, u32[]{:S(2)}, u32[]{:S(2)}) collective-permute-start(f32[40,512]{1,0:T(8,128)S(1)} %add.17), channel_id=1, source_target_pairs={{0,4},{4,0},{8,12},{12,8},{1,5},{5,1},{9,13},{13,9},{2,6},{6,2},{1... | collective-permute-start | bytes 245768 | tf_op jit(solution)/shard_map/ppermute | solution.py:824
  53.3 2.7 %turned_matrices.1 = (bf16[2048,512]{1,0:T(8,128)(2,1)S(1)}, bf16[512,512]{1,0:T(8,128)(2,1)S(1)}, bf16[512,512]{1,0:T(8,128)(2,1)S(1)}) custom-call(f32[512,2048]{1,0:T(8,128)} %out_hbm.2, f32[512,512]{1,0:T(8,128)} %up_hbm.3), custom_call_target="tpu_custom_call" | custom-call | flops 134217728 | bytes 8388608 | tf_op jit(solution)/shard_map/turned_matrices/pallas_call | solution.py:54
  56.1 0.5 collective-permute-done.9
  56.6 2.7 %collective-permute-start.11 = (f32[40,512]{1,0:T(8,128)S(1)}, f32[40,512]{1,0:T(8,128)S(1)}, u32[]{:S(2)}, u32[]{:S(2)}) collective-permute-start(f32[40,512]{1,0:T(8,128)S(1)} %add.18), channel_id=1, source_target_pairs={{0,8},{4,12},{8,0},{12,4},{1,9},{5,13},{9,1},{13,5},{2,10},{6,14},... | collective-permute-start | bytes 245768 | tf_op jit(solution)/shard_map/ppermute | solution.py:824
  59.3 4.2 %collective-permute-done.11 = f32[40,512]{1,0:T(8,128)S(1)} collective-permute-done((f32[40,512]{1,0:T(8,128)S(1)}, f32[40,512]{1,0:T(8,128)S(1)}, u32[]{:S(2)}, u32[]{:S(2)}) %collective-permute-start.11) | collective-permute-done | bytes 81952 | tf_op jit(solution)/shard_map/ppermute | solution.py:824
  63.5 2.5 %reparam.1 = (f32[10,512]{1,0:T(8,128)}, f32[512,512]{1,0:T(8,128)}, f32[1,512]{1,0:T(1,128)}, f32[512,256]{1,0:T(8,128)}, f32[1,256]{1,0:T(1,128)}, /*index=5*/...) custom-call(f32[40,512]{1,0:T(8,128)S(1)} %add.19.refs_0_, ...), custom_call_target="tpu_custom_call", output_to_operand_aliasing={{5}: (8, {}), {6}: (9, {})} | custom-call | flops 134217728 | bytes 8388608 | tf_op jit(solution)/shard_map/reparam/pallas_call | solution.py:54
  (23 shorter events, 0.5 us)
Async XLA Ops:
  0.6 3.8 %collective-permute-start.1 = (bf16[1,512,1536]{2,1,0:T(8,128)(2,1)}, bf16[1,512,1536]{2,1,0:T(8,128)(2,1)S(1)}, u32[]{:S(2)}, u32[]{:S(2)}) collective-permute-start(bf16[1,512,1536]{2,1,0:T(8,128)(2,1)} %refs_19_.1), channel_id=1, source_target_pairs={{0,16},{16,0},{1,17},{17,1},{2,18},{18,2},{3,19},{19,3},{4,20},{20... | collective-permute-start | bytes 4718600 | tf_op jit(solution)/shard_map/ppermute | solution.py:747
  2.0 2.2 %collective-permute-start = (f32[1,6656]{1,0:T(1,128)S(1)}, f32[1,6656]{1,0:T(1,128)S(1)}, u32[]{:S(2)}, u32[]{:S(2)}) collective-permute-start(f32[1,6656]{1,0:T(1,128)S(1)} %small_parameters.1.own_small.refs_0_), channel_id=1, source_target_pairs={{0,16},{16,0},{1,17},{17,1},{2,18},{18,2},{3,19},{19,3},{4,20},{20... | collective-permute-start | bytes 79880 | tf_op jit(solution)/shard_map/ppermute | solution.py:747
  2.2 9.5 %collective-permute-start.2 = (bf16[1,512,512]{2,1,0:T(8,128)(2,1)}, bf16[1,512,512]{2,1,0:T(8,128)(2,1)S(1)}, u32[]{:S(2)}, u32[]{:S(2)}) collective-permute-start(bf16[1,512,512]{2,1,0:T(8,128)(2,1)} %refs_20_.1), channel_id=1, source_target_pairs={{0,16},{16,0},{1,17},{17,1},{2,18},{18,2},{3,19},{19,3},{4,20},{20... | collective-permute-start | bytes 1572872 | tf_op jit(solution)/shard_map/ppermute | solution.py:747
  2.6 9.0 %collective-permute-start.3 = (bf16[1,512,2048]{2,1,0:T(8,128)(2,1)}, bf16[1,512,2048]{2,1,0:T(8,128)(2,1)S(1)}, u32[]{:S(2)}, u32[]{:S(2)}) collective-permute-start(bf16[1,512,2048]{2,1,0:T(8,128)(2,1)} %refs_21_.1), channel_id=1, source_target_pairs={{0,16},{16,0},{1,17},{17,1},{2,18},{18,2},{3,19},{19,3},{4,20},{20... | collective-permute-start | bytes 6291464 | tf_op jit(solution)/shard_map/ppermute | solution.py:747
  2.7 9.0 %collective-permute-start.4 = (bf16[1,2048,512]{2,1,0:T(8,128)(2,1)}, bf16[1,2048,512]{2,1,0:T(8,128)(2,1)S(1)}, u32[]{:S(2)}, u32[]{:S(2)}) collective-permute-start(bf16[1,2048,512]{2,1,0:T(8,128)(2,1)} %refs_22_.1), channel_id=1, source_target_pairs={{0,16},{16,0},{1,17},{17,1},{2,18},{18,2},{3,19},{19,3},{4,20},{20... | collective-permute-start | bytes 6291464 | tf_op jit(solution)/shard_map/ppermute | solution.py:747
  4.4 7.2 %copy-start.1 = (bf16[1,512,1536]{2,1,0:T(8,128)(2,1)}, bf16[1,512,1536]{2,1,0:T(8,128)(2,1)S(1)}, u32[]{:S(2)}) copy-start(bf16[1,512,1536]{2,1,0:T(8,128)(2,1)S(1)} %collective-permute-done.1.other_qkv.refs_14_) | copy-start | bytes 4718596
  11.6 2.2 %copy-start.4 = (bf16[1,512,512]{2,1,0:T(8,128)(2,1)}, bf16[1,512,512]{2,1,0:T(8,128)(2,1)S(1)}, u32[]{:S(2)}) copy-start(bf16[1,512,512]{2,1,0:T(8,128)(2,1)S(1)} %collective-permute-done.2.refs_15_) | copy-start | bytes 1572868
  11.7 1.4 %copy-start.2 = (bf16[1,512,2048]{2,1,0:T(8,128)(2,1)}, bf16[1,512,2048]{2,1,0:T(8,128)(2,1)S(1)}, u32[]{:S(2)}) copy-start(bf16[1,512,2048]{2,1,0:T(8,128)(2,1)S(1)} %collective-permute-done.3.refs_16_) | copy-start | bytes 6291460
  11.7 2.0 %copy-start.3 = (bf16[1,2048,512]{2,1,0:T(8,128)(2,1)}, bf16[1,2048,512]{2,1,0:T(8,128)(2,1)S(1)}, u32[]{:S(2)}) copy-start(bf16[1,2048,512]{2,1,0:T(8,128)(2,1)S(1)} %collective-permute-done.4.refs_17_) | copy-start | bytes 6291460
  38.1 2.8 %collective-permute-start.5 = (f32[40,512]{1,0:T(8,128)S(1)}, f32[40,512]{1,0:T(8,128)S(1)}, u32[]{:S(2)}, u32[]{:S(2)}) collective-permute-start(f32[40,512]{1,0:T(8,128)S(1)} %get-tuple-element.117), channel_id=1, source_target_pairs={{0,16},{16,0},{1,17},{17,1},{2,18},{18,2},{3,19},{19,3},{4,20},{20... | collective-permute-start | bytes 245768 | tf_op jit(solution)/shard_map/ppermute | solution.py:824
  40.8 5.9 %collective-permute-start.7 = (bf16[512,512]{1,0:T(8,128)(2,1)S(1)}, bf16[512,512]{1,0:T(8,128)(2,1)S(1)}, u32[]{:S(2)}, u32[]{:S(2)}) collective-permute-start(bf16[512,512]{1,0:T(8,128)(2,1)S(1)} %get-tuple-element.120), channel_id=1, source_target_pairs={{0,16},{16,0},{1,17},{17,1},{2,18},{18,2},{3,19},{19,3},{4,20},{20... | collective-permute-start | bytes 1572872 | tf_op jit(solution)/shard_map/ppermute | solution.py:747
  41.2 5.6 %collective-permute-start.6 = (f32[40,512]{1,0:T(8,128)S(1)}, f32[40,512]{1,0:T(8,128)S(1)}, u32[]{:S(2)}, u32[]{:S(2)}) collective-permute-start(f32[40,512]{1,0:T(8,128)S(1)} %add.15), channel_id=1, source_target_pairs={{0,1},{1,0},{2,3},{3,2},{4,5},{5,4},{6,7},{7,6},{8,9},{9,8},{10,11... | collective-permute-start | bytes 245768 | tf_op jit(solution)/shard_map/ppermute | solution.py:824
  46.8 4.8 %collective-permute-start.8 = (f32[40,512]{1,0:T(8,128)S(1)}, f32[40,512]{1,0:T(8,128)S(1)}, u32[]{:S(2)}, u32[]{:S(2)}) collective-permute-start(f32[40,512]{1,0:T(8,128)S(1)} %add.16), channel_id=1, source_target_pairs={{0,2},{1,3},{2,0},{3,1},{4,6},{5,7},{6,4},{7,5},{8,10},{9,11},{10,... | collective-permute-start | bytes 245768 | tf_op jit(solution)/shard_map/ppermute | solution.py:824
  51.6 5.0 %collective-permute-start.10 = (f32[512,512]{1,0:T(8,128)S(1)}, f32[512,512]{1,0:T(8,128)S(1)}, u32[]{:S(2)}, u32[]{:S(2)}) collective-permute-start(f32[512,512]{1,0:T(8,128)S(1)} %get-tuple-element.142), channel_id=1, source_target_pairs={{0,16},{16,0},{1,17},{17,1},{2,18},{18,2},{3,19},{19,3},{4,20},{20... | collective-permute-start | bytes 3145736 | tf_op jit(solution)/shard_map/ppermute | solution.py:747
  51.7 11.9 %copy-start = (f32[10,512]{1,0:T(8,128)S(1)}, f32[10,512]{1,0:T(8,128)}, u32[]{:S(2)}) copy-start(f32[10,512]{1,0:T(8,128)} %refs_2_) | copy-start | bytes 61444
  51.7 4.9 %collective-permute-start.9 = (f32[40,512]{1,0:T(8,128)S(1)}, f32[40,512]{1,0:T(8,128)S(1)}, u32[]{:S(2)}, u32[]{:S(2)}) collective-permute-start(f32[40,512]{1,0:T(8,128)S(1)} %add.17), channel_id=1, source_target_pairs={{0,4},{4,0},{8,12},{12,8},{1,5},{5,1},{9,13},{13,9},{2,6},{6,2},{1... | collective-permute-start | bytes 245768 | tf_op jit(solution)/shard_map/ppermute | solution.py:824
  56.6 6.9 %collective-permute-start.11 = (f32[40,512]{1,0:T(8,128)S(1)}, f32[40,512]{1,0:T(8,128)S(1)}, u32[]{:S(2)}, u32[]{:S(2)}) collective-permute-start(f32[40,512]{1,0:T(8,128)S(1)} %add.18), channel_id=1, source_target_pairs={{0,8},{4,12},{8,0},{12,4},{1,9},{5,13},{9,1},{13,5},{2,10},{6,14},... | collective-permute-start | bytes 245768 | tf_op jit(solution)/shard_map/ppermute | solution.py:824

commit v4 on v3

--- a/solution.py
+++ b/solution.py
@@ -37,9 +37,9 @@
 
 NO_COPIES = ((),) * 4
 MIB = 1024 * 1024
-FIRST_MIB = 40
-MIDDLE_MIB = 34
-LATE_MIB = 16
+EARLY_MIB = 24
+MIDDLE_MIB = 22
+LATE_MIB = 12
 
 G1, B1, G2, B2, B_ATTN, B_OUT, B_QKV, B_IN = 0, 1, 2, 3, 4, 5, 6, 9
 SMALL = 13 * D
@@ -404,7 +404,7 @@
 
 def small_call(*arrays):
     (packed,) = call_kernel(
-        small_kernel, "small_parameters", in_hbm(*arrays), vmem([((1, SMALL), f32)]), [], 8, 8, SMALL
+        small_kernel, "small_parameters", in_hbm(*arrays), vmem([((1, SMALL), f32)]), [], 8, LATE_MIB, SMALL
     )
     return packed
 
@@ -418,6 +418,56 @@
         arrivals[part].wait()
         states = few_rows_dot(units, out_w[:, cols]) + out_b[:, cols]
         low[part] = jnp.where(real, states, 0.0).astype(bf16)
+
+
+OPENING_SHAPES = (
+    ((SEQ, D), bf16),
+    ((SEQ, D), f32),
+    ((P_ROWS, BLK), f32),
+    ((4, PAD, D), bf16),
+    ((PREFIX, D), f32),
+    ((2 * 8, SEQ), f32),
+    ((D, 3 * D), bf16),
+)
+
+
+def opening_kernel(x_hbm, seg_hbm, embed_hbm, up_hbm, up_b_hbm, out_hbm, out_b_hbm, tables_hbm, qkv_hbm,
+                   x_ref, hat, mask, low, hidden, tables, own_qkv, seg, embed, up_w, up_b, out_w, out_b, sems):
+    section = lax.axis_index("pipe")
+    copies = Copies(sems)
+    x_copy = copies.start(x_hbm.at[section, 0], x_ref)
+    seg_copy = copies.start(seg_hbm.at[section], seg)
+    prefix_copies = [
+        copies.start(src, dst)
+        for src, dst in ((embed_hbm, embed), (up_hbm, up_w), (up_b_hbm, up_b.at[0]), (out_b_hbm, out_b.at[0]))
+    ]
+    parts = [
+        copies.start(out_hbm.at[:, i * D : (i + 1) * D], out_w.at[:, i * D : (i + 1) * D])
+        for i in range(4)
+    ]
+    late = [copies.start(tables_hbm, tables), copies.start(qkv_hbm.at[0], own_qkv)]
+    seg_copy.wait()
+    fill_mask(seg, mask)
+    x_copy.wait()
+    hat[...], _ = normalized(x_ref[...].astype(f32))
+    wait_all(*prefix_copies)
+    prefix_states(embed, up_w, up_b, out_w, out_b, parts, hidden, low)
+    wait_all(*late)
+
+
+def opening_call(*arrays):
+    scratch = [
+        ((1, SEQ), jnp.int32),
+        ((PREFIX, D), f32),
+        ((D, D), f32),
+        ((1, D), f32),
+        ((D, 4 * D), f32),
+        ((1, 4 * D), f32),
+    ]
+    return call_kernel(
+        opening_kernel, "opening", in_hbm(*arrays), vmem(OPENING_SHAPES), scratch, 12, EARLY_MIB,
+        2 * 6 * PAD * D * 5 * D,
+    )
 
 
 HEAD_SHAPES = (
@@ -431,66 +481,60 @@
 )
 FIRST_SHAPES = HEAD_SHAPES + (
     ((SEQ, D), bf16),
-    ((4, PAD, D), bf16),
-    ((P_ROWS, BLK), f32),
+    ((2, 1, SMALL), f32),
+    ((2, D, 3 * D), bf16),
+    ((2, D, D), bf16),
+    ((2, D, FF), bf16),
+    ((2, FF, D), bf16),
     ((SEQ, D), bf16),
-    ((1, SMALL), f32),
-    ((D, 3 * D), bf16),
-    ((PREFIX, D), f32),
 )
 
 
-def first_kernel(own_small, other_small, other_qkv, x_hbm, seg_hbm, own_qkv, embed_hbm, up_hbm, up_b_hbm,
-                 out_hbm, out_b_hbm, tables_hbm, *refs):
-    q_t, k_t, v_m, p_ref, pp_ref, inv_ref, mixed_ref, two_ref, low, mask_ref, x_ref, small_ref = refs[:12]
-    w_ref, hidden, embed, up_w, up_b, out_w, out_b, tables, seg, k_m, v_t, sems = refs[12:]
+def first_kernel(own_small, other_small, own_qkv, other_qkv, hat_ref, mask, low, tables,
+                 attn_hbm, ff_in_hbm, ff_out_hbm, cot_hbm,
+                 q_t, k_t, v_m, p_ref, pp_ref, inv_ref, mixed_ref, two_ref, small, w_qkv, w_attn, w_in,
+                 w_out, cot_ref, k_m, v_t, sems):
     section = lax.axis_index("pipe")
-    here = section == 0
     copies = Copies(sems)
-    x_copy = copies.start(x_hbm.at[section, 0], x_ref)
-    seg_copy = copies.start(seg_hbm.at[section], seg)
-    small_copy = copies.of_layer(here, own_small, other_small, small_ref)
-    late = [
-        copies.of_layer(here, own_qkv.at[0, rows], other_qkv.at[0, rows], w_ref.at[rows])
-        for rows in (slice(i * BLK, (i + 1) * BLK) for i in range(4))
+    now = [
+        copies.start(own_small, small.at[section]),
+        copies.start(other_small, small.at[1 - section]),
+        copies.start(own_qkv, w_qkv.at[section]),
+        copies.start(other_qkv.at[0], w_qkv.at[1 - section]),
     ]
-    late.append(copies.start(tables_hbm, tables))
-    prefix_copies = [
-        copies.start(src, dst)
-        for src, dst in ((embed_hbm, embed), (up_hbm, up_w), (up_b_hbm, up_b.at[0]), (out_b_hbm, out_b.at[0]))
+    later = [
+        copies.start(ff_in_hbm.at[0], w_in.at[section]),
+        copies.start(attn_hbm.at[0], w_attn.at[section]),
+        copies.start(ff_out_hbm.at[0], w_out.at[section]),
+        copies.start(cot_hbm.at[section, 0], cot_ref),
     ]
-    parts = [
-        copies.start(out_hbm.at[:, i * D : (i + 1) * D], out_w.at[:, i * D : (i + 1) * D])
-        for i in range(4)
-    ]
-    seg_copy.wait()
-    fill_mask(seg, mask_ref)
-    wait_all(x_copy, small_copy)
-    hat, _ = normalized(x_ref[...].astype(f32))
-    normed = (hat * small_row(small_ref, G1) + small_row(small_ref, B1)).astype(bf16)
-    two_ref[...] = (hat * small_row(small_ref, G2) + small_row(small_ref, B2)).astype(bf16)
-    wait_all(*late)
-    project_heads(normed, w_ref, small_ref, tables[:8, :], tables[8:, :], q_t, k_t, k_m, v_m, v_t)
-    wait_all(*prefix_copies)
-    prefix_states(embed, up_w, up_b, out_w, out_b, parts, hidden, low)
-    attend(q_t, k_m, v_t, low.at[0], low.at[1], mask_ref, p_ref, pp_ref, inv_ref, mixed_ref)
-
-
-def first_call(smalls, other_qkv, *arrays):
-    scratch = [
-        ((PREFIX, D), f32),
-        ((D, D), f32),
-        ((1, D), f32),
-        ((D, 4 * D), f32),
-        ((1, 4 * D), f32),
-        ((2 * 8, SEQ), f32),
-        ((1, SEQ), jnp.int32),
-        ((SEQ, D), bf16),
-        ((D, SEQ), bf16),
-    ]
+    wait_all(*now)
+    hat = hat_ref[...]
+    zero = small.at[0]
+    normed = (hat * small_row(zero, G1) + small_row(zero, B1)).astype(bf16)
+    two_ref[...] = (hat * small_row(zero, G2) + small_row(zero, B2)).astype(bf16)
+    project_heads(normed, w_qkv.at[0], zero, tables[:8, :], tables[8:, :], q_t, k_t, k_m, v_m, v_t)
+    attend(q_t, k_m, v_t, low.at[0], low.at[1], mask, p_ref, pp_ref, inv_ref, mixed_ref)
+    wait_all(*later)
+
+
+def first_call(ready, *arrays):
     return call_kernel(
-        first_kernel, "first_attention", in_vmem(*smalls) + anywhere(other_qkv) + in_hbm(*arrays),
-        vmem(FIRST_SHAPES), scratch, 16, FIRST_MIB, 200 * SEQ * D * 3 * D,
+        first_kernel, "first_attention", in_vmem(*ready) + in_hbm(*arrays), vmem(FIRST_SHAPES),
+        [((SEQ, D), bf16), ((D, SEQ), bf16)], 8, EARLY_MIB, 200 * SEQ * D * 3 * D,
+    )
+
+
+def feed_kernel(two, small, other_in, w_in_before, act_ref, slope_ref, w_in, sems):
+    wait_all(Copies(sems).start(other_in.at[0], w_in.at[1 - lax.axis_index("pipe")]))
+    feed_in(two[...], w_in.at[0], small.at[0], act_ref, slope_ref, NO_COPIES)
+
+
+def feed_call(*arrays):
+    shapes = [((SEQ, FF), bf16), ((SEQ, FF), bf16), ((2, D, FF), bf16)]
+    return call_kernel(
+        feed_kernel, "first_feed", in_vmem(*arrays), vmem(shapes), [], 1, LATE_MIB, 2 * SEQ * D * FF,
+        {3: 2},
     )
 
 
@@ -503,83 +547,48 @@
     ((D, SEQ), bf16),
     ((SEQ, D), f32),
     ((SEQ, D), bf16),
-    ((SEQ, FF), bf16),
     ((3 * D, SEQ), bf16),
     ((4 * PREFIX, D), f32),
-    ((1, SMALL), f32),
-    ((D, FF), bf16),
-    ((FF, D), bf16),
-    ((D, D), bf16),
-    ((FF, D), bf16),
+    ((2, D, D), bf16),
+    ((2, FF, D), bf16),
 )
 
 
-def middle_kernel(*refs):
-    def take(count):
-        nonlocal refs
-        taken, refs = refs[:count], refs[count:]
-        return taken
-
-    own_small, other_small, q0, k0, v0, p0, pp0, inv0, mixed0, two0, low, mask, x_ref, small_zero = take(14)
-    other = take(4)
-    (cot_hbm,) = take(1)
-    own = take(4)
-    (tables_hbm,) = take(1)
-    (h_one, act_one, mixed_one, grad_one, grad_low, slope_zero, packed_zero, prefix_grad,
-     small_one, w_in_zero, w_out_zero, w_attn, w_out) = take(13)
-    w_attn_zero, w_qkv, w_in = take(3)
-    q_t, k_t, v_m, p_ref, pp_ref, inv_ref = take(6)
-    cot_ref, tables, act_zero, slope_one, k_m, v_t, dq, dk, dv, packed, pre_grad, sems = refs
+def middle_kernel(w_attn_before, w_out_before, q0, k0, v0, p0, pp0, inv0, mixed0, small, w_qkv, w_in,
+                  other_attn, other_out, cot_ref, x_ref, act_zero, low, mask, tables,
+                  h_one, act_one, mixed_one, grad_one, grad_low, packed_zero, prefix_grad, w_attn, w_out,
+                  q_t, k_t, v_m, p_ref, pp_ref, inv_ref, slope_one, k_m, v_t, dq, dk, dv, packed, pre_grad,
+                  sems):
     section = lax.axis_index("pipe")
-    zero, one = section == 0, section == 1
     copies = Copies(sems)
-
-    def weights(here, which, dst, index=()):
-        index = (0,) + index
-        view = dst.at[index[1:]] if len(index) > 1 else dst
-        return copies.of_layer(here, own[which].at[index], other[which].at[index], view)
-
-    everything = slice(None)
-    in_zero = [[weights(zero, 2, w_in_zero, (everything, chunk_of(i)))] for i in range(4)]
-    out_copies = [weights(zero, 1, w_attn_zero)]
-    out_copies += [weights(zero, 3, w_out_zero, (chunk_of(i),)) for i in range(4)]
-    feed_in(two0[...], w_in_zero, small_zero, act_zero, slope_zero, in_zero)
-    head_copies = [
-        copies.of_layer(one, own_small, other_small, small_one),
-        weights(one, 0, w_qkv),
-        copies.start(tables_hbm, tables),
-    ]
-    in_one = [[weights(one, 2, w_in, (everything, chunk_of(i)))] for i in range(4)]
-    wait_all(*out_copies)
+    wait_all(
+        copies.start(other_attn.at[0], w_attn.at[1 - section]),
+        copies.start(other_out.at[0], w_out.at[1 - section]),
+    )
+    small_one = small.at[1]
     h_one[...] = layer_result(
-        x_ref[...].astype(f32), mixed0[...], w_attn_zero[...], act_zero, w_out_zero[...], small_zero
+        x_ref[...].astype(f32), mixed0[...], w_attn[0], act_zero, w_out[0], small.at[0]
     ).astype(bf16)
 
-    back_copies = [copies.start(cot_hbm.at[section, 0], cot_ref)]
-    back_copies += [weights(one, 3, w_out, (chunk_of(i),)) for i in range(4)]
-    attn_copy = weights(one, 1, w_attn)
-    wait_all(*head_copies)
     cos, sin = tables[:8, :], tables[8:, :]
     hat, _ = normalized(h_one[...].astype(f32))
     normed = (hat * small_row(small_one, G1) + small_row(small_one, B1)).astype(bf16)
     two = (hat * small_row(small_one, G2) + small_row(small_one, B2)).astype(bf16)
-    project_heads(normed, w_qkv, small_one, cos, sin, q_t, k_t, k_m, v_m, v_t)
+    project_heads(normed, w_qkv.at[1], small_one, cos, sin, q_t, k_t, k_m, v_m, v_t)
     attend(q_t, k_m, v_t, low.at[2], low.at[3], mask, p_ref, pp_ref, inv_ref, mixed_one)
-    feed_in(two, w_in, small_one, act_one, slope_one, in_one)
-
-    wait_all(*back_copies)
+    feed_in(two, w_in.at[1], small_one, act_one, slope_one, NO_COPIES)
+
     grad = cot_ref[...]
-    grad_two = feed_back(grad, w_out, w_in, slope_one, NO_COPIES)
-    attn_copy.wait()
-    dq[...] = dot(w_attn[...], grad, NT)
+    grad_two = feed_back(grad, w_out.at[1], w_in.at[1], slope_one, NO_COPIES)
+    dq[...] = dot(w_attn[1], grad, NT)
     attend_back(dq, q_t, k_t, v_m, low.at[2], low.at[3], p_ref, pp_ref, inv_ref, mixed_one,
                 dq, dk, dv, pre_grad, 2 * PAD)
     pack_grads(dq, dk, dv, cos, sin, packed)
-    result = norms_back(grad, h_one[...].astype(f32), grad_two, packed[...], w_qkv[...], small_one)
+    result = norms_back(grad, h_one[...].astype(f32), grad_two, packed[...], w_qkv[1], small_one)
     grad_one[...] = result
     grad_low[...] = result.astype(bf16)
 
-    dq[...] = dot(w_attn_zero[...], grad_low[...], NT)
+    dq[...] = dot(w_attn[0], grad_low[...], NT)
     attend_back(dq, q0, k0, v0, low.at[0], low.at[1], p0, pp0, inv0, mixed0,
                 dq, dk, dv, pre_grad, 0)
     for part in range(4):
@@ -589,12 +598,8 @@
     pack_grads(dq, dk, dv, cos, sin, packed_zero)
 
 
-def middle_call(saved, other, *arrays):
-    scratch = (((D, D), bf16), ((D, 3 * D), bf16), ((D, FF), bf16)) + HEAD_SHAPES[:6]
-    scratch += (
-        ((SEQ, D), bf16),
-        ((2 * 8, SEQ), f32),
-        ((SEQ, FF), bf16),
+def middle_call(*arrays):
+    scratch = HEAD_SHAPES[:6] + (
         ((SEQ, FF), bf16),
         ((SEQ, D), bf16),
         ((D, SEQ), bf16),
@@ -605,42 +610,36 @@
         ((4 * PAD, D), f32),
     )
     return call_kernel(
-        middle_kernel, "middle", in_vmem(*saved) + anywhere(*other) + in_hbm(*arrays),
-        vmem(MIDDLE_OUTS), scratch, 24, MIDDLE_MIB, 20 * SEQ * D * 6 * D,
-    )
-
-
-def hand_over(section, values, keep, send_ref, whole, sem):
-    @pl.when(section == 0)
-    def _():
-        keep[...] = values[0]
-        send_ref[...] = values[1]
-
-    @pl.when(section != 0)
-    def _():
-        keep[...] = values[1]
-        send_ref[...] = values[0]
-
-    wait_all(Copies(sem).start(keep, whole.at[0, section, 0]))
-
-
-def result_kernel(h_one, act, mixed, small, w_attn, w_out, whole, send_ref, keep, sem):
-    result = layer_result(
-        h_one[...].astype(f32), mixed[...], w_attn[...], act, w_out[...], small
+        middle_kernel, "middle", in_vmem(*arrays), vmem(MIDDLE_OUTS), scratch, 2, MIDDLE_MIB,
+        20 * SEQ * D * 6 * D, {0: 7, 1: 8},
+    )
+
+
+def hand_over(section, values, send_ref, whole, sems):
+    copies = Copies(sems)
+    wait_all(
+        copies.of_layer(section == 0, values[0], values[1], whole.at[0, section, 0]),
+        copies.of_layer(section == 0, values[1], values[0], send_ref),
+    )
+
+
+def result_kernel(h_one, act, mixed, small, w_attn, w_out, whole, send_ref, result, sems):
+    result[...] = layer_result(
+        h_one[...].astype(f32), mixed[...], w_attn[1], act, w_out[1], small.at[1]
     ).astype(bf16)
-    hand_over(lax.axis_index("pipe"), (h_one[...], result), keep, send_ref, whole, sem)
+    hand_over(lax.axis_index("pipe"), (h_one, result), send_ref, whole, sems)
 
 
 def result_call(*arrays):
     return call_kernel(
         result_kernel, "layer_one_out", in_vmem(*arrays),
         [(pltpu.HBM, (1, 2, 1, SEQ, D), bf16), (pltpu.VMEM, (SEQ, D), bf16)],
-        [((SEQ, D), bf16)], 1, LATE_MIB, 2 * SEQ * D * (D + FF),
+        [((SEQ, D), bf16)], 2, LATE_MIB, 2 * SEQ * D * (D + FF),
     )
 
 
 def feed_back_kernel(grad, slope, w_in, w_out, total):
-    total[...] = feed_back(grad[...], w_out, w_in, slope, NO_COPIES)
+    total[...] = feed_back(grad[...], w_out.at[0], w_in.at[0], slope, NO_COPIES)
 
 
 def feed_back_call(*arrays):
@@ -651,18 +650,18 @@
     return total
 
 
-def norms_kernel(x_ref, grad, two, packed, grad_one, small, w_qkv, whole, send_ref, keep, sem):
-    result = norms_back(
-        grad[...], x_ref[...].astype(f32), two[...], packed[...], w_qkv[...], small
-    )
-    hand_over(lax.axis_index("pipe"), (result, grad_one[...]), keep, send_ref, whole, sem)
+def norms_kernel(x_ref, grad, two, packed, grad_one, small, w_qkv, whole, send_ref, result, sems):
+    result[...] = norms_back(
+        grad[...], x_ref[...].astype(f32), two[...], packed[...], w_qkv[0], small.at[0]
+    )
+    hand_over(lax.axis_index("pipe"), (result, grad_one), send_ref, whole, sems)
 
 
 def norms_call(*arrays):
     return call_kernel(
         norms_kernel, "layer_zero_norms", in_vmem(*arrays),
         [(pltpu.HBM, (1, 2, 1, SEQ, D), f32), (pltpu.VMEM, (SEQ, D), f32)],
-        [((SEQ, D), f32)], 1, LATE_MIB, 6 * SEQ * D * D,
+        [((SEQ, D), f32)], 2, LATE_MIB, 6 * SEQ * D * D,
     )
 
 
@@ -788,29 +787,31 @@
     small, prefix_embed = lax.optimization_barrier((small, prefix_embed))
     tables = jnp.asarray(rope_tables())
     _, *later = lax.optimization_barrier((small, attn_weight, ff_in_weight, ff_out_weight))
-    own = (qkv_weight, attn_weight, ff_in_weight, ff_out_weight)
-    other = (other_qkv,) + tuple(swapped(weight) for weight in later)
-    *saved, qkv_zero, hidden_units = first_call(
-        (small, other_small), other_qkv, block_input, segments, qkv_weight, prefix_embed, up_weight,
-        up_bias, out_weight, out_bias, tables,
-    )
-    x_zero, small_zero = saved[10:]
-    (h_one, act_one, mixed_one, grad_one, grad_low, slope_zero, packed_zero, prefix_grad, small_one,
-     in_zero, out_zero, attn_one, out_one) = middle_call(
-        (small, other_small, *saved), other, cotangent, *own, tables
+    other_attn, other_in, other_out = (swapped(weight) for weight in later)
+    x_zero, hat_zero, mask, low, hidden_units, tables, own_qkv = opening_call(
+        block_input, segments, prefix_embed, up_weight, up_bias, out_weight, out_bias, tables, qkv_weight
+    )
+    *heads, two_zero, small, w_qkv, w_attn, w_in, w_out, cot = first_call(
+        (small, other_small, own_qkv, other_qkv, hat_zero, mask, low, tables),
+        attn_weight, ff_in_weight, ff_out_weight, cotangent,
+    )
+    act_zero, slope_zero, w_in = feed_call(two_zero, small, other_in, w_in)
+    h_one, act_one, mixed_one, grad_one, grad_low, packed_zero, prefix_grad, w_attn, w_out = middle_call(
+        w_attn, w_out, *heads, small, w_qkv, w_in, other_attn, other_out, cot, x_zero, act_zero, low, mask,
+        tables,
     )
 
     def layer_one_out(state):
-        keep, send = result_call(state["h_one"], act_one, mixed_one, small_one, attn_one, out_one)
+        keep, send = result_call(state["h_one"], act_one, mixed_one, small, w_attn, w_out)
         return dict(state, act=keep, act_send=send)
 
     def layer_zero_feed(state):
-        two = feed_back_call(state["grad_low"], slope_zero, in_zero, out_zero)
+        two = feed_back_call(state["grad_low"], slope_zero, w_in, w_out)
         return dict(state, grad_two=two, act_other=swapped(state["act_send"]))
 
     def layer_zero_norms(state):
         keep, send = norms_call(
-            x_zero, grad_low, state["grad_two"], packed_zero, grad_one, small_zero, qkv_zero
+            x_zero, grad_low, state["grad_two"], packed_zero, grad_one, small, w_qkv
         )
         return dict(state, grad=keep, grad_send=send)
 
@@ -818,14 +819,19 @@
         turned = turn_call(state["out_weight"], up_weight)
         return dict(state, grad_other=swapped(state["grad_send"]), turned=turned)
 
-    works = [layer_one_out, layer_zero_feed, layer_zero_norms, swap_grads]
+    works = [None, layer_one_out, layer_zero_feed, layer_zero_norms, swap_grads]
     state = {"h_one": h_one, "grad_low": grad_low, "out_weight": out_weight}
     for axis, pairs in hops("pipe") + hops("dp") + hops("grp"):
-        moved = lax.ppermute(prefix_grad, axis, pairs)
-        if works:
-            state = works.pop(0)(state)
+        if axis == "pipe":
+            moved = lax.ppermute(prefix_grad, axis, pairs)
+        else:
+            prefix_grad = lax.reduce_precision(prefix_grad, 8, 7)
+            moved = lax.ppermute(prefix_grad.astype(bf16), axis, pairs)
+        work = works.pop(0) if works else None
+        if work:
+            state = work(state)
         prefix_grad, moved, state = lax.optimization_barrier((prefix_grad, moved, state))
-        prefix_grad = prefix_grad + moved
+        prefix_grad = prefix_grad + moved.astype(f32)
     for work in works:
         state = work(state)
     col_width = 2 * D // lax.axis_size("dp")

time: 66.5 us -> 55.7 us (0.84)
  waiting for transfers between devices: 6.31 us -> 1.87 us
  Pallas kernels: 45.3 us -> 41.7 us
  local copies, waits for them, and re-layouts: 2.14 us -> 0.01 us
  starting transfers between devices: 11.5 us -> 10.8 us
    ppermute x5 -> x1, starting transfers between devices: 9.47 us -> 0.14 us  [local(): moved = lax.ppermute(prefix_grad, axis, pairs)]
    ppermute x0 -> x4, starting transfers between devices: none -> 8.59 us  [local(): moved = lax.ppermute(prefix_grad.astype(bf16), axis, pairs)]
    ppermute x5 -> x1, waiting for transfers between devices: 5.03 us -> 1.21 us  [local(): moved = lax.ppermute(prefix_grad, axis, pairs)]
    pallas_call x8 -> x10, Pallas kernels: 45.3 us -> 41.7 us  [call_kernel(): pl.pallas_call(kernel, name=name, out_shape=[space(shape, dtype) for spac...]
    unnamed x10 -> x2, local copies, waits for them, and re-layouts: 2.14 us -> 0.01 us
    ppermute x7, waiting for transfers between devices: 1.29 us -> 0.02 us  [swapped(): return lax.ppermute(array_in, 'pipe', [(0, 1), (1, 0)])]
  transfers between devices with their start and end apart: 12 -> 12, of which waited for: 5 -> 4; matrix products, arithmetic and copies ran while one was open for 0% -> 0% of each run, Pallas kernels for 28% -> 37%
where the time goes in v4:
time: 55.7 us; the launch traced here: 55.4 us
  Pallas kernels  41.7 us (75%)
  starting transfers between devices  10.8 us (19%)
  waiting for transfers between devices  1.87 us (3%)
  between operations  0.98 us (2%)
    pallas_call x10, Pallas kernels, call_kernel(): pl.pallas_call(kernel, name=name, out_shape=[space(shape, dtype) for spac...  41.7 us
    ppermute x4, starting transfers between devices, local(): moved = lax.ppermute(prefix_grad.astype(bf16), axis, pairs)  8.59 us
    ppermute x7, starting transfers between devices, swapped(): return lax.ppermute(array_in, 'pipe', [(0, 1), (1, 0)])  2.1 us
    ppermute x1, waiting for transfers between devices, local(): moved = lax.ppermute(prefix_grad, axis, pairs)  1.21 us
  transfers between devices with their start and end apart: 12, of which 4 were waited for; matrix products, arithmetic and copies ran while one was open for 0% of the time, Pallas kernels for 37%

profile of v4, /device:TPU:0, one launch (start us, length us, event | category | flops | bytes accessed | tf_op | source)
XLA Modules:
  0.0 55.4 jit_solution(10913799967148174041)
XLA Ops:
  0.6 0.5 collective-permute-start.1
  1.2 0.9 %small_parameters.1.own_small = f32[1,6656]{1,0:T(1,128)S(1)} custom-call(f32[1,512]{1,0:T(1,128)} %gain_one.1, f32[1,512]{1,0:T(1,128)} %shift_one.1, f32[1,512]{1,0:T(1,128)} %gain_two.1, f32[1,512]{1,0:T(1,128)} %shift_two.1, f32[1,512]{1,0:T(1,128)} %attn_b.1, f32[1,512]{1,0:T(1,128)} %out_b.1, f32[1,1536]{1,0:T(1,128)} %qkv_b.1, f32[1,2048]{1,0:T(1,128)} %in_b.1), custom_call_target="tpu_custom_call" | custom-call | flops 6656 | bytes 8388608 | tf_op jit(solution)/shard_map/small_parameters/pallas_call | solution.py:54
  2.0 0.1 collective-permute-start
  2.2 0.5 collective-permute-start.3
  2.7 0.4 collective-permute-start.4
  3.1 3.3 %opening.1 = (bf16[512,512]{1,0:T(8,128)(2,1)S(1)}, f32[512,512]{1,0:T(8,128)S(1)}, f32[1152,128]{1,0:T(8,128)S(1)}, bf16[4,16,512]{2,1,0:T(8,128)(2,1)S(1)}, f3...) custom-call(bf16[2,1,512,512]{3,2,1,0:T(8,128)(2,1)} %x_hbm.1, s32[2,1,512]{2,1,0:T(1,128)} %seg_hbm.1, ...), custom_call_target="tpu_custom_call" | custom-call | flops 251658240 | bytes 8388608 | tf_op jit(solution)/shard_map/opening/pallas_call | solution.py:54
  6.5 4.0 %first_attention.1 = (bf16[512,512]{1,0:T(8,128)(2,1)S(1)}, bf16[512,512]{1,0:T(8,128)(2,1)S(1)}, bf16[512,512]{1,0:T(8,128)(2,1)S(1)}, bf16[4,1152,256]{2,1,0:T...) custom-call(f32[1,6656]{1,0:T(1,128)S(1)} %small_parameters.1.own_sm, ...), custom_call_target="tpu_custom_call" | custom-call | flops 80530636800 | bytes 8388608 | tf_op jit(solution)/shard_map/first_attention/pallas_call | solution.py:54
  10.5 2.7 %first_feed.1 = (bf16[512,2048]{1,0:T(8,128)(2,1)S(1)}, bf16[512,2048]{1,0:T(8,128)(2,1)S(1)}, bf16[2,512,2048]{2,1,0:T(8,128)(2,1)S(1)}) custom-call(bf16[512,512]{1,0:T(8,128)(2,1)S(1)} %get-tuple-element.110.two, f32[2,1,6656]{2,1,0:T(1,128)S(1)} %get-tuple-element.108.small, ...), custom_call_target="tpu_custom_call", output_to_operand_aliasing={{2}: (3, {})} | custom-call | flops 1073741824 | bytes 8388608 | tf_op jit(solution)/shard_map/first_feed/pallas_call | solution.py:54
  13.2 18.5 %middle.1 = (bf16[512,512]{1,0:T(8,128)(2,1)S(1)}, bf16[512,2048]{1,0:T(8,128)(2,1)S(1)}, bf16[512,512]{1,0:T(8,128)(2,1)S(1)}, f32[512,512]{1,0:T(8,128)S(1)}, ...) custom-call(bf16[2,512,512]{2,1,0:T(8,128)(2,1)S(1)} %get-tuple-elem, ...), custom_call_target="tpu_custom_call", output_to_operand_aliasing={{7}: (0, {}), {8}: (1, {})} | custom-call | flops 16106127360 | bytes 8388608 | tf_op jit(solution)/shard_map/middle/pallas_call | solution.py:54
  31.7 0.1 collective-permute-start.5
  31.8 1.2 %collective-permute-done.5 = f32[40,512]{1,0:T(8,128)S(1)} collective-permute-done((f32[40,512]{1,0:T(8,128)S(1)}, f32[40,512]{1,0:T(8,128)S(1)}, u32[]{:S(2)}, u32[]{:S(2)}) %collective-permute-start.5) | collective-permute-done | bytes 81952 | tf_op jit(solution)/shard_map/ppermute | solution.py:826
  33.1 2.7 %collective-permute-start.6 = (bf16[40,512]{1,0:T(8,128)(2,1)S(1)}, bf16[40,512]{1,0:T(8,128)(2,1)S(1)}, u32[]{:S(2)}, u32[]{:S(2)}) collective-permute-start(bf16[40,512]{1,0:T(8,128)(2,1)S(1)} %get-tuple-element.183), channel_id=1, source_target_pairs={{0,1},{1,0},{2,3},{3,2},{4,5},{5,4},{6,7},{7,6},{8,9},{9,8},{10,11... | collective-permute-start | bytes 122888 | tf_op jit(solution)/shard_map/ppermute | solution.py:829
  35.8 2.0 %layer_one_out.1 = (bf16[1,2,1,512,512]{4,3,2,1,0:T(8,128)(2,1)}, bf16[512,512]{1,0:T(8,128)(2,1)S(1)}) custom-call(bf16[512,512]{1,0:T(8,128)(2,1)S(1)} %get-tuple-element.124.h_one, bf16[512,2048]{1,0:T(8,128)(2,1)S(1)} %get-tuple-element.125.act, bf16[512,512]{1,0:T(8,128)(2,1)S(1)} %get-tuple-element.126.mixed, ...), custom_call_target="tpu_custom_call" | custom-call | flops 1342177280 | bytes 8388608 | tf_op jit(solution)/shard_map/layer_one_out/pallas_call | solution.py:54
  37.8 0.1 collective-permute-done.6
  37.8 0.4 collective-permute-start.8
  38.3 1.6 %collective-permute-start.7 = (bf16[40,512]{1,0:T(8,128)(2,1)S(1)}, bf16[40,512]{1,0:T(8,128)(2,1)S(1)}, u32[]{:S(2)}, u32[]{:S(2)}) collective-permute-start(bf16[40,512]{1,0:T(8,128)(2,1)S(1)} %get-tuple-element.181), channel_id=1, source_target_pairs={{0,2},{1,3},{2,0},{3,1},{4,6},{5,7},{6,4},{7,5},{8,10},{9,11},{10,... | collective-permute-start | bytes 122888 | tf_op jit(solution)/shard_map/ppermute | solution.py:829
  39.9 2.4 %layer_zero_feed_back.1.two = f32[512,512]{1,0:T(8,128)S(1)} custom-call(bf16[512,512]{1,0:T(8,128)(2,1)S(1)} %get-tuple-element.137.grad, bf16[512,2048]{1,0:T(8,128)(2,1)S(1)} %get-tuple-element.138.slope, bf16[2,512,2048]{2,1,0:T(8,128)(2,1)S(1)} %get-tuple-element.113.w_in, bf16[2,2048,512]{2,1,0:T(8,128)(2,1)S(1)} %get-tuple-element.128.w_out), custom_call_target="tpu_custom_call" | custom-call | flops 2147483648 | bytes 8388608 | tf_op jit(solution)/shard_map/layer_zero_feed_back/pallas_call | solution.py:54
  42.2 0.1 collective-permute-done.7
  42.4 1.6 %collective-permute-start.9 = (bf16[40,512]{1,0:T(8,128)(2,1)S(1)}, bf16[40,512]{1,0:T(8,128)(2,1)S(1)}, u32[]{:S(2)}, u32[]{:S(2)}) collective-permute-start(bf16[40,512]{1,0:T(8,128)(2,1)S(1)} %get-tuple-element.179), channel_id=1, source_target_pairs={{0,4},{4,0},{8,12},{12,8},{1,5},{5,1},{9,13},{13,9},{2,6},{6,2},{1... | collective-permute-start | bytes 122888 | tf_op jit(solution)/shard_map/ppermute | solution.py:829
  44.0 2.7 %layer_zero_norms.1 = (f32[1,2,1,512,512]{4,3,2,1,0:T(8,128)}, f32[512,512]{1,0:T(8,128)S(1)}) custom-call(bf16[512,512]{1,0:T(8,128)(2,1)S(1)} %get-tuple-element.117.x_ref, bf16[512,512]{1,0:T(8,128)(2,1)S(1)} %get-tuple-element.137.grad, f32[512,512]{1,0:T(8,128)S(1)} %layer_zero_feed_back.1.two, bf16[1536,512]{1,0:T(8,128)(2,1)S(1)} %get-tuple-element.145.packed, ...), custom_call_target="tpu_custom_call" | custom-call | flops 805306368 | bytes 8388608 | tf_op jit(solution)/shard_map/layer_zero_norms/pallas_call | solution.py:54
  46.9 2.7 %collective-permute-start.10 = (bf16[40,512]{1,0:T(8,128)(2,1)S(1)}, bf16[40,512]{1,0:T(8,128)(2,1)S(1)}, u32[]{:S(2)}, u32[]{:S(2)}) collective-permute-start(bf16[40,512]{1,0:T(8,128)(2,1)S(1)} %get-tuple-element.177), channel_id=1, source_target_pairs={{0,8},{4,12},{8,0},{12,4},{1,9},{5,13},{9,1},{13,5},{2,10},{6,14},... | collective-permute-start | bytes 122888 | tf_op jit(solution)/shard_map/ppermute | solution.py:829
  49.5 2.7 %turned_matrices.1 = (bf16[2048,512]{1,0:T(8,128)(2,1)S(1)}, bf16[512,512]{1,0:T(8,128)(2,1)S(1)}, bf16[512,512]{1,0:T(8,128)(2,1)S(1)}) custom-call(f32[512,2048]{1,0:T(8,128)} %out_hbm.2, f32[512,512]{1,0:T(8,128)} %up_hbm.3), custom_call_target="tpu_custom_call" | custom-call | flops 134217728 | bytes 8388608 | tf_op jit(solution)/shard_map/turned_matrices/pallas_call | solution.py:54
  52.3 0.4 collective-permute-done.10
  52.8 2.5 %reparam.1 = (f32[10,512]{1,0:T(8,128)}, f32[512,512]{1,0:T(8,128)}, f32[1,512]{1,0:T(1,128)}, f32[512,256]{1,0:T(8,128)}, f32[1,256]{1,0:T(1,128)}, /*index=5*/...) custom-call(f32[40,512]{1,0:T(8,128)S(1)} %convert_add_fusion.refs_0_, ...), custom_call_target="tpu_custom_call", output_to_operand_aliasing={{5}: (8, {}), {6}: (9, {})} | custom-call | flops 134217728 | bytes 8388608 | tf_op jit(solution)/shard_map/reparam/pallas_call | solution.py:54
  (17 shorter events, 0.2 us)
Async XLA Ops:
  0.6 5.9 %collective-permute-start.1 = (bf16[1,512,1536]{2,1,0:T(8,128)(2,1)}, bf16[1,512,1536]{2,1,0:T(8,128)(2,1)S(1)}, u32[]{:S(2)}, u32[]{:S(2)}) collective-permute-start(bf16[1,512,1536]{2,1,0:T(8,128)(2,1)} %qkv_hbm.1), channel_id=1, source_target_pairs={{0,16},{16,0},{1,17},{17,1},{2,18},{18,2},{3,19},{19,3},{4,20},{20... | collective-permute-start | bytes 4718600 | tf_op jit(solution)/shard_map/ppermute | solution.py:746
  2.0 4.4 %collective-permute-start = (f32[1,6656]{1,0:T(1,128)S(1)}, f32[1,6656]{1,0:T(1,128)S(1)}, u32[]{:S(2)}, u32[]{:S(2)}) collective-permute-start(f32[1,6656]{1,0:T(1,128)S(1)} %small_parameters.1.own_small), channel_id=1, source_target_pairs={{0,16},{16,0},{1,17},{17,1},{2,18},{18,2},{3,19},{19,3},{4,20},{20... | collective-permute-start | bytes 79880 | tf_op jit(solution)/shard_map/ppermute | solution.py:746
  2.2 11.0 %collective-permute-start.3 = (bf16[1,512,512]{2,1,0:T(8,128)(2,1)}, bf16[1,512,512]{2,1,0:T(8,128)(2,1)S(1)}, u32[]{:S(2)}, u32[]{:S(2)}) collective-permute-start(bf16[1,512,512]{2,1,0:T(8,128)(2,1)} %attn_hbm.1), channel_id=1, source_target_pairs={{0,16},{16,0},{1,17},{17,1},{2,18},{18,2},{3,19},{19,3},{4,20},{20... | collective-permute-start | bytes 1572872 | tf_op jit(solution)/shard_map/ppermute | solution.py:746
  2.6 7.9 %collective-permute-start.2 = (bf16[1,512,2048]{2,1,0:T(8,128)(2,1)}, bf16[1,512,2048]{2,1,0:T(8,128)(2,1)S(1)}, u32[]{:S(2)}, u32[]{:S(2)}) collective-permute-start(bf16[1,512,2048]{2,1,0:T(8,128)(2,1)} %ff_in_hbm.1), channel_id=1, source_target_pairs={{0,16},{16,0},{1,17},{17,1},{2,18},{18,2},{3,19},{19,3},{4,20},{20... | collective-permute-start | bytes 6291464 | tf_op jit(solution)/shard_map/ppermute | solution.py:746
  2.7 10.5 %collective-permute-start.4 = (bf16[1,2048,512]{2,1,0:T(8,128)(2,1)}, bf16[1,2048,512]{2,1,0:T(8,128)(2,1)S(1)}, u32[]{:S(2)}, u32[]{:S(2)}) collective-permute-start(bf16[1,2048,512]{2,1,0:T(8,128)(2,1)} %ff_out_hbm.1), channel_id=1, source_target_pairs={{0,16},{16,0},{1,17},{17,1},{2,18},{18,2},{3,19},{19,3},{4,20},{20... | collective-permute-start | bytes 6291464 | tf_op jit(solution)/shard_map/ppermute | solution.py:746
  31.7 1.3 %collective-permute-start.5 = (f32[40,512]{1,0:T(8,128)S(1)}, f32[40,512]{1,0:T(8,128)S(1)}, u32[]{:S(2)}, u32[]{:S(2)}) collective-permute-start(f32[40,512]{1,0:T(8,128)S(1)} %get-tuple-element.122), channel_id=1, source_target_pairs={{0,16},{16,0},{1,17},{17,1},{2,18},{18,2},{3,19},{19,3},{4,20},{20... | collective-permute-start | bytes 245768 | tf_op jit(solution)/shard_map/ppermute | solution.py:826
  33.1 4.8 %collective-permute-start.6 = (bf16[40,512]{1,0:T(8,128)(2,1)S(1)}, bf16[40,512]{1,0:T(8,128)(2,1)S(1)}, u32[]{:S(2)}, u32[]{:S(2)}) collective-permute-start(bf16[40,512]{1,0:T(8,128)(2,1)S(1)} %get-tuple-element.183), channel_id=1, source_target_pairs={{0,1},{1,0},{2,3},{3,2},{4,5},{5,4},{6,7},{7,6},{8,9},{9,8},{10,11... | collective-permute-start | bytes 122888 | tf_op jit(solution)/shard_map/ppermute | solution.py:829
  37.8 4.5 %collective-permute-start.8 = (bf16[512,512]{1,0:T(8,128)(2,1)S(1)}, bf16[512,512]{1,0:T(8,128)(2,1)S(1)}, u32[]{:S(2)}, u32[]{:S(2)}) collective-permute-start(bf16[512,512]{1,0:T(8,128)(2,1)S(1)} %get-tuple-element.136), channel_id=1, source_target_pairs={{0,16},{16,0},{1,17},{17,1},{2,18},{18,2},{3,19},{19,3},{4,20},{20... | collective-permute-start | bytes 1572872 | tf_op jit(solution)/shard_map/ppermute | solution.py:746
  38.3 4.1 %collective-permute-start.7 = (bf16[40,512]{1,0:T(8,128)(2,1)S(1)}, bf16[40,512]{1,0:T(8,128)(2,1)S(1)}, u32[]{:S(2)}, u32[]{:S(2)}) collective-permute-start(bf16[40,512]{1,0:T(8,128)(2,1)S(1)} %get-tuple-element.181), channel_id=1, source_target_pairs={{0,2},{1,3},{2,0},{3,1},{4,6},{5,7},{6,4},{7,5},{8,10},{9,11},{10,... | collective-permute-start | bytes 122888 | tf_op jit(solution)/shard_map/ppermute | solution.py:829
  42.4 4.4 %collective-permute-start.9 = (bf16[40,512]{1,0:T(8,128)(2,1)S(1)}, bf16[40,512]{1,0:T(8,128)(2,1)S(1)}, u32[]{:S(2)}, u32[]{:S(2)}) collective-permute-start(bf16[40,512]{1,0:T(8,128)(2,1)S(1)} %get-tuple-element.179), channel_id=1, source_target_pairs={{0,4},{4,0},{8,12},{12,8},{1,5},{5,1},{9,13},{13,9},{2,6},{6,2},{1... | collective-permute-start | bytes 122888 | tf_op jit(solution)/shard_map/ppermute | solution.py:829
  46.8 6.0 %collective-permute-start.11 = (f32[512,512]{1,0:T(8,128)S(1)}, f32[512,512]{1,0:T(8,128)S(1)}, u32[]{:S(2)}, u32[]{:S(2)}) collective-permute-start(f32[512,512]{1,0:T(8,128)S(1)} %get-tuple-element.155), channel_id=1, source_target_pairs={{0,16},{16,0},{1,17},{17,1},{2,18},{18,2},{3,19},{19,3},{4,20},{20... | collective-permute-start | bytes 3145736 | tf_op jit(solution)/shard_map/ppermute | solution.py:746
  46.9 5.9 %copy-start = (f32[10,512]{1,0:T(8,128)S(1)}, f32[10,512]{1,0:T(8,128)}, u32[]{:S(2)}) copy-start(f32[10,512]{1,0:T(8,128)} %refs_2_) | copy-start | bytes 61444
  46.9 5.8 %collective-permute-start.10 = (bf16[40,512]{1,0:T(8,128)(2,1)S(1)}, bf16[40,512]{1,0:T(8,128)(2,1)S(1)}, u32[]{:S(2)}, u32[]{:S(2)}) collective-permute-start(bf16[40,512]{1,0:T(8,128)(2,1)S(1)} %get-tuple-element.177), channel_id=1, source_target_pairs={{0,8},{4,12},{8,0},{12,4},{1,9},{5,13},{9,1},{13,5},{2,10},{6,14},... | collective-permute-start | bytes 122888 | tf_op jit(solution)/shard_map/ppermute | solution.py:829

commit v5 on v4

--- a/solution.py
+++ b/solution.py
@@ -204,18 +204,27 @@
     return slice(end - live, end), slice(block * BLK, end), slice(start, start + live)
 
 
+def pair_rows(pair):
+    return slice(pair * BLK, (pair + 1) * BLK)
+
+
+def both_heads(rows, tokens):
+    return jnp.concatenate([rows[:PAD, tokens], rows[PAD:, tokens]], axis=1)
+
+
 def attend(q_t, k_m, v_t, pre_k, pre_v, mask_ref, p_ref, pp_ref, inv_ref, mixed_ref):
-    pad_mask = jnp.where(lax.broadcasted_iota(jnp.int32, (PAD, 1), 0) < PREFIX, 0.0, NEG)
+    real = lax.rem(lax.broadcasted_iota(jnp.int32, (2 * PAD, 1), 0), PAD) < PREFIX
+    pad_mask = jnp.where(real, 0.0, NEG)
 
     def score(feats, block):
         keys, tokens, rows = geometry(block)
         queries = block_diagonal(q_t[feats, tokens])
         mask = mask_ref[rows, :]
-        scores = dot(k_m[keys, feats], queries, NN) + jnp.concatenate([mask, mask], axis=1)
-        return scores, dot(pre_k[:, feats], queries, NN) + pad_mask
+        return dot(k_m[keys, feats], queries, NN) + jnp.concatenate([mask, mask], axis=1)
 
     def soften(pair, block, scores, pre_scores):
-        _, _, rows = geometry(block)
+        _, tokens, rows = geometry(block)
+        pre_scores = both_heads(pre_scores, tokens)
         peak = jnp.maximum(
             jnp.max(scores, axis=0, keepdims=True), jnp.max(pre_scores, axis=0, keepdims=True)
         )
@@ -226,59 +235,76 @@
         expo = expo.astype(bf16)
         pre_expo = pre_expo.astype(bf16)
         p_ref[pair, rows, :] = expo
-        pp_ref[pair, block] = pre_expo
-        inv_ref[pair, block] = jnp.broadcast_to(inverse, (8, 2 * BLK))
-        return expo, pre_expo, inverse
-
-    def mix(feats, block, expo, pre_expo, inverse):
+        pp_ref[pair, :PAD, tokens] = pre_expo[:, :BLK]
+        pp_ref[pair, PAD:, tokens] = pre_expo[:, BLK:]
+        inv_ref[2 * pair : 2 * pair + 1, tokens] = inverse[:, :BLK]
+        inv_ref[2 * pair + 1 : 2 * pair + 2, tokens] = inverse[:, BLK:]
+        return expo, inverse
+
+    def mix(feats, block, pre_mixed, expo, inverse):
         keys, tokens, _ = geometry(block)
-        mixed = dot(v_t[feats, keys], expo, NN) + dot(pre_v[:, feats], pre_expo, TN)
-        mixed_ref[feats, tokens] = (from_diagonal(mixed) * per_head(inverse)).astype(bf16)
+        mixed = from_diagonal(dot(v_t[feats, keys], expo, NN)) + pre_mixed[:, tokens]
+        mixed_ref[feats, tokens] = (mixed * per_head(inverse)).astype(bf16)
 
     for pair in range(PAIRS):
-        feats = slice(pair * BLK, (pair + 1) * BLK)
+        feats = pair_rows(pair)
+        pre_scores = dot(pre_k[:, feats], q_t[feats, :], NN) + pad_mask
         scores = [score(feats, block) for block in range(BLOCKS)]
-        soft = [soften(pair, block, *scores[block]) for block in range(BLOCKS)]
+        soft = [soften(pair, block, scores[block], pre_scores) for block in range(BLOCKS)]
+        pre_mixed = dot(pre_v[:, feats], pp_ref[pair], TN)
         for block in range(BLOCKS):
-            mix(feats, block, *soft[block])
-
-
-def attend_back(grad_t, q_t, k_t, v_m, pre_k, pre_v, p_ref, pp_ref, inv_ref, mixed_ref,
-                dq_ref, dk_ref, dv_ref, pre_grad, pre_row):
-    def value_grads(pair, feats, block):
+            mix(feats, block, pre_mixed, *soft[block])
+
+
+def prefix_back(grad_t, q_t, pre_v, pp_ref, inv_ref, mixed_ref, scaled_ref, inner_ref, pre_ds_ref, pre_grad, pre_row):
+    first_half = lax.broadcasted_iota(jnp.int32, (1, BLK), 1) < HD
+
+    def own_head(both):
+        return jnp.where(first_half, both[:PAD], both[PAD:])
+
+    for pair in range(PAIRS):
+        feats = pair_rows(pair)
+        inner = []
+        for head in (2 * pair, 2 * pair + 1):
+            rows = slice(head * HD, (head + 1) * HD)
+            scaled = (grad_t[rows, :] * inv_ref[head : head + 1, :]).astype(bf16)
+            scaled_ref[rows, :] = scaled
+            products = scaled.astype(f32) * mixed_ref[rows, :].astype(f32)
+            inner.append(jnp.sum(products, axis=0, keepdims=True))
+            inner_ref[head : head + 1, :] = inner[-1]
+        inner = jnp.concatenate([jnp.broadcast_to(row, (PAD, SEQ)) for row in inner], axis=0)
+        grads = scaled_ref[feats, :]
+        probs = pp_ref[pair]
+        grad_probs = dot(pre_v[:, feats], grads, NN)
+        grad_scores = (probs.astype(f32) * (grad_probs - inner)).astype(bf16)
+        pre_ds_ref[pair] = grad_scores
+        pre_grad[pre_row : pre_row + PREFIX, feats] = (
+            own_head(dot(grad_scores, q_t[feats, :], NT))[:PREFIX] * K_BACK
+        )
+        pre_grad[pre_row + PREFIX : pre_row + 2 * PREFIX, feats] = own_head(dot(probs, grads, NT))[:PREFIX]
+
+
+def attend_back(scaled_ref, inner_ref, pre_ds_ref, q_t, k_t, v_m, pre_k, p_ref, dq_ref, dk_ref, dv_ref):
+    def value_grads(feats, block):
         keys, tokens, _ = geometry(block)
-        scaled = (grad_t[feats, tokens] * per_head(inv_ref[pair, block][0:1, :])).astype(bf16)
-        products = scaled.astype(f32) * mixed_ref[feats, tokens].astype(f32)
+        grads = block_diagonal(scaled_ref[feats, tokens])
+        return grads, dot(v_m[keys, feats], grads, NN)
+
+    def score_grads(pair, block, grad_probs):
+        _, tokens, rows = geometry(block)
         inner = jnp.concatenate(
-            [
-                jnp.sum(products[:HD], axis=0, keepdims=True),
-                jnp.sum(products[HD:], axis=0, keepdims=True),
-            ],
+            [inner_ref[2 * pair : 2 * pair + 1, tokens], inner_ref[2 * pair + 1 : 2 * pair + 2, tokens]],
             axis=1,
         )
-        grads = block_diagonal(scaled)
-        return grads, inner, dot(v_m[keys, feats], grads, NN), dot(pre_v[:, feats], grads, NN)
-
-    def score_grads(pair, block, inner, grad_probs, pre_grad_probs):
-        _, _, rows = geometry(block)
-        probs = p_ref[pair, rows, :].astype(f32)
-        pre_probs = pp_ref[pair, block].astype(f32)
-        return (
-            (probs * (grad_probs - inner)).astype(bf16),
-            (pre_probs * (pre_grad_probs - inner)).astype(bf16),
-        )
-
-    def out_grads(pair, feats, block, grads, grad_scores, pre_scores):
+        return (p_ref[pair, rows, :].astype(f32) * (grad_probs - inner)).astype(bf16)
+
+    def out_grads(pair, feats, block, pre_dq, grads, grad_scores):
         keys, tokens, rows = geometry(block)
         queries = block_diagonal(q_t[feats, tokens])
-        dq = dot(k_t[feats, keys], grad_scores, NN) + dot(pre_k[:, feats], pre_scores, TN)
-        dq_ref[feats, tokens] = from_diagonal(dq)
-        return (
-            dot(queries, grad_scores, NT),
-            dot(grads, p_ref[pair, rows, :], NT),
-            dot(pre_scores, queries, NT),
-            dot(pp_ref[pair, block], grads, NT),
+        dq_ref[feats, tokens] = (
+            from_diagonal(dot(k_t[feats, keys], grad_scores, NN)) + pre_dq[:, tokens]
         )
+        return dot(queries, grad_scores, NT), dot(grads, p_ref[pair, rows, :], NT)
 
     def by_keys(outs, which, key_block):
         total = None
@@ -290,21 +316,18 @@
         return total
 
     for pair in range(PAIRS):
-        feats = slice(pair * BLK, (pair + 1) * BLK)
-        first = [value_grads(pair, feats, block) for block in range(BLOCKS)]
-        second = [score_grads(pair, block, *first[block][1:]) for block in range(BLOCKS)]
+        feats = pair_rows(pair)
+        first = [value_grads(feats, block) for block in range(BLOCKS)]
+        second = [score_grads(pair, block, first[block][1]) for block in range(BLOCKS)]
+        pre_dq = dot(pre_k[:, feats], pre_ds_ref[pair], TN)
         outs = [
-            out_grads(pair, feats, block, first[block][0], *second[block])
+            out_grads(pair, feats, block, pre_dq, first[block][0], second[block])
             for block in range(BLOCKS)
         ]
         for key_block in range(BLOCKS):
             keys = slice(key_block * BLK, (key_block + 1) * BLK)
             dk_ref[feats, keys] = by_keys(outs, 0, key_block)
             dv_ref[feats, keys] = by_keys(outs, 1, key_block)
-        pre_dk = outs[0][2] + outs[1][2] + outs[2][2] + outs[3][2]
-        pre_dv = outs[0][3] + outs[1][3] + outs[2][3] + outs[3][3]
-        pre_grad[pre_row : pre_row + PAD, feats] = pre_dk * K_BACK
-        pre_grad[pre_row + PAD : pre_row + 2 * PAD, feats] = pre_dv
 
 
 def pack_grads(dq_ref, dk_ref, dv_ref, cos, sin, packed_t):
@@ -409,30 +432,38 @@
     return packed
 
 
-def prefix_states(embed, up_w, up_b, out_w, out_b, arrivals, hidden, low):
+def prefix_states(embed, up_w, up_b, out_w, out_b, arrivals, hidden, low, wide, up_high, up_rest):
     units = jnp.tanh(few_rows_dot(embed[...], up_w[...])[:PREFIX] + up_b[...])
     hidden[...] = units
+    up_high[...], up_rest[...] = halves(jnp.transpose(up_w[...]))
     real = lax.broadcasted_iota(jnp.int32, (PAD, 1), 0) < PREFIX
+    first_head = lax.rem(lax.broadcasted_iota(jnp.int32, (1, D), 1), BLK) < HD
     for part in range(4):
         cols = slice(part * D, (part + 1) * D)
         arrivals[part].wait()
-        states = few_rows_dot(units, out_w[:, cols]) + out_b[:, cols]
-        low[part] = jnp.where(real, states, 0.0).astype(bf16)
+        states = jnp.where(real, few_rows_dot(units, out_w[:, cols]) + out_b[:, cols], 0.0)
+        low[part, :PAD, :] = jnp.where(first_head, states, 0.0).astype(bf16)
+        low[part, PAD:, :] = jnp.where(first_head, 0.0, states).astype(bf16)
+        wide[cols, :] = jnp.transpose(out_w[:, cols].astype(bf16))
 
 
 OPENING_SHAPES = (
     ((SEQ, D), bf16),
     ((SEQ, D), f32),
     ((P_ROWS, BLK), f32),
-    ((4, PAD, D), bf16),
+    ((4, 2 * PAD, D), bf16),
     ((PREFIX, D), f32),
+    ((4 * D, D), bf16),
+    ((D, D), bf16),
+    ((D, D), bf16),
     ((2 * 8, SEQ), f32),
     ((D, 3 * D), bf16),
 )
 
 
 def opening_kernel(x_hbm, seg_hbm, embed_hbm, up_hbm, up_b_hbm, out_hbm, out_b_hbm, tables_hbm, qkv_hbm,
-                   x_ref, hat, mask, low, hidden, tables, own_qkv, seg, embed, up_w, up_b, out_w, out_b, sems):
+                   x_ref, hat, mask, low, hidden, wide, up_high, up_rest, tables, own_qkv, seg, embed, up_w, up_b,
+                   out_w, out_b, sems):
     section = lax.axis_index("pipe")
     copies = Copies(sems)
     x_copy = copies.start(x_hbm.at[section, 0], x_ref)
@@ -451,7 +482,7 @@
     x_copy.wait()
     hat[...], _ = normalized(x_ref[...].astype(f32))
     wait_all(*prefix_copies)
-    prefix_states(embed, up_w, up_b, out_w, out_b, parts, hidden, low)
+    prefix_states(embed, up_w, up_b, out_w, out_b, parts, hidden, low, wide, up_high, up_rest)
     wait_all(*late)
 
 
@@ -475,8 +506,8 @@
     ((D, SEQ), bf16),
     ((SEQ, D), bf16),
     ((PAIRS, P_ROWS, 2 * BLK), bf16),
-    ((PAIRS, BLOCKS, PAD, 2 * BLK), bf16),
-    ((PAIRS, BLOCKS, 8, 2 * BLK), f32),
+    ((PAIRS, 2 * PAD, SEQ), bf16),
+    ((HEADS, SEQ), f32),
     ((D, SEQ), bf16),
 )
 FIRST_SHAPES = HEAD_SHAPES + (
@@ -547,18 +578,21 @@
     ((D, SEQ), bf16),
     ((SEQ, D), f32),
     ((SEQ, D), bf16),
-    ((3 * D, SEQ), bf16),
+    ((D, SEQ), bf16),
+    ((HEADS, SEQ), f32),
+    ((PAIRS, 2 * PAD, SEQ), bf16),
     ((4 * PREFIX, D), f32),
     ((2, D, D), bf16),
     ((2, FF, D), bf16),
 )
 
 
-def middle_kernel(w_attn_before, w_out_before, q0, k0, v0, p0, pp0, inv0, mixed0, small, w_qkv, w_in,
+def middle_kernel(w_attn_before, w_out_before, q0, pp0, inv0, mixed0, small, w_qkv, w_in,
                   other_attn, other_out, cot_ref, x_ref, act_zero, low, mask, tables,
-                  h_one, act_one, mixed_one, grad_one, grad_low, packed_zero, prefix_grad, w_attn, w_out,
-                  q_t, k_t, v_m, p_ref, pp_ref, inv_ref, slope_one, k_m, v_t, dq, dk, dv, packed, pre_grad,
-                  sems):
+                  h_one, act_one, mixed_one, grad_one, grad_low, scaled_zero, inner_zero, pre_ds_zero,
+                  prefix_grad, w_attn, w_out,
+                  q_t, k_t, v_m, p_ref, pp_ref, inv_ref, scaled, inner, pre_ds, slope_one, k_m, v_t,
+                  dq, dk, dv, packed, sems):
     section = lax.axis_index("pipe")
     copies = Copies(sems)
     wait_all(
@@ -581,25 +615,22 @@
     grad = cot_ref[...]
     grad_two = feed_back(grad, w_out.at[1], w_in.at[1], slope_one, NO_COPIES)
     dq[...] = dot(w_attn[1], grad, NT)
-    attend_back(dq, q_t, k_t, v_m, low.at[2], low.at[3], p_ref, pp_ref, inv_ref, mixed_one,
-                dq, dk, dv, pre_grad, 2 * PAD)
+    prefix_back(dq, q_t, low.at[3], pp_ref, inv_ref, mixed_one, scaled, inner, pre_ds, prefix_grad, 2 * PREFIX)
+    attend_back(scaled, inner, pre_ds, q_t, k_t, v_m, low.at[2], p_ref, dq, dk, dv)
     pack_grads(dq, dk, dv, cos, sin, packed)
     result = norms_back(grad, h_one[...].astype(f32), grad_two, packed[...], w_qkv[1], small_one)
     grad_one[...] = result
     grad_low[...] = result.astype(bf16)
 
     dq[...] = dot(w_attn[0], grad_low[...], NT)
-    attend_back(dq, q0, k0, v0, low.at[0], low.at[1], p0, pp0, inv0, mixed0,
-                dq, dk, dv, pre_grad, 0)
-    for part in range(4):
-        prefix_grad[part * PREFIX : (part + 1) * PREFIX, :] = pre_grad[
-            part * PAD : part * PAD + PREFIX, :
-        ]
-    pack_grads(dq, dk, dv, cos, sin, packed_zero)
+    prefix_back(dq, q0, low.at[1], pp0, inv0, mixed0, scaled_zero, inner_zero, pre_ds_zero, prefix_grad, 0)
 
 
 def middle_call(*arrays):
     scratch = HEAD_SHAPES[:6] + (
+        ((D, SEQ), bf16),
+        ((HEADS, SEQ), f32),
+        ((PAIRS, 2 * PAD, SEQ), bf16),
         ((SEQ, FF), bf16),
         ((SEQ, D), bf16),
         ((D, SEQ), bf16),
@@ -607,35 +638,46 @@
         ((D, SEQ), f32),
         ((D, SEQ), f32),
         ((3 * D, SEQ), bf16),
-        ((4 * PAD, D), f32),
     )
     return call_kernel(
         middle_kernel, "middle", in_vmem(*arrays), vmem(MIDDLE_OUTS), scratch, 2, MIDDLE_MIB,
-        20 * SEQ * D * 6 * D, {0: 7, 1: 8},
-    )
-
-
-def hand_over(section, values, send_ref, whole, sems):
+        20 * SEQ * D * 6 * D, {0: 9, 1: 10},
+    )
+
+
+def hand_over(values, keep, send, sems):
+    here = lax.axis_index("pipe") == 0
     copies = Copies(sems)
     wait_all(
-        copies.of_layer(section == 0, values[0], values[1], whole.at[0, section, 0]),
-        copies.of_layer(section == 0, values[1], values[0], send_ref),
-    )
-
-
-def result_kernel(h_one, act, mixed, small, w_attn, w_out, whole, send_ref, result, sems):
+        copies.of_layer(here, values[0], values[1], keep),
+        copies.of_layer(here, values[1], values[0], send),
+    )
+
+
+def result_kernel(h_one, act, mixed, small, w_attn, w_out, keep, send, result, sems):
     result[...] = layer_result(
         h_one[...].astype(f32), mixed[...], w_attn[1], act, w_out[1], small.at[1]
     ).astype(bf16)
-    hand_over(lax.axis_index("pipe"), (h_one, result), send_ref, whole, sems)
+    hand_over((h_one, result), keep, send, sems)
 
 
 def result_call(*arrays):
     return call_kernel(
-        result_kernel, "layer_one_out", in_vmem(*arrays),
-        [(pltpu.HBM, (1, 2, 1, SEQ, D), bf16), (pltpu.VMEM, (SEQ, D), bf16)],
+        result_kernel, "layer_one_out", in_vmem(*arrays), vmem([((SEQ, D), bf16)] * 2),
         [((SEQ, D), bf16)], 2, LATE_MIB, 2 * SEQ * D * (D + FF),
     )
+
+
+def heads_back_kernel(scaled, inner, pre_ds, q_t, k_t, v_m, low, p_ref, tables, packed, dq, dk, dv):
+    attend_back(scaled, inner, pre_ds, q_t, k_t, v_m, low.at[0], p_ref, dq, dk, dv)
+    pack_grads(dq, dk, dv, tables[:8, :], tables[8:, :], packed)
+
+
+def heads_back_call(*arrays):
+    return call_kernel(
+        heads_back_kernel, "layer_zero_attention_back", in_vmem(*arrays), vmem([((3 * D, SEQ), bf16)]),
+        [((D, SEQ), f32)] * 3, 0, LATE_MIB, 10 * SEQ * SEQ * D,
+    )[0]
 
 
 def feed_back_kernel(grad, slope, w_in, w_out, total):
@@ -650,41 +692,32 @@
     return total
 
 
-def norms_kernel(x_ref, grad, two, packed, grad_one, small, w_qkv, whole, send_ref, result, sems):
+def norms_kernel(x_ref, grad, two, packed, grad_one, small, w_qkv, keep, send, result, sems):
     result[...] = norms_back(
         grad[...], x_ref[...].astype(f32), two[...], packed[...], w_qkv[0], small.at[0]
     )
-    hand_over(lax.axis_index("pipe"), (result, grad_one), send_ref, whole, sems)
+    hand_over((result, grad_one), keep, send, sems)
 
 
 def norms_call(*arrays):
     return call_kernel(
-        norms_kernel, "layer_zero_norms", in_vmem(*arrays),
-        [(pltpu.HBM, (1, 2, 1, SEQ, D), f32), (pltpu.VMEM, (SEQ, D), f32)],
+        norms_kernel, "layer_zero_norms", in_vmem(*arrays), vmem([((SEQ, D), f32)] * 2),
         [((SEQ, D), f32)], 2, LATE_MIB, 6 * SEQ * D * D,
     )
 
 
-def turn_kernel(out_hbm, up_hbm, wide, up_high, up_rest, out_w, up_w, sems):
+def place_kernel(act, grad, act_out, grad_out, sems):
+    section = lax.axis_index("pipe")
     copies = Copies(sems)
-    up = copies.start(up_hbm, up_w)
-    parts = [
-        copies.start(out_hbm.at[:, i * D : (i + 1) * D], out_w.at[:, i * D : (i + 1) * D])
-        for i in range(4)
-    ]
-    up.wait()
-    up_high[...], up_rest[...] = halves(jnp.transpose(up_w[...]))
-    for part in range(4):
-        cols = slice(part * D, (part + 1) * D)
-        parts[part].wait()
-        wide[cols, :] = jnp.transpose(out_w[:, cols].astype(bf16))
-
-
-def turn_call(*arrays):
+    wait_all(
+        copies.start(grad, grad_out.at[0, section, 0]), copies.start(act, act_out.at[0, section, 0])
+    )
+
+
+def place_call(act, grad):
+    wholes = [(pltpu.HBM, (1, 2, 1, SEQ, D), bf16), (pltpu.HBM, (1, 2, 1, SEQ, D), f32)]
     return call_kernel(
-        turn_kernel, "turned_matrices", in_hbm(*arrays),
-        vmem([((4 * D, D), bf16), ((D, D), bf16), ((D, D), bf16)]),
-        [((D, 4 * D), f32), ((D, D), f32)], 5, LATE_MIB, SEQ * D * D,
+        place_kernel, "place_own", in_vmem(act, grad), wholes, [], 2, LATE_MIB, 2 * SEQ * D
     )
 
 
@@ -695,8 +728,8 @@
     shard = lax.axis_index("dp")
     copies = Copies(sems)
     placed = [
+        copies.start(grad_other, grad_out.at[0, 1 - section, 0]),
         copies.start(act_other, act_out.at[0, 1 - section, 0]),
-        copies.start(grad_other, grad_out.at[0, 1 - section, 0]),
     ]
     units = hidden[...]
     both = jnp.zeros((2 * PAD, D), f32)
@@ -709,12 +742,7 @@
     grad_pre = grad_units * (1.0 - units * units)
     d_up_b[...] = jnp.sum(grad_pre, axis=0, keepdims=True)
     d_up[...] = stacked_dot(embed[...], grad_pre)
-    placed += [copies.start(d_up_b, results[2]), copies.start(d_up, results[1])]
-    high, rest = halves(padded(grad_pre))
-    both = dot(jnp.concatenate([high, rest], axis=0), up_high[...], NN)
-    both = both[:PAD] + both[PAD:] + dot(high, up_rest[...], NN)
-    d_embed[...] = both[:PREFIX]
-    placed.append(copies.start(d_embed, results[0]))
+    placed += [copies.start(d_up, results[1]), copies.start(d_up_b, results[2])]
     column = section * (2 * D) + shard * col_width
     own_cols = jnp.zeros((PREFIX, col_width), f32)
     for part in range(4):
@@ -726,6 +754,11 @@
     d_out[...] = stacked_dot(units, own_cols)
     d_out_b[...] = jnp.sum(own_cols, axis=0, keepdims=True)
     placed += [copies.start(d_out, results[3]), copies.start(d_out_b, results[4])]
+    high, rest = halves(padded(grad_pre))
+    both = dot(jnp.concatenate([high, rest], axis=0), up_high[...], NN)
+    both = both[:PAD] + both[PAD:] + dot(high, up_rest[...], NN)
+    d_embed[...] = both[:PREFIX]
+    placed.append(copies.start(d_embed, results[0]))
     wait_all(*placed)
 
 
@@ -788,56 +821,59 @@
     tables = jnp.asarray(rope_tables())
     _, *later = lax.optimization_barrier((small, attn_weight, ff_in_weight, ff_out_weight))
     other_attn, other_in, other_out = (swapped(weight) for weight in later)
-    x_zero, hat_zero, mask, low, hidden_units, tables, own_qkv = opening_call(
+    x_zero, hat_zero, mask, low, hidden_units, wide, up_high, up_rest, tables, own_qkv = opening_call(
         block_input, segments, prefix_embed, up_weight, up_bias, out_weight, out_bias, tables, qkv_weight
     )
-    *heads, two_zero, small, w_qkv, w_attn, w_in, w_out, cot = first_call(
+    q0, k0, v0, p0, pp0, inv0, mixed0, two_zero, small, w_qkv, w_attn, w_in, w_out, cot = first_call(
         (small, other_small, own_qkv, other_qkv, hat_zero, mask, low, tables),
         attn_weight, ff_in_weight, ff_out_weight, cotangent,
     )
     act_zero, slope_zero, w_in = feed_call(two_zero, small, other_in, w_in)
-    h_one, act_one, mixed_one, grad_one, grad_low, packed_zero, prefix_grad, w_attn, w_out = middle_call(
-        w_attn, w_out, *heads, small, w_qkv, w_in, other_attn, other_out, cot, x_zero, act_zero, low, mask,
-        tables,
+    (h_one, act_one, mixed_one, grad_one, grad_low, scaled_zero, inner_zero, pre_ds_zero, prefix_grad,
+     w_attn, w_out) = middle_call(
+        w_attn, w_out, q0, pp0, inv0, mixed0, small, w_qkv, w_in, other_attn, other_out, cot, x_zero,
+        act_zero, low, mask, tables,
     )
 
     def layer_one_out(state):
-        keep, send = result_call(state["h_one"], act_one, mixed_one, small, w_attn, w_out)
-        return dict(state, act=keep, act_send=send)
+        own, send = result_call(state["h_one"], act_one, mixed_one, small, w_attn, w_out)
+        return dict(state, act_own=own, act_send=send)
+
+    def layer_zero_attention(state):
+        packed = heads_back_call(
+            state["scaled"], inner_zero, pre_ds_zero, q0, k0, v0, low, p0, tables
+        )
+        return dict(state, packed=packed, act_other=swapped(state["act_send"]))
 
     def layer_zero_feed(state):
-        two = feed_back_call(state["grad_low"], slope_zero, w_in, w_out)
-        return dict(state, grad_two=two, act_other=swapped(state["act_send"]))
+        return dict(state, two=feed_back_call(state["grad_low"], slope_zero, w_in, w_out))
 
     def layer_zero_norms(state):
-        keep, send = norms_call(
-            x_zero, grad_low, state["grad_two"], packed_zero, grad_one, small, w_qkv
-        )
-        return dict(state, grad=keep, grad_send=send)
+        own, send = norms_call(x_zero, grad_low, state["two"], state["packed"], grad_one, small, w_qkv)
+        return dict(state, grad_own=own, grad_send=send)
 
     def swap_grads(state):
-        turned = turn_call(state["out_weight"], up_weight)
-        return dict(state, grad_other=swapped(state["grad_send"]), turned=turned)
-
-    works = [None, layer_one_out, layer_zero_feed, layer_zero_norms, swap_grads]
-    state = {"h_one": h_one, "grad_low": grad_low, "out_weight": out_weight}
+        wholes = place_call(state["act_own"], state["grad_own"])
+        return dict(state, grad_other=swapped(state["grad_send"]), wholes=wholes)
+
+    works = [layer_one_out, layer_zero_attention, layer_zero_feed, layer_zero_norms, swap_grads]
+    state = {"h_one": h_one, "grad_low": grad_low, "scaled": scaled_zero}
     for axis, pairs in hops("pipe") + hops("dp") + hops("grp"):
         if axis == "pipe":
             moved = lax.ppermute(prefix_grad, axis, pairs)
         else:
             prefix_grad = lax.reduce_precision(prefix_grad, 8, 7)
             moved = lax.ppermute(prefix_grad.astype(bf16), axis, pairs)
-        work = works.pop(0) if works else None
-        if work:
-            state = work(state)
+        if works:
+            state = works.pop(0)(state)
         prefix_grad, moved, state = lax.optimization_barrier((prefix_grad, moved, state))
         prefix_grad = prefix_grad + moved.astype(f32)
     for work in works:
         state = work(state)
     col_width = 2 * D // lax.axis_size("dp")
     grad_embed, grad_up, grad_up_b, grad_out, grad_out_b, activations, input_grads = final_call(
-        col_width, (state["act"], state["grad"]), prefix_grad, hidden_units, prefix_embed,
-        *state["turned"], state["act_other"], state["grad_other"],
+        col_width, state["wholes"], prefix_grad, hidden_units, prefix_embed, wide, up_high, up_rest,
+        state["act_other"], state["grad_other"],
     )
     return (
         activations,

time: 55.7 us -> 53.1 us (0.953)
  Pallas kernels: 41.7 us -> 39.3 us
    pallas_call x10 -> x11, Pallas kernels: 41.7 us -> 39.3 us  [call_kernel(): pl.pallas_call(kernel, name=name, out_shape=[space(shape, dtype) for spac...]
    ppermute x1, waiting for transfers between devices: 1.21 us -> 0.01 us  [local(): moved = lax.ppermute(prefix_grad, axis, pairs)]
    ppermute x4, waiting for transfers between devices: 0.65 us -> 1.79 us  [local(): moved = lax.ppermute(prefix_grad.astype(bf16), axis, pairs)]
  transfers between devices with their start and end apart: 12 -> 12, of which waited for: 4 -> 3; matrix products, arithmetic and copies ran while one was open for 0% -> 0% of each run, Pallas kernels for 37% -> 39%
where the time goes in v5:
time: 53.1 us; the launch traced here: 52.9 us
  Pallas kernels  39.3 us (74%)
  starting transfers between devices  10.7 us (20%)
  waiting for transfers between devices  1.82 us (3%)
  between operations  0.99 us (2%)
    pallas_call x11, Pallas kernels, call_kernel(): pl.pallas_call(kernel, name=name, out_shape=[space(shape, dtype) for spac...  39.3 us
    ppermute x4, starting transfers between devices, local(): moved = lax.ppermute(prefix_grad.astype(bf16), axis, pairs)  8.5 us
    ppermute x7, starting transfers between devices, swapped(): return lax.ppermute(array_in, 'pipe', [(0, 1), (1, 0)])  2.1 us
    ppermute x4, waiting for transfers between devices, local(): moved = lax.ppermute(prefix_grad.astype(bf16), axis, pairs)  1.79 us
  transfers between devices with their start and end apart: 12, of which 3 were waited for; matrix products, arithmetic and copies ran while one was open for 0% of the time, Pallas kernels for 39%

profile of v5, /device:TPU:0, one launch (start us, length us, event | category | flops | bytes accessed | tf_op | source)
XLA Modules:
  0.0 52.9 jit_solution(16848354937540848014)
XLA Ops:
  0.6 0.5 collective-permute-start.1
  1.2 0.9 %small_parameters.1.own_small = f32[1,6656]{1,0:T(1,128)S(1)} custom-call(f32[1,512]{1,0:T(1,128)} %gain_one.1, f32[1,512]{1,0:T(1,128)} %shift_one.1, f32[1,512]{1,0:T(1,128)} %gain_two.1, f32[1,512]{1,0:T(1,128)} %shift_two.1, f32[1,512]{1,0:T(1,128)} %attn_b.1, f32[1,512]{1,0:T(1,128)} %out_b.1, f32[1,1536]{1,0:T(1,128)} %qkv_b.1, f32[1,2048]{1,0:T(1,128)} %in_b.1), custom_call_target="tpu_custom_call" | custom-call | flops 6656 | bytes 8388608 | tf_op jit(solution)/shard_map/small_parameters/pallas_call | solution.py:54
  2.0 0.1 collective-permute-start
  2.2 0.5 collective-permute-start.3
  2.7 0.4 collective-permute-start.4
  3.1 3.3 %opening.1 = (bf16[512,512]{1,0:T(8,128)(2,1)S(1)}, f32[512,512]{1,0:T(8,128)S(1)}, f32[1152,128]{1,0:T(8,128)S(1)}, bf16[4,32,512]{2,1,0:T(8,128)(2,1)S(1)}, f3...) custom-call(bf16[2,1,512,512]{3,2,1,0:T(8,128)(2,1)} %x_hbm.1, ...), custom_call_target="tpu_custom_call" | custom-call | flops 251658240 | bytes 8388608 | tf_op jit(solution)/shard_map/opening/pallas_call | solution.py:54
  6.5 3.9 %first_attention.1 = (bf16[512,512]{1,0:T(8,128)(2,1)S(1)}, bf16[512,512]{1,0:T(8,128)(2,1)S(1)}, bf16[512,512]{1,0:T(8,128)(2,1)S(1)}, bf16[4,1152,256]{2,1,0:T...) custom-call(f32[1,6656]{1,0:T(1,128)S(1)} %small_parameters.1.own_sm, ...), custom_call_target="tpu_custom_call" | custom-call | flops 80530636800 | bytes 8388608 | tf_op jit(solution)/shard_map/first_attention/pallas_call | solution.py:54
  10.5 2.7 %first_feed.1 = (bf16[512,2048]{1,0:T(8,128)(2,1)S(1)}, bf16[512,2048]{1,0:T(8,128)(2,1)S(1)}, bf16[2,512,2048]{2,1,0:T(8,128)(2,1)S(1)}) custom-call(bf16[512,512]{1,0:T(8,128)(2,1)S(1)} %get-tuple-element.108.two, f32[2,1,6656]{2,1,0:T(1,128)S(1)} %get-tuple-element.106.small, ...), custom_call_target="tpu_custom_call", output_to_operand_aliasing={{2}: (3, {})} | custom-call | flops 1073741824 | bytes 8388608 | tf_op jit(solution)/shard_map/first_feed/pallas_call | solution.py:54
  13.2 16.2 %middle.1 = (bf16[512,512]{1,0:T(8,128)(2,1)S(1)}, bf16[512,2048]{1,0:T(8,128)(2,1)S(1)}, bf16[512,512]{1,0:T(8,128)(2,1)S(1)}, f32[512,512]{1,0:T(8,128)S(1)}, ...) custom-call(bf16[2,512,512]{2,1,0:T(8,128)(2,1)S(1)} %get-tuple-elem, ...), custom_call_target="tpu_custom_call", output_to_operand_aliasing={{9}: (0, {}), {10}: (1, {})} | custom-call | flops 16106127360 | bytes 8388608 | tf_op jit(solution)/shard_map/middle/pallas_call | solution.py:54
  29.3 0.1 collective-permute-start.5
  29.5 1.6 %layer_one_out.1 = (bf16[512,512]{1,0:T(8,128)(2,1)S(1)}, bf16[512,512]{1,0:T(8,128)(2,1)S(1)}) custom-call(bf16[512,512]{1,0:T(8,128)(2,1)S(1)} %get-tuple-element.118.h_one, bf16[512,2048]{1,0:T(8,128)(2,1)S(1)} %get-tuple-element.119.act, bf16[512,512]{1,0:T(8,128)(2,1)S(1)} %get-tuple-element.120.mixed, f32[2,1,6656]{2,1,0:T(1,128)S(1)} %get-tuple-element.106.small, ...), custom_call_target="tpu_custom_call" | custom-call | flops 1342177280 | bytes 8388608 | tf_op jit(solution)/shard_map/layer_one_out/pallas_call | solution.py:54
  31.1 0.5 collective-permute-start.7
  31.7 2.6 %collective-permute-start.6 = (bf16[40,512]{1,0:T(8,128)(2,1)S(1)}, bf16[40,512]{1,0:T(8,128)(2,1)S(1)}, u32[]{:S(2)}, u32[]{:S(2)}) collective-permute-start(bf16[40,512]{1,0:T(8,128)(2,1)S(1)} %get-tuple-element.185), channel_id=1, source_target_pairs={{0,1},{1,0},{2,3},{3,2},{4,5},{5,4},{6,7},{7,6},{8,9},{9,8},{10,11... | collective-permute-start | bytes 122888 | tf_op jit(solution)/shard_map/ppermute | solution.py:866
  34.3 2.7 %layer_zero_attention_back.1.packed = bf16[1536,512]{1,0:T(8,128)(2,1)S(1)} custom-call(bf16[512,512]{1,0:T(8,128)(2,1)S(1)} %get-tuple-element.132.scaled, f32[8,512]{1,0:T(8,128)S(1)} %get-tuple-element.133.inner, bf16[4,32,512]{2,1,0:T(8,128)(2,1)S(1)} %get-tuple-element.134.pre_ds, bf16[512,512]{1,0:T(8,128)(2,1)S(1)} %get-tuple-element.102.q0.q_t, ...), custom_call_target="tpu_custom_call" | custom-call | flops 1342177280 | bytes 8388608 | tf_op jit(solution)/shard_map/layer_zero_attention_back/pallas_call | solution.py:54
  37.0 1.6 %collective-permute-start.8 = (bf16[40,512]{1,0:T(8,128)(2,1)S(1)}, bf16[40,512]{1,0:T(8,128)(2,1)S(1)}, u32[]{:S(2)}, u32[]{:S(2)}) collective-permute-start(bf16[40,512]{1,0:T(8,128)(2,1)S(1)} %get-tuple-element.183), channel_id=1, source_target_pairs={{0,2},{1,3},{2,0},{3,1},{4,6},{5,7},{6,4},{7,5},{8,10},{9,11},{10,... | collective-permute-start | bytes 122888 | tf_op jit(solution)/shard_map/ppermute | solution.py:866
  38.6 2.4 %layer_zero_feed_back.1.two = f32[512,512]{1,0:T(8,128)S(1)} custom-call(bf16[512,512]{1,0:T(8,128)(2,1)S(1)} %get-tuple-element.142.grad, bf16[512,2048]{1,0:T(8,128)(2,1)S(1)} %get-tuple-element.144.slope, bf16[2,512,2048]{2,1,0:T(8,128)(2,1)S(1)} %get-tuple-element.111.w_in, bf16[2,2048,512]{2,1,0:T(8,128)(2,1)S(1)} %get-tuple-element.122.w_out), custom_call_target="tpu_custom_call" | custom-call | flops 2147483648 | bytes 8388608 | tf_op jit(solution)/shard_map/layer_zero_feed_back/pallas_call | solution.py:54
  40.9 0.1 collective-permute-done.8
  41.1 1.6 %collective-permute-start.9 = (bf16[40,512]{1,0:T(8,128)(2,1)S(1)}, bf16[40,512]{1,0:T(8,128)(2,1)S(1)}, u32[]{:S(2)}, u32[]{:S(2)}) collective-permute-start(bf16[40,512]{1,0:T(8,128)(2,1)S(1)} %get-tuple-element.181), channel_id=1, source_target_pairs={{0,4},{4,0},{8,12},{12,8},{1,5},{5,1},{9,13},{13,9},{2,6},{6,2},{1... | collective-permute-start | bytes 122888 | tf_op jit(solution)/shard_map/ppermute | solution.py:866
  42.7 1.9 %layer_zero_norms.1 = (f32[512,512]{1,0:T(8,128)S(1)}, f32[512,512]{1,0:T(8,128)S(1)}) custom-call(bf16[512,512]{1,0:T(8,128)(2,1)S(1)} %get-tuple-element.115.x_ref, bf16[512,512]{1,0:T(8,128)(2,1)S(1)} %get-tuple-element.142.grad, f32[512,512]{1,0:T(8,128)S(1)} %layer_zero_feed_back.1.two, bf16[1536,512]{1,0:T(8,128)(2,1)S(1)} %layer_zero_attention_back.1.packed, ...), custom_call_target="tpu_custom_call" | custom-call | flops 805306368 | bytes 8388608 | tf_op jit(solution)/shard_map/layer_zero_norms/pallas_call | solution.py:54
  44.6 0.5 collective-permute-done.9
  45.2 2.6 %collective-permute-start.10 = (bf16[40,512]{1,0:T(8,128)(2,1)S(1)}, bf16[40,512]{1,0:T(8,128)(2,1)S(1)}, u32[]{:S(2)}, u32[]{:S(2)}) collective-permute-start(bf16[40,512]{1,0:T(8,128)(2,1)S(1)} %get-tuple-element.179), channel_id=1, source_target_pairs={{0,8},{4,12},{8,0},{12,4},{1,9},{5,13},{9,1},{13,5},{2,10},{6,14},... | collective-permute-start | bytes 122888 | tf_op jit(solution)/shard_map/ppermute | solution.py:866
  47.8 1.2 %place_own.1 = (bf16[1,2,1,512,512]{4,3,2,1,0:T(8,128)(2,1)}, f32[1,2,1,512,512]{4,3,2,1,0:T(8,128)}) custom-call(bf16[512,512]{1,0:T(8,128)(2,1)S(1)} %get-tuple-element.157.act, f32[512,512]{1,0:T(8,128)S(1)} %get-tuple-element.159.grad), custom_call_target="tpu_custom_call" | custom-call | flops 524288 | bytes 8388608 | tf_op jit(solution)/shard_map/place_own/pallas_call | solution.py:54
  49.0 1.2 %collective-permute-done.10 = bf16[40,512]{1,0:T(8,128)(2,1)S(1)} collective-permute-done((bf16[40,512]{1,0:T(8,128)(2,1)S(1)}, bf16[40,512]{1,0:T(8,128)(2,1)S(1)}, u32[]{:S(2)}, u32[]{:S(2)}) %collective-permute-start.10) | collective-permute-done | bytes 40992 | tf_op jit(solution)/shard_map/ppermute | solution.py:866
  50.2 2.5 %reparam.1 = (f32[10,512]{1,0:T(8,128)}, f32[512,512]{1,0:T(8,128)}, f32[1,512]{1,0:T(1,128)}, f32[512,256]{1,0:T(8,128)}, f32[1,256]{1,0:T(1,128)}, /*index=5*/...) custom-call(f32[40,512]{1,0:T(8,128)S(1)} %convert_add_fusion.refs_0_, ...), custom_call_target="tpu_custom_call", output_to_operand_aliasing={{5}: (8, {}), {6}: (9, {})} | custom-call | flops 134217728 | bytes 8388608 | tf_op jit(solution)/shard_map/reparam/pallas_call | solution.py:54
  (18 shorter events, 0.2 us)
Async XLA Ops:
  0.6 5.9 %collective-permute-start.1 = (bf16[1,512,1536]{2,1,0:T(8,128)(2,1)}, bf16[1,512,1536]{2,1,0:T(8,128)(2,1)S(1)}, u32[]{:S(2)}, u32[]{:S(2)}) collective-permute-start(bf16[1,512,1536]{2,1,0:T(8,128)(2,1)} %qkv_hbm.1), channel_id=1, source_target_pairs={{0,16},{16,0},{1,17},{17,1},{2,18},{18,2},{3,19},{19,3},{4,20},{20... | collective-permute-start | bytes 4718600 | tf_op jit(solution)/shard_map/ppermute | solution.py:779
  2.0 4.4 %collective-permute-start = (f32[1,6656]{1,0:T(1,128)S(1)}, f32[1,6656]{1,0:T(1,128)S(1)}, u32[]{:S(2)}, u32[]{:S(2)}) collective-permute-start(f32[1,6656]{1,0:T(1,128)S(1)} %small_parameters.1.own_small), channel_id=1, source_target_pairs={{0,16},{16,0},{1,17},{17,1},{2,18},{18,2},{3,19},{19,3},{4,20},{20... | collective-permute-start | bytes 79880 | tf_op jit(solution)/shard_map/ppermute | solution.py:779
  2.2 11.0 %collective-permute-start.3 = (bf16[1,512,512]{2,1,0:T(8,128)(2,1)}, bf16[1,512,512]{2,1,0:T(8,128)(2,1)S(1)}, u32[]{:S(2)}, u32[]{:S(2)}) collective-permute-start(bf16[1,512,512]{2,1,0:T(8,128)(2,1)} %attn_hbm.1), channel_id=1, source_target_pairs={{0,16},{16,0},{1,17},{17,1},{2,18},{18,2},{3,19},{19,3},{4,20},{20... | collective-permute-start | bytes 1572872 | tf_op jit(solution)/shard_map/ppermute | solution.py:779
  2.6 7.8 %collective-permute-start.2 = (bf16[1,512,2048]{2,1,0:T(8,128)(2,1)}, bf16[1,512,2048]{2,1,0:T(8,128)(2,1)S(1)}, u32[]{:S(2)}, u32[]{:S(2)}) collective-permute-start(bf16[1,512,2048]{2,1,0:T(8,128)(2,1)} %ff_in_hbm.1), channel_id=1, source_target_pairs={{0,16},{16,0},{1,17},{17,1},{2,18},{18,2},{3,19},{19,3},{4,20},{20... | collective-permute-start | bytes 6291464 | tf_op jit(solution)/shard_map/ppermute | solution.py:779
  2.7 10.5 %collective-permute-start.4 = (bf16[1,2048,512]{2,1,0:T(8,128)(2,1)}, bf16[1,2048,512]{2,1,0:T(8,128)(2,1)S(1)}, u32[]{:S(2)}, u32[]{:S(2)}) collective-permute-start(bf16[1,2048,512]{2,1,0:T(8,128)(2,1)} %ff_out_hbm.1), channel_id=1, source_target_pairs={{0,16},{16,0},{1,17},{17,1},{2,18},{18,2},{3,19},{19,3},{4,20},{20... | collective-permute-start | bytes 6291464 | tf_op jit(solution)/shard_map/ppermute | solution.py:779
  29.3 1.8 %collective-permute-start.5 = (f32[40,512]{1,0:T(8,128)S(1)}, f32[40,512]{1,0:T(8,128)S(1)}, u32[]{:S(2)}, u32[]{:S(2)}) collective-permute-start(f32[40,512]{1,0:T(8,128)S(1)} %get-tuple-element.127), channel_id=1, source_target_pairs={{0,16},{16,0},{1,17},{17,1},{2,18},{18,2},{3,19},{19,3},{4,20},{20... | collective-permute-start | bytes 245768 | tf_op jit(solution)/shard_map/ppermute | solution.py:863
  31.1 5.8 %collective-permute-start.7 = (bf16[512,512]{1,0:T(8,128)(2,1)S(1)}, bf16[512,512]{1,0:T(8,128)(2,1)S(1)}, u32[]{:S(2)}, u32[]{:S(2)}) collective-permute-start(bf16[512,512]{1,0:T(8,128)(2,1)S(1)} %get-tuple-element.129), channel_id=1, source_target_pairs={{0,16},{16,0},{1,17},{17,1},{2,18},{18,2},{3,19},{19,3},{4,20},{20... | collective-permute-start | bytes 1572872 | tf_op jit(solution)/shard_map/ppermute | solution.py:779
  31.7 5.3 %collective-permute-start.6 = (bf16[40,512]{1,0:T(8,128)(2,1)S(1)}, bf16[40,512]{1,0:T(8,128)(2,1)S(1)}, u32[]{:S(2)}, u32[]{:S(2)}) collective-permute-start(bf16[40,512]{1,0:T(8,128)(2,1)S(1)} %get-tuple-element.185), channel_id=1, source_target_pairs={{0,1},{1,0},{2,3},{3,2},{4,5},{5,4},{6,7},{7,6},{8,9},{9,8},{10,11... | collective-permute-start | bytes 122888 | tf_op jit(solution)/shard_map/ppermute | solution.py:866
  37.0 4.1 %collective-permute-start.8 = (bf16[40,512]{1,0:T(8,128)(2,1)S(1)}, bf16[40,512]{1,0:T(8,128)(2,1)S(1)}, u32[]{:S(2)}, u32[]{:S(2)}) collective-permute-start(bf16[40,512]{1,0:T(8,128)(2,1)S(1)} %get-tuple-element.183), channel_id=1, source_target_pairs={{0,2},{1,3},{2,0},{3,1},{4,6},{5,7},{6,4},{7,5},{8,10},{9,11},{10,... | collective-permute-start | bytes 122888 | tf_op jit(solution)/shard_map/ppermute | solution.py:866
  41.1 4.1 %collective-permute-start.9 = (bf16[40,512]{1,0:T(8,128)(2,1)S(1)}, bf16[40,512]{1,0:T(8,128)(2,1)S(1)}, u32[]{:S(2)}, u32[]{:S(2)}) collective-permute-start(bf16[40,512]{1,0:T(8,128)(2,1)S(1)} %get-tuple-element.181), channel_id=1, source_target_pairs={{0,4},{4,0},{8,12},{12,8},{1,5},{5,1},{9,13},{13,9},{2,6},{6,2},{1... | collective-permute-start | bytes 122888 | tf_op jit(solution)/shard_map/ppermute | solution.py:866
  42.7 7.4 %copy-start = (f32[10,512]{1,0:T(8,128)S(1)}, f32[10,512]{1,0:T(8,128)}, u32[]{:S(2)}) copy-start(f32[10,512]{1,0:T(8,128)} %refs_2_) | copy-start | bytes 61444
  45.1 5.0 %collective-permute-start.11 = (f32[512,512]{1,0:T(8,128)S(1)}, f32[512,512]{1,0:T(8,128)S(1)}, u32[]{:S(2)}, u32[]{:S(2)}) collective-permute-start(f32[512,512]{1,0:T(8,128)S(1)} %get-tuple-element.158), channel_id=1, source_target_pairs={{0,16},{16,0},{1,17},{17,1},{2,18},{18,2},{3,19},{19,3},{4,20},{20... | collective-permute-start | bytes 3145736 | tf_op jit(solution)/shard_map/ppermute | solution.py:779
  45.2 5.0 %collective-permute-start.10 = (bf16[40,512]{1,0:T(8,128)(2,1)S(1)}, bf16[40,512]{1,0:T(8,128)(2,1)S(1)}, u32[]{:S(2)}, u32[]{:S(2)}) collective-permute-start(bf16[40,512]{1,0:T(8,128)(2,1)S(1)} %get-tuple-element.179), channel_id=1, source_target_pairs={{0,8},{4,12},{8,0},{12,4},{1,9},{5,13},{9,1},{13,5},{2,10},{6,14},... | collective-permute-start | bytes 122888 | tf_op jit(solution)/shard_map/ppermute | solution.py:866

commit v6 on v5

--- a/solution.py
+++ b/solution.py
@@ -228,60 +228,80 @@
         peak = jnp.maximum(
             jnp.max(scores, axis=0, keepdims=True), jnp.max(pre_scores, axis=0, keepdims=True)
         )
-        expo = jnp.exp2(scores - peak)
+        expo = jnp.exp2(scores - peak).astype(bf16)
         pre_expo = jnp.exp2(pre_scores - peak)
-        total = jnp.sum(expo, axis=0, keepdims=True) + jnp.sum(pre_expo, axis=0, keepdims=True)
-        inverse = 1.0 / total
-        expo = expo.astype(bf16)
-        pre_expo = pre_expo.astype(bf16)
         p_ref[pair, rows, :] = expo
-        pp_ref[pair, :PAD, tokens] = pre_expo[:, :BLK]
-        pp_ref[pair, PAD:, tokens] = pre_expo[:, BLK:]
+        pp_ref[pair, :PAD, tokens] = pre_expo[:, :BLK].astype(bf16)
+        pp_ref[pair, PAD:, tokens] = pre_expo[:, BLK:].astype(bf16)
+        return expo, jnp.sum(pre_expo, axis=0, keepdims=True)
+
+    def mix(pair, block, pre_mixed, expo, pre_total):
+        feats = pair_rows(pair)
+        keys, tokens, _ = geometry(block)
+        ones = jnp.ones((PAD, expo.shape[0]), bf16)
+        mixed = dot(jnp.concatenate([v_t[feats, keys], ones], axis=0), expo, NN)
+        inverse = 1.0 / (mixed[BLK : BLK + 1] + pre_total)
         inv_ref[2 * pair : 2 * pair + 1, tokens] = inverse[:, :BLK]
         inv_ref[2 * pair + 1 : 2 * pair + 2, tokens] = inverse[:, BLK:]
-        return expo, inverse
-
-    def mix(feats, block, pre_mixed, expo, inverse):
-        keys, tokens, _ = geometry(block)
-        mixed = from_diagonal(dot(v_t[feats, keys], expo, NN)) + pre_mixed[:, tokens]
+        mixed = from_diagonal(mixed[:BLK]) + pre_mixed[:, tokens]
         mixed_ref[feats, tokens] = (mixed * per_head(inverse)).astype(bf16)
 
-    for pair in range(PAIRS):
+    def score_all(pair):
         feats = pair_rows(pair)
         pre_scores = dot(pre_k[:, feats], q_t[feats, :], NN) + pad_mask
-        scores = [score(feats, block) for block in range(BLOCKS)]
+        return pre_scores, [score(feats, block) for block in range(BLOCKS)]
+
+    def mix_all(pair, soft):
+        pre_mixed = dot(pre_v[:, pair_rows(pair)], pp_ref[pair], TN)
+        for block in range(BLOCKS):
+            mix(pair, block, pre_mixed, *soft[block])
+
+    ahead, behind = score_all(0), None
+    for pair in range(PAIRS):
+        pre_scores, scores = ahead
+        if pair + 1 < PAIRS:
+            ahead = score_all(pair + 1)
         soft = [soften(pair, block, scores[block], pre_scores) for block in range(BLOCKS)]
-        pre_mixed = dot(pre_v[:, feats], pp_ref[pair], TN)
-        for block in range(BLOCKS):
-            mix(feats, block, pre_mixed, *soft[block])
-
-
-def prefix_back(grad_t, q_t, pre_v, pp_ref, inv_ref, mixed_ref, scaled_ref, inner_ref, pre_ds_ref, pre_grad, pre_row):
-    first_half = lax.broadcasted_iota(jnp.int32, (1, BLK), 1) < HD
-
-    def own_head(both):
-        return jnp.where(first_half, both[:PAD], both[PAD:])
-
-    for pair in range(PAIRS):
-        feats = pair_rows(pair)
+        if behind is not None:
+            mix_all(*behind)
+        behind = (pair, soft)
+    mix_all(*behind)
+
+
+def prefix_back(w_attn, grad, q_t, pre_v, pp_ref, inv_ref, mixed_ref, scaled_ref, inner_ref, pre_ds_ref, turned,
+                pre_grad, pre_row):
+    turned[...] = jnp.transpose(grad)
+
+    def scale(pair):
+        grad_mixed = dot(w_attn[pair_rows(pair), :], turned[...], NN)
         inner = []
-        for head in (2 * pair, 2 * pair + 1):
+        for place in range(2):
+            head = 2 * pair + place
             rows = slice(head * HD, (head + 1) * HD)
-            scaled = (grad_t[rows, :] * inv_ref[head : head + 1, :]).astype(bf16)
+            scaled = grad_mixed[place * HD : (place + 1) * HD] * inv_ref[head : head + 1, :]
+            scaled = scaled.astype(bf16)
             scaled_ref[rows, :] = scaled
             products = scaled.astype(f32) * mixed_ref[rows, :].astype(f32)
             inner.append(jnp.sum(products, axis=0, keepdims=True))
             inner_ref[head : head + 1, :] = inner[-1]
-        inner = jnp.concatenate([jnp.broadcast_to(row, (PAD, SEQ)) for row in inner], axis=0)
-        grads = scaled_ref[feats, :]
-        probs = pp_ref[pair]
-        grad_probs = dot(pre_v[:, feats], grads, NN)
-        grad_scores = (probs.astype(f32) * (grad_probs - inner)).astype(bf16)
-        pre_ds_ref[pair] = grad_scores
-        pre_grad[pre_row : pre_row + PREFIX, feats] = (
-            own_head(dot(grad_scores, q_t[feats, :], NT))[:PREFIX] * K_BACK
-        )
-        pre_grad[pre_row + PREFIX : pre_row + 2 * PREFIX, feats] = own_head(dot(probs, grads, NT))[:PREFIX]
+        return jnp.concatenate([jnp.broadcast_to(row, (PAD, SEQ)) for row in inner], axis=0)
+
+    pairs = range(PAIRS)
+    inner = [scale(pair) for pair in pairs]
+    grad_probs = [dot(pre_v[:, pair_rows(pair)], scaled_ref[pair_rows(pair), :], NN) for pair in pairs]
+    for pair in pairs:
+        probs = pp_ref[pair].astype(f32)
+        pre_ds_ref[pair] = (probs * (grad_probs[pair] - inner[pair])).astype(bf16)
+    keys = [dot(q_t[pair_rows(pair), :], pre_ds_ref[pair], NT) for pair in pairs]
+    values = [dot(scaled_ref[pair_rows(pair), :], pp_ref[pair], NT) for pair in pairs]
+    first_head = lax.rem(lax.broadcasted_iota(jnp.int32, (1, D), 1), BLK) < HD
+
+    def own_head(parts):
+        both = jnp.transpose(jnp.concatenate(parts, axis=0))
+        return jnp.where(first_head, both[:PREFIX], both[PAD : PAD + PREFIX])
+
+    pre_grad[pre_row : pre_row + PREFIX, :] = own_head(keys) * K_BACK
+    pre_grad[pre_row + PREFIX : pre_row + 2 * PREFIX, :] = own_head(values)
 
 
 def attend_back(scaled_ref, inner_ref, pre_ds_ref, q_t, k_t, v_m, pre_k, p_ref, dq_ref, dk_ref, dv_ref):
@@ -591,7 +611,7 @@
                   other_attn, other_out, cot_ref, x_ref, act_zero, low, mask, tables,
                   h_one, act_one, mixed_one, grad_one, grad_low, scaled_zero, inner_zero, pre_ds_zero,
                   prefix_grad, w_attn, w_out,
-                  q_t, k_t, v_m, p_ref, pp_ref, inv_ref, scaled, inner, pre_ds, slope_one, k_m, v_t,
+                  q_t, k_t, v_m, p_ref, pp_ref, inv_ref, scaled, inner, pre_ds, turned, slope_one, k_m, v_t,
                   dq, dk, dv, packed, sems):
     section = lax.axis_index("pipe")
     copies = Copies(sems)
@@ -614,16 +634,16 @@
 
     grad = cot_ref[...]
     grad_two = feed_back(grad, w_out.at[1], w_in.at[1], slope_one, NO_COPIES)
-    dq[...] = dot(w_attn[1], grad, NT)
-    prefix_back(dq, q_t, low.at[3], pp_ref, inv_ref, mixed_one, scaled, inner, pre_ds, prefix_grad, 2 * PREFIX)
+    prefix_back(w_attn.at[1], grad, q_t, low.at[3], pp_ref, inv_ref, mixed_one, scaled, inner, pre_ds, turned,
+                prefix_grad, 2 * PREFIX)
     attend_back(scaled, inner, pre_ds, q_t, k_t, v_m, low.at[2], p_ref, dq, dk, dv)
     pack_grads(dq, dk, dv, cos, sin, packed)
     result = norms_back(grad, h_one[...].astype(f32), grad_two, packed[...], w_qkv[1], small_one)
     grad_one[...] = result
     grad_low[...] = result.astype(bf16)
 
-    dq[...] = dot(w_attn[0], grad_low[...], NT)
-    prefix_back(dq, q0, low.at[1], pp0, inv0, mixed0, scaled_zero, inner_zero, pre_ds_zero, prefix_grad, 0)
+    prefix_back(w_attn.at[0], grad_low[...], q0, low.at[1], pp0, inv0, mixed0, scaled_zero, inner_zero,
+                pre_ds_zero, turned, prefix_grad, 0)
 
 
 def middle_call(*arrays):
@@ -631,6 +651,7 @@
         ((D, SEQ), bf16),
         ((HEADS, SEQ), f32),
         ((PAIRS, 2 * PAD, SEQ), bf16),
+        ((D, SEQ), bf16),
         ((SEQ, FF), bf16),
         ((SEQ, D), bf16),
         ((D, SEQ), bf16),
@@ -706,31 +727,35 @@
     )
 
 
-def place_kernel(act, grad, act_out, grad_out, sems):
+def place_kernel(act, act_other, grad, grad_other, act_out, grad_out, sems):
     section = lax.axis_index("pipe")
     copies = Copies(sems)
     wait_all(
-        copies.start(grad, grad_out.at[0, section, 0]), copies.start(act, act_out.at[0, section, 0])
-    )
-
-
-def place_call(act, grad):
+        *[
+            copies.start(value, whole.at[0, where, 0])
+            for value, whole, where in (
+                (grad, grad_out, section),
+                (grad_other, grad_out, 1 - section),
+                (act, act_out, section),
+                (act_other, act_out, 1 - section),
+            )
+        ]
+    )
+
+
+def place_call(*arrays):
     wholes = [(pltpu.HBM, (1, 2, 1, SEQ, D), bf16), (pltpu.HBM, (1, 2, 1, SEQ, D), f32)]
     return call_kernel(
-        place_kernel, "place_own", in_vmem(act, grad), wholes, [], 2, LATE_MIB, 2 * SEQ * D
-    )
-
-
-def final_kernel(col_width, grads_ref, hidden, embed, wide, up_high, up_rest, act_other, grad_other,
-                 act_in, grad_in, *refs):
-    results, (act_out, grad_out, d_embed, d_up, d_up_b, d_out, d_out_b, sems) = refs[:5], refs[5:]
+        place_kernel, "place_outputs", in_vmem(*arrays), wholes, [], 4, LATE_MIB, 2 * SEQ * D
+    )
+
+
+def final_kernel(col_width, grads_ref, hidden, embed, wide, up_high, up_rest, *refs):
+    results, (d_embed, d_up, d_up_b, d_out, d_out_b, sems) = refs[:5], refs[5:]
     section = lax.axis_index("pipe")
     shard = lax.axis_index("dp")
     copies = Copies(sems)
-    placed = [
-        copies.start(grad_other, grad_out.at[0, 1 - section, 0]),
-        copies.start(act_other, act_out.at[0, 1 - section, 0]),
-    ]
+    placed = []
     units = hidden[...]
     both = jnp.zeros((2 * PAD, D), f32)
     for part in range(4):
@@ -762,16 +787,14 @@
     wait_all(*placed)
 
 
-def final_call(col_width, wholes, *arrays):
+def final_call(col_width, *arrays):
     def body(*refs):
         final_kernel(col_width, *refs)
 
     shapes = [((PREFIX, D), f32), ((D, D), f32), ((1, D), f32), ((D, col_width), f32), ((1, col_width), f32)]
-    whole_shapes = [((1, 2, 1, SEQ, D), bf16), ((1, 2, 1, SEQ, D), f32)]
     return call_kernel(
-        body, "reparam", in_vmem(*arrays) + in_hbm(*wholes),
-        [(pltpu.HBM, *pair) for pair in shapes + whole_shapes], shapes, 7, LATE_MIB, SEQ * D * D,
-        {8: 5, 9: 6},
+        body, "reparam", in_vmem(*arrays), [(pltpu.HBM, *pair) for pair in shapes], shapes, 5, LATE_MIB,
+        SEQ * D * D,
     )
 
 
@@ -853,8 +876,8 @@
         return dict(state, grad_own=own, grad_send=send)
 
     def swap_grads(state):
-        wholes = place_call(state["act_own"], state["grad_own"])
-        return dict(state, grad_other=swapped(state["grad_send"]), wholes=wholes)
+        other = swapped(state["grad_send"])
+        return {"wholes": place_call(state["act_own"], state["act_other"], state["grad_own"], other)}
 
     works = [layer_one_out, layer_zero_attention, layer_zero_feed, layer_zero_norms, swap_grads]
     state = {"h_one": h_one, "grad_low": grad_low, "scaled": scaled_zero}
@@ -871,10 +894,10 @@
     for work in works:
         state = work(state)
     col_width = 2 * D // lax.axis_size("dp")
-    grad_embed, grad_up, grad_up_b, grad_out, grad_out_b, activations, input_grads = final_call(
-        col_width, state["wholes"], prefix_grad, hidden_units, prefix_embed, wide, up_high, up_rest,
-        state["act_other"], state["grad_other"],
-    )
+    grad_embed, grad_up, grad_up_b, grad_out, grad_out_b = final_call(
+        col_width, prefix_grad, hidden_units, prefix_embed, wide, up_high, up_rest
+    )
+    activations, input_grads = state["wholes"]
     return (
         activations,
         input_grads,

time: 53.1 us -> 51.4 us (0.968)
  Pallas kernels: 39.3 us -> 38.2 us
  waiting for transfers between devices: 1.82 us -> 1.25 us
    pallas_call x11, Pallas kernels: 39.3 us -> 38.2 us  [call_kernel(): pl.pallas_call(kernel, name=name, out_shape=[space(shape, dtype) for spac...]
    ppermute x4, waiting for transfers between devices: 1.79 us -> 1.23 us  [local(): moved = lax.ppermute(prefix_grad.astype(bf16), axis, pairs)]
  transfers between devices with their start and end apart: 12 -> 12, of which waited for: 3 -> 3; matrix products, arithmetic and copies ran while one was open for 0% -> 0% of each run, Pallas kernels for 39% -> 40%
where the time goes in v6:
time: 51.4 us; the launch traced here: 51.2 us
  Pallas kernels  38.2 us (74%)
  starting transfers between devices  10.8 us (21%)
  waiting for transfers between devices  1.25 us (2%)
  between operations  0.99 us (2%)
    pallas_call x11, Pallas kernels, call_kernel(): pl.pallas_call(kernel, name=name, out_shape=[space(shape, dtype) for spac...  38.2 us
    ppermute x4, starting transfers between devices, local(): moved = lax.ppermute(prefix_grad.astype(bf16), axis, pairs)  8.51 us
    ppermute x7, starting transfers between devices, swapped(): return lax.ppermute(array_in, 'pipe', [(0, 1), (1, 0)])  2.1 us
    ppermute x4, waiting for transfers between devices, local(): moved = lax.ppermute(prefix_grad.astype(bf16), axis, pairs)  1.23 us
  transfers between devices with their start and end apart: 12, of which 3 were waited for; matrix products, arithmetic and copies ran while one was open for 0% of the time, Pallas kernels for 40%

profile of v6, /device:TPU:0, one launch (start us, length us, event | category | flops | bytes accessed | tf_op | source)
XLA Modules:
  0.0 51.2 jit_solution(7977768541743749858)
XLA Ops:
  0.6 0.5 %collective-permute-start.1 = (bf16[1,512,1536]{2,1,0:T(8,128)(2,1)}, bf16[1,512,1536]{2,1,0:T(8,128)(2,1)S(1)}, u32[]{:S(2)}, u32[]{:S(2)}) collective-permute-start(bf16[1,512,1536]{2,1,0:T(8,128)(2,1)} %qkv_hbm.1), channel_id=1, source_target_pairs={{0,16},{16,0},{1,17},{17,1},{2,18},{18,2},{3,19},{19,3},{4,20},{20... | collective-permute-start | bytes 4718600 | tf_op jit(solution)/shard_map/ppermute | solution.py:802
  1.2 0.9 %small_parameters.1.own_small = f32[1,6656]{1,0:T(1,128)S(1)} custom-call(f32[1,512]{1,0:T(1,128)} %gain_one.1, f32[1,512]{1,0:T(1,128)} %shift_one.1, f32[1,512]{1,0:T(1,128)} %gain_two.1, f32[1,512]{1,0:T(1,128)} %shift_two.1, f32[1,512]{1,0:T(1,128)} %attn_b.1, f32[1,512]{1,0:T(1,128)} %out_b.1, f32[1,1536]{1,0:T(1,128)} %qkv_b.1, f32[1,2048]{1,0:T(1,128)} %in_b.1), custom_call_target="tpu_custom_call" | custom-call | flops 6656 | bytes 8388608 | tf_op jit(solution)/shard_map/small_parameters/pallas_call | solution.py:54
  2.0 0.1 collective-permute-start
  2.2 0.5 collective-permute-start.3
  2.7 0.4 collective-permute-start.4
  3.1 3.3 %opening.1 = (bf16[512,512]{1,0:T(8,128)(2,1)S(1)}, f32[512,512]{1,0:T(8,128)S(1)}, f32[1152,128]{1,0:T(8,128)S(1)}, bf16[4,32,512]{2,1,0:T(8,128)(2,1)S(1)}, f3...) custom-call(bf16[2,1,512,512]{3,2,1,0:T(8,128)(2,1)} %x_hbm.1, ...), custom_call_target="tpu_custom_call" | custom-call | flops 251658240 | bytes 8388608 | tf_op jit(solution)/shard_map/opening/pallas_call | solution.py:54
  6.5 3.5 %first_attention.1 = (bf16[512,512]{1,0:T(8,128)(2,1)S(1)}, bf16[512,512]{1,0:T(8,128)(2,1)S(1)}, bf16[512,512]{1,0:T(8,128)(2,1)S(1)}, bf16[4,1152,256]{2,1,0:T...) custom-call(f32[1,6656]{1,0:T(1,128)S(1)} %small_parameters.1.own_sm, ...), custom_call_target="tpu_custom_call" | custom-call | flops 80530636800 | bytes 8388608 | tf_op jit(solution)/shard_map/first_attention/pallas_call | solution.py:54
  10.0 2.7 %first_feed.1 = (bf16[512,2048]{1,0:T(8,128)(2,1)S(1)}, bf16[512,2048]{1,0:T(8,128)(2,1)S(1)}, bf16[2,512,2048]{2,1,0:T(8,128)(2,1)S(1)}) custom-call(bf16[512,512]{1,0:T(8,128)(2,1)S(1)} %get-tuple-element.104.two, f32[2,1,6656]{2,1,0:T(1,128)S(1)} %get-tuple-element.102.small, ...), custom_call_target="tpu_custom_call", output_to_operand_aliasing={{2}: (3, {})} | custom-call | flops 1073741824 | bytes 8388608 | tf_op jit(solution)/shard_map/first_feed/pallas_call | solution.py:54
  12.7 15.5 %middle.1 = (bf16[512,512]{1,0:T(8,128)(2,1)S(1)}, bf16[512,2048]{1,0:T(8,128)(2,1)S(1)}, bf16[512,512]{1,0:T(8,128)(2,1)S(1)}, f32[512,512]{1,0:T(8,128)S(1)}, ...) custom-call(bf16[2,512,512]{2,1,0:T(8,128)(2,1)S(1)} %get-tuple-elem, ...), custom_call_target="tpu_custom_call", output_to_operand_aliasing={{9}: (0, {}), {10}: (1, {})} | custom-call | flops 16106127360 | bytes 8388608 | tf_op jit(solution)/shard_map/middle/pallas_call | solution.py:54
  28.3 0.1 collective-permute-start.5
  28.4 1.6 %layer_one_out.1 = (bf16[512,512]{1,0:T(8,128)(2,1)S(1)}, bf16[512,512]{1,0:T(8,128)(2,1)S(1)}) custom-call(bf16[512,512]{1,0:T(8,128)(2,1)S(1)} %get-tuple-element.114.h_one, bf16[512,2048]{1,0:T(8,128)(2,1)S(1)} %get-tuple-element.115.act, bf16[512,512]{1,0:T(8,128)(2,1)S(1)} %get-tuple-element.116.mixed, f32[2,1,6656]{2,1,0:T(1,128)S(1)} %get-tuple-element.102.small, ...), custom_call_target="tpu_custom_call" | custom-call | flops 1342177280 | bytes 8388608 | tf_op jit(solution)/shard_map/layer_one_out/pallas_call | solution.py:54
  30.1 0.5 collective-permute-start.7
  30.6 2.6 %collective-permute-start.6 = (bf16[40,512]{1,0:T(8,128)(2,1)S(1)}, bf16[40,512]{1,0:T(8,128)(2,1)S(1)}, u32[]{:S(2)}, u32[]{:S(2)}) collective-permute-start(bf16[40,512]{1,0:T(8,128)(2,1)S(1)} %get-tuple-element.177), channel_id=1, source_target_pairs={{0,1},{1,0},{2,3},{3,2},{4,5},{5,4},{6,7},{7,6},{8,9},{9,8},{10,11... | collective-permute-start | bytes 122888 | tf_op jit(solution)/shard_map/ppermute | solution.py:889
  33.2 2.7 %layer_zero_attention_back.1.packed = bf16[1536,512]{1,0:T(8,128)(2,1)S(1)} custom-call(bf16[512,512]{1,0:T(8,128)(2,1)S(1)} %get-tuple-element.128.scaled, f32[8,512]{1,0:T(8,128)S(1)} %get-tuple-element.129.inner, bf16[4,32,512]{2,1,0:T(8,128)(2,1)S(1)} %get-tuple-element.130.pre_ds, bf16[512,512]{1,0:T(8,128)(2,1)S(1)} %get-tuple-element.98.q0.q_t, ...), custom_call_target="tpu_custom_call" | custom-call | flops 1342177280 | bytes 8388608 | tf_op jit(solution)/shard_map/layer_zero_attention_back/pallas_call | solution.py:54
  35.9 1.6 %collective-permute-start.8 = (bf16[40,512]{1,0:T(8,128)(2,1)S(1)}, bf16[40,512]{1,0:T(8,128)(2,1)S(1)}, u32[]{:S(2)}, u32[]{:S(2)}) collective-permute-start(bf16[40,512]{1,0:T(8,128)(2,1)S(1)} %get-tuple-element.175), channel_id=1, source_target_pairs={{0,2},{1,3},{2,0},{3,1},{4,6},{5,7},{6,4},{7,5},{8,10},{9,11},{10,... | collective-permute-start | bytes 122888 | tf_op jit(solution)/shard_map/ppermute | solution.py:889
  37.5 2.4 %layer_zero_feed_back.1.two = f32[512,512]{1,0:T(8,128)S(1)} custom-call(bf16[512,512]{1,0:T(8,128)(2,1)S(1)} %get-tuple-element.138.grad, bf16[512,2048]{1,0:T(8,128)(2,1)S(1)} %get-tuple-element.140.slope, bf16[2,512,2048]{2,1,0:T(8,128)(2,1)S(1)} %get-tuple-element.107.w_in, bf16[2,2048,512]{2,1,0:T(8,128)(2,1)S(1)} %get-tuple-element.118.w_out), custom_call_target="tpu_custom_call" | custom-call | flops 2147483648 | bytes 8388608 | tf_op jit(solution)/shard_map/layer_zero_feed_back/pallas_call | solution.py:54
  39.8 0.1 collective-permute-done.8
  40.0 1.6 %collective-permute-start.9 = (bf16[40,512]{1,0:T(8,128)(2,1)S(1)}, bf16[40,512]{1,0:T(8,128)(2,1)S(1)}, u32[]{:S(2)}, u32[]{:S(2)}) collective-permute-start(bf16[40,512]{1,0:T(8,128)(2,1)S(1)} %get-tuple-element.173), channel_id=1, source_target_pairs={{0,4},{4,0},{8,12},{12,8},{1,5},{5,1},{9,13},{13,9},{2,6},{6,2},{1... | collective-permute-start | bytes 122888 | tf_op jit(solution)/shard_map/ppermute | solution.py:889
  41.6 1.9 %layer_zero_norms.1 = (f32[512,512]{1,0:T(8,128)S(1)}, f32[512,512]{1,0:T(8,128)S(1)}) custom-call(bf16[512,512]{1,0:T(8,128)(2,1)S(1)} %get-tuple-element.111.x_ref, bf16[512,512]{1,0:T(8,128)(2,1)S(1)} %get-tuple-element.138.grad, f32[512,512]{1,0:T(8,128)S(1)} %layer_zero_feed_back.1.two, bf16[1536,512]{1,0:T(8,128)(2,1)S(1)} %layer_zero_attention_back.1.packed, ...), custom_call_target="tpu_custom_call" | custom-call | flops 805306368 | bytes 8388608 | tf_op jit(solution)/shard_map/layer_zero_norms/pallas_call | solution.py:54
  43.5 0.5 collective-permute-done.9
  44.1 2.7 %collective-permute-start.10 = (bf16[40,512]{1,0:T(8,128)(2,1)S(1)}, bf16[40,512]{1,0:T(8,128)(2,1)S(1)}, u32[]{:S(2)}, u32[]{:S(2)}) collective-permute-start(bf16[40,512]{1,0:T(8,128)(2,1)S(1)} %get-tuple-element.171), channel_id=1, source_target_pairs={{0,8},{4,12},{8,0},{12,4},{1,9},{5,13},{9,1},{13,5},{2,10},{6,14},... | collective-permute-start | bytes 122888 | tf_op jit(solution)/shard_map/ppermute | solution.py:889
  46.7 1.7 %place_outputs.1 = (bf16[1,2,1,512,512]{4,3,2,1,0:T(8,128)(2,1)}, f32[1,2,1,512,512]{4,3,2,1,0:T(8,128)}) custom-call(bf16[512,512]{1,0:T(8,128)(2,1)S(1)} %get-tuple-element.152.act, bf16[512,512]{1,0:T(8,128)(2,1)S(1)} %collective-permute-done.7.act_other, f32[512,512]{1,0:T(8,128)S(1)} %get-tuple-element.154.grad, ...), custom_call_target="tpu_custom_call" | custom-call | flops 524288 | bytes 8388608 | tf_op jit(solution)/shard_map/place_outputs/pallas_call | solution.py:54
  48.4 0.6 %collective-permute-done.10 = bf16[40,512]{1,0:T(8,128)(2,1)S(1)} collective-permute-done((bf16[40,512]{1,0:T(8,128)(2,1)S(1)}, bf16[40,512]{1,0:T(8,128)(2,1)S(1)}, u32[]{:S(2)}, u32[]{:S(2)}) %collective-permute-start.10) | collective-permute-done | bytes 40992 | tf_op jit(solution)/shard_map/ppermute | solution.py:889
  49.1 2.0 %reparam.1 = (f32[10,512]{1,0:T(8,128)}, f32[512,512]{1,0:T(8,128)}, f32[1,512]{1,0:T(1,128)}, f32[512,256]{1,0:T(8,128)}, f32[1,256]{1,0:T(1,128)}) custom-call(f32[40,512]{1,0:T(8,128)S(1)} %convert_add_fusion.refs_0_, f32[10,512]{1,0:T(8,128)S(1)} %get-tuple-element.162.refs_1_, f32[10,512]{1,0:T(8,128)S(1)} %copy-done, ...), custom_call_target="tpu_custom_call" | custom-call | flops 134217728 | bytes 8388608 | tf_op jit(solution)/shard_map/reparam/pallas_call | solution.py:54
  (18 shorter events, 0.2 us)
Async XLA Ops:
  0.6 5.9 %collective-permute-start.1 = (bf16[1,512,1536]{2,1,0:T(8,128)(2,1)}, bf16[1,512,1536]{2,1,0:T(8,128)(2,1)S(1)}, u32[]{:S(2)}, u32[]{:S(2)}) collective-permute-start(bf16[1,512,1536]{2,1,0:T(8,128)(2,1)} %qkv_hbm.1), channel_id=1, source_target_pairs={{0,16},{16,0},{1,17},{17,1},{2,18},{18,2},{3,19},{19,3},{4,20},{20... | collective-permute-start | bytes 4718600 | tf_op jit(solution)/shard_map/ppermute | solution.py:802
  2.0 4.4 %collective-permute-start = (f32[1,6656]{1,0:T(1,128)S(1)}, f32[1,6656]{1,0:T(1,128)S(1)}, u32[]{:S(2)}, u32[]{:S(2)}) collective-permute-start(f32[1,6656]{1,0:T(1,128)S(1)} %small_parameters.1.own_small), channel_id=1, source_target_pairs={{0,16},{16,0},{1,17},{17,1},{2,18},{18,2},{3,19},{19,3},{4,20},{20... | collective-permute-start | bytes 79880 | tf_op jit(solution)/shard_map/ppermute | solution.py:802
  2.2 10.5 %collective-permute-start.3 = (bf16[1,512,512]{2,1,0:T(8,128)(2,1)}, bf16[1,512,512]{2,1,0:T(8,128)(2,1)S(1)}, u32[]{:S(2)}, u32[]{:S(2)}) collective-permute-start(bf16[1,512,512]{2,1,0:T(8,128)(2,1)} %attn_hbm.1), channel_id=1, source_target_pairs={{0,16},{16,0},{1,17},{17,1},{2,18},{18,2},{3,19},{19,3},{4,20},{20... | collective-permute-start | bytes 1572872 | tf_op jit(solution)/shard_map/ppermute | solution.py:802
  2.6 7.4 %collective-permute-start.2 = (bf16[1,512,2048]{2,1,0:T(8,128)(2,1)}, bf16[1,512,2048]{2,1,0:T(8,128)(2,1)S(1)}, u32[]{:S(2)}, u32[]{:S(2)}) collective-permute-start(bf16[1,512,2048]{2,1,0:T(8,128)(2,1)} %ff_in_hbm.1), channel_id=1, source_target_pairs={{0,16},{16,0},{1,17},{17,1},{2,18},{18,2},{3,19},{19,3},{4,20},{20... | collective-permute-start | bytes 6291464 | tf_op jit(solution)/shard_map/ppermute | solution.py:802
  2.7 10.0 %collective-permute-start.4 = (bf16[1,2048,512]{2,1,0:T(8,128)(2,1)}, bf16[1,2048,512]{2,1,0:T(8,128)(2,1)S(1)}, u32[]{:S(2)}, u32[]{:S(2)}) collective-permute-start(bf16[1,2048,512]{2,1,0:T(8,128)(2,1)} %ff_out_hbm.1), channel_id=1, source_target_pairs={{0,16},{16,0},{1,17},{17,1},{2,18},{18,2},{3,19},{19,3},{4,20},{20... | collective-permute-start | bytes 6291464 | tf_op jit(solution)/shard_map/ppermute | solution.py:802
  28.3 1.8 %collective-permute-start.5 = (f32[40,512]{1,0:T(8,128)S(1)}, f32[40,512]{1,0:T(8,128)S(1)}, u32[]{:S(2)}, u32[]{:S(2)}) collective-permute-start(f32[40,512]{1,0:T(8,128)S(1)} %get-tuple-element.123), channel_id=1, source_target_pairs={{0,16},{16,0},{1,17},{17,1},{2,18},{18,2},{3,19},{19,3},{4,20},{20... | collective-permute-start | bytes 245768 | tf_op jit(solution)/shard_map/ppermute | solution.py:886
  30.1 5.8 %collective-permute-start.7 = (bf16[512,512]{1,0:T(8,128)(2,1)S(1)}, bf16[512,512]{1,0:T(8,128)(2,1)S(1)}, u32[]{:S(2)}, u32[]{:S(2)}) collective-permute-start(bf16[512,512]{1,0:T(8,128)(2,1)S(1)} %get-tuple-element.125), channel_id=1, source_target_pairs={{0,16},{16,0},{1,17},{17,1},{2,18},{18,2},{3,19},{19,3},{4,20},{20... | collective-permute-start | bytes 1572872 | tf_op jit(solution)/shard_map/ppermute | solution.py:802
  30.6 5.3 %collective-permute-start.6 = (bf16[40,512]{1,0:T(8,128)(2,1)S(1)}, bf16[40,512]{1,0:T(8,128)(2,1)S(1)}, u32[]{:S(2)}, u32[]{:S(2)}) collective-permute-start(bf16[40,512]{1,0:T(8,128)(2,1)S(1)} %get-tuple-element.177), channel_id=1, source_target_pairs={{0,1},{1,0},{2,3},{3,2},{4,5},{5,4},{6,7},{7,6},{8,9},{9,8},{10,11... | collective-permute-start | bytes 122888 | tf_op jit(solution)/shard_map/ppermute | solution.py:889
  35.9 4.1 %collective-permute-start.8 = (bf16[40,512]{1,0:T(8,128)(2,1)S(1)}, bf16[40,512]{1,0:T(8,128)(2,1)S(1)}, u32[]{:S(2)}, u32[]{:S(2)}) collective-permute-start(bf16[40,512]{1,0:T(8,128)(2,1)S(1)} %get-tuple-element.175), channel_id=1, source_target_pairs={{0,2},{1,3},{2,0},{3,1},{4,6},{5,7},{6,4},{7,5},{8,10},{9,11},{10,... | collective-permute-start | bytes 122888 | tf_op jit(solution)/shard_map/ppermute | solution.py:889
  40.0 4.1 %collective-permute-start.9 = (bf16[40,512]{1,0:T(8,128)(2,1)S(1)}, bf16[40,512]{1,0:T(8,128)(2,1)S(1)}, u32[]{:S(2)}, u32[]{:S(2)}) collective-permute-start(bf16[40,512]{1,0:T(8,128)(2,1)S(1)} %get-tuple-element.173), channel_id=1, source_target_pairs={{0,4},{4,0},{8,12},{12,8},{1,5},{5,1},{9,13},{13,9},{2,6},{6,2},{1... | collective-permute-start | bytes 122888 | tf_op jit(solution)/shard_map/ppermute | solution.py:889
  43.5 5.5 %copy-start = (f32[10,512]{1,0:T(8,128)S(1)}, f32[10,512]{1,0:T(8,128)}, u32[]{:S(2)}) copy-start(f32[10,512]{1,0:T(8,128)} %refs_2_) | copy-start | bytes 61444
  44.0 2.7 %collective-permute-start.11 = (f32[512,512]{1,0:T(8,128)S(1)}, f32[512,512]{1,0:T(8,128)S(1)}, u32[]{:S(2)}, u32[]{:S(2)}) collective-permute-start(f32[512,512]{1,0:T(8,128)S(1)} %get-tuple-element.155), channel_id=1, source_target_pairs={{0,16},{16,0},{1,17},{17,1},{2,18},{18,2},{3,19},{19,3},{4,20},{20... | collective-permute-start | bytes 3145736 | tf_op jit(solution)/shard_map/ppermute | solution.py:802
  44.1 5.0 %collective-permute-start.10 = (bf16[40,512]{1,0:T(8,128)(2,1)S(1)}, bf16[40,512]{1,0:T(8,128)(2,1)S(1)}, u32[]{:S(2)}, u32[]{:S(2)}) collective-permute-start(bf16[40,512]{1,0:T(8,128)(2,1)S(1)} %get-tuple-element.171), channel_id=1, source_target_pairs={{0,8},{4,12},{8,0},{12,4},{1,9},{5,13},{9,1},{13,5},{2,10},{6,14},... | collective-permute-start | bytes 122888 | tf_op jit(solution)/shard_map/ppermute | solution.py:889

commit v7 on v6

--- a/solution.py
+++ b/solution.py
@@ -35,10 +35,9 @@
 NT = (((1,), (1,)), ((), ()))
 TN = (((0,), (0,)), ((), ()))
 
-NO_COPIES = ((),) * 4
 MIB = 1024 * 1024
 EARLY_MIB = 24
-MIDDLE_MIB = 22
+MIDDLE_MIB = 23
 LATE_MIB = 12
 
 G1, B1, G2, B2, B_ATTN, B_OUT, B_QKV, B_IN = 0, 1, 2, 3, 4, 5, 6, 9
@@ -356,27 +355,54 @@
     packed_t[2 * D :, :] = dv_ref[...].astype(bf16)
 
 
-def gelu_both(before):
-    cdf = 0.5 + 0.5 * lax.erf(before * (0.5**0.5))
-    density = jnp.exp2(before * before * (-0.5 * LOG2E)) * (1.0 / math.sqrt(2.0 * math.pi))
-    return before * cdf, cdf + before * density
+ROOT_HALF = 0.5**0.5
+
+
+def gelu_both(scaled):
+    cdf = ROOT_HALF + ROOT_HALF * lax.erf(scaled)
+    density = jnp.exp2(scaled * scaled * (-LOG2E)) * (2.0 / math.sqrt(2.0 * math.pi))
+    return scaled * cdf, cdf + scaled * density
 
 
 FF_CHUNK = 512
+FF_ROWS = 256
+
+
+def second_norm(hat, small_ref):
+    gain = small_row(small_ref, G2) * ROOT_HALF
+    return (hat * gain + small_row(small_ref, B2) * ROOT_HALF).astype(bf16)
 
 
 def chunk_of(index):
     return slice(index * FF_CHUNK, (index + 1) * FF_CHUNK)
 
 
-def feed_in(normed, w_ref, small_ref, act_ref, slope_ref, arrivals):
+def feed_in(normed, w_ref, small_ref, act_ref, slope_ref):
     for chunk in range(FF // FF_CHUNK):
         cols = chunk_of(chunk)
-        wait_all(*arrivals[chunk])
-        before = dot(normed, w_ref[:, cols], NN) + small_row(small_ref, B_IN + chunk)
-        act, slope = gelu_both(before)
-        act_ref[:, cols] = act.astype(bf16)
-        slope_ref[:, cols] = slope.astype(bf16)
+        bias = small_row(small_ref, B_IN + chunk) * ROOT_HALF
+        for start in range(0, SEQ, FF_ROWS):
+            rows = slice(start, start + FF_ROWS)
+            act, slope = gelu_both(dot(normed[rows], w_ref[:, cols], NN) + bias)
+            act_ref[rows, cols] = act.astype(bf16)
+            slope_ref[rows, cols] = slope.astype(bf16)
+
+
+def feed_both(normed, grad, w_in, w_out, small_ref, act_ref):
+    total = jnp.zeros((SEQ, D), f32)
+    for chunk in range(FF // FF_CHUNK):
+        cols = chunk_of(chunk)
+        bias = small_row(small_ref, B_IN + chunk) * ROOT_HALF
+        slopes = []
+        for start in range(0, SEQ, FF_ROWS):
+            rows = slice(start, start + FF_ROWS)
+            act, slope = gelu_both(dot(normed[rows], w_in[:, cols], NN) + bias)
+            act_ref[rows, cols] = act.astype(bf16)
+            slopes.append(slope.astype(bf16))
+        grad_act = dot(grad, w_out[cols, :], NT)
+        grad_before = (grad_act * jnp.concatenate(slopes, axis=0).astype(f32)).astype(bf16)
+        total = total + dot(grad_before, w_in[:, cols], NT)
+    return total * ROOT_HALF
 
 
 def layer_result(hidden, mixed_t, w_attn, act_ref, w_out, small_ref):
@@ -385,23 +411,21 @@
     return hidden + attn_out + ff_out
 
 
-def feed_back(grad, w_out, w_in, slope_ref, arrivals):
+def feed_back(grad, w_out, w_in, slope_ref):
     total = jnp.zeros((SEQ, D), f32)
     for chunk in range(FF // FF_CHUNK):
         cols = chunk_of(chunk)
-        wait_all(*arrivals[chunk])
         grad_act = dot(grad, w_out[cols, :], NT)
         grad_before = (grad_act * slope_ref[:, cols].astype(f32)).astype(bf16)
         total = total + dot(grad_before, w_in[:, cols], NT)
-    return total
-
-
-def norms_back(grad, hidden, grad_two, packed_t, w_qkv, small_ref):
+    return total * ROOT_HALF
+
+
+def norms_back(grad, hat, scale, grad_two, packed_t, w_qkv, small_ref):
     grad_one = jnp.transpose(dot(w_qkv, packed_t, NN))
     grad_hat = (
         grad_one * small_row(small_ref, G1) + grad_two * small_row(small_ref, G2)
     )
-    hat, scale = normalized(hidden)
     mean_one = jnp.mean(grad_hat, axis=-1, keepdims=True)
     mean_two = jnp.mean(grad_hat * hat, axis=-1, keepdims=True)
     return grad.astype(f32) + scale * (grad_hat - mean_one - hat * mean_two)
@@ -563,7 +587,7 @@
     hat = hat_ref[...]
     zero = small.at[0]
     normed = (hat * small_row(zero, G1) + small_row(zero, B1)).astype(bf16)
-    two_ref[...] = (hat * small_row(zero, G2) + small_row(zero, B2)).astype(bf16)
+    two_ref[...] = second_norm(hat, zero)
     project_heads(normed, w_qkv.at[0], zero, tables[:8, :], tables[8:, :], q_t, k_t, k_m, v_m, v_t)
     attend(q_t, k_m, v_t, low.at[0], low.at[1], mask, p_ref, pp_ref, inv_ref, mixed_ref)
     wait_all(*later)
@@ -578,7 +602,7 @@
 
 def feed_kernel(two, small, other_in, w_in_before, act_ref, slope_ref, w_in, sems):
     wait_all(Copies(sems).start(other_in.at[0], w_in.at[1 - lax.axis_index("pipe")]))
-    feed_in(two[...], w_in.at[0], small.at[0], act_ref, slope_ref, NO_COPIES)
+    feed_in(two[...], w_in.at[0], small.at[0], act_ref, slope_ref)
 
 
 def feed_call(*arrays):
@@ -611,7 +635,7 @@
                   other_attn, other_out, cot_ref, x_ref, act_zero, low, mask, tables,
                   h_one, act_one, mixed_one, grad_one, grad_low, scaled_zero, inner_zero, pre_ds_zero,
                   prefix_grad, w_attn, w_out,
-                  q_t, k_t, v_m, p_ref, pp_ref, inv_ref, scaled, inner, pre_ds, turned, slope_one, k_m, v_t,
+                  q_t, k_t, v_m, p_ref, pp_ref, inv_ref, scaled, inner, pre_ds, turned, k_m, v_t,
                   dq, dk, dv, packed, sems):
     section = lax.axis_index("pipe")
     copies = Copies(sems)
@@ -625,20 +649,20 @@
     ).astype(bf16)
 
     cos, sin = tables[:8, :], tables[8:, :]
-    hat, _ = normalized(h_one[...].astype(f32))
+    hat, scale = normalized(h_one[...].astype(f32))
+    grad_one[...] = hat
     normed = (hat * small_row(small_one, G1) + small_row(small_one, B1)).astype(bf16)
-    two = (hat * small_row(small_one, G2) + small_row(small_one, B2)).astype(bf16)
+    two = second_norm(hat, small_one)
     project_heads(normed, w_qkv.at[1], small_one, cos, sin, q_t, k_t, k_m, v_m, v_t)
     attend(q_t, k_m, v_t, low.at[2], low.at[3], mask, p_ref, pp_ref, inv_ref, mixed_one)
-    feed_in(two, w_in.at[1], small_one, act_one, slope_one, NO_COPIES)
 
     grad = cot_ref[...]
-    grad_two = feed_back(grad, w_out.at[1], w_in.at[1], slope_one, NO_COPIES)
+    grad_two = feed_both(two, grad, w_in.at[1], w_out.at[1], small_one, act_one)
     prefix_back(w_attn.at[1], grad, q_t, low.at[3], pp_ref, inv_ref, mixed_one, scaled, inner, pre_ds, turned,
                 prefix_grad, 2 * PREFIX)
     attend_back(scaled, inner, pre_ds, q_t, k_t, v_m, low.at[2], p_ref, dq, dk, dv)
     pack_grads(dq, dk, dv, cos, sin, packed)
-    result = norms_back(grad, h_one[...].astype(f32), grad_two, packed[...], w_qkv[1], small_one)
+    result = norms_back(grad, grad_one[...], scale, grad_two, packed[...], w_qkv[1], small_one)
     grad_one[...] = result
     grad_low[...] = result.astype(bf16)
 
@@ -652,7 +676,6 @@
         ((HEADS, SEQ), f32),
         ((PAIRS, 2 * PAD, SEQ), bf16),
         ((D, SEQ), bf16),
-        ((SEQ, FF), bf16),
         ((SEQ, D), bf16),
         ((D, SEQ), bf16),
         ((D, SEQ), f32),
@@ -702,7 +725,7 @@
 
 
 def feed_back_kernel(grad, slope, w_in, w_out, total):
-    total[...] = feed_back(grad[...], w_out.at[0], w_in.at[0], slope, NO_COPIES)
+    total[...] = feed_back(grad[...], w_out.at[0], w_in.at[0], slope)
 
 
 def feed_back_call(*arrays):
@@ -714,9 +737,8 @@
 
 
 def norms_kernel(x_ref, grad, two, packed, grad_one, small, w_qkv, keep, send, result, sems):
-    result[...] = norms_back(
-        grad[...], x_ref[...].astype(f32), two[...], packed[...], w_qkv[0], small.at[0]
-    )
+    hat, scale = normalized(x_ref[...].astype(f32))
+    result[...] = norms_back(grad[...], hat, scale, two[...], packed[...], w_qkv[0], small.at[0])
     hand_over((result, grad_one), keep, send, sems)
 
 

time: 51.4 us -> 50.7 us (0.986)
  Pallas kernels: 38.2 us -> 37.4 us
    pallas_call x11, Pallas kernels: 38.2 us -> 37.4 us  [call_kernel(): pl.pallas_call(kernel, name=name, out_shape=[space(shape, dtype) for spac...]
where the time goes in v7:
time: 50.7 us; the launch traced here: 50.5 us
  Pallas kernels  37.4 us (74%)
  starting transfers between devices  10.8 us (21%)
  waiting for transfers between devices  1.27 us (3%)
  between operations  1 us (2%)
    pallas_call x11, Pallas kernels, call_kernel(): pl.pallas_call(kernel, name=name, out_shape=[space(shape, dtype) for spac...  37.4 us
    ppermute x4, starting transfers between devices, local(): moved = lax.ppermute(prefix_grad.astype(bf16), axis, pairs)  8.51 us
    ppermute x7, starting transfers between devices, swapped(): return lax.ppermute(array_in, 'pipe', [(0, 1), (1, 0)])  2.09 us
    ppermute x4, waiting for transfers between devices, local(): moved = lax.ppermute(prefix_grad.astype(bf16), axis, pairs)  1.25 us
  transfers between devices with their start and end apart: 12, of which 3 were waited for; matrix products, arithmetic and copies ran while one was open for 0% of the time, Pallas kernels for 40%

profile of v7, /device:TPU:0, one launch (start us, length us, event | category | flops | bytes accessed | tf_op | source)
XLA Modules:
  0.0 50.5 jit_solution(7520788471708856705)
XLA Ops:
  0.6 0.5 %collective-permute-start.1 = (bf16[1,512,1536]{2,1,0:T(8,128)(2,1)}, bf16[1,512,1536]{2,1,0:T(8,128)(2,1)S(1)}, u32[]{:S(2)}, u32[]{:S(2)}) collective-permute-start(bf16[1,512,1536]{2,1,0:T(8,128)(2,1)} %qkv_hbm.1), channel_id=1, source_target_pairs={{0,16},{16,0},{1,17},{17,1},{2,18},{18,2},{3,19},{19,3},{4,20},{20... | collective-permute-start | bytes 4718600 | tf_op jit(solution)/shard_map/ppermute | solution.py:824
  1.2 0.9 %small_parameters.1.own_small = f32[1,6656]{1,0:T(1,128)S(1)} custom-call(f32[1,512]{1,0:T(1,128)} %gain_one.1, f32[1,512]{1,0:T(1,128)} %shift_one.1, f32[1,512]{1,0:T(1,128)} %gain_two.1, f32[1,512]{1,0:T(1,128)} %shift_two.1, f32[1,512]{1,0:T(1,128)} %attn_b.1, f32[1,512]{1,0:T(1,128)} %out_b.1, f32[1,1536]{1,0:T(1,128)} %qkv_b.1, f32[1,2048]{1,0:T(1,128)} %in_b.1), custom_call_target="tpu_custom_call" | custom-call | flops 6656 | bytes 8388608 | tf_op jit(solution)/shard_map/small_parameters/pallas_call | solution.py:53
  2.0 0.1 collective-permute-start
  2.2 0.5 collective-permute-start.3
  2.7 0.4 collective-permute-start.4
  3.1 3.3 %opening.1 = (bf16[512,512]{1,0:T(8,128)(2,1)S(1)}, f32[512,512]{1,0:T(8,128)S(1)}, f32[1152,128]{1,0:T(8,128)S(1)}, bf16[4,32,512]{2,1,0:T(8,128)(2,1)S(1)}, f3...) custom-call(bf16[2,1,512,512]{3,2,1,0:T(8,128)(2,1)} %x_hbm.1, ...), custom_call_target="tpu_custom_call" | custom-call | flops 251658240 | bytes 8388608 | tf_op jit(solution)/shard_map/opening/pallas_call | solution.py:53
  6.5 3.5 %first_attention.1 = (bf16[512,512]{1,0:T(8,128)(2,1)S(1)}, bf16[512,512]{1,0:T(8,128)(2,1)S(1)}, bf16[512,512]{1,0:T(8,128)(2,1)S(1)}, bf16[4,1152,256]{2,1,0:T...) custom-call(f32[1,6656]{1,0:T(1,128)S(1)} %small_parameters.1.own_sm, ...), custom_call_target="tpu_custom_call" | custom-call | flops 80530636800 | bytes 8388608 | tf_op jit(solution)/shard_map/first_attention/pallas_call | solution.py:53
  10.0 2.4 %first_feed.1 = (bf16[512,2048]{1,0:T(8,128)(2,1)S(1)}, bf16[512,2048]{1,0:T(8,128)(2,1)S(1)}, bf16[2,512,2048]{2,1,0:T(8,128)(2,1)S(1)}) custom-call(bf16[512,512]{1,0:T(8,128)(2,1)S(1)} %get-tuple-element.104.two, f32[2,1,6656]{2,1,0:T(1,128)S(1)} %get-tuple-element.102.small, ...), custom_call_target="tpu_custom_call", output_to_operand_aliasing={{2}: (3, {})} | custom-call | flops 1073741824 | bytes 8388608 | tf_op jit(solution)/shard_map/first_feed/pallas_call | solution.py:53
  12.4 15.0 %middle.1 = (bf16[512,512]{1,0:T(8,128)(2,1)S(1)}, bf16[512,2048]{1,0:T(8,128)(2,1)S(1)}, bf16[512,512]{1,0:T(8,128)(2,1)S(1)}, f32[512,512]{1,0:T(8,128)S(1)}, ...) custom-call(bf16[2,512,512]{2,1,0:T(8,128)(2,1)S(1)} %get-tuple-elem, ...), custom_call_target="tpu_custom_call", output_to_operand_aliasing={{9}: (0, {}), {10}: (1, {})} | custom-call | flops 16106127360 | bytes 8388608 | tf_op jit(solution)/shard_map/middle/pallas_call | solution.py:53
  27.5 0.2 collective-permute-start.5
  27.6 1.6 %layer_one_out.1 = (bf16[512,512]{1,0:T(8,128)(2,1)S(1)}, bf16[512,512]{1,0:T(8,128)(2,1)S(1)}) custom-call(bf16[512,512]{1,0:T(8,128)(2,1)S(1)} %get-tuple-element.114.h_one, bf16[512,2048]{1,0:T(8,128)(2,1)S(1)} %get-tuple-element.115.act, bf16[512,512]{1,0:T(8,128)(2,1)S(1)} %get-tuple-element.116.mixed, f32[2,1,6656]{2,1,0:T(1,128)S(1)} %get-tuple-element.102.small, ...), custom_call_target="tpu_custom_call" | custom-call | flops 1342177280 | bytes 8388608 | tf_op jit(solution)/shard_map/layer_one_out/pallas_call | solution.py:53
  29.3 0.5 collective-permute-start.7
  29.8 2.6 %collective-permute-start.6 = (bf16[40,512]{1,0:T(8,128)(2,1)S(1)}, bf16[40,512]{1,0:T(8,128)(2,1)S(1)}, u32[]{:S(2)}, u32[]{:S(2)}) collective-permute-start(bf16[40,512]{1,0:T(8,128)(2,1)S(1)} %get-tuple-element.177), channel_id=1, source_target_pairs={{0,1},{1,0},{2,3},{3,2},{4,5},{5,4},{6,7},{7,6},{8,9},{9,8},{10,11... | collective-permute-start | bytes 122888 | tf_op jit(solution)/shard_map/ppermute | solution.py:911
  32.4 2.7 %layer_zero_attention_back.1.packed = bf16[1536,512]{1,0:T(8,128)(2,1)S(1)} custom-call(bf16[512,512]{1,0:T(8,128)(2,1)S(1)} %get-tuple-element.128.scaled, f32[8,512]{1,0:T(8,128)S(1)} %get-tuple-element.129.inner, bf16[4,32,512]{2,1,0:T(8,128)(2,1)S(1)} %get-tuple-element.130.pre_ds, bf16[512,512]{1,0:T(8,128)(2,1)S(1)} %get-tuple-element.98.q0.q_t, ...), custom_call_target="tpu_custom_call" | custom-call | flops 1342177280 | bytes 8388608 | tf_op jit(solution)/shard_map/layer_zero_attention_back/pallas_call | solution.py:53
  35.1 1.6 %collective-permute-start.8 = (bf16[40,512]{1,0:T(8,128)(2,1)S(1)}, bf16[40,512]{1,0:T(8,128)(2,1)S(1)}, u32[]{:S(2)}, u32[]{:S(2)}) collective-permute-start(bf16[40,512]{1,0:T(8,128)(2,1)S(1)} %get-tuple-element.175), channel_id=1, source_target_pairs={{0,2},{1,3},{2,0},{3,1},{4,6},{5,7},{6,4},{7,5},{8,10},{9,11},{10,... | collective-permute-start | bytes 122888 | tf_op jit(solution)/shard_map/ppermute | solution.py:911
  36.7 2.4 %layer_zero_feed_back.1.two = f32[512,512]{1,0:T(8,128)S(1)} custom-call(bf16[512,512]{1,0:T(8,128)(2,1)S(1)} %get-tuple-element.138.grad, bf16[512,2048]{1,0:T(8,128)(2,1)S(1)} %get-tuple-element.140.slope, bf16[2,512,2048]{2,1,0:T(8,128)(2,1)S(1)} %get-tuple-element.107.w_in, bf16[2,2048,512]{2,1,0:T(8,128)(2,1)S(1)} %get-tuple-element.118.w_out), custom_call_target="tpu_custom_call" | custom-call | flops 2147483648 | bytes 8388608 | tf_op jit(solution)/shard_map/layer_zero_feed_back/pallas_call | solution.py:53
  39.1 0.1 collective-permute-done.8
  39.2 1.6 %collective-permute-start.9 = (bf16[40,512]{1,0:T(8,128)(2,1)S(1)}, bf16[40,512]{1,0:T(8,128)(2,1)S(1)}, u32[]{:S(2)}, u32[]{:S(2)}) collective-permute-start(bf16[40,512]{1,0:T(8,128)(2,1)S(1)} %get-tuple-element.173), channel_id=1, source_target_pairs={{0,4},{4,0},{8,12},{12,8},{1,5},{5,1},{9,13},{13,9},{2,6},{6,2},{1... | collective-permute-start | bytes 122888 | tf_op jit(solution)/shard_map/ppermute | solution.py:911
  40.8 1.9 %layer_zero_norms.1 = (f32[512,512]{1,0:T(8,128)S(1)}, f32[512,512]{1,0:T(8,128)S(1)}) custom-call(bf16[512,512]{1,0:T(8,128)(2,1)S(1)} %get-tuple-element.111.x_ref, bf16[512,512]{1,0:T(8,128)(2,1)S(1)} %get-tuple-element.138.grad, f32[512,512]{1,0:T(8,128)S(1)} %layer_zero_feed_back.1.two, bf16[1536,512]{1,0:T(8,128)(2,1)S(1)} %layer_zero_attention_back.1.packed, ...), custom_call_target="tpu_custom_call" | custom-call | flops 805306368 | bytes 8388608 | tf_op jit(solution)/shard_map/layer_zero_norms/pallas_call | solution.py:53
  42.8 0.5 %collective-permute-done.9 = bf16[40,512]{1,0:T(8,128)(2,1)S(1)} collective-permute-done((bf16[40,512]{1,0:T(8,128)(2,1)S(1)}, bf16[40,512]{1,0:T(8,128)(2,1)S(1)}, u32[]{:S(2)}, u32[]{:S(2)}) %collective-permute-start.9) | collective-permute-done | bytes 40992 | tf_op jit(solution)/shard_map/ppermute | solution.py:911
  43.3 2.6 %collective-permute-start.10 = (bf16[40,512]{1,0:T(8,128)(2,1)S(1)}, bf16[40,512]{1,0:T(8,128)(2,1)S(1)}, u32[]{:S(2)}, u32[]{:S(2)}) collective-permute-start(bf16[40,512]{1,0:T(8,128)(2,1)S(1)} %get-tuple-element.171), channel_id=1, source_target_pairs={{0,8},{4,12},{8,0},{12,4},{1,9},{5,13},{9,1},{13,5},{2,10},{6,14},... | collective-permute-start | bytes 122888 | tf_op jit(solution)/shard_map/ppermute | solution.py:911
  45.9 1.7 %place_outputs.1 = (bf16[1,2,1,512,512]{4,3,2,1,0:T(8,128)(2,1)}, f32[1,2,1,512,512]{4,3,2,1,0:T(8,128)}) custom-call(bf16[512,512]{1,0:T(8,128)(2,1)S(1)} %get-tuple-element.152.act, bf16[512,512]{1,0:T(8,128)(2,1)S(1)} %collective-permute-done.7.act_other, f32[512,512]{1,0:T(8,128)S(1)} %get-tuple-element.154.grad, ...), custom_call_target="tpu_custom_call" | custom-call | flops 524288 | bytes 8388608 | tf_op jit(solution)/shard_map/place_outputs/pallas_call | solution.py:53
  47.6 0.6 %collective-permute-done.10 = bf16[40,512]{1,0:T(8,128)(2,1)S(1)} collective-permute-done((bf16[40,512]{1,0:T(8,128)(2,1)S(1)}, bf16[40,512]{1,0:T(8,128)(2,1)S(1)}, u32[]{:S(2)}, u32[]{:S(2)}) %collective-permute-start.10) | collective-permute-done | bytes 40992 | tf_op jit(solution)/shard_map/ppermute | solution.py:911
  48.3 2.0 %reparam.1 = (f32[10,512]{1,0:T(8,128)}, f32[512,512]{1,0:T(8,128)}, f32[1,512]{1,0:T(1,128)}, f32[512,256]{1,0:T(8,128)}, f32[1,256]{1,0:T(1,128)}) custom-call(f32[40,512]{1,0:T(8,128)S(1)} %convert_add_fusion.refs_0_, f32[10,512]{1,0:T(8,128)S(1)} %get-tuple-element.162.refs_1_, f32[10,512]{1,0:T(8,128)S(1)} %copy-done, ...), custom_call_target="tpu_custom_call" | custom-call | flops 134217728 | bytes 8388608 | tf_op jit(solution)/shard_map/reparam/pallas_call | solution.py:53
  (18 shorter events, 0.2 us)
Async XLA Ops:
  0.6 5.9 %collective-permute-start.1 = (bf16[1,512,1536]{2,1,0:T(8,128)(2,1)}, bf16[1,512,1536]{2,1,0:T(8,128)(2,1)S(1)}, u32[]{:S(2)}, u32[]{:S(2)}) collective-permute-start(bf16[1,512,1536]{2,1,0:T(8,128)(2,1)} %qkv_hbm.1), channel_id=1, source_target_pairs={{0,16},{16,0},{1,17},{17,1},{2,18},{18,2},{3,19},{19,3},{4,20},{20... | collective-permute-start | bytes 4718600 | tf_op jit(solution)/shard_map/ppermute | solution.py:824
  2.0 4.4 %collective-permute-start = (f32[1,6656]{1,0:T(1,128)S(1)}, f32[1,6656]{1,0:T(1,128)S(1)}, u32[]{:S(2)}, u32[]{:S(2)}) collective-permute-start(f32[1,6656]{1,0:T(1,128)S(1)} %small_parameters.1.own_small), channel_id=1, source_target_pairs={{0,16},{16,0},{1,17},{17,1},{2,18},{18,2},{3,19},{19,3},{4,20},{20... | collective-permute-start | bytes 79880 | tf_op jit(solution)/shard_map/ppermute | solution.py:824
  2.2 10.2 %collective-permute-start.3 = (bf16[1,512,512]{2,1,0:T(8,128)(2,1)}, bf16[1,512,512]{2,1,0:T(8,128)(2,1)S(1)}, u32[]{:S(2)}, u32[]{:S(2)}) collective-permute-start(bf16[1,512,512]{2,1,0:T(8,128)(2,1)} %attn_hbm.1), channel_id=1, source_target_pairs={{0,16},{16,0},{1,17},{17,1},{2,18},{18,2},{3,19},{19,3},{4,20},{20... | collective-permute-start | bytes 1572872 | tf_op jit(solution)/shard_map/ppermute | solution.py:824
  2.6 7.4 %collective-permute-start.2 = (bf16[1,512,2048]{2,1,0:T(8,128)(2,1)}, bf16[1,512,2048]{2,1,0:T(8,128)(2,1)S(1)}, u32[]{:S(2)}, u32[]{:S(2)}) collective-permute-start(bf16[1,512,2048]{2,1,0:T(8,128)(2,1)} %ff_in_hbm.1), channel_id=1, source_target_pairs={{0,16},{16,0},{1,17},{17,1},{2,18},{18,2},{3,19},{19,3},{4,20},{20... | collective-permute-start | bytes 6291464 | tf_op jit(solution)/shard_map/ppermute | solution.py:824
  2.7 9.7 %collective-permute-start.4 = (bf16[1,2048,512]{2,1,0:T(8,128)(2,1)}, bf16[1,2048,512]{2,1,0:T(8,128)(2,1)S(1)}, u32[]{:S(2)}, u32[]{:S(2)}) collective-permute-start(bf16[1,2048,512]{2,1,0:T(8,128)(2,1)} %ff_out_hbm.1), channel_id=1, source_target_pairs={{0,16},{16,0},{1,17},{17,1},{2,18},{18,2},{3,19},{19,3},{4,20},{20... | collective-permute-start | bytes 6291464 | tf_op jit(solution)/shard_map/ppermute | solution.py:824
  27.5 1.8 %collective-permute-start.5 = (f32[40,512]{1,0:T(8,128)S(1)}, f32[40,512]{1,0:T(8,128)S(1)}, u32[]{:S(2)}, u32[]{:S(2)}) collective-permute-start(f32[40,512]{1,0:T(8,128)S(1)} %get-tuple-element.123), channel_id=1, source_target_pairs={{0,16},{16,0},{1,17},{17,1},{2,18},{18,2},{3,19},{19,3},{4,20},{20... | collective-permute-start | bytes 245768 | tf_op jit(solution)/shard_map/ppermute | solution.py:908
  29.3 5.8 %collective-permute-start.7 = (bf16[512,512]{1,0:T(8,128)(2,1)S(1)}, bf16[512,512]{1,0:T(8,128)(2,1)S(1)}, u32[]{:S(2)}, u32[]{:S(2)}) collective-permute-start(bf16[512,512]{1,0:T(8,128)(2,1)S(1)} %get-tuple-element.125), channel_id=1, source_target_pairs={{0,16},{16,0},{1,17},{17,1},{2,18},{18,2},{3,19},{19,3},{4,20},{20... | collective-permute-start | bytes 1572872 | tf_op jit(solution)/shard_map/ppermute | solution.py:824
  29.8 5.3 %collective-permute-start.6 = (bf16[40,512]{1,0:T(8,128)(2,1)S(1)}, bf16[40,512]{1,0:T(8,128)(2,1)S(1)}, u32[]{:S(2)}, u32[]{:S(2)}) collective-permute-start(bf16[40,512]{1,0:T(8,128)(2,1)S(1)} %get-tuple-element.177), channel_id=1, source_target_pairs={{0,1},{1,0},{2,3},{3,2},{4,5},{5,4},{6,7},{7,6},{8,9},{9,8},{10,11... | collective-permute-start | bytes 122888 | tf_op jit(solution)/shard_map/ppermute | solution.py:911
  35.1 4.1 %collective-permute-start.8 = (bf16[40,512]{1,0:T(8,128)(2,1)S(1)}, bf16[40,512]{1,0:T(8,128)(2,1)S(1)}, u32[]{:S(2)}, u32[]{:S(2)}) collective-permute-start(bf16[40,512]{1,0:T(8,128)(2,1)S(1)} %get-tuple-element.175), channel_id=1, source_target_pairs={{0,2},{1,3},{2,0},{3,1},{4,6},{5,7},{6,4},{7,5},{8,10},{9,11},{10,... | collective-permute-start | bytes 122888 | tf_op jit(solution)/shard_map/ppermute | solution.py:911
  39.2 4.1 %collective-permute-start.9 = (bf16[40,512]{1,0:T(8,128)(2,1)S(1)}, bf16[40,512]{1,0:T(8,128)(2,1)S(1)}, u32[]{:S(2)}, u32[]{:S(2)}) collective-permute-start(bf16[40,512]{1,0:T(8,128)(2,1)S(1)} %get-tuple-element.173), channel_id=1, source_target_pairs={{0,4},{4,0},{8,12},{12,8},{1,5},{5,1},{9,13},{13,9},{2,6},{6,2},{1... | collective-permute-start | bytes 122888 | tf_op jit(solution)/shard_map/ppermute | solution.py:911
  42.7 5.5 %copy-start = (f32[10,512]{1,0:T(8,128)S(1)}, f32[10,512]{1,0:T(8,128)}, u32[]{:S(2)}) copy-start(f32[10,512]{1,0:T(8,128)} %refs_2_) | copy-start | bytes 61444
  43.3 2.7 %collective-permute-start.11 = (f32[512,512]{1,0:T(8,128)S(1)}, f32[512,512]{1,0:T(8,128)S(1)}, u32[]{:S(2)}, u32[]{:S(2)}) collective-permute-start(f32[512,512]{1,0:T(8,128)S(1)} %get-tuple-element.155), channel_id=1, source_target_pairs={{0,16},{16,0},{1,17},{17,1},{2,18},{18,2},{3,19},{19,3},{4,20},{20... | collective-permute-start | bytes 3145736 | tf_op jit(solution)/shard_map/ppermute | solution.py:824
  43.3 5.0 %collective-permute-start.10 = (bf16[40,512]{1,0:T(8,128)(2,1)S(1)}, bf16[40,512]{1,0:T(8,128)(2,1)S(1)}, u32[]{:S(2)}, u32[]{:S(2)}) collective-permute-start(bf16[40,512]{1,0:T(8,128)(2,1)S(1)} %get-tuple-element.171), channel_id=1, source_target_pairs={{0,8},{4,12},{8,0},{12,4},{1,9},{5,13},{9,1},{13,5},{2,10},{6,14},... | collective-permute-start | bytes 122888 | tf_op jit(solution)/shard_map/ppermute | solution.py:911

commit v8 on v7

--- a/solution.py
+++ b/solution.py
@@ -377,10 +377,11 @@
     return slice(index * FF_CHUNK, (index + 1) * FF_CHUNK)
 
 
-def feed_in(normed, w_ref, small_ref, act_ref, slope_ref):
+def feed_in(normed, w_ref, small_ref, act_ref, slope_ref, between):
     for chunk in range(FF // FF_CHUNK):
         cols = chunk_of(chunk)
         bias = small_row(small_ref, B_IN + chunk) * ROOT_HALF
+        between(chunk)
         for start in range(0, SEQ, FF_ROWS):
             rows = slice(start, start + FF_ROWS)
             act, slope = gelu_both(dot(normed[rows], w_ref[:, cols], NN) + bias)
@@ -421,14 +422,17 @@
     return total * ROOT_HALF
 
 
-def norms_back(grad, hat, scale, grad_two, packed_t, w_qkv, small_ref):
-    grad_one = jnp.transpose(dot(w_qkv, packed_t, NN))
-    grad_hat = (
-        grad_one * small_row(small_ref, G1) + grad_two * small_row(small_ref, G2)
-    )
-    mean_one = jnp.mean(grad_hat, axis=-1, keepdims=True)
-    mean_two = jnp.mean(grad_hat * hat, axis=-1, keepdims=True)
-    return grad.astype(f32) + scale * (grad_hat - mean_one - hat * mean_two)
+def norms_back(grad, hat, scale, grad_two, packed_t, w_qkv, small_ref, out_ref):
+    halves_of = [slice(start, start + FF_ROWS) for start in range(0, SEQ, FF_ROWS)]
+    products = [dot(w_qkv, packed_t[:, tokens], NN) for tokens in halves_of]
+    for tokens, product in zip(halves_of, products):
+        here = hat[tokens, :]
+        grad_hat = jnp.transpose(product) * small_row(small_ref, G1)
+        grad_hat = grad_hat + grad_two[tokens, :] * small_row(small_ref, G2)
+        mean_one = jnp.mean(grad_hat, axis=-1, keepdims=True)
+        mean_two = jnp.mean(grad_hat * here, axis=-1, keepdims=True)
+        change = scale[tokens] * (grad_hat - mean_one - here * mean_two)
+        out_ref[tokens, :] = grad[tokens, :].astype(f32) + change
 
 
 def halves(values):
@@ -476,28 +480,36 @@
     return packed
 
 
-def prefix_states(embed, up_w, up_b, out_w, out_b, arrivals, hidden, low, wide, up_high, up_rest):
-    units = jnp.tanh(few_rows_dot(embed[...], up_w[...])[:PREFIX] + up_b[...])
-    hidden[...] = units
-    up_high[...], up_rest[...] = halves(jnp.transpose(up_w[...]))
+def prefix_state(units, layer, part, out_w, out_b, low, wide):
     real = lax.broadcasted_iota(jnp.int32, (PAD, 1), 0) < PREFIX
     first_head = lax.rem(lax.broadcasted_iota(jnp.int32, (1, D), 1), BLK) < HD
-    for part in range(4):
-        cols = slice(part * D, (part + 1) * D)
-        arrivals[part].wait()
-        states = jnp.where(real, few_rows_dot(units, out_w[:, cols]) + out_b[:, cols], 0.0)
-        low[part, :PAD, :] = jnp.where(first_head, states, 0.0).astype(bf16)
-        low[part, PAD:, :] = jnp.where(first_head, 0.0, states).astype(bf16)
-        wide[cols, :] = jnp.transpose(out_w[:, cols].astype(bf16))
+    cols = slice(part * D, (part + 1) * D)
+    bias = out_b[:, (2 * layer + part) * D : (2 * layer + part + 1) * D]
+    high, rest = halves(padded(units))
+    wide[:, cols] = out_w[:, cols].astype(bf16)
+    both = dot(jnp.concatenate([high, rest], axis=0), wide[:, cols], NN)
+    states = jnp.where(real, both[:PAD] + both[PAD:] + bias, 0.0)
+    low[part, :PAD, :] = jnp.where(first_head, states, 0.0).astype(bf16)
+    low[part, PAD:, :] = jnp.where(first_head, 0.0, states).astype(bf16)
+
+
+def layer_parts(copies, layer, out_hbm, out_w):
+    return [
+        copies.start(
+            out_hbm.at[:, (2 * layer + part) * D : (2 * layer + part + 1) * D],
+            out_w.at[:, part * D : (part + 1) * D],
+        )
+        for part in range(2)
+    ]
 
 
 OPENING_SHAPES = (
     ((SEQ, D), bf16),
     ((SEQ, D), f32),
     ((P_ROWS, BLK), f32),
-    ((4, 2 * PAD, D), bf16),
+    ((2, 2 * PAD, D), bf16),
     ((PREFIX, D), f32),
-    ((4 * D, D), bf16),
+    ((D, 2 * D), bf16),
     ((D, D), bf16),
     ((D, D), bf16),
     ((2 * 8, SEQ), f32),
@@ -516,17 +528,19 @@
         copies.start(src, dst)
         for src, dst in ((embed_hbm, embed), (up_hbm, up_w), (up_b_hbm, up_b.at[0]), (out_b_hbm, out_b.at[0]))
     ]
-    parts = [
-        copies.start(out_hbm.at[:, i * D : (i + 1) * D], out_w.at[:, i * D : (i + 1) * D])
-        for i in range(4)
-    ]
+    parts = layer_parts(copies, 0, out_hbm, out_w)
     late = [copies.start(tables_hbm, tables), copies.start(qkv_hbm.at[0], own_qkv)]
     seg_copy.wait()
     fill_mask(seg, mask)
     x_copy.wait()
     hat[...], _ = normalized(x_ref[...].astype(f32))
     wait_all(*prefix_copies)
-    prefix_states(embed, up_w, up_b, out_w, out_b, parts, hidden, low, wide, up_high, up_rest)
+    units = jnp.tanh(few_rows_dot(embed[...], up_w[...])[:PREFIX] + up_b[...])
+    hidden[...] = units
+    up_high[...], up_rest[...] = halves(up_w[...])
+    for part in range(2):
+        parts[part].wait()
+        prefix_state(units, 0, part, out_w, out_b, low, wide)
     wait_all(*late)
 
 
@@ -536,7 +550,7 @@
         ((PREFIX, D), f32),
         ((D, D), f32),
         ((1, D), f32),
-        ((D, 4 * D), f32),
+        ((D, 2 * D), f32),
         ((1, 4 * D), f32),
     ]
     return call_kernel(
@@ -562,13 +576,16 @@
     ((2, D, FF), bf16),
     ((2, FF, D), bf16),
     ((SEQ, D), bf16),
+    ((D, 2 * D), f32),
+    ((1, 4 * D), f32),
 )
 
 
 def first_kernel(own_small, other_small, own_qkv, other_qkv, hat_ref, mask, low, tables,
                  attn_hbm, ff_in_hbm, ff_out_hbm, cot_hbm,
+                 out_hbm, out_b_hbm,
                  q_t, k_t, v_m, p_ref, pp_ref, inv_ref, mixed_ref, two_ref, small, w_qkv, w_attn, w_in,
-                 w_out, cot_ref, k_m, v_t, sems):
+                 w_out, cot_ref, out_w, out_b, k_m, v_t, sems):
     section = lax.axis_index("pipe")
     copies = Copies(sems)
     now = [
@@ -577,9 +594,11 @@
         copies.start(own_qkv, w_qkv.at[section]),
         copies.start(other_qkv.at[0], w_qkv.at[1 - section]),
     ]
+    parts = layer_parts(copies, 1, out_hbm, out_w)
     later = [
         copies.start(ff_in_hbm.at[0], w_in.at[section]),
         copies.start(attn_hbm.at[0], w_attn.at[section]),
+        copies.start(out_b_hbm, out_b.at[0]),
         copies.start(ff_out_hbm.at[0], w_out.at[section]),
         copies.start(cot_hbm.at[section, 0], cot_ref),
     ]
@@ -590,23 +609,30 @@
     two_ref[...] = second_norm(hat, zero)
     project_heads(normed, w_qkv.at[0], zero, tables[:8, :], tables[8:, :], q_t, k_t, k_m, v_m, v_t)
     attend(q_t, k_m, v_t, low.at[0], low.at[1], mask, p_ref, pp_ref, inv_ref, mixed_ref)
-    wait_all(*later)
+    wait_all(*later, *parts)
 
 
 def first_call(ready, *arrays):
     return call_kernel(
         first_kernel, "first_attention", in_vmem(*ready) + in_hbm(*arrays), vmem(FIRST_SHAPES),
-        [((SEQ, D), bf16), ((D, SEQ), bf16)], 8, EARLY_MIB, 200 * SEQ * D * 3 * D,
-    )
-
-
-def feed_kernel(two, small, other_in, w_in_before, act_ref, slope_ref, w_in, sems):
+        [((SEQ, D), bf16), ((D, SEQ), bf16)], 11, EARLY_MIB, 200 * SEQ * D * 3 * D,
+    )
+
+
+def feed_kernel(two, small, other_in, w_in_before, hidden, out_w, out_b, act_ref, slope_ref, w_in, low_one, wide_one,
+                sems):
     wait_all(Copies(sems).start(other_in.at[0], w_in.at[1 - lax.axis_index("pipe")]))
-    feed_in(two[...], w_in.at[0], small.at[0], act_ref, slope_ref)
+
+    def between(chunk):
+        if chunk in (0, 2):
+            prefix_state(hidden[...], 1, chunk // 2, out_w, out_b, low_one, wide_one)
+
+    feed_in(two[...], w_in.at[0], small.at[0], act_ref, slope_ref, between)
 
 
 def feed_call(*arrays):
     shapes = [((SEQ, FF), bf16), ((SEQ, FF), bf16), ((2, D, FF), bf16)]
+    shapes += [((2, 2 * PAD, D), bf16), ((D, 2 * D), bf16)]
     return call_kernel(
         feed_kernel, "first_feed", in_vmem(*arrays), vmem(shapes), [], 1, LATE_MIB, 2 * SEQ * D * FF,
         {3: 2},
@@ -632,7 +658,7 @@
 
 
 def middle_kernel(w_attn_before, w_out_before, q0, pp0, inv0, mixed0, small, w_qkv, w_in,
-                  other_attn, other_out, cot_ref, x_ref, act_zero, low, mask, tables,
+                  other_attn, other_out, cot_ref, x_ref, act_zero, low, low_one, mask, tables,
                   h_one, act_one, mixed_one, grad_one, grad_low, scaled_zero, inner_zero, pre_ds_zero,
                   prefix_grad, w_attn, w_out,
                   q_t, k_t, v_m, p_ref, pp_ref, inv_ref, scaled, inner, pre_ds, turned, k_m, v_t,
@@ -654,17 +680,16 @@
     normed = (hat * small_row(small_one, G1) + small_row(small_one, B1)).astype(bf16)
     two = second_norm(hat, small_one)
     project_heads(normed, w_qkv.at[1], small_one, cos, sin, q_t, k_t, k_m, v_m, v_t)
-    attend(q_t, k_m, v_t, low.at[2], low.at[3], mask, p_ref, pp_ref, inv_ref, mixed_one)
+    attend(q_t, k_m, v_t, low_one.at[0], low_one.at[1], mask, p_ref, pp_ref, inv_ref, mixed_one)
 
     grad = cot_ref[...]
     grad_two = feed_both(two, grad, w_in.at[1], w_out.at[1], small_one, act_one)
-    prefix_back(w_attn.at[1], grad, q_t, low.at[3], pp_ref, inv_ref, mixed_one, scaled, inner, pre_ds, turned,
+    prefix_back(w_attn.at[1], grad, q_t, low_one.at[1], pp_ref, inv_ref, mixed_one, scaled, inner, pre_ds, turned,
                 prefix_grad, 2 * PREFIX)
-    attend_back(scaled, inner, pre_ds, q_t, k_t, v_m, low.at[2], p_ref, dq, dk, dv)
+    attend_back(scaled, inner, pre_ds, q_t, k_t, v_m, low_one.at[0], p_ref, dq, dk, dv)
     pack_grads(dq, dk, dv, cos, sin, packed)
-    result = norms_back(grad, grad_one[...], scale, grad_two, packed[...], w_qkv[1], small_one)
-    grad_one[...] = result
-    grad_low[...] = result.astype(bf16)
+    norms_back(cot_ref, grad_one, scale, grad_two, packed, w_qkv[1], small_one, grad_one)
+    grad_low[...] = grad_one[...].astype(bf16)
 
     prefix_back(w_attn.at[0], grad_low[...], q0, low.at[1], pp0, inv0, mixed0, scaled_zero, inner_zero,
                 pre_ds_zero, turned, prefix_grad, 0)
@@ -738,7 +763,7 @@
 
 def norms_kernel(x_ref, grad, two, packed, grad_one, small, w_qkv, keep, send, result, sems):
     hat, scale = normalized(x_ref[...].astype(f32))
-    result[...] = norms_back(grad[...], hat, scale, two[...], packed[...], w_qkv[0], small.at[0])
+    norms_back(grad, hat, scale, two, packed, w_qkv[0], small.at[0], result)
     hand_over((result, grad_one), keep, send, sems)
 
 
@@ -749,26 +774,32 @@
     )
 
 
-def place_kernel(act, act_other, grad, grad_other, act_out, grad_out, sems):
+def place_kernel(act, act_other, grad, grad_other, wide_zero, wide_one, up_high, up_rest,
+                 act_out, grad_out, wide_t, up_high_t, up_rest_t, sems):
     section = lax.axis_index("pipe")
     copies = Copies(sems)
-    wait_all(
-        *[
-            copies.start(value, whole.at[0, where, 0])
-            for value, whole, where in (
-                (grad, grad_out, section),
-                (grad_other, grad_out, 1 - section),
-                (act, act_out, section),
-                (act_other, act_out, 1 - section),
-            )
-        ]
-    )
+    placed = [
+        copies.start(value, whole.at[0, where, 0])
+        for value, whole, where in (
+            (grad, grad_out, section),
+            (grad_other, grad_out, 1 - section),
+            (act, act_out, section),
+            (act_other, act_out, 1 - section),
+        )
+    ]
+    for part in range(4):
+        cols = slice(part % 2 * D, (part % 2 + 1) * D)
+        wide_t[part * D : (part + 1) * D, :] = jnp.transpose((wide_zero, wide_one)[part // 2][:, cols])
+    up_high_t[...] = jnp.transpose(up_high[...])
+    up_rest_t[...] = jnp.transpose(up_rest[...])
+    wait_all(*placed)
 
 
 def place_call(*arrays):
-    wholes = [(pltpu.HBM, (1, 2, 1, SEQ, D), bf16), (pltpu.HBM, (1, 2, 1, SEQ, D), f32)]
+    outs = [(pltpu.HBM, (1, 2, 1, SEQ, D), bf16), (pltpu.HBM, (1, 2, 1, SEQ, D), f32)]
+    outs += vmem([((4 * D, D), bf16), ((D, D), bf16), ((D, D), bf16)])
     return call_kernel(
-        place_kernel, "place_outputs", in_vmem(*arrays), wholes, [], 4, LATE_MIB, 2 * SEQ * D
+        place_kernel, "place_outputs", in_vmem(*arrays), outs, [], 4, LATE_MIB, 2 * SEQ * D
     )
 
 
@@ -869,15 +900,17 @@
     x_zero, hat_zero, mask, low, hidden_units, wide, up_high, up_rest, tables, own_qkv = opening_call(
         block_input, segments, prefix_embed, up_weight, up_bias, out_weight, out_bias, tables, qkv_weight
     )
-    q0, k0, v0, p0, pp0, inv0, mixed0, two_zero, small, w_qkv, w_attn, w_in, w_out, cot = first_call(
+    q0, k0, v0, p0, pp0, inv0, mixed0, two_zero, small, w_qkv, w_attn, w_in, w_out, cot, out_w, out_b = first_call(
         (small, other_small, own_qkv, other_qkv, hat_zero, mask, low, tables),
-        attn_weight, ff_in_weight, ff_out_weight, cotangent,
-    )
-    act_zero, slope_zero, w_in = feed_call(two_zero, small, other_in, w_in)
+        attn_weight, ff_in_weight, ff_out_weight, cotangent, out_weight, out_bias,
+    )
+    act_zero, slope_zero, w_in, low_one, wide_one = feed_call(
+        two_zero, small, other_in, w_in, hidden_units, out_w, out_b
+    )
     (h_one, act_one, mixed_one, grad_one, grad_low, scaled_zero, inner_zero, pre_ds_zero, prefix_grad,
      w_attn, w_out) = middle_call(
         w_attn, w_out, q0, pp0, inv0, mixed0, small, w_qkv, w_in, other_attn, other_out, cot, x_zero,
-        act_zero, low, mask, tables,
+        act_zero, low, low_one, mask, tables,
     )
 
     def layer_one_out(state):
@@ -899,7 +932,10 @@
 
     def swap_grads(state):
         other = swapped(state["grad_send"])
-        return {"wholes": place_call(state["act_own"], state["act_other"], state["grad_own"], other)}
+        act, grad, *turned = place_call(
+            state["act_own"], state["act_other"], state["grad_own"], other, wide, wide_one, up_high, up_rest
+        )
+        return {"wholes": (act, grad), "turned": turned}
 
     works = [layer_one_out, layer_zero_attention, layer_zero_feed, layer_zero_norms, swap_grads]
     state = {"h_one": h_one, "grad_low": grad_low, "scaled": scaled_zero}
@@ -917,7 +953,7 @@
         state = work(state)
     col_width = 2 * D // lax.axis_size("dp")
     grad_embed, grad_up, grad_up_b, grad_out, grad_out_b = final_call(
-        col_width, prefix_grad, hidden_units, prefix_embed, wide, up_high, up_rest
+        col_width, prefix_grad, hidden_units, prefix_embed, *state["turned"]
     )
     activations, input_grads = state["wholes"]
     return (

time: 50.7 us -> 50.5 us (level)
  waiting for transfers between devices: 1.27 us -> 0.67 us
    ppermute x4, waiting for transfers between devices: 1.25 us -> 0.65 us  [local(): moved = lax.ppermute(prefix_grad.astype(bf16), axis, pairs)]
  transfers between devices with their start and end apart: 12 -> 12, of which waited for: 3 -> 2; matrix products, arithmetic and copies ran while one was open for 0% -> 0% of each run, Pallas kernels for 40% -> 41%
where the time goes in v8:
time: 50.5 us; the launch traced here: 50.3 us
  Pallas kernels  37.8 us (75%)
  starting transfers between devices  10.7 us (21%)
  between operations  1 us (2%)
  waiting for transfers between devices  0.67 us (1%)
    pallas_call x11, Pallas kernels, call_kernel(): pl.pallas_call(kernel, name=name, out_shape=[space(shape, dtype) for spac...  37.8 us
    ppermute x4, starting transfers between devices, local(): moved = lax.ppermute(prefix_grad.astype(bf16), axis, pairs)  8.5 us
    ppermute x7, starting transfers between devices, swapped(): return lax.ppermute(array_in, 'pipe', [(0, 1), (1, 0)])  2.1 us
  transfers between devices with their start and end apart: 12, of which 2 were waited for; matrix products, arithmetic and copies ran while one was open for 0% of the time, Pallas kernels for 41%

profile of v8, /device:TPU:0, one launch (start us, length us, event | category | flops | bytes accessed | tf_op | source)
XLA Modules:
  0.0 50.3 jit_solution(4304853304492886893)
XLA Ops:
  0.6 0.5 %collective-permute-start.1 = (bf16[1,512,1536]{2,1,0:T(8,128)(2,1)}, bf16[1,512,1536]{2,1,0:T(8,128)(2,1)S(1)}, u32[]{:S(2)}, u32[]{:S(2)}) collective-permute-start(bf16[1,512,1536]{2,1,0:T(8,128)(2,1)} %qkv_hbm.1), channel_id=1, source_target_pairs={{0,16},{16,0},{1,17},{17,1},{2,18},{18,2},{3,19},{19,3},{4,20},{20... | collective-permute-start | bytes 4718600 | tf_op jit(solution)/shard_map/ppermute | solution.py:855
  1.2 0.9 %small_parameters.1.own_small = f32[1,6656]{1,0:T(1,128)S(1)} custom-call(f32[1,512]{1,0:T(1,128)} %gain_one.1, f32[1,512]{1,0:T(1,128)} %shift_one.1, f32[1,512]{1,0:T(1,128)} %gain_two.1, f32[1,512]{1,0:T(1,128)} %shift_two.1, f32[1,512]{1,0:T(1,128)} %attn_b.1, f32[1,512]{1,0:T(1,128)} %out_b.1, f32[1,1536]{1,0:T(1,128)} %qkv_b.1, f32[1,2048]{1,0:T(1,128)} %in_b.1), custom_call_target="tpu_custom_call" | custom-call | flops 6656 | bytes 8388608 | tf_op jit(solution)/shard_map/small_parameters/pallas_call | solution.py:53
  2.0 0.1 collective-permute-start
  2.2 0.5 collective-permute-start.3
  2.6 0.1 collective-permute-start.2
  2.7 0.4 collective-permute-start.4
  3.1 2.7 %opening.1 = (bf16[512,512]{1,0:T(8,128)(2,1)S(1)}, f32[512,512]{1,0:T(8,128)S(1)}, f32[1152,128]{1,0:T(8,128)S(1)}, bf16[2,32,512]{2,1,0:T(8,128)(2,1)S(1)}, f3...) custom-call(bf16[2,1,512,512]{3,2,1,0:T(8,128)(2,1)} %x_hbm.1, ...), custom_call_target="tpu_custom_call" | custom-call | flops 251658240 | bytes 8388608 | tf_op jit(solution)/shard_map/opening/pallas_call | solution.py:53
  5.9 3.6 %first_attention.1 = (bf16[512,512]{1,0:T(8,128)(2,1)S(1)}, bf16[512,512]{1,0:T(8,128)(2,1)S(1)}, bf16[512,512]{1,0:T(8,128)(2,1)S(1)}, bf16[4,1152,256]{2,1,0:T...) custom-call(f32[1,6656]{1,0:T(1,128)S(1)} %small_parameters.1.own_sm, ...), custom_call_target="tpu_custom_call" | custom-call | flops 80530636800 | bytes 8388608 | tf_op jit(solution)/shard_map/first_attention/pallas_call | solution.py:53
  9.5 2.6 %first_feed.1 = (bf16[512,2048]{1,0:T(8,128)(2,1)S(1)}, bf16[512,2048]{1,0:T(8,128)(2,1)S(1)}, bf16[2,512,2048]{2,1,0:T(8,128)(2,1)S(1)}, bf16[2,32,512]{2,1,0:T(8,128)(2,1)S(1)}, bf16[512,1024]{1,0:T(8,128)(2,1)S(1)}) custom-call(bf16[512,512]{1,0:T(8,128)(2,1)S(1)} %get-tuple-element.114.two, ...), custom_call_target="tpu_custom_call", output_to_operand_aliasing={{2}: (3, {})} | custom-call | flops 1073741824 | bytes 8388608 | tf_op jit(solution)/shard_map/first_feed/pallas_call | solution.py:53
  12.1 15.1 %middle.1 = (bf16[512,512]{1,0:T(8,128)(2,1)S(1)}, bf16[512,2048]{1,0:T(8,128)(2,1)S(1)}, bf16[512,512]{1,0:T(8,128)(2,1)S(1)}, f32[512,512]{1,0:T(8,128)S(1)}, ...) custom-call(bf16[2,512,512]{2,1,0:T(8,128)(2,1)S(1)} %get-tuple-elem, ...), custom_call_target="tpu_custom_call", output_to_operand_aliasing={{9}: (0, {}), {10}: (1, {})} | custom-call | flops 16106127360 | bytes 8388608 | tf_op jit(solution)/shard_map/middle/pallas_call | solution.py:53
  27.3 0.1 collective-permute-start.5
  27.4 1.6 %layer_one_out.1 = (bf16[512,512]{1,0:T(8,128)(2,1)S(1)}, bf16[512,512]{1,0:T(8,128)(2,1)S(1)}) custom-call(bf16[512,512]{1,0:T(8,128)(2,1)S(1)} %get-tuple-element.128.h_one, bf16[512,2048]{1,0:T(8,128)(2,1)S(1)} %get-tuple-element.129.act, bf16[512,512]{1,0:T(8,128)(2,1)S(1)} %get-tuple-element.130.mixed, f32[2,1,6656]{2,1,0:T(1,128)S(1)} %get-tuple-element.112.small, ...), custom_call_target="tpu_custom_call" | custom-call | flops 1342177280 | bytes 8388608 | tf_op jit(solution)/shard_map/layer_one_out/pallas_call | solution.py:53
  29.1 0.5 collective-permute-start.7
  29.6 2.6 %collective-permute-start.6 = (bf16[40,512]{1,0:T(8,128)(2,1)S(1)}, bf16[40,512]{1,0:T(8,128)(2,1)S(1)}, u32[]{:S(2)}, u32[]{:S(2)}) collective-permute-start(bf16[40,512]{1,0:T(8,128)(2,1)S(1)} %get-tuple-element.197), channel_id=1, source_target_pairs={{0,1},{1,0},{2,3},{3,2},{4,5},{5,4},{6,7},{7,6},{8,9},{9,8},{10,11... | collective-permute-start | bytes 122888 | tf_op jit(solution)/shard_map/ppermute | solution.py:947
  32.2 2.7 %layer_zero_attention_back.1.packed = bf16[1536,512]{1,0:T(8,128)(2,1)S(1)} custom-call(bf16[512,512]{1,0:T(8,128)(2,1)S(1)} %get-tuple-element.142.scaled, f32[8,512]{1,0:T(8,128)S(1)} %get-tuple-element.143.inner, bf16[4,32,512]{2,1,0:T(8,128)(2,1)S(1)} %get-tuple-element.144.pre_ds, bf16[512,512]{1,0:T(8,128)(2,1)S(1)} %get-tuple-element.108.q0.q_t, ...), custom_call_target="tpu_custom_call" | custom-call | flops 1342177280 | bytes 8388608 | tf_op jit(solution)/shard_map/layer_zero_attention_back/pallas_call | solution.py:53
  34.9 1.6 %collective-permute-start.8 = (bf16[40,512]{1,0:T(8,128)(2,1)S(1)}, bf16[40,512]{1,0:T(8,128)(2,1)S(1)}, u32[]{:S(2)}, u32[]{:S(2)}) collective-permute-start(bf16[40,512]{1,0:T(8,128)(2,1)S(1)} %get-tuple-element.195), channel_id=1, source_target_pairs={{0,2},{1,3},{2,0},{3,1},{4,6},{5,7},{6,4},{7,5},{8,10},{9,11},{10,... | collective-permute-start | bytes 122888 | tf_op jit(solution)/shard_map/ppermute | solution.py:947
  36.5 2.4 %layer_zero_feed_back.1.two = f32[512,512]{1,0:T(8,128)S(1)} custom-call(bf16[512,512]{1,0:T(8,128)(2,1)S(1)} %get-tuple-element.152.grad, bf16[512,2048]{1,0:T(8,128)(2,1)S(1)} %get-tuple-element.154.slope, bf16[2,512,2048]{2,1,0:T(8,128)(2,1)S(1)} %get-tuple-element.120.w_in, bf16[2,2048,512]{2,1,0:T(8,128)(2,1)S(1)} %get-tuple-element.132.w_out), custom_call_target="tpu_custom_call" | custom-call | flops 2147483648 | bytes 8388608 | tf_op jit(solution)/shard_map/layer_zero_feed_back/pallas_call | solution.py:53
  38.9 0.1 collective-permute-done.8
  39.0 1.6 %collective-permute-start.9 = (bf16[40,512]{1,0:T(8,128)(2,1)S(1)}, bf16[40,512]{1,0:T(8,128)(2,1)S(1)}, u32[]{:S(2)}, u32[]{:S(2)}) collective-permute-start(bf16[40,512]{1,0:T(8,128)(2,1)S(1)} %get-tuple-element.193), channel_id=1, source_target_pairs={{0,4},{4,0},{8,12},{12,8},{1,5},{5,1},{9,13},{13,9},{2,6},{6,2},{1... | collective-permute-start | bytes 122888 | tf_op jit(solution)/shard_map/ppermute | solution.py:947
  40.6 1.9 %layer_zero_norms.1 = (f32[512,512]{1,0:T(8,128)S(1)}, f32[512,512]{1,0:T(8,128)S(1)}) custom-call(bf16[512,512]{1,0:T(8,128)(2,1)S(1)} %get-tuple-element.124.x_ref, bf16[512,512]{1,0:T(8,128)(2,1)S(1)} %get-tuple-element.152.grad, f32[512,512]{1,0:T(8,128)S(1)} %layer_zero_feed_back.1.two, bf16[1536,512]{1,0:T(8,128)(2,1)S(1)} %layer_zero_attention_back.1.packed, ...), custom_call_target="tpu_custom_call" | custom-call | flops 805306368 | bytes 8388608 | tf_op jit(solution)/shard_map/layer_zero_norms/pallas_call | solution.py:53
  42.5 0.5 %collective-permute-done.9 = bf16[40,512]{1,0:T(8,128)(2,1)S(1)} collective-permute-done((bf16[40,512]{1,0:T(8,128)(2,1)S(1)}, bf16[40,512]{1,0:T(8,128)(2,1)S(1)}, u32[]{:S(2)}, u32[]{:S(2)}) %collective-permute-start.9) | collective-permute-done | bytes 40992 | tf_op jit(solution)/shard_map/ppermute | solution.py:947
  43.1 2.6 %collective-permute-start.10 = (bf16[40,512]{1,0:T(8,128)(2,1)S(1)}, bf16[40,512]{1,0:T(8,128)(2,1)S(1)}, u32[]{:S(2)}, u32[]{:S(2)}) collective-permute-start(bf16[40,512]{1,0:T(8,128)(2,1)S(1)} %get-tuple-element.191), channel_id=1, source_target_pairs={{0,8},{4,12},{8,0},{12,4},{1,9},{5,13},{9,1},{13,5},{2,10},{6,14},... | collective-permute-start | bytes 122888 | tf_op jit(solution)/shard_map/ppermute | solution.py:947
  45.7 2.4 %place_outputs.1 = (bf16[1,2,1,512,512]{4,3,2,1,0:T(8,128)(2,1)}, f32[1,2,1,512,512]{4,3,2,1,0:T(8,128)}, bf16[2048,512]{1,0:T(8,128)(2,1)S(1)}, bf16[512,512]{1,0:T(8,128)(2,1)S(1)}, bf16[512,512]{1,0:T(8,128)(2,1)S(1)}) custom-call(bf16[512,512]{1,0:T(8,128)(2,1)S(1)} %get-tuple-element.166.act, bf16[512,512]{1,0:T(8,128)(2,1)S(1)} %collective-permute-done.7.act_other, ...), custom_call_target="tpu_custom_call" | custom-call | flops 524288 | bytes 8388608 | tf_op jit(solution)/shard_map/place_outputs/pallas_call | solution.py:53
  48.1 2.0 %reparam.1 = (f32[10,512]{1,0:T(8,128)}, f32[512,512]{1,0:T(8,128)}, f32[1,512]{1,0:T(1,128)}, f32[512,256]{1,0:T(8,128)}, f32[1,256]{1,0:T(1,128)}) custom-call(f32[40,512]{1,0:T(8,128)S(1)} %convert_add_fusion.refs_0_, f32[10,512]{1,0:T(8,128)S(1)} %get-tuple-element.117.hidden.refs_1_, f32[10,512]{1,0:T(8,128)S(1)} %copy-done, ...), custom_call_target="tpu_custom_call" | custom-call | flops 134217728 | bytes 8388608 | tf_op jit(solution)/shard_map/reparam/pallas_call | solution.py:53
  (18 shorter events, 0.1 us)
Async XLA Ops:
  0.6 5.2 %collective-permute-start.1 = (bf16[1,512,1536]{2,1,0:T(8,128)(2,1)}, bf16[1,512,1536]{2,1,0:T(8,128)(2,1)S(1)}, u32[]{:S(2)}, u32[]{:S(2)}) collective-permute-start(bf16[1,512,1536]{2,1,0:T(8,128)(2,1)} %qkv_hbm.1), channel_id=1, source_target_pairs={{0,16},{16,0},{1,17},{17,1},{2,18},{18,2},{3,19},{19,3},{4,20},{20... | collective-permute-start | bytes 4718600 | tf_op jit(solution)/shard_map/ppermute | solution.py:855
  2.0 3.8 %collective-permute-start = (f32[1,6656]{1,0:T(1,128)S(1)}, f32[1,6656]{1,0:T(1,128)S(1)}, u32[]{:S(2)}, u32[]{:S(2)}) collective-permute-start(f32[1,6656]{1,0:T(1,128)S(1)} %small_parameters.1.own_small), channel_id=1, source_target_pairs={{0,16},{16,0},{1,17},{17,1},{2,18},{18,2},{3,19},{19,3},{4,20},{20... | collective-permute-start | bytes 79880 | tf_op jit(solution)/shard_map/ppermute | solution.py:855
  2.2 9.9 %collective-permute-start.3 = (bf16[1,512,512]{2,1,0:T(8,128)(2,1)}, bf16[1,512,512]{2,1,0:T(8,128)(2,1)S(1)}, u32[]{:S(2)}, u32[]{:S(2)}) collective-permute-start(bf16[1,512,512]{2,1,0:T(8,128)(2,1)} %attn_hbm.1), channel_id=1, source_target_pairs={{0,16},{16,0},{1,17},{17,1},{2,18},{18,2},{3,19},{19,3},{4,20},{20... | collective-permute-start | bytes 1572872 | tf_op jit(solution)/shard_map/ppermute | solution.py:855
  2.6 6.8 %collective-permute-start.2 = (bf16[1,512,2048]{2,1,0:T(8,128)(2,1)}, bf16[1,512,2048]{2,1,0:T(8,128)(2,1)S(1)}, u32[]{:S(2)}, u32[]{:S(2)}) collective-permute-start(bf16[1,512,2048]{2,1,0:T(8,128)(2,1)} %ff_in_hbm.1), channel_id=1, source_target_pairs={{0,16},{16,0},{1,17},{17,1},{2,18},{18,2},{3,19},{19,3},{4,20},{20... | collective-permute-start | bytes 6291464 | tf_op jit(solution)/shard_map/ppermute | solution.py:855
  2.7 9.4 %collective-permute-start.4 = (bf16[1,2048,512]{2,1,0:T(8,128)(2,1)}, bf16[1,2048,512]{2,1,0:T(8,128)(2,1)S(1)}, u32[]{:S(2)}, u32[]{:S(2)}) collective-permute-start(bf16[1,2048,512]{2,1,0:T(8,128)(2,1)} %ff_out_hbm.1), channel_id=1, source_target_pairs={{0,16},{16,0},{1,17},{17,1},{2,18},{18,2},{3,19},{19,3},{4,20},{20... | collective-permute-start | bytes 6291464 | tf_op jit(solution)/shard_map/ppermute | solution.py:855
  27.3 1.8 %collective-permute-start.5 = (f32[40,512]{1,0:T(8,128)S(1)}, f32[40,512]{1,0:T(8,128)S(1)}, u32[]{:S(2)}, u32[]{:S(2)}) collective-permute-start(f32[40,512]{1,0:T(8,128)S(1)} %get-tuple-element.137), channel_id=1, source_target_pairs={{0,16},{16,0},{1,17},{17,1},{2,18},{18,2},{3,19},{19,3},{4,20},{20... | collective-permute-start | bytes 245768 | tf_op jit(solution)/shard_map/ppermute | solution.py:944
  29.1 5.8 %collective-permute-start.7 = (bf16[512,512]{1,0:T(8,128)(2,1)S(1)}, bf16[512,512]{1,0:T(8,128)(2,1)S(1)}, u32[]{:S(2)}, u32[]{:S(2)}) collective-permute-start(bf16[512,512]{1,0:T(8,128)(2,1)S(1)} %get-tuple-element.139), channel_id=1, source_target_pairs={{0,16},{16,0},{1,17},{17,1},{2,18},{18,2},{3,19},{19,3},{4,20},{20... | collective-permute-start | bytes 1572872 | tf_op jit(solution)/shard_map/ppermute | solution.py:855
  29.6 5.3 %collective-permute-start.6 = (bf16[40,512]{1,0:T(8,128)(2,1)S(1)}, bf16[40,512]{1,0:T(8,128)(2,1)S(1)}, u32[]{:S(2)}, u32[]{:S(2)}) collective-permute-start(bf16[40,512]{1,0:T(8,128)(2,1)S(1)} %get-tuple-element.197), channel_id=1, source_target_pairs={{0,1},{1,0},{2,3},{3,2},{4,5},{5,4},{6,7},{7,6},{8,9},{9,8},{10,11... | collective-permute-start | bytes 122888 | tf_op jit(solution)/shard_map/ppermute | solution.py:947
  34.9 4.1 %collective-permute-start.8 = (bf16[40,512]{1,0:T(8,128)(2,1)S(1)}, bf16[40,512]{1,0:T(8,128)(2,1)S(1)}, u32[]{:S(2)}, u32[]{:S(2)}) collective-permute-start(bf16[40,512]{1,0:T(8,128)(2,1)S(1)} %get-tuple-element.195), channel_id=1, source_target_pairs={{0,2},{1,3},{2,0},{3,1},{4,6},{5,7},{6,4},{7,5},{8,10},{9,11},{10,... | collective-permute-start | bytes 122888 | tf_op jit(solution)/shard_map/ppermute | solution.py:947
  39.0 4.1 %collective-permute-start.9 = (bf16[40,512]{1,0:T(8,128)(2,1)S(1)}, bf16[40,512]{1,0:T(8,128)(2,1)S(1)}, u32[]{:S(2)}, u32[]{:S(2)}) collective-permute-start(bf16[40,512]{1,0:T(8,128)(2,1)S(1)} %get-tuple-element.193), channel_id=1, source_target_pairs={{0,4},{4,0},{8,12},{12,8},{1,5},{5,1},{9,13},{13,9},{2,6},{6,2},{1... | collective-permute-start | bytes 122888 | tf_op jit(solution)/shard_map/ppermute | solution.py:947
  43.1 2.7 %collective-permute-start.11 = (f32[512,512]{1,0:T(8,128)S(1)}, f32[512,512]{1,0:T(8,128)S(1)}, u32[]{:S(2)}, u32[]{:S(2)}) collective-permute-start(f32[512,512]{1,0:T(8,128)S(1)} %get-tuple-element.169), channel_id=1, source_target_pairs={{0,16},{16,0},{1,17},{17,1},{2,18},{18,2},{3,19},{19,3},{4,20},{20... | collective-permute-start | bytes 3145736 | tf_op jit(solution)/shard_map/ppermute | solution.py:855
  43.1 5.0 %collective-permute-start.10 = (bf16[40,512]{1,0:T(8,128)(2,1)S(1)}, bf16[40,512]{1,0:T(8,128)(2,1)S(1)}, u32[]{:S(2)}, u32[]{:S(2)}) collective-permute-start(bf16[40,512]{1,0:T(8,128)(2,1)S(1)} %get-tuple-element.191), channel_id=1, source_target_pairs={{0,8},{4,12},{8,0},{12,4},{1,9},{5,13},{9,1},{13,5},{2,10},{6,14},... | collective-permute-start | bytes 122888 | tf_op jit(solution)/shard_map/ppermute | solution.py:947
  45.7 2.4 %copy-start = (f32[10,512]{1,0:T(8,128)S(1)}, f32[10,512]{1,0:T(8,128)}, u32[]{:S(2)}) copy-start(f32[10,512]{1,0:T(8,128)} %refs_2_) | copy-start | bytes 61444

commit v9 on v7

--- a/solution.py
+++ b/solution.py
@@ -772,6 +772,9 @@
     )
 
 
+QUARTER = D // 4
+
+
 def final_kernel(col_width, grads_ref, hidden, embed, wide, up_high, up_rest, *refs):
     results, (d_embed, d_up, d_up_b, d_out, d_out_b, sems) = refs[:5], refs[5:]
     section = lax.axis_index("pipe")
@@ -788,8 +791,11 @@
     grad_units = (both[:PAD] + both[PAD:])[:PREFIX]
     grad_pre = grad_units * (1.0 - units * units)
     d_up_b[...] = jnp.sum(grad_pre, axis=0, keepdims=True)
-    d_up[...] = stacked_dot(embed[...], grad_pre)
-    placed += [copies.start(d_up, results[1]), copies.start(d_up_b, results[2])]
+    for start in range(0, D, QUARTER):
+        rows = slice(start, start + QUARTER)
+        d_up[rows, :] = stacked_dot(embed[:, rows], grad_pre)
+        placed.append(copies.start(d_up.at[rows], results[1].at[rows]))
+    placed.append(copies.start(d_up_b, results[2]))
     column = section * (2 * D) + shard * col_width
     own_cols = jnp.zeros((PREFIX, col_width), f32)
     for part in range(4):
@@ -815,7 +821,7 @@
 
     shapes = [((PREFIX, D), f32), ((D, D), f32), ((1, D), f32), ((D, col_width), f32), ((1, col_width), f32)]
     return call_kernel(
-        body, "reparam", in_vmem(*arrays), [(pltpu.HBM, *pair) for pair in shapes], shapes, 5, LATE_MIB,
+        body, "reparam", in_vmem(*arrays), [(pltpu.HBM, *pair) for pair in shapes], shapes, 8, LATE_MIB,
         SEQ * D * D,
     )
 

time: 50.7 us -> 50.5 us (level)
  no operation moved by 1% of the time
where the time goes in v9:
time: 50.5 us; the launch traced here: 50.3 us
  Pallas kernels  37.2 us (74%)
  starting transfers between devices  10.8 us (21%)
  waiting for transfers between devices  1.27 us (3%)
  between operations  1 us (2%)
    pallas_call x11, Pallas kernels, call_kernel(): pl.pallas_call(kernel, name=name, out_shape=[space(shape, dtype) for spac...  37.2 us
    ppermute x4, starting transfers between devices, local(): moved = lax.ppermute(prefix_grad.astype(bf16), axis, pairs)  8.51 us
    ppermute x7, starting transfers between devices, swapped(): return lax.ppermute(array_in, 'pipe', [(0, 1), (1, 0)])  2.09 us
    ppermute x4, waiting for transfers between devices, local(): moved = lax.ppermute(prefix_grad.astype(bf16), axis, pairs)  1.25 us
  transfers between devices with their start and end apart: 12, of which 3 were waited for; matrix products, arithmetic and copies ran while one was open for 0% of the time, Pallas kernels for 40%

profile of v9, /device:TPU:0, one launch (start us, length us, event | category | flops | bytes accessed | tf_op | source)
XLA Modules:
  0.0 50.3 jit_solution(5790973129850708442)
XLA Ops:
  0.6 0.5 %collective-permute-start.1 = (bf16[1,512,1536]{2,1,0:T(8,128)(2,1)}, bf16[1,512,1536]{2,1,0:T(8,128)(2,1)S(1)}, u32[]{:S(2)}, u32[]{:S(2)}) collective-permute-start(bf16[1,512,1536]{2,1,0:T(8,128)(2,1)} %qkv_hbm.1), channel_id=1, source_target_pairs={{0,16},{16,0},{1,17},{17,1},{2,18},{18,2},{3,19},{19,3},{4,20},{20... | collective-permute-start | bytes 4718600 | tf_op jit(solution)/shard_map/ppermute | solution.py:830
  1.2 0.9 %small_parameters.1.own_small = f32[1,6656]{1,0:T(1,128)S(1)} custom-call(f32[1,512]{1,0:T(1,128)} %gain_one.1, f32[1,512]{1,0:T(1,128)} %shift_one.1, f32[1,512]{1,0:T(1,128)} %gain_two.1, f32[1,512]{1,0:T(1,128)} %shift_two.1, f32[1,512]{1,0:T(1,128)} %attn_b.1, f32[1,512]{1,0:T(1,128)} %out_b.1, f32[1,1536]{1,0:T(1,128)} %qkv_b.1, f32[1,2048]{1,0:T(1,128)} %in_b.1), custom_call_target="tpu_custom_call" | custom-call | flops 6656 | bytes 8388608 | tf_op jit(solution)/shard_map/small_parameters/pallas_call | solution.py:53
  2.0 0.1 collective-permute-start
  2.2 0.5 collective-permute-start.3
  2.7 0.4 collective-permute-start.4
  3.1 3.3 %opening.1 = (bf16[512,512]{1,0:T(8,128)(2,1)S(1)}, f32[512,512]{1,0:T(8,128)S(1)}, f32[1152,128]{1,0:T(8,128)S(1)}, bf16[4,32,512]{2,1,0:T(8,128)(2,1)S(1)}, f3...) custom-call(bf16[2,1,512,512]{3,2,1,0:T(8,128)(2,1)} %x_hbm.1, ...), custom_call_target="tpu_custom_call" | custom-call | flops 251658240 | bytes 8388608 | tf_op jit(solution)/shard_map/opening/pallas_call | solution.py:53
  6.5 3.5 %first_attention.1 = (bf16[512,512]{1,0:T(8,128)(2,1)S(1)}, bf16[512,512]{1,0:T(8,128)(2,1)S(1)}, bf16[512,512]{1,0:T(8,128)(2,1)S(1)}, bf16[4,1152,256]{2,1,0:T...) custom-call(f32[1,6656]{1,0:T(1,128)S(1)} %small_parameters.1.own_sm, ...), custom_call_target="tpu_custom_call" | custom-call | flops 80530636800 | bytes 8388608 | tf_op jit(solution)/shard_map/first_attention/pallas_call | solution.py:53
  10.0 2.4 %first_feed.1 = (bf16[512,2048]{1,0:T(8,128)(2,1)S(1)}, bf16[512,2048]{1,0:T(8,128)(2,1)S(1)}, bf16[2,512,2048]{2,1,0:T(8,128)(2,1)S(1)}) custom-call(bf16[512,512]{1,0:T(8,128)(2,1)S(1)} %get-tuple-element.104.two, f32[2,1,6656]{2,1,0:T(1,128)S(1)} %get-tuple-element.102.small, ...), custom_call_target="tpu_custom_call", output_to_operand_aliasing={{2}: (3, {})} | custom-call | flops 1073741824 | bytes 8388608 | tf_op jit(solution)/shard_map/first_feed/pallas_call | solution.py:53
  12.4 15.0 %middle.1 = (bf16[512,512]{1,0:T(8,128)(2,1)S(1)}, bf16[512,2048]{1,0:T(8,128)(2,1)S(1)}, bf16[512,512]{1,0:T(8,128)(2,1)S(1)}, f32[512,512]{1,0:T(8,128)S(1)}, ...) custom-call(bf16[2,512,512]{2,1,0:T(8,128)(2,1)S(1)} %get-tuple-elem, ...), custom_call_target="tpu_custom_call", output_to_operand_aliasing={{9}: (0, {}), {10}: (1, {})} | custom-call | flops 16106127360 | bytes 8388608 | tf_op jit(solution)/shard_map/middle/pallas_call | solution.py:53
  27.5 0.2 collective-permute-start.5
  27.6 1.6 %layer_one_out.1 = (bf16[512,512]{1,0:T(8,128)(2,1)S(1)}, bf16[512,512]{1,0:T(8,128)(2,1)S(1)}) custom-call(bf16[512,512]{1,0:T(8,128)(2,1)S(1)} %get-tuple-element.114.h_one, bf16[512,2048]{1,0:T(8,128)(2,1)S(1)} %get-tuple-element.115.act, bf16[512,512]{1,0:T(8,128)(2,1)S(1)} %get-tuple-element.116.mixed, f32[2,1,6656]{2,1,0:T(1,128)S(1)} %get-tuple-element.102.small, ...), custom_call_target="tpu_custom_call" | custom-call | flops 1342177280 | bytes 8388608 | tf_op jit(solution)/shard_map/layer_one_out/pallas_call | solution.py:53
  29.3 0.5 collective-permute-start.7
  29.8 2.6 %collective-permute-start.6 = (bf16[40,512]{1,0:T(8,128)(2,1)S(1)}, bf16[40,512]{1,0:T(8,128)(2,1)S(1)}, u32[]{:S(2)}, u32[]{:S(2)}) collective-permute-start(bf16[40,512]{1,0:T(8,128)(2,1)S(1)} %get-tuple-element.177), channel_id=1, source_target_pairs={{0,1},{1,0},{2,3},{3,2},{4,5},{5,4},{6,7},{7,6},{8,9},{9,8},{10,11... | collective-permute-start | bytes 122888 | tf_op jit(solution)/shard_map/ppermute | solution.py:917
  32.4 2.7 %layer_zero_attention_back.1.packed = bf16[1536,512]{1,0:T(8,128)(2,1)S(1)} custom-call(bf16[512,512]{1,0:T(8,128)(2,1)S(1)} %get-tuple-element.128.scaled, f32[8,512]{1,0:T(8,128)S(1)} %get-tuple-element.129.inner, bf16[4,32,512]{2,1,0:T(8,128)(2,1)S(1)} %get-tuple-element.130.pre_ds, bf16[512,512]{1,0:T(8,128)(2,1)S(1)} %get-tuple-element.98.q0.q_t, ...), custom_call_target="tpu_custom_call" | custom-call | flops 1342177280 | bytes 8388608 | tf_op jit(solution)/shard_map/layer_zero_attention_back/pallas_call | solution.py:53
  35.1 1.6 %collective-permute-start.8 = (bf16[40,512]{1,0:T(8,128)(2,1)S(1)}, bf16[40,512]{1,0:T(8,128)(2,1)S(1)}, u32[]{:S(2)}, u32[]{:S(2)}) collective-permute-start(bf16[40,512]{1,0:T(8,128)(2,1)S(1)} %get-tuple-element.175), channel_id=1, source_target_pairs={{0,2},{1,3},{2,0},{3,1},{4,6},{5,7},{6,4},{7,5},{8,10},{9,11},{10,... | collective-permute-start | bytes 122888 | tf_op jit(solution)/shard_map/ppermute | solution.py:917
  36.7 2.4 %layer_zero_feed_back.1.two = f32[512,512]{1,0:T(8,128)S(1)} custom-call(bf16[512,512]{1,0:T(8,128)(2,1)S(1)} %get-tuple-element.138.grad, bf16[512,2048]{1,0:T(8,128)(2,1)S(1)} %get-tuple-element.140.slope, bf16[2,512,2048]{2,1,0:T(8,128)(2,1)S(1)} %get-tuple-element.107.w_in, bf16[2,2048,512]{2,1,0:T(8,128)(2,1)S(1)} %get-tuple-element.118.w_out), custom_call_target="tpu_custom_call" | custom-call | flops 2147483648 | bytes 8388608 | tf_op jit(solution)/shard_map/layer_zero_feed_back/pallas_call | solution.py:53
  39.1 0.1 collective-permute-done.8
  39.2 1.6 %collective-permute-start.9 = (bf16[40,512]{1,0:T(8,128)(2,1)S(1)}, bf16[40,512]{1,0:T(8,128)(2,1)S(1)}, u32[]{:S(2)}, u32[]{:S(2)}) collective-permute-start(bf16[40,512]{1,0:T(8,128)(2,1)S(1)} %get-tuple-element.173), channel_id=1, source_target_pairs={{0,4},{4,0},{8,12},{12,8},{1,5},{5,1},{9,13},{13,9},{2,6},{6,2},{1... | collective-permute-start | bytes 122888 | tf_op jit(solution)/shard_map/ppermute | solution.py:917
  40.8 1.9 %layer_zero_norms.1 = (f32[512,512]{1,0:T(8,128)S(1)}, f32[512,512]{1,0:T(8,128)S(1)}) custom-call(bf16[512,512]{1,0:T(8,128)(2,1)S(1)} %get-tuple-element.111.x_ref, bf16[512,512]{1,0:T(8,128)(2,1)S(1)} %get-tuple-element.138.grad, f32[512,512]{1,0:T(8,128)S(1)} %layer_zero_feed_back.1.two, bf16[1536,512]{1,0:T(8,128)(2,1)S(1)} %layer_zero_attention_back.1.packed, ...), custom_call_target="tpu_custom_call" | custom-call | flops 805306368 | bytes 8388608 | tf_op jit(solution)/shard_map/layer_zero_norms/pallas_call | solution.py:53
  42.8 0.5 %collective-permute-done.9 = bf16[40,512]{1,0:T(8,128)(2,1)S(1)} collective-permute-done((bf16[40,512]{1,0:T(8,128)(2,1)S(1)}, bf16[40,512]{1,0:T(8,128)(2,1)S(1)}, u32[]{:S(2)}, u32[]{:S(2)}) %collective-permute-start.9) | collective-permute-done | bytes 40992 | tf_op jit(solution)/shard_map/ppermute | solution.py:917
  43.3 2.6 %collective-permute-start.10 = (bf16[40,512]{1,0:T(8,128)(2,1)S(1)}, bf16[40,512]{1,0:T(8,128)(2,1)S(1)}, u32[]{:S(2)}, u32[]{:S(2)}) collective-permute-start(bf16[40,512]{1,0:T(8,128)(2,1)S(1)} %get-tuple-element.171), channel_id=1, source_target_pairs={{0,8},{4,12},{8,0},{12,4},{1,9},{5,13},{9,1},{13,5},{2,10},{6,14},... | collective-permute-start | bytes 122888 | tf_op jit(solution)/shard_map/ppermute | solution.py:917
  45.9 1.7 %place_outputs.1 = (bf16[1,2,1,512,512]{4,3,2,1,0:T(8,128)(2,1)}, f32[1,2,1,512,512]{4,3,2,1,0:T(8,128)}) custom-call(bf16[512,512]{1,0:T(8,128)(2,1)S(1)} %get-tuple-element.152.act, bf16[512,512]{1,0:T(8,128)(2,1)S(1)} %collective-permute-done.7.act_other, f32[512,512]{1,0:T(8,128)S(1)} %get-tuple-element.154.grad, ...), custom_call_target="tpu_custom_call" | custom-call | flops 524288 | bytes 8388608 | tf_op jit(solution)/shard_map/place_outputs/pallas_call | solution.py:53
  47.6 0.6 %collective-permute-done.10 = bf16[40,512]{1,0:T(8,128)(2,1)S(1)} collective-permute-done((bf16[40,512]{1,0:T(8,128)(2,1)S(1)}, bf16[40,512]{1,0:T(8,128)(2,1)S(1)}, u32[]{:S(2)}, u32[]{:S(2)}) %collective-permute-start.10) | collective-permute-done | bytes 40992 | tf_op jit(solution)/shard_map/ppermute | solution.py:917
  48.3 1.9 %reparam.1 = (f32[10,512]{1,0:T(8,128)}, f32[512,512]{1,0:T(8,128)}, f32[1,512]{1,0:T(1,128)}, f32[512,256]{1,0:T(8,128)}, f32[1,256]{1,0:T(1,128)}) custom-call(f32[40,512]{1,0:T(8,128)S(1)} %convert_add_fusion.refs_0_, f32[10,512]{1,0:T(8,128)S(1)} %get-tuple-element.162.refs_1_, f32[10,512]{1,0:T(8,128)S(1)} %copy-done, ...), custom_call_target="tpu_custom_call" | custom-call | flops 134217728 | bytes 8388608 | tf_op jit(solution)/shard_map/reparam/pallas_call | solution.py:53
  (18 shorter events, 0.2 us)
Async XLA Ops:
  0.6 5.9 %collective-permute-start.1 = (bf16[1,512,1536]{2,1,0:T(8,128)(2,1)}, bf16[1,512,1536]{2,1,0:T(8,128)(2,1)S(1)}, u32[]{:S(2)}, u32[]{:S(2)}) collective-permute-start(bf16[1,512,1536]{2,1,0:T(8,128)(2,1)} %qkv_hbm.1), channel_id=1, source_target_pairs={{0,16},{16,0},{1,17},{17,1},{2,18},{18,2},{3,19},{19,3},{4,20},{20... | collective-permute-start | bytes 4718600 | tf_op jit(solution)/shard_map/ppermute | solution.py:830
  2.0 4.4 %collective-permute-start = (f32[1,6656]{1,0:T(1,128)S(1)}, f32[1,6656]{1,0:T(1,128)S(1)}, u32[]{:S(2)}, u32[]{:S(2)}) collective-permute-start(f32[1,6656]{1,0:T(1,128)S(1)} %small_parameters.1.own_small), channel_id=1, source_target_pairs={{0,16},{16,0},{1,17},{17,1},{2,18},{18,2},{3,19},{19,3},{4,20},{20... | collective-permute-start | bytes 79880 | tf_op jit(solution)/shard_map/ppermute | solution.py:830
  2.2 10.2 %collective-permute-start.3 = (bf16[1,512,512]{2,1,0:T(8,128)(2,1)}, bf16[1,512,512]{2,1,0:T(8,128)(2,1)S(1)}, u32[]{:S(2)}, u32[]{:S(2)}) collective-permute-start(bf16[1,512,512]{2,1,0:T(8,128)(2,1)} %attn_hbm.1), channel_id=1, source_target_pairs={{0,16},{16,0},{1,17},{17,1},{2,18},{18,2},{3,19},{19,3},{4,20},{20... | collective-permute-start | bytes 1572872 | tf_op jit(solution)/shard_map/ppermute | solution.py:830
  2.6 7.4 %collective-permute-start.2 = (bf16[1,512,2048]{2,1,0:T(8,128)(2,1)}, bf16[1,512,2048]{2,1,0:T(8,128)(2,1)S(1)}, u32[]{:S(2)}, u32[]{:S(2)}) collective-permute-start(bf16[1,512,2048]{2,1,0:T(8,128)(2,1)} %ff_in_hbm.1), channel_id=1, source_target_pairs={{0,16},{16,0},{1,17},{17,1},{2,18},{18,2},{3,19},{19,3},{4,20},{20... | collective-permute-start | bytes 6291464 | tf_op jit(solution)/shard_map/ppermute | solution.py:830
  2.7 9.7 %collective-permute-start.4 = (bf16[1,2048,512]{2,1,0:T(8,128)(2,1)}, bf16[1,2048,512]{2,1,0:T(8,128)(2,1)S(1)}, u32[]{:S(2)}, u32[]{:S(2)}) collective-permute-start(bf16[1,2048,512]{2,1,0:T(8,128)(2,1)} %ff_out_hbm.1), channel_id=1, source_target_pairs={{0,16},{16,0},{1,17},{17,1},{2,18},{18,2},{3,19},{19,3},{4,20},{20... | collective-permute-start | bytes 6291464 | tf_op jit(solution)/shard_map/ppermute | solution.py:830
  27.5 1.8 %collective-permute-start.5 = (f32[40,512]{1,0:T(8,128)S(1)}, f32[40,512]{1,0:T(8,128)S(1)}, u32[]{:S(2)}, u32[]{:S(2)}) collective-permute-start(f32[40,512]{1,0:T(8,128)S(1)} %get-tuple-element.123), channel_id=1, source_target_pairs={{0,16},{16,0},{1,17},{17,1},{2,18},{18,2},{3,19},{19,3},{4,20},{20... | collective-permute-start | bytes 245768 | tf_op jit(solution)/shard_map/ppermute | solution.py:914
  29.3 5.8 %collective-permute-start.7 = (bf16[512,512]{1,0:T(8,128)(2,1)S(1)}, bf16[512,512]{1,0:T(8,128)(2,1)S(1)}, u32[]{:S(2)}, u32[]{:S(2)}) collective-permute-start(bf16[512,512]{1,0:T(8,128)(2,1)S(1)} %get-tuple-element.125), channel_id=1, source_target_pairs={{0,16},{16,0},{1,17},{17,1},{2,18},{18,2},{3,19},{19,3},{4,20},{20... | collective-permute-start | bytes 1572872 | tf_op jit(solution)/shard_map/ppermute | solution.py:830
  29.8 5.3 %collective-permute-start.6 = (bf16[40,512]{1,0:T(8,128)(2,1)S(1)}, bf16[40,512]{1,0:T(8,128)(2,1)S(1)}, u32[]{:S(2)}, u32[]{:S(2)}) collective-permute-start(bf16[40,512]{1,0:T(8,128)(2,1)S(1)} %get-tuple-element.177), channel_id=1, source_target_pairs={{0,1},{1,0},{2,3},{3,2},{4,5},{5,4},{6,7},{7,6},{8,9},{9,8},{10,11... | collective-permute-start | bytes 122888 | tf_op jit(solution)/shard_map/ppermute | solution.py:917
  35.1 4.1 %collective-permute-start.8 = (bf16[40,512]{1,0:T(8,128)(2,1)S(1)}, bf16[40,512]{1,0:T(8,128)(2,1)S(1)}, u32[]{:S(2)}, u32[]{:S(2)}) collective-permute-start(bf16[40,512]{1,0:T(8,128)(2,1)S(1)} %get-tuple-element.175), channel_id=1, source_target_pairs={{0,2},{1,3},{2,0},{3,1},{4,6},{5,7},{6,4},{7,5},{8,10},{9,11},{10,... | collective-permute-start | bytes 122888 | tf_op jit(solution)/shard_map/ppermute | solution.py:917
  39.2 4.1 %collective-permute-start.9 = (bf16[40,512]{1,0:T(8,128)(2,1)S(1)}, bf16[40,512]{1,0:T(8,128)(2,1)S(1)}, u32[]{:S(2)}, u32[]{:S(2)}) collective-permute-start(bf16[40,512]{1,0:T(8,128)(2,1)S(1)} %get-tuple-element.173), channel_id=1, source_target_pairs={{0,4},{4,0},{8,12},{12,8},{1,5},{5,1},{9,13},{13,9},{2,6},{6,2},{1... | collective-permute-start | bytes 122888 | tf_op jit(solution)/shard_map/ppermute | solution.py:917
  42.7 5.5 %copy-start = (f32[10,512]{1,0:T(8,128)S(1)}, f32[10,512]{1,0:T(8,128)}, u32[]{:S(2)}) copy-start(f32[10,512]{1,0:T(8,128)} %refs_2_) | copy-start | bytes 61444
  43.3 2.7 %collective-permute-start.11 = (f32[512,512]{1,0:T(8,128)S(1)}, f32[512,512]{1,0:T(8,128)S(1)}, u32[]{:S(2)}, u32[]{:S(2)}) collective-permute-start(f32[512,512]{1,0:T(8,128)S(1)} %get-tuple-element.155), channel_id=1, source_target_pairs={{0,16},{16,0},{1,17},{17,1},{2,18},{18,2},{3,19},{19,3},{4,20},{20... | collective-permute-start | bytes 3145736 | tf_op jit(solution)/shard_map/ppermute | solution.py:830
  43.3 5.0 %collective-permute-start.10 = (bf16[40,512]{1,0:T(8,128)(2,1)S(1)}, bf16[40,512]{1,0:T(8,128)(2,1)S(1)}, u32[]{:S(2)}, u32[]{:S(2)}) collective-permute-start(bf16[40,512]{1,0:T(8,128)(2,1)S(1)} %get-tuple-element.171), channel_id=1, source_target_pairs={{0,8},{4,12},{8,0},{12,4},{1,9},{5,13},{9,1},{13,5},{2,10},{6,14},... | collective-permute-start | bytes 122888 | tf_op jit(solution)/shard_map/ppermute | solution.py:917

commit v10 on v8

--- a/solution.py
+++ b/solution.py
@@ -303,6 +303,28 @@
     pre_grad[pre_row + PREFIX : pre_row + 2 * PREFIX, :] = own_head(values)
 
 
+def by_keys(outs, key_block):
+    total = None
+    for block in range(BLOCKS):
+        place = key_block - (block + 1 - LIVE[block])
+        if 0 <= place < LIVE[block]:
+            part = outs[block][:, place * BLK : (place + 1) * BLK]
+            total = part if total is None else total + part
+    return total
+
+
+def values_back(scaled_ref, p_ref, packed_v):
+    for pair in range(PAIRS):
+        feats = pair_rows(pair)
+        outs = []
+        for block in range(BLOCKS):
+            _, tokens, rows = geometry(block)
+            outs.append(dot(block_diagonal(scaled_ref[feats, tokens]), p_ref[pair, rows, :], NT))
+        for key_block in range(BLOCKS):
+            keys = slice(key_block * BLK, (key_block + 1) * BLK)
+            packed_v[feats, keys] = by_keys(outs, key_block).astype(bf16)
+
+
 def attend_back(scaled_ref, inner_ref, pre_ds_ref, q_t, k_t, v_m, pre_k, p_ref, dq_ref, dk_ref, dv_ref):
     def value_grads(feats, block):
         keys, tokens, _ = geometry(block)
@@ -323,16 +345,8 @@
         dq_ref[feats, tokens] = (
             from_diagonal(dot(k_t[feats, keys], grad_scores, NN)) + pre_dq[:, tokens]
         )
-        return dot(queries, grad_scores, NT), dot(grads, p_ref[pair, rows, :], NT)
-
-    def by_keys(outs, which, key_block):
-        total = None
-        for block in range(BLOCKS):
-            place = key_block - (block + 1 - LIVE[block])
-            if 0 <= place < LIVE[block]:
-                part = outs[block][which][:, place * BLK : (place + 1) * BLK]
-                total = part if total is None else total + part
-        return total
+        dk = dot(queries, grad_scores, NT)
+        return dk, None if dv_ref is None else dot(grads, p_ref[pair, rows, :], NT)
 
     for pair in range(PAIRS):
         feats = pair_rows(pair)
@@ -345,14 +359,14 @@
         ]
         for key_block in range(BLOCKS):
             keys = slice(key_block * BLK, (key_block + 1) * BLK)
-            dk_ref[feats, keys] = by_keys(outs, 0, key_block)
-            dv_ref[feats, keys] = by_keys(outs, 1, key_block)
-
-
-def pack_grads(dq_ref, dk_ref, dv_ref, cos, sin, packed_t):
+            dk_ref[feats, keys] = by_keys([out[0] for out in outs], key_block)
+            if dv_ref is not None:
+                dv_ref[feats, keys] = by_keys([out[1] for out in outs], key_block)
+
+
+def pack_grads(dq_ref, dk_ref, cos, sin, packed_t):
     packed_t[:D, :] = (rope_heads(dq_ref[...], cos, -sin) * Q_BACK).astype(bf16)
     packed_t[D : 2 * D, :] = (rope_heads(dk_ref[...], cos, -sin) * K_BACK).astype(bf16)
-    packed_t[2 * D :, :] = dv_ref[...].astype(bf16)
 
 
 ROOT_HALF = 0.5**0.5
@@ -422,9 +436,12 @@
     return total * ROOT_HALF
 
 
-def norms_back(grad, hat, scale, grad_two, packed_t, w_qkv, small_ref, out_ref):
+def norms_back(grad, hat, scale, grad_two, packed_t, packed_v, w_qkv, small_ref, out_ref):
     halves_of = [slice(start, start + FF_ROWS) for start in range(0, SEQ, FF_ROWS)]
-    products = [dot(w_qkv, packed_t[:, tokens], NN) for tokens in halves_of]
+    products = [
+        dot(w_qkv[:, : 2 * D], packed_t[:, tokens], NN) + dot(w_qkv[:, 2 * D :], packed_v[:, tokens], NN)
+        for tokens in halves_of
+    ]
     for tokens, product in zip(halves_of, products):
         here = hat[tokens, :]
         grad_hat = jnp.transpose(product) * small_row(small_ref, G1)
@@ -662,7 +679,7 @@
                   h_one, act_one, mixed_one, grad_one, grad_low, scaled_zero, inner_zero, pre_ds_zero,
                   prefix_grad, w_attn, w_out,
                   q_t, k_t, v_m, p_ref, pp_ref, inv_ref, scaled, inner, pre_ds, turned, k_m, v_t,
-                  dq, dk, dv, packed, sems):
+                  dq, dk, dv, packed, packed_v, sems):
     section = lax.axis_index("pipe")
     copies = Copies(sems)
     wait_all(
@@ -687,8 +704,9 @@
     prefix_back(w_attn.at[1], grad, q_t, low_one.at[1], pp_ref, inv_ref, mixed_one, scaled, inner, pre_ds, turned,
                 prefix_grad, 2 * PREFIX)
     attend_back(scaled, inner, pre_ds, q_t, k_t, v_m, low_one.at[0], p_ref, dq, dk, dv)
-    pack_grads(dq, dk, dv, cos, sin, packed)
-    norms_back(cot_ref, grad_one, scale, grad_two, packed, w_qkv[1], small_one, grad_one)
+    pack_grads(dq, dk, cos, sin, packed)
+    packed_v[...] = dv[...].astype(bf16)
+    norms_back(cot_ref, grad_one, scale, grad_two, packed, packed_v, w_qkv.at[1], small_one, grad_one)
     grad_low[...] = grad_one[...].astype(bf16)
 
     prefix_back(w_attn.at[0], grad_low[...], q0, low.at[1], pp0, inv0, mixed0, scaled_zero, inner_zero,
@@ -706,7 +724,8 @@
         ((D, SEQ), f32),
         ((D, SEQ), f32),
         ((D, SEQ), f32),
-        ((3 * D, SEQ), bf16),
+        ((2 * D, SEQ), bf16),
+        ((D, SEQ), bf16),
     )
     return call_kernel(
         middle_kernel, "middle", in_vmem(*arrays), vmem(MIDDLE_OUTS), scratch, 2, MIDDLE_MIB,
@@ -737,15 +756,15 @@
     )
 
 
-def heads_back_kernel(scaled, inner, pre_ds, q_t, k_t, v_m, low, p_ref, tables, packed, dq, dk, dv):
-    attend_back(scaled, inner, pre_ds, q_t, k_t, v_m, low.at[0], p_ref, dq, dk, dv)
-    pack_grads(dq, dk, dv, tables[:8, :], tables[8:, :], packed)
+def heads_back_kernel(scaled, inner, pre_ds, q_t, k_t, v_m, low, p_ref, tables, packed, dq, dk):
+    attend_back(scaled, inner, pre_ds, q_t, k_t, v_m, low.at[0], p_ref, dq, dk, None)
+    pack_grads(dq, dk, tables[:8, :], tables[8:, :], packed)
 
 
 def heads_back_call(*arrays):
     return call_kernel(
-        heads_back_kernel, "layer_zero_attention_back", in_vmem(*arrays), vmem([((3 * D, SEQ), bf16)]),
-        [((D, SEQ), f32)] * 3, 0, LATE_MIB, 10 * SEQ * SEQ * D,
+        heads_back_kernel, "layer_zero_attention_back", in_vmem(*arrays), vmem([((2 * D, SEQ), bf16)]),
+        [((D, SEQ), f32)] * 2, 0, LATE_MIB, 10 * SEQ * SEQ * D,
     )[0]
 
 
@@ -761,16 +780,18 @@
     return total
 
 
-def norms_kernel(x_ref, grad, two, packed, grad_one, small, w_qkv, keep, send, result, sems):
+def norms_kernel(x_ref, grad, two, packed, scaled, p_ref, grad_one, small, w_qkv, keep, send, result, packed_v,
+                 sems):
+    values_back(scaled, p_ref, packed_v)
     hat, scale = normalized(x_ref[...].astype(f32))
-    norms_back(grad, hat, scale, two, packed, w_qkv[0], small.at[0], result)
+    norms_back(grad, hat, scale, two, packed, packed_v, w_qkv.at[0], small.at[0], result)
     hand_over((result, grad_one), keep, send, sems)
 
 
 def norms_call(*arrays):
     return call_kernel(
         norms_kernel, "layer_zero_norms", in_vmem(*arrays), vmem([((SEQ, D), f32)] * 2),
-        [((SEQ, D), f32)], 2, LATE_MIB, 6 * SEQ * D * D,
+        [((SEQ, D), f32), ((D, SEQ), bf16)], 2, LATE_MIB, 6 * SEQ * D * D,
     )
 
 
@@ -803,6 +824,9 @@
     )
 
 
+QUARTER = D // 4
+
+
 def final_kernel(col_width, grads_ref, hidden, embed, wide, up_high, up_rest, *refs):
     results, (d_embed, d_up, d_up_b, d_out, d_out_b, sems) = refs[:5], refs[5:]
     section = lax.axis_index("pipe")
@@ -819,8 +843,11 @@
     grad_units = (both[:PAD] + both[PAD:])[:PREFIX]
     grad_pre = grad_units * (1.0 - units * units)
     d_up_b[...] = jnp.sum(grad_pre, axis=0, keepdims=True)
-    d_up[...] = stacked_dot(embed[...], grad_pre)
-    placed += [copies.start(d_up, results[1]), copies.start(d_up_b, results[2])]
+    for start in range(0, D, QUARTER):
+        rows = slice(start, start + QUARTER)
+        d_up[rows, :] = stacked_dot(embed[:, rows], grad_pre)
+        placed.append(copies.start(d_up.at[rows], results[1].at[rows]))
+    placed.append(copies.start(d_up_b, results[2]))
     column = section * (2 * D) + shard * col_width
     own_cols = jnp.zeros((PREFIX, col_width), f32)
     for part in range(4):
@@ -846,7 +873,7 @@
 
     shapes = [((PREFIX, D), f32), ((D, D), f32), ((1, D), f32), ((D, col_width), f32), ((1, col_width), f32)]
     return call_kernel(
-        body, "reparam", in_vmem(*arrays), [(pltpu.HBM, *pair) for pair in shapes], shapes, 5, LATE_MIB,
+        body, "reparam", in_vmem(*arrays), [(pltpu.HBM, *pair) for pair in shapes], shapes, 8, LATE_MIB,
         SEQ * D * D,
     )
 
@@ -927,7 +954,9 @@
         return dict(state, two=feed_back_call(state["grad_low"], slope_zero, w_in, w_out))
 
     def layer_zero_norms(state):
-        own, send = norms_call(x_zero, grad_low, state["two"], state["packed"], grad_one, small, w_qkv)
+        own, send = norms_call(
+            x_zero, grad_low, state["two"], state["packed"], scaled_zero, p0, grad_one, small, w_qkv
+        )
         return dict(state, grad_own=own, grad_send=send)
 
     def swap_grads(state):

time: 50.5 us -> 50.4 us (level)
  starting transfers between devices: 10.7 us -> 11.3 us
  transfers between devices with their start and end apart: 12 -> 12, of which waited for: 2 -> 1; matrix products, arithmetic and copies ran while one was open for 0% -> 0% of each run, Pallas kernels for 41% -> 41%
where the time goes in v10:
time: 50.4 us; the launch traced here: 50.2 us
  Pallas kernels  37.6 us (75%)
  starting transfers between devices  11.3 us (22%)
  between operations  1.01 us (2%)
    pallas_call x11, Pallas kernels, call_kernel(): pl.pallas_call(kernel, name=name, out_shape=[space(shape, dtype) for spac...  37.6 us
    ppermute x4, starting transfers between devices, local(): moved = lax.ppermute(prefix_grad.astype(bf16), axis, pairs)  8.96 us
    ppermute x7, starting transfers between devices, swapped(): return lax.ppermute(array_in, 'pipe', [(0, 1), (1, 0)])  2.17 us
  transfers between devices with their start and end apart: 12, of which 1 were waited for; matrix products, arithmetic and copies ran while one was open for 0% of the time, Pallas kernels for 41%

profile of v10, /device:TPU:0, one launch (start us, length us, event | category | flops | bytes accessed | tf_op | source)
XLA Modules:
  0.0 50.2 jit_solution(6480405860062700623)
XLA Ops:
  0.6 0.5 %collective-permute-start.1 = (bf16[1,512,1536]{2,1,0:T(8,128)(2,1)}, bf16[1,512,1536]{2,1,0:T(8,128)(2,1)S(1)}, u32[]{:S(2)}, u32[]{:S(2)}) collective-permute-start(bf16[1,512,1536]{2,1,0:T(8,128)(2,1)} %qkv_hbm.1), channel_id=1, source_target_pairs={{0,16},{16,0},{1,17},{17,1},{2,18},{18,2},{3,19},{19,3},{4,20},{20... | collective-permute-start | bytes 4718600 | tf_op jit(solution)/shard_map/ppermute | solution.py:882
  1.2 0.9 %small_parameters.1.own_small = f32[1,6656]{1,0:T(1,128)S(1)} custom-call(f32[1,512]{1,0:T(1,128)} %gain_one.1, f32[1,512]{1,0:T(1,128)} %shift_one.1, f32[1,512]{1,0:T(1,128)} %gain_two.1, f32[1,512]{1,0:T(1,128)} %shift_two.1, f32[1,512]{1,0:T(1,128)} %attn_b.1, f32[1,512]{1,0:T(1,128)} %out_b.1, f32[1,1536]{1,0:T(1,128)} %qkv_b.1, f32[1,2048]{1,0:T(1,128)} %in_b.1), custom_call_target="tpu_custom_call" | custom-call | flops 6656 | bytes 8388608 | tf_op jit(solution)/shard_map/small_parameters/pallas_call | solution.py:53
  2.0 0.1 collective-permute-start
  2.2 0.5 collective-permute-start.3
  2.6 0.1 collective-permute-start.2
  2.7 0.4 collective-permute-start.4
  3.1 2.7 %opening.1 = (bf16[512,512]{1,0:T(8,128)(2,1)S(1)}, f32[512,512]{1,0:T(8,128)S(1)}, f32[1152,128]{1,0:T(8,128)S(1)}, bf16[2,32,512]{2,1,0:T(8,128)(2,1)S(1)}, f3...) custom-call(bf16[2,1,512,512]{3,2,1,0:T(8,128)(2,1)} %x_hbm.1, ...), custom_call_target="tpu_custom_call" | custom-call | flops 251658240 | bytes 8388608 | tf_op jit(solution)/shard_map/opening/pallas_call | solution.py:53
  5.9 3.6 %first_attention.1 = (bf16[512,512]{1,0:T(8,128)(2,1)S(1)}, bf16[512,512]{1,0:T(8,128)(2,1)S(1)}, bf16[512,512]{1,0:T(8,128)(2,1)S(1)}, bf16[4,1152,256]{2,1,0:T...) custom-call(f32[1,6656]{1,0:T(1,128)S(1)} %small_parameters.1.own_sm, ...), custom_call_target="tpu_custom_call" | custom-call | flops 80530636800 | bytes 8388608 | tf_op jit(solution)/shard_map/first_attention/pallas_call | solution.py:53
  9.5 2.6 %first_feed.1 = (bf16[512,2048]{1,0:T(8,128)(2,1)S(1)}, bf16[512,2048]{1,0:T(8,128)(2,1)S(1)}, bf16[2,512,2048]{2,1,0:T(8,128)(2,1)S(1)}, bf16[2,32,512]{2,1,0:T(8,128)(2,1)S(1)}, bf16[512,1024]{1,0:T(8,128)(2,1)S(1)}) custom-call(bf16[512,512]{1,0:T(8,128)(2,1)S(1)} %get-tuple-element.114.two, ...), custom_call_target="tpu_custom_call", output_to_operand_aliasing={{2}: (3, {})} | custom-call | flops 1073741824 | bytes 8388608 | tf_op jit(solution)/shard_map/first_feed/pallas_call | solution.py:53
  12.1 15.1 %middle.1 = (bf16[512,512]{1,0:T(8,128)(2,1)S(1)}, bf16[512,2048]{1,0:T(8,128)(2,1)S(1)}, bf16[512,512]{1,0:T(8,128)(2,1)S(1)}, f32[512,512]{1,0:T(8,128)S(1)}, ...) custom-call(bf16[2,512,512]{2,1,0:T(8,128)(2,1)S(1)} %get-tuple-elem, ...), custom_call_target="tpu_custom_call", output_to_operand_aliasing={{9}: (0, {}), {10}: (1, {})} | custom-call | flops 16106127360 | bytes 8388608 | tf_op jit(solution)/shard_map/middle/pallas_call | solution.py:53
  27.2 0.1 collective-permute-start.5
  27.4 1.6 %layer_one_out.1 = (bf16[512,512]{1,0:T(8,128)(2,1)S(1)}, bf16[512,512]{1,0:T(8,128)(2,1)S(1)}) custom-call(bf16[512,512]{1,0:T(8,128)(2,1)S(1)} %get-tuple-element.128.h_one, bf16[512,2048]{1,0:T(8,128)(2,1)S(1)} %get-tuple-element.129.act, bf16[512,512]{1,0:T(8,128)(2,1)S(1)} %get-tuple-element.130.mixed, f32[2,1,6656]{2,1,0:T(1,128)S(1)} %get-tuple-element.112.small, ...), custom_call_target="tpu_custom_call" | custom-call | flops 1342177280 | bytes 8388608 | tf_op jit(solution)/shard_map/layer_one_out/pallas_call | solution.py:53
  29.0 0.5 collective-permute-start.7
  29.6 2.6 %collective-permute-start.6 = (bf16[40,512]{1,0:T(8,128)(2,1)S(1)}, bf16[40,512]{1,0:T(8,128)(2,1)S(1)}, u32[]{:S(2)}, u32[]{:S(2)}) collective-permute-start(bf16[40,512]{1,0:T(8,128)(2,1)S(1)} %get-tuple-element.197), channel_id=1, source_target_pairs={{0,1},{1,0},{2,3},{3,2},{4,5},{5,4},{6,7},{7,6},{8,9},{9,8},{10,11... | collective-permute-start | bytes 122888 | tf_op jit(solution)/shard_map/ppermute | solution.py:976
  32.2 2.0 %layer_zero_attention_back.1.packed = bf16[1024,512]{1,0:T(8,128)(2,1)S(1)} custom-call(bf16[512,512]{1,0:T(8,128)(2,1)S(1)} %get-tuple-element.142.scaled, f32[8,512]{1,0:T(8,128)S(1)} %get-tuple-element.143.inner, bf16[4,32,512]{2,1,0:T(8,128)(2,1)S(1)} %get-tuple-element.144.pre_ds, bf16[512,512]{1,0:T(8,128)(2,1)S(1)} %get-tuple-element.108.q0.q_t, ...), custom_call_target="tpu_custom_call" | custom-call | flops 1342177280 | bytes 8388608 | tf_op jit(solution)/shard_map/layer_zero_attention_back/pallas_call | solution.py:53
  34.2 0.2 collective-permute-done.6
  34.4 1.9 %collective-permute-start.8 = (bf16[40,512]{1,0:T(8,128)(2,1)S(1)}, bf16[40,512]{1,0:T(8,128)(2,1)S(1)}, u32[]{:S(2)}, u32[]{:S(2)}) collective-permute-start(bf16[40,512]{1,0:T(8,128)(2,1)S(1)} %get-tuple-element.195), channel_id=1, source_target_pairs={{0,2},{1,3},{2,0},{3,1},{4,6},{5,7},{6,4},{7,5},{8,10},{9,11},{10,... | collective-permute-start | bytes 122888 | tf_op jit(solution)/shard_map/ppermute | solution.py:976
  36.3 2.4 %layer_zero_feed_back.1.two = f32[512,512]{1,0:T(8,128)S(1)} custom-call(bf16[512,512]{1,0:T(8,128)(2,1)S(1)} %get-tuple-element.152.grad, bf16[512,2048]{1,0:T(8,128)(2,1)S(1)} %get-tuple-element.154.slope, bf16[2,512,2048]{2,1,0:T(8,128)(2,1)S(1)} %get-tuple-element.120.w_in, bf16[2,2048,512]{2,1,0:T(8,128)(2,1)S(1)} %get-tuple-element.132.w_out), custom_call_target="tpu_custom_call" | custom-call | flops 2147483648 | bytes 8388608 | tf_op jit(solution)/shard_map/layer_zero_feed_back/pallas_call | solution.py:53
  38.7 1.7 %collective-permute-start.9 = (bf16[40,512]{1,0:T(8,128)(2,1)S(1)}, bf16[40,512]{1,0:T(8,128)(2,1)S(1)}, u32[]{:S(2)}, u32[]{:S(2)}) collective-permute-start(bf16[40,512]{1,0:T(8,128)(2,1)S(1)} %get-tuple-element.193), channel_id=1, source_target_pairs={{0,4},{4,0},{8,12},{12,8},{1,5},{5,1},{9,13},{13,9},{2,6},{6,2},{1... | collective-permute-start | bytes 122888 | tf_op jit(solution)/shard_map/ppermute | solution.py:976
  40.4 2.5 %layer_zero_norms.1 = (f32[512,512]{1,0:T(8,128)S(1)}, f32[512,512]{1,0:T(8,128)S(1)}) custom-call(bf16[512,512]{1,0:T(8,128)(2,1)S(1)} %get-tuple-element.124.x_ref, bf16[512,512]{1,0:T(8,128)(2,1)S(1)} %get-tuple-element.152.grad, f32[512,512]{1,0:T(8,128)S(1)} %layer_zero_feed_back.1.two, bf16[1024,512]{1,0:T(8,128)(2,1)S(1)} %layer_zero_attention_back.1.packed, ...), custom_call_target="tpu_custom_call" | custom-call | flops 805306368 | bytes 8388608 | tf_op jit(solution)/shard_map/layer_zero_norms/pallas_call | solution.py:53
  43.0 0.1 collective-permute-start.11
  43.1 2.7 %collective-permute-start.10 = (bf16[40,512]{1,0:T(8,128)(2,1)S(1)}, bf16[40,512]{1,0:T(8,128)(2,1)S(1)}, u32[]{:S(2)}, u32[]{:S(2)}) collective-permute-start(bf16[40,512]{1,0:T(8,128)(2,1)S(1)} %get-tuple-element.191), channel_id=1, source_target_pairs={{0,8},{4,12},{8,0},{12,4},{1,9},{5,13},{9,1},{13,5},{2,10},{6,14},... | collective-permute-start | bytes 122888 | tf_op jit(solution)/shard_map/ppermute | solution.py:976
  45.8 2.4 %place_outputs.1 = (bf16[1,2,1,512,512]{4,3,2,1,0:T(8,128)(2,1)}, f32[1,2,1,512,512]{4,3,2,1,0:T(8,128)}, bf16[2048,512]{1,0:T(8,128)(2,1)S(1)}, bf16[512,512]{1,0:T(8,128)(2,1)S(1)}, bf16[512,512]{1,0:T(8,128)(2,1)S(1)}) custom-call(bf16[512,512]{1,0:T(8,128)(2,1)S(1)} %get-tuple-element.166.act, bf16[512,512]{1,0:T(8,128)(2,1)S(1)} %collective-permute-done.7.act_other, ...), custom_call_target="tpu_custom_call" | custom-call | flops 524288 | bytes 8388608 | tf_op jit(solution)/shard_map/place_outputs/pallas_call | solution.py:53
  48.2 1.9 %reparam.1 = (f32[10,512]{1,0:T(8,128)}, f32[512,512]{1,0:T(8,128)}, f32[1,512]{1,0:T(1,128)}, f32[512,256]{1,0:T(8,128)}, f32[1,256]{1,0:T(1,128)}) custom-call(f32[40,512]{1,0:T(8,128)S(1)} %convert_add_fusion.refs_0_, f32[10,512]{1,0:T(8,128)S(1)} %get-tuple-element.117.hidden.refs_1_, f32[10,512]{1,0:T(8,128)S(1)} %copy-done, ...), custom_call_target="tpu_custom_call" | custom-call | flops 134217728 | bytes 8388608 | tf_op jit(solution)/shard_map/reparam/pallas_call | solution.py:53
  (18 shorter events, 0.1 us)
Async XLA Ops:
  0.6 5.2 %collective-permute-start.1 = (bf16[1,512,1536]{2,1,0:T(8,128)(2,1)}, bf16[1,512,1536]{2,1,0:T(8,128)(2,1)S(1)}, u32[]{:S(2)}, u32[]{:S(2)}) collective-permute-start(bf16[1,512,1536]{2,1,0:T(8,128)(2,1)} %qkv_hbm.1), channel_id=1, source_target_pairs={{0,16},{16,0},{1,17},{17,1},{2,18},{18,2},{3,19},{19,3},{4,20},{20... | collective-permute-start | bytes 4718600 | tf_op jit(solution)/shard_map/ppermute | solution.py:882
  2.0 3.8 %collective-permute-start = (f32[1,6656]{1,0:T(1,128)S(1)}, f32[1,6656]{1,0:T(1,128)S(1)}, u32[]{:S(2)}, u32[]{:S(2)}) collective-permute-start(f32[1,6656]{1,0:T(1,128)S(1)} %small_parameters.1.own_small), channel_id=1, source_target_pairs={{0,16},{16,0},{1,17},{17,1},{2,18},{18,2},{3,19},{19,3},{4,20},{20... | collective-permute-start | bytes 79880 | tf_op jit(solution)/shard_map/ppermute | solution.py:882
  2.2 9.9 %collective-permute-start.3 = (bf16[1,512,512]{2,1,0:T(8,128)(2,1)}, bf16[1,512,512]{2,1,0:T(8,128)(2,1)S(1)}, u32[]{:S(2)}, u32[]{:S(2)}) collective-permute-start(bf16[1,512,512]{2,1,0:T(8,128)(2,1)} %attn_hbm.1), channel_id=1, source_target_pairs={{0,16},{16,0},{1,17},{17,1},{2,18},{18,2},{3,19},{19,3},{4,20},{20... | collective-permute-start | bytes 1572872 | tf_op jit(solution)/shard_map/ppermute | solution.py:882
  2.6 6.8 %collective-permute-start.2 = (bf16[1,512,2048]{2,1,0:T(8,128)(2,1)}, bf16[1,512,2048]{2,1,0:T(8,128)(2,1)S(1)}, u32[]{:S(2)}, u32[]{:S(2)}) collective-permute-start(bf16[1,512,2048]{2,1,0:T(8,128)(2,1)} %ff_in_hbm.1), channel_id=1, source_target_pairs={{0,16},{16,0},{1,17},{17,1},{2,18},{18,2},{3,19},{19,3},{4,20},{20... | collective-permute-start | bytes 6291464 | tf_op jit(solution)/shard_map/ppermute | solution.py:882
  2.7 9.4 %collective-permute-start.4 = (bf16[1,2048,512]{2,1,0:T(8,128)(2,1)}, bf16[1,2048,512]{2,1,0:T(8,128)(2,1)S(1)}, u32[]{:S(2)}, u32[]{:S(2)}) collective-permute-start(bf16[1,2048,512]{2,1,0:T(8,128)(2,1)} %ff_out_hbm.1), channel_id=1, source_target_pairs={{0,16},{16,0},{1,17},{17,1},{2,18},{18,2},{3,19},{19,3},{4,20},{20... | collective-permute-start | bytes 6291464 | tf_op jit(solution)/shard_map/ppermute | solution.py:882
  27.2 1.8 %collective-permute-start.5 = (f32[40,512]{1,0:T(8,128)S(1)}, f32[40,512]{1,0:T(8,128)S(1)}, u32[]{:S(2)}, u32[]{:S(2)}) collective-permute-start(f32[40,512]{1,0:T(8,128)S(1)} %get-tuple-element.137), channel_id=1, source_target_pairs={{0,16},{16,0},{1,17},{17,1},{2,18},{18,2},{3,19},{19,3},{4,20},{20... | collective-permute-start | bytes 245768 | tf_op jit(solution)/shard_map/ppermute | solution.py:973
  29.0 5.3 %collective-permute-start.7 = (bf16[512,512]{1,0:T(8,128)(2,1)S(1)}, bf16[512,512]{1,0:T(8,128)(2,1)S(1)}, u32[]{:S(2)}, u32[]{:S(2)}) collective-permute-start(bf16[512,512]{1,0:T(8,128)(2,1)S(1)} %get-tuple-element.139), channel_id=1, source_target_pairs={{0,16},{16,0},{1,17},{17,1},{2,18},{18,2},{3,19},{19,3},{4,20},{20... | collective-permute-start | bytes 1572872 | tf_op jit(solution)/shard_map/ppermute | solution.py:882
  29.6 4.8 %collective-permute-start.6 = (bf16[40,512]{1,0:T(8,128)(2,1)S(1)}, bf16[40,512]{1,0:T(8,128)(2,1)S(1)}, u32[]{:S(2)}, u32[]{:S(2)}) collective-permute-start(bf16[40,512]{1,0:T(8,128)(2,1)S(1)} %get-tuple-element.197), channel_id=1, source_target_pairs={{0,1},{1,0},{2,3},{3,2},{4,5},{5,4},{6,7},{7,6},{8,9},{9,8},{10,11... | collective-permute-start | bytes 122888 | tf_op jit(solution)/shard_map/ppermute | solution.py:976
  34.4 4.3 %collective-permute-start.8 = (bf16[40,512]{1,0:T(8,128)(2,1)S(1)}, bf16[40,512]{1,0:T(8,128)(2,1)S(1)}, u32[]{:S(2)}, u32[]{:S(2)}) collective-permute-start(bf16[40,512]{1,0:T(8,128)(2,1)S(1)} %get-tuple-element.195), channel_id=1, source_target_pairs={{0,2},{1,3},{2,0},{3,1},{4,6},{5,7},{6,4},{7,5},{8,10},{9,11},{10,... | collective-permute-start | bytes 122888 | tf_op jit(solution)/shard_map/ppermute | solution.py:976
  38.7 4.3 %collective-permute-start.9 = (bf16[40,512]{1,0:T(8,128)(2,1)S(1)}, bf16[40,512]{1,0:T(8,128)(2,1)S(1)}, u32[]{:S(2)}, u32[]{:S(2)}) collective-permute-start(bf16[40,512]{1,0:T(8,128)(2,1)S(1)} %get-tuple-element.193), channel_id=1, source_target_pairs={{0,4},{4,0},{8,12},{12,8},{1,5},{5,1},{9,13},{13,9},{2,6},{6,2},{1... | collective-permute-start | bytes 122888 | tf_op jit(solution)/shard_map/ppermute | solution.py:976
  43.0 2.8 %collective-permute-start.11 = (f32[512,512]{1,0:T(8,128)S(1)}, f32[512,512]{1,0:T(8,128)S(1)}, u32[]{:S(2)}, u32[]{:S(2)}) collective-permute-start(f32[512,512]{1,0:T(8,128)S(1)} %get-tuple-element.169), channel_id=1, source_target_pairs={{0,16},{16,0},{1,17},{17,1},{2,18},{18,2},{3,19},{19,3},{4,20},{20... | collective-permute-start | bytes 3145736 | tf_op jit(solution)/shard_map/ppermute | solution.py:882
  43.1 5.0 %collective-permute-start.10 = (bf16[40,512]{1,0:T(8,128)(2,1)S(1)}, bf16[40,512]{1,0:T(8,128)(2,1)S(1)}, u32[]{:S(2)}, u32[]{:S(2)}) collective-permute-start(bf16[40,512]{1,0:T(8,128)(2,1)S(1)} %get-tuple-element.191), channel_id=1, source_target_pairs={{0,8},{4,12},{8,0},{12,4},{1,9},{5,13},{9,1},{13,5},{2,10},{6,14},... | collective-permute-start | bytes 122888 | tf_op jit(solution)/shard_map/ppermute | solution.py:976
  45.8 2.4 %copy-start = (f32[10,512]{1,0:T(8,128)S(1)}, f32[10,512]{1,0:T(8,128)}, u32[]{:S(2)}) copy-start(f32[10,512]{1,0:T(8,128)} %refs_2_) | copy-start | bytes 61444
